TPU v7x, 128 devices: a whole 4x4x4 slice. The times are simulated.
128 devices in a mesh: wide: 16 (over y_lo, z, core), narrow: 8 (over y_hi, x).
Axes of the slice: x: 4, y: 4 (y_hi: 2, y_lo: 2; y = y_hi * 2 + y_lo), z: 4, core: 2. Of those that a mesh axis runs over, the one named last changes fastest.
Arguments:
- coeffs: bfloat16 [1, 2048, 16, 2048], P(None, 'wide', None, 'narrow'), may hold values from -6 to 6
- ham_one: bfloat16 [2048, 2048], replicated, may hold values from -0.125 to 0.125
- grid_one: bfloat16 [2048, 2048], replicated, may hold values from -0.125 to 0.125
- ham_two: bfloat16 [2048, 2048], P('wide'), may hold values from -0.125 to 0.125
- grid_two: bfloat16 [2048, 2048], P('wide'), may hold values from -0.125 to 0.125
- pair_potential: float32 [2048, 2048], P(None, ('wide', 'narrow')), may hold values from 0.1 to 3
- third_energy: float32 [16], replicated, may hold values from 0.5 to 3
Outputs:
- result: bfloat16 [1, 2048, 16, 2048], P(None, ('wide', 'narrow'))
All inputs are finite; a program needn't handle non-finite values.
Results may differ from a plain program's by a relative error of at most 0.0055.
Values may be sent and summed in bfloat16 or wider, within the bound.
No kernel may reach another device: no remote copies, remote signals or barrier semaphores. Data moves between devices by JAX's collectives and lax.ppermute only.
A program may use at most 256 MiB of HBM per device.

v0:
```python
import jax
import jax.numpy as jnp
from jax import lax
from jax.sharding import PartitionSpec as P


def right_mul(left, matrix):
    return lax.dot_general(
        left, matrix, (((1,), (1,)), ((), ())), preferred_element_type=jnp.float32
    )


def order_columns(matrix, n_wide, n_narrow):
    rows = matrix.shape[0]
    count = matrix.shape[1] // (n_wide * n_narrow)
    viewed = matrix.reshape(rows, n_wide, n_narrow, count)
    return viewed.transpose(0, 2, 1, 3).reshape(rows, matrix.shape[1])


def order_rows(matrix, n_wide, n_narrow):
    cols = matrix.shape[1]
    count = matrix.shape[0] // (n_wide * n_narrow)
    viewed = matrix.reshape(n_wide, n_narrow, count, cols)
    return viewed.transpose(1, 0, 2, 3).reshape(matrix.shape[0], cols)


def point_major(tensor):
    dims = tensor.shape
    return jnp.swapaxes(tensor, 2, 3).reshape(dims[0], dims[1], dims[2] * dims[3])


def state_major(tensor, states):
    dims = tensor.shape
    points = dims[2] // states
    return jnp.swapaxes(tensor.reshape(dims[0], dims[1], points, states), 2, 3)


def on_device(coeffs, ham_one, grid_one, ham_two, grid_two, pair_potential, third_energy):
    n_narrow = lax.axis_size("narrow")
    n_wide = lax.axis_size("wide")
    rowwise = lax.all_to_all(coeffs, "narrow", split_axis=1, concat_axis=3, tiled=True)
    shape = rowwise.shape
    states = shape[2]
    flat = rowwise.reshape(-1, shape[3])
    full_ham, full_grid = (
        lax.all_gather(ham_two, "wide", axis=0, tiled=True),
        lax.all_gather(grid_two, "wide", axis=0, tiled=True),
    )
    applied = right_mul(flat, full_ham)
    forward = right_mul(flat, full_grid).astype(jnp.bfloat16)
    carried = (point_major(rowwise), point_major(forward.reshape(shape)))
    middle = (
        lax.all_to_all(carried[0], "wide", split_axis=2, concat_axis=1, tiled=True),
        lax.all_to_all(carried[1], "wide", split_axis=2, concat_axis=1, tiled=True),
    )
    full_c, full_g = (
        lax.all_to_all(middle[0], "narrow", split_axis=2, concat_axis=1, tiled=True),
        lax.all_to_all(middle[1], "narrow", split_axis=2, concat_axis=1, tiled=True),
    )
    ham_used = order_rows(order_columns(ham_one, n_wide, n_narrow), n_wide, n_narrow)
    grid_used = order_columns(grid_one, n_wide, n_narrow)
    across = jnp.einsum("ai,vic->vac", ham_used, full_c, preferred_element_type=jnp.float32).astype(
        jnp.bfloat16
    )
    grid_vals = jnp.einsum("ai,vic->vac", grid_used, full_g, preferred_element_type=jnp.float32)
    potential = jnp.repeat(pair_potential, states, axis=1)
    weighted = (grid_vals * potential[None, :, :]).astype(jnp.bfloat16)
    back_one = jnp.einsum(
        "ai,vac->vic", grid_used, weighted, preferred_element_type=jnp.float32
    ).astype(jnp.bfloat16)
    middle_back = (
        lax.all_to_all(across, "narrow", split_axis=1, concat_axis=2, tiled=True),
        lax.all_to_all(back_one, "narrow", split_axis=1, concat_axis=2, tiled=True),
    )
    across_rows, back_rows = (
        lax.all_to_all(middle_back[0], "wide", split_axis=1, concat_axis=2, tiled=True),
        lax.all_to_all(middle_back[1], "wide", split_axis=1, concat_axis=2, tiled=True),
    )
    back_flat = state_major(back_rows, states).reshape(-1, shape[3])
    across_flat = state_major(across_rows, states).reshape(-1, shape[3])
    back_two = jnp.dot(back_flat, full_grid, preferred_element_type=jnp.float32)
    energy = (third_energy[None, None, :, None] * rowwise.astype(jnp.float32)).reshape(-1, shape[3])
    total = applied + across_flat.astype(jnp.float32) + back_two + energy
    return total.astype(jnp.bfloat16).reshape(shape)


def solution(mesh):
    return jax.shard_map(
        on_device,
        mesh=mesh,
        in_specs=(
            P(None, "wide", None, "narrow"),
            P(),
            P(),
            P("wide", None),
            P("wide", None),
            P(None, ("wide", "narrow")),
            P(),
        ),
        out_specs=P(None, ("wide", "narrow"), None, None),
        check_vma=False,
    )
```

profile of v0, /device:TPU:1, one launch (start us, length us, event | category | flops | bytes accessed | tf_op | source)
XLA Modules:
  0.0 1135.0 jit_solution(713798827898305148)
XLA Ops:
  8.0 23.8 %all_to_all.147 = bf16[1,128,16,256]{3,2,0,1:T(8,128)(2,1)S(1)} all-to-all(bf16[1,128,16,256]{3,2,0,1:T(8,128)(2,1)} %bitcast.175), channel_id=1, replica_groups=mesh['wide'=16,'narrow'=8] {'narrow'}, dimensions={1} | all-to-all | bytes 2097152 | tf_op jit(solution)/shard_map/all_to_all | solution.py:41
  32.4 5.9 copy.71
  38.3 18.1 %reshape.69 = bf16[1,16,32768]{2,1,0:T(8,128)(2,1)S(1)} reshape(bf16[1,16,2048,16]{3,2,1,0:T(8,128)(2,1)} %bitcast.138) | data formatting | bytes 2097152 | tf_op jit(solution)/shard_map/reshape | solution.py:29
  56.4 25.1 %copy.72 = bf16[1,16,32768]{1,0,2:T(2,128)(2,1)} copy(bf16[1,16,32768]{2,1,0:T(8,128)(2,1)S(1)} %reshape.69) | data formatting | bytes 2097152 | tf_op jit(solution)/shard_map/reshape | solution.py:29
  82.1 179.3 %reduce = bf16[32768,16]{1,0:T(8,128)(2,1)} reduce(bf16[32768,1,16]{2,1,0:T(2,128)(2,1)} %bitcast.130, bf16[]{:T(256)} %broadcast.6), dimensions={1}, to_apply=%bitcast.100.reduce_sub_computation | reduce | bytes 2097154
  261.4 10.4 reshape.85
  271.9 22.6 %all_to_all.148 = bf16[16,2,16384]{2,1,0:T(2,128)(2,1)S(1)} all-to-all(bf16[16,2,16384]{2,1,0:T(2,128)(2,1)S(1)} %reshape.85), channel_id=1, replica_groups=mesh['wide'=16,'narrow'=8] {'wide'}, dimensions={0} | all-to-all | bytes 2097152 | tf_op jit(solution)/shard_map/all_to_all | solution.py:53
  294.4 14.1 %reshape.86 = bf16[32768,1,16]{2,1,0:T(2,128)(2,1)} reshape(bf16[16,2,16384]{2,1,0:T(2,128)(2,1)S(1)} %all_to_all.148) | data formatting | bytes 2097152
  308.5 29.6 %copy.73 = bf16[1,16,32768]{2,1,0:T(8,128)(2,1)S(1)} copy(bf16[1,16,32768]{1,0,2:T(2,128)(2,1)} %bitcast.131) | data formatting | bytes 2097152 | tf_op jit(solution)/shard_map/all_to_all | solution.py:53
  340.4 4.6 copy.75
  345.0 11.6 %reduce.1 = bf16[2048,256]{1,0:T(8,128)(2,1)} reduce(bf16[2048,1,256]{2,1,0:T(2,128)(2,1)S(1)} %bitcast.151, bf16[]{:T(256)} %broadcast.6), dimensions={1}, to_apply=%bitcast.102.reduce_sub_computation | reduce | bytes 2097154
  363.4 6.1 convolution_convert_fusion.1
  369.5 5.8 copy.86
  375.4 18.0 %reshape.74 = bf16[1,16,32768]{2,1,0:T(8,128)(2,1)S(1)} reshape(bf16[1,16,2048,16]{3,2,1,0:T(8,128)(2,1)} %bitcast.136) | data formatting | bytes 2097152 | tf_op jit(solution)/shard_map/reshape | solution.py:29
  393.4 25.5 %copy.87 = bf16[1,16,32768]{1,0,2:T(2,128)(2,1)} copy(bf16[1,16,32768]{2,1,0:T(8,128)(2,1)S(1)} %reshape.74) | data formatting | bytes 2097152 | tf_op jit(solution)/shard_map/reshape | solution.py:29
  418.9 179.2 %reduce.4 = bf16[32768,16]{1,0:T(8,128)(2,1)} reduce(bf16[32768,1,16]{2,1,0:T(2,128)(2,1)} %bitcast.132, bf16[]{:T(256)} %broadcast.6), dimensions={1}, to_apply=%bitcast.108.reduce_sub_computation | reduce | bytes 2097154
  598.0 11.2 reshape.93
  609.3 5.8 all-to-all-start.5
  615.1 12.3 %copy.77 = bf16[2048,2048]{0,1:T(8,128)(2,1)} copy(bf16[2048,2048]{1,0:T(8,128)(2,1)} %param.8) | data formatting | bytes 16777216 | tf_op args[1]
  627.5 88.2 %copy.78 = bf16[2048,8,16,16]{3,2,1,0:T(8,128)(2,1)} copy(bf16[2048,8,16,16]{0,3,1,2:T(8,128)(2,1)} %bitcast.135) | data formatting | bytes 16777216 | tf_op jit(solution)/shard_map/transpose | solution.py:17
  715.6 113.4 %reshape_reshape.3 = bf16[16,8,16,2048]{3,2,1,0:T(8,128)(2,1)} reshape(bf16[2048,8,16,16]{3,2,1,0:T(8,128)(2,1)} %copy.78) | data formatting | bytes 16777216 | tf_op jit(solution)/shard_map/reshape;reshape | solution.py:23
  829.0 8.3 copy.79
  839.0 5.8 fusion.4
  846.5 10.6 reduce.2
  858.2 7.2 all-to-all-start.3
  865.4 15.4 %reshape.94 = bf16[32768,1,16]{2,1,0:T(2,128)(2,1)} reshape(bf16[16,2,16384]{2,1,0:T(2,128)(2,1)} %all-to-all-done.5) | data formatting | bytes 2097152
  880.8 29.6 %copy.88 = bf16[1,16,32768]{2,1,0:T(8,128)(2,1)S(1)} copy(bf16[1,16,32768]{1,0,2:T(2,128)(2,1)} %bitcast.133) | data formatting | bytes 2097152 | tf_op jit(solution)/shard_map/all_to_all | solution.py:54
  917.4 11.7 %reduce.5 = bf16[2048,256]{1,0:T(8,128)(2,1)} reduce(bf16[2048,1,256]{2,1,0:T(2,128)(2,1)S(1)} %bitcast.153, bf16[]{:T(256)} %broadcast.6), dimensions={1}, to_apply=%bitcast.110.reduce_sub_computation | reduce | bytes 2097154
  931.1 6.6 all-to-all-start.6
  937.8 12.3 %copy.92 = bf16[2048,2048]{0,1:T(8,128)(2,1)} copy(bf16[2048,2048]{1,0:T(8,128)(2,1)} %param.9) | data formatting | bytes 16777216 | tf_op args[2]
  950.1 8.3 copy.93
  960.9 4.7 copy.82
  965.6 6.9 reduce.3
  974.1 6.5 all-to-all-start.4
  988.7 11.6 %fusion.5 = bf16[1,2048,256]{1,2,0:T(8,128)(2,1)} fusion(bf16[2048,2048]{0,1:T(8,128)(2,1)} %bitcast.148, f32[1,2048,256]{1,2,0:T(8,128)S(1)} %bitcast.172, bf16[2048,256]{1,0:T(8,128)(2,1)} %bitcast.179), kind=kOutput, calls=%fused_computation.11 | convolution fusion | flops 4296540160 | bytes 12582912 | tf_op jit(solution)/shard_map/ai,vac->vic/dot_general | solution.py:68
  1000.2 4.6 copy.94
  1004.9 11.7 %reduce.6 = bf16[2048,256]{1,0:T(8,128)(2,1)} reduce(bf16[2048,1,256]{2,1,0:T(2,128)(2,1)S(1)} %bitcast.155, bf16[]{:T(256)} %broadcast.6), dimensions={1}, to_apply=%bitcast.112.reduce_sub_computation | reduce | bytes 2097154
  1018.7 7.8 all-to-all-start.7
  1028.2 15.7 %all-to-all-done.7 = bf16[8,2,32768]{2,1,0:T(2,128)(2,1)} async-done(((bf16[8,2,32768]{2,1,0:T(2,128)(2,1)}), bf16[8,2,32768]{2,1,0:T(2,128)(2,1)}, u32[]{:S(2)}, u32[]{:S(2)}) %all-to-all-start.7) | async-done | bytes 1048608 | tf_op jit(solution)/shard_map/all_to_all | solution.py:73
  1051.7 4.7 copy.96
  1056.4 7.8 reduce.7
  1066.9 5.8 all-to-all-start.8
  1074.2 9.0 reshape.83
  1083.2 9.8 copy.85
  1093.1 7.1 convolution_add_fusion.1
  1105.7 8.2 reshape.79
  1113.9 6.7 copy.98
  1120.6 7.3 fusion.3
  (60 shorter events, 58.4 us)
Async XLA Ops:
  6.5 356.9 %all-gather.5.cloned.1.call-start = ((), (), s32[]{:S(2)}) async-start(), calls=%async_computation.10 | async-start | bytes 8912896 | tf_op jit(solution)/shard_map/all_gather | solution.py:47
  7.3 1085.8 %all-gather.3.cloned.1.call-start = ((), (), s32[]{:S(2)}) async-start(), calls=%async_computation.9 | async-start | bytes 8912896 | tf_op jit(solution)/shard_map/all_gather | solution.py:46
  358.8 250.5 %all-to-all-start.2 = ((bf16[8,2,32768]{2,1,0:T(2,128)(2,1)}), bf16[8,2,32768]{2,1,0:T(2,128)(2,1)S(1)}, u32[]{:S(2)}, u32[]{:S(2)}) async-start(bf16[8,2,32768]{2,1,0:T(2,128)(2,1)} %reshape.87), calls=%async_computation.2 | async-start | bytes 2097152 | tf_op jit(solution)/shard_map/all_to_all | solution.py:57
  363.4 12.0 %copy-start = (bf16[32,8,8,256]{3,1,2,0:T(8,128)(2,1)}, bf16[32,8,8,256]{3,1,2,0:T(8,128)(2,1)S(1)}, u32[]{:S(2)}) copy-start(bf16[32,8,8,256]{3,1,2,0:T(8,128)(2,1)S(1)} %copy.104) | copy-start | bytes 3145732
  609.3 249.0 %all-to-all-start.5 = ((bf16[16,2,16384]{2,1,0:T(2,128)(2,1)}), bf16[16,2,16384]{2,1,0:T(2,128)(2,1)}, u32[]{:S(2)}, u32[]{:S(2)}) async-start(bf16[16,2,16384]{2,1,0:T(2,128)(2,1)} %reshape.93), calls=%async_computation.5 | async-start | bytes 2097152 | tf_op jit(solution)/shard_map/all_to_all | solution.py:54
  858.2 72.9 %all-to-all-start.3 = ((bf16[8,2,32768]{2,1,0:T(2,128)(2,1)}), bf16[8,2,32768]{2,1,0:T(2,128)(2,1)S(1)}, u32[]{:S(2)}, u32[]{:S(2)}) async-start(bf16[8,2,32768]{2,1,0:T(2,128)(2,1)} %reshape.89), calls=%async_computation.3 | async-start | bytes 2097152 | tf_op jit(solution)/shard_map/all_to_all | solution.py:72
  931.1 43.0 %all-to-all-start.6 = ((bf16[8,2,32768]{2,1,0:T(2,128)(2,1)}), bf16[8,2,32768]{2,1,0:T(2,128)(2,1)}, u32[]{:S(2)}, u32[]{:S(2)}) async-start(bf16[8,2,32768]{2,1,0:T(2,128)(2,1)} %reshape.95), calls=%async_computation.6 | async-start | bytes 2097152 | tf_op jit(solution)/shard_map/all_to_all | solution.py:58
  965.6 22.8 %copy-start.2 = (f32[2048,16]{0,1:T(8,128)S(1)}, f32[2048,16]{0,1:T(8,128)}, u32[]{:S(2)}) copy-start(f32[2048,16]{0,1:T(8,128)} %param.12) | copy-start | bytes 393220
  974.1 44.5 %all-to-all-start.4 = ((bf16[16,2,16384]{2,1,0:T(2,128)(2,1)}), bf16[16,2,16384]{2,1,0:T(2,128)(2,1)S(1)}, u32[]{:S(2)}, u32[]{:S(2)}) async-start(bf16[16,2,16384]{2,1,0:T(2,128)(2,1)} %reshape.91), calls=%async_computation.4 | async-start | bytes 2097152 | tf_op jit(solution)/shard_map/all_to_all | solution.py:76
  1000.2 26.2 %copy-start.3 = (f32[16]{0:T(128)S(1)}, f32[16]{0:T(128)}, u32[]{:S(2)}) copy-start(f32[16]{0:T(128)} %param.13) | copy-start | bytes 196
  1018.7 25.3 %all-to-all-start.7 = ((bf16[8,2,32768]{2,1,0:T(2,128)(2,1)}), bf16[8,2,32768]{2,1,0:T(2,128)(2,1)}, u32[]{:S(2)}, u32[]{:S(2)}) async-start(bf16[8,2,32768]{2,1,0:T(2,128)(2,1)} %reshape.97), calls=%async_computation.7 | async-start | bytes 2097152 | tf_op jit(solution)/shard_map/all_to_all | solution.py:73
  1066.9 33.4 %all-to-all-start.8 = ((bf16[16,2,16384]{2,1,0:T(2,128)(2,1)}), bf16[16,2,16384]{2,1,0:T(2,128)(2,1)}, u32[]{:S(2)}, u32[]{:S(2)}) async-start(bf16[16,2,16384]{2,1,0:T(2,128)(2,1)} %reshape.99), calls=%async_computation.8 | async-start | bytes 2097152 | tf_op jit(solution)/shard_map/all_to_all | solution.py:77
  1083.2 9.9 copy-start.1
Sparse Core Ops, SparseCore 0:
  9.1 61.1 all-gather.4
  72.0 54.6 all-gather.2
where the time goes:
time: 1150 us; the launch traced here: 1140 us
  local copies, waits for them, and re-layouts  556 us (48%)
  other arithmetic  419 us (36%)
  blocking collectives  46.4 us (4%)
  starting transfers between devices  44.1 us (4%)
  matrix products  37.9 us (3%)
  waiting for transfers between devices  17.2 us (1%)
  between operations  14 us (1%)
    unnamed x8, other arithmetic  419 us
    another operation x1, local copies, waits for them, and re-layouts, order_rows(): viewed = matrix.reshape(n_wide, n_narrow, count, cols)  113 us
    unnamed x35, local copies, waits for them, and re-layouts  109 us
    transpose x2, local copies, waits for them, and re-layouts, order_columns(): return viewed.transpose(0, 2, 1, 3).reshape(rows, matrix.shape[1])  96.4 us
    reshape x4, local copies, waits for them, and re-layouts, point_major(): jnp.swapaxes(tensor, 2, 3).reshape(dims[0], dims[1], dims[2] * dims[3])  86.7 us
    all_to_all x4, local copies, waits for them, and re-layouts, on_device(): lax.all_to_all(carried[1], 'wide', split_axis=2, concat_axis=1, tiled=True)  35.9 us
    all_to_all x4, local copies, waits for them, and re-layouts, on_device(): lax.all_to_all(carried[0], 'wide', split_axis=2, concat_axis=1, tiled=True)  35.9 us
    all_to_all x1, blocking collectives, on_device(): lax.all_to_all(coeffs, 'narrow', split_axis=1, concat_axis=3, tiled=True)  23.8 us
  transfers between devices with their start and end apart: 9, of which 1 were waited for; matrix products, arithmetic and copies ran while one was open for 87% of the time, Pallas kernels for 0%

commit v1 on v0

v1 whole, which is shorter than its diff:
```python
import jax
import jax.numpy as jnp
from jax import lax
from jax.experimental import pallas as pl
from jax.experimental.pallas import tpu as pltpu
from jax.sharding import PartitionSpec as P

MIB = 1 << 20


def dot_f32(left, right, contract):
    return lax.dot_general(
        left, right, (contract, ((), ())), preferred_element_type=jnp.float32
    )


def potential_step(p_ref, g_ref, v_ref, q_ref, acc_ref):
    step = pl.program_id(0)
    blocks, rows, width = p_ref.shape

    @pl.when(step == 0)
    def _():
        acc_ref[...] = jnp.zeros_like(acc_ref)

    vals = dot_f32(p_ref[0], g_ref[:, :width], ((1,), (1,)))
    for part in range(1, blocks):
        cols = slice(part * width, (part + 1) * width)
        vals += dot_f32(p_ref[part], g_ref[:, cols], ((1,), (1,)))
    weighted = (vals * v_ref[...].astype(jnp.float32)).astype(jnp.bfloat16)
    acc_ref[...] += dot_f32(weighted, g_ref[...], ((1,), (0,)))

    @pl.when(step == pl.num_programs(0) - 1)
    def _():
        for part in range(blocks):
            cols = slice(part * width, (part + 1) * width)
            q_ref[part] = acc_ref[:, cols].astype(q_ref.dtype)


def grid_two_pass(values, grid_two, potential, tile=512):
    blocks, rows, width = values.shape
    points = grid_two.shape[0]
    cols = blocks * width
    return pl.pallas_call(
        potential_step,
        grid=(points // tile,),
        in_specs=[
            pl.BlockSpec((blocks, rows, width), lambda b: (0, 0, 0)),
            pl.BlockSpec((tile, cols), lambda b: (b, 0)),
            pl.BlockSpec((rows, tile), lambda b: (0, b)),
        ],
        out_specs=pl.BlockSpec((blocks, rows, width), lambda b: (0, 0, 0)),
        out_shape=jax.ShapeDtypeStruct(values.shape, jnp.bfloat16),
        scratch_shapes=[pltpu.VMEM((rows, cols), jnp.float32)],
        compiler_params=pltpu.CompilerParams(vmem_limit_bytes=32 * MIB),
        cost_estimate=pl.CostEstimate(
            flops=4 * rows * cols * points,
            bytes_accessed=2 * (points * cols + rows * points + 2 * rows * cols),
            transcendentals=0,
        ),
        name="grid_two_pass",
    )(values, grid_two, potential)


def finish_step(s_ref, a_ref, o_ref):
    moved = jnp.swapaxes(s_ref[:, 0].astype(jnp.float32), 0, 1)
    total = moved + a_ref[...].reshape(moved.shape)
    o_ref[...] = total.astype(o_ref.dtype)


def finish(back, applied):
    states, blocks, rows, width = back.shape
    return pl.pallas_call(
        finish_step,
        grid=(blocks,),
        in_specs=[
            pl.BlockSpec((states, 1, rows, width), lambda j: (0, j, 0, 0)),
            pl.BlockSpec((rows * states, width), lambda j: (0, j)),
        ],
        out_specs=pl.BlockSpec((rows, states, width), lambda j: (0, 0, j)),
        out_shape=jax.ShapeDtypeStruct((rows, states, blocks * width), jnp.bfloat16),
        cost_estimate=pl.CostEstimate(
            flops=2 * applied.size, bytes_accessed=8 * applied.size, transcendentals=0
        ),
        name="finish",
    )(back, applied)


def on_device(coeffs, ham_one, grid_one, ham_two, grid_two, pair_potential, third_energy):
    n_wide = lax.axis_size("wide")
    n_narrow = lax.axis_size("narrow")
    both = ("wide", "narrow")
    local = coeffs[0]
    rows, states, width = local.shape
    n_one, own_points = pair_potential.shape
    part = n_one // n_narrow
    assert states == n_wide

    full_grid = lax.all_gather(grid_two, "wide", axis=0, tiled=True)
    by_state = lax.all_to_all(jnp.swapaxes(local, 0, 1), "wide", 0, 0, tiled=True)
    one_state = by_state.reshape(n_one, width)
    own_rows = lax.all_to_all(
        local.reshape(n_narrow, rows // n_narrow * states, width), "narrow", 0, 0, tiled=True
    )
    full_ham = lax.all_gather(ham_two, "wide", axis=0, tiled=True)

    slim = pair_potential.astype(jnp.bfloat16).reshape(n_narrow, part, own_points)
    slim = jnp.swapaxes(slim, 1, 2)
    slim = jnp.broadcast_to(slim[None], (n_wide,) + slim.shape)
    slim = lax.all_to_all(
        slim.reshape(n_wide * n_narrow, own_points, part), both, 0, 0, tiled=True
    )
    potential = slim.reshape(n_wide * n_narrow * own_points, part).T

    energy = third_energy[lax.axis_index("wide")]
    up = dot_f32(grid_one, one_state, ((1,), (0,))).astype(jnp.bfloat16)
    side = dot_f32(ham_one, one_state, ((1,), (0,))) + energy * one_state.astype(jnp.float32)

    up_rows = lax.all_to_all(up.reshape(n_narrow, part, width), "narrow", 0, 0, tiled=True)
    down_rows = grid_two_pass(up_rows, full_grid, potential)
    down = lax.all_to_all(down_rows, "narrow", 0, 0, tiled=True).reshape(n_one, width)
    back = (dot_f32(grid_one, down, ((0,), (0,))) + side).astype(jnp.bfloat16)
    count = n_one // (n_wide * n_narrow)
    back = lax.all_to_all(back.reshape(n_wide * n_narrow, count, width), both, 0, 0, tiled=True)

    shape = own_rows.shape
    flat = jnp.swapaxes(own_rows, 0, 1).reshape(shape[1], n_narrow * width)
    applied = dot_f32(flat, full_ham, ((1,), (1,)))
    out = finish(back.reshape(n_wide, n_narrow, count, width), applied)
    return out[None]


def solution(mesh):
    return jax.shard_map(
        on_device,
        mesh=mesh,
        in_specs=(
            P(None, "wide", None, "narrow"),
            P(),
            P(),
            P("wide", None),
            P("wide", None),
            P(None, ("wide", "narrow")),
            P(),
        ),
        out_specs=P(None, ("wide", "narrow"), None, None),
        check_vma=False,
    )
```

time: 1150 us -> 206 us (0.18); the launches traced: 1140 us -> 205 us
  local copies, waits for them, and re-layouts: 556 us -> 13.6 us
  other arithmetic: 419 us -> 0.91 us
  waiting for transfers between devices: 17.2 us -> 97.7 us
  blocking collectives: 46.4 us -> 0 us
  Pallas kernels: 0 us -> 12.7 us
  matrix products: 37.9 us -> 26.2 us
    unnamed x8 -> x0, other arithmetic: 419 us -> none
    another operation x1 -> x0, local copies, waits for them, and re-layouts: 113 us -> none  [order_rows(): viewed = matrix.reshape(n_wide, n_narrow, count, cols)]
    transpose x4 -> x2, local copies, waits for them, and re-layouts: 111 us -> 1.5 us  [the longest x1 1.49 us: on_device(): flat = jnp.swapaxes(own_rows, 0, 1).reshape(shape[1], n_narrow * width)]
    unnamed x35 -> x10, local copies, waits for them, and re-layouts: 109 us -> 6.92 us
    reshape x6 -> x2, local copies, waits for them, and re-layouts: 101 us -> 2.14 us  [the longest x1 1.5 us: on_device(): potential = slim.reshape(n_wide * n_narrow * own_points, part).T]
    all_to_all x18 -> x0, local copies, waits for them, and re-layouts: 95.4 us -> none  [the longest x4 35.9 us: on_device(): lax.all_to_all(carried[1], 'wide', split_axis=2, concat_axis=1, tiled=True)]
    all_to_all x7 -> x6, waiting for transfers between devices: 15.8 us -> 72 us  [the longest x1 22.8 us: on_device(): lax.all_to_all(jnp.swapaxes(local, 0, 1), 'wide', 0, 0, tiled=True)]
    all_to_all x2 -> x0, blocking collectives: 46.4 us -> none  [the longest x1 23.8 us: on_device(): lax.all_to_all(coeffs, 'narrow', split_axis=1, concat_axis=3, tiled=True)]
  transfers between devices with their start and end apart: 9 -> 8, of which waited for: 1 -> 7; matrix products, arithmetic and copies ran while one was open for 87% -> 18% of each run, Pallas kernels for 0% -> 3%
where the time goes in v1:
time: 206 us; the launch traced here: 205 us
  waiting for transfers between devices  97.7 us (47%)
  starting transfers between devices  40.7 us (20%)
  matrix products  26.2 us (13%)
  local copies, waits for them, and re-layouts  13.6 us (7%)
  between operations  13.5 us (7%)
  Pallas kernels  12.7 us (6%)
    dot_general x4, matrix products, dot_f32(): lax.dot_general(left, right, (contract, ((), ())), preferred_element_type...  26.2 us
    all_to_all x1, waiting for transfers between devices, on_device(): lax.all_to_all(jnp.swapaxes(local, 0, 1), 'wide', 0, 0, tiled=True)  22.8 us
    all_gather x1, waiting for transfers between devices, on_device(): full_ham = lax.all_gather(ham_two, 'wide', axis=0, tiled=True)  22.7 us
    all_to_all x1, waiting for transfers between devices, on_device(): lax.all_to_all(down_rows, 'narrow', 0, 0, tiled=True).reshape(n_one, width)  16.8 us
    all_to_all x1, waiting for transfers between devices, on_device(): lax.all_to_all(up.reshape(n_narrow, part, width), 'narrow', 0, 0, tiled=T...  16.5 us
    all_to_all x1, waiting for transfers between devices, on_device(): lax.all_to_all(slim.reshape(n_wide * n_narrow, own_points, part), both, 0...  11.4 us
    all_to_all x1, starting transfers between devices, on_device(): lax.all_to_all(slim.reshape(n_wide * n_narrow, own_points, part), both, 0...  8.26 us
    all_to_all x1, starting transfers between devices, on_device(): lax.all_to_all(jnp.swapaxes(local, 0, 1), 'wide', 0, 0, tiled=True)  7.84 us
  transfers between devices with their start and end apart: 8, of which 7 were waited for; matrix products, arithmetic and copies ran while one was open for 18% of the time, Pallas kernels for 3%

profile of v1, /device:TPU:1, one launch (start us, length us, event | category | flops | bytes accessed | tf_op | source)
XLA Modules:
  0.0 205.3 jit_solution(15328397172398082896)
XLA Ops:
  6.5 0.0 all-gather.3.cloned.1.call-start
  6.5 0.7 all-gather.3.cloned.1.call-update
  7.3 0.0 all-gather.5.cloned.1.call-start
  7.3 0.7 all-gather.5.cloned.1.call-update
  8.0 2.5 %copy.34 = bf16[1,128,16,256]{3,1,2,0:T(8,128)(2,1)} copy(bf16[1,128,16,256]{3,2,1,0:T(8,128)(2,1)} %param.7) | data formatting | bytes 2097152 | tf_op args[0]
  10.5 7.8 %all-to-all-start = ((bf16[16,128,256]{2,1,0:T(8,128)(2,1)}), bf16[16,128,256]{2,1,0:T(8,128)(2,1)S(1)}, u32[]{:S(2)}, u32[]{:S(2)}) async-start(bf16[16,128,256]{2,1,0:T(8,128)(2,1)} %bitcast.37), calls=%async_computation | async-start | bytes 2097152 | tf_op jit(solution)/shard_map/all_to_all | solution.py:99
  18.4 0.9 convert_element_type.13
  19.3 22.8 %all-to-all-done = bf16[16,128,256]{2,1,0:T(8,128)(2,1)S(1)} async-done(((bf16[16,128,256]{2,1,0:T(8,128)(2,1)}), bf16[16,128,256]{2,1,0:T(8,128)(2,1)S(1)}, u32[]{:S(2)}, u32[]{:S(2)}) %all-to-all-start) | async-done | bytes 1048608 | tf_op jit(solution)/shard_map/all_to_all | solution.py:99
  42.2 1.1 broadcast_in_dim.4
  43.3 8.3 %all-to-all-start.2 = ((bf16[128,16,256]{2,1,0:T(8,128)(2,1)}), bf16[128,16,256]{2,1,0:T(8,128)(2,1)S(1)}, u32[]{:S(2)}, u32[]{:S(2)}) async-start(bf16[128,16,256]{2,1,0:T(8,128)(2,1)} %bitcast.5), calls=%async_computation.2 | async-start | bytes 2097152 | tf_op jit(solution)/shard_map/all_to_all | solution.py:109
  51.5 6.9 %convolution_convert_fusion = bf16[2048,256]{1,0:T(8,128)(2,1)} fusion(bf16[2048,2048]{1,0:T(8,128)(2,1)} %param.9, bf16[2048,256]{1,0:T(8,128)(2,1)S(1)} %bitcast.40), kind=kOutput, calls=%fused_computation.4 | convolution fusion | flops 2148007936 | bytes 10485760 | tf_op jit(solution)/shard_map/dot_general | solution.py:12
  58.4 11.4 %all-to-all-done.2 = bf16[128,16,256]{2,1,0:T(8,128)(2,1)S(1)} async-done(((bf16[128,16,256]{2,1,0:T(8,128)(2,1)}), bf16[128,16,256]{2,1,0:T(8,128)(2,1)S(1)}, u32[]{:S(2)}, u32[]{:S(2)}) %all-to-all-start.2) | async-done | bytes 1048608 | tf_op jit(solution)/shard_map/all_to_all | solution.py:109
  69.8 0.0 copy-start.1
  69.8 6.7 %all-to-all-start.1 = ((bf16[8,256,256]{2,1,0:T(8,128)(2,1)}), bf16[8,256,256]{2,1,0:T(8,128)(2,1)S(1)}, u32[]{:S(2)}, u32[]{:S(2)}) async-start(bf16[8,256,256]{2,1,0:T(8,128)(2,1)} %bitcast.45), calls=%async_computation.1 | async-start | bytes 2097152 | tf_op jit(solution)/shard_map/all_to_all | solution.py:118
  76.5 0.0 copy-done.1
  76.5 1.5 copy.26
  78.0 16.5 %all-to-all-done.1.p_ref = bf16[8,256,256]{2,1,0:T(8,128)(2,1)S(1)} async-done(((bf16[8,256,256]{2,1,0:T(8,128)(2,1)}), bf16[8,256,256]{2,1,0:T(8,128)(2,1)S(1)}, u32[]{:S(2)}, u32[]{:S(2)}) %all-to-all-start.1) | async-done | bytes 1048608 | tf_op jit(solution)/shard_map/all_to_all | solution.py:118
  94.5 1.5 all-gather.3.cloned.1.call-done.g_ref
  96.0 0.0 copy-start
  96.0 3.4 %copy-done = bf16[2048,2048]{1,0:T(8,128)(2,1)S(1)} copy-done((bf16[2048,2048]{1,0:T(8,128)(2,1)S(1)}, bf16[2048,2048]{1,0:T(8,128)(2,1)}, u32[]{:S(2)}) %copy-start) | copy-done | bytes 8388632
  99.4 0.0 copy-start.3
  99.4 6.8 %grid_two_pass.1 = bf16[8,256,256]{2,1,0:T(8,128)(2,1)} custom-call(bf16[8,256,256]{2,1,0:T(8,128)(2,1)S(1)} %all-to-all-done.1.p_ref, bf16[2048,2048]{1,0:T(8,128)(2,1)S(1)} %copy-done, bf16[256,2048]{1,0:T(8,128)(2,1)S(1)} %bitcast.38), custom_call_target="tpu_custom_call" | custom-call | flops 4294967296 | bytes 11534336 | tf_op jit(solution)/shard_map/grid_two_pass/pallas_call | solution.py:43
  106.2 6.4 %all-to-all-start.3 = ((bf16[8,256,256]{2,1,0:T(8,128)(2,1)}), bf16[8,256,256]{2,1,0:T(8,128)(2,1)S(1)}, u32[]{:S(2)}, u32[]{:S(2)}) async-start(bf16[8,256,256]{2,1,0:T(8,128)(2,1)} %grid_two_pass.1), calls=%async_computation.3 | async-start | bytes 2097152 | tf_op jit(solution)/shard_map/all_to_all | solution.py:120
  112.6 0.0 copy-done.3
  112.6 0.6 dynamic_slice.3
  113.2 0.6 copy.31
  113.8 16.8 %all-to-all-done.3 = bf16[8,256,256]{2,1,0:T(8,128)(2,1)S(1)} async-done(((bf16[8,256,256]{2,1,0:T(8,128)(2,1)}), bf16[8,256,256]{2,1,0:T(8,128)(2,1)S(1)}, u32[]{:S(2)}, u32[]{:S(2)}) %all-to-all-start.3) | async-done | bytes 1048608 | tf_op jit(solution)/shard_map/all_to_all | solution.py:120
  130.7 4.3 %all-to-all-start.5 = ((bf16[8,256,256]{2,1,0:T(8,128)(2,1)}), bf16[8,256,256]{2,1,0:T(8,128)(2,1)}, u32[]{:S(2)}, u32[]{:S(2)}) async-start(bf16[8,256,256]{2,1,0:T(8,128)(2,1)} %bitcast.13), calls=%async_computation.5 | async-start | bytes 2097152 | tf_op jit(solution)/shard_map/all_to_all | solution.py:101
  134.9 6.5 %convolution_add_fusion = f32[2048,256]{0,1:T(8,128)S(1)} fusion(bf16[2048,2048]{1,0:T(8,128)(2,1)} %param.8, bf16[2048,256]{1,0:T(8,128)(2,1)S(1)} %bitcast.42, bf16[2048,256]{0,1:T(8,128)(2,1)S(1)} %copy.31, f32[]{:T(128)} %bitcast.10), kind=kOutput, calls=%fused_computation.2 | convolution fusion | flops 2149056512 | bytes 12582916 | tf_op jit(solution)/shard_map/dot_general | solution.py:12
  141.4 5.7 %fusion.1 = bf16[2048,256]{0,1:T(8,128)(2,1)S(1)} fusion(f32[2048,256]{0,1:T(8,128)S(1)} %convolution_add_fusion, bf16[2048,256]{1,0:T(8,128)(2,1)S(1)} %bitcast.39, bf16[2048,2048]{1,0:T(8,128)(2,1)} %param.9), kind=kOutput, calls=%fused_computation.3 | convolution fusion | flops 2148532224 | bytes 12582912 | tf_op jit(solution)/shard_map/dot_general | solution.py:12
  147.1 1.3 copy.28
  148.5 4.4 %all-to-all-done.5 = bf16[8,256,256]{2,1,0:T(8,128)(2,1)} async-done(((bf16[8,256,256]{2,1,0:T(8,128)(2,1)}), bf16[8,256,256]{2,1,0:T(8,128)(2,1)}, u32[]{:S(2)}, u32[]{:S(2)}) %all-to-all-start.5) | async-done | bytes 1048608 | tf_op jit(solution)/shard_map/all_to_all | solution.py:101
  152.9 7.2 %all-to-all-start.4 = ((bf16[128,16,256]{2,1,0:T(8,128)(2,1)}), bf16[128,16,256]{2,1,0:T(8,128)(2,1)S(1)}, u32[]{:S(2)}, u32[]{:S(2)}) async-start(bf16[128,16,256]{2,1,0:T(8,128)(2,1)} %bitcast.11), calls=%async_computation.4 | async-start | bytes 2097152 | tf_op jit(solution)/shard_map/all_to_all | solution.py:123
  160.1 1.5 copy.29
  161.6 22.7 %all-gather.5.cloned.1.call-done = bf16[2048,2048]{1,0:T(8,128)(2,1)} async-done(((bf16[128,2048]{1,0:T(8,128)(2,1)}), bf16[2048,2048]{1,0:T(8,128)(2,1)}) %all-gather.5.cloned.1.call-update) | async-done | bytes 8388624 | tf_op jit(solution)/shard_map/all_gather | solution.py:104
  184.3 7.2 %fusion.2.a_ref = f32[256,2048]{1,0:T(8,128)} fusion(bf16[256,2048]{0,1:T(8,128)(2,1)S(1)} %bitcast.46, bf16[2048,2048]{1,0:T(8,128)(2,1)} %all-gather.5.cloned.1.call-done), kind=kOutput, calls=%fused_computation.6 | convolution fusion | flops 2147483648 | bytes 11534336 | tf_op jit(solution)/shard_map/dot_general | solution.py:12
  191.5 0.0 all-to-all-done.4
  191.5 0.0 copy-start.2
  191.5 1.0 copy-done.2
  192.5 5.9 %finish.1 = bf16[16,16,2048]{2,1,0:T(8,128)(2,1)} custom-call(bf16[16,8,16,256]{3,2,1,0:T(8,128)(2,1)} %bitcast.44, f32[256,2048]{1,0:T(8,128)} %fusion.2.a_ref), custom_call_target="tpu_custom_call" | custom-call | flops 1048576 | bytes 4194304 | tf_op jit(solution)/shard_map/finish/pallas_call | solution.py:72
  (2 shorter events, 0.0 us)
Async XLA Ops:
  6.5 89.5 %all-gather.3.cloned.1.call-start = ((), (), s32[]{:S(2)}) async-start(), calls=%async_computation.6 | async-start | bytes 8912896 | tf_op jit(solution)/shard_map/all_gather | solution.py:98
  7.3 177.1 %all-gather.5.cloned.1.call-start = ((), (), s32[]{:S(2)}) async-start(), calls=%async_computation.7 | async-start | bytes 8912896 | tf_op jit(solution)/shard_map/all_gather | solution.py:104
  10.5 31.6 %all-to-all-start = ((bf16[16,128,256]{2,1,0:T(8,128)(2,1)}), bf16[16,128,256]{2,1,0:T(8,128)(2,1)S(1)}, u32[]{:S(2)}, u32[]{:S(2)}) async-start(bf16[16,128,256]{2,1,0:T(8,128)(2,1)} %bitcast.37), calls=%async_computation | async-start | bytes 2097152 | tf_op jit(solution)/shard_map/all_to_all | solution.py:99
  43.3 26.6 %all-to-all-start.2 = ((bf16[128,16,256]{2,1,0:T(8,128)(2,1)}), bf16[128,16,256]{2,1,0:T(8,128)(2,1)S(1)}, u32[]{:S(2)}, u32[]{:S(2)}) async-start(bf16[128,16,256]{2,1,0:T(8,128)(2,1)} %bitcast.5), calls=%async_computation.2 | async-start | bytes 2097152 | tf_op jit(solution)/shard_map/all_to_all | solution.py:109
  69.8 6.7 %copy-start.1 = (bf16[128,16,256]{2,1,0:T(8,128)(2,1)}, bf16[128,16,256]{2,1,0:T(8,128)(2,1)S(1)}, u32[]{:S(2)}) copy-start(bf16[128,16,256]{2,1,0:T(8,128)(2,1)S(1)} %all-to-all-done.2) | copy-start | bytes 3145732
  69.8 24.7 %all-to-all-start.1 = ((bf16[8,256,256]{2,1,0:T(8,128)(2,1)}), bf16[8,256,256]{2,1,0:T(8,128)(2,1)S(1)}, u32[]{:S(2)}, u32[]{:S(2)}) async-start(bf16[8,256,256]{2,1,0:T(8,128)(2,1)} %bitcast.45), calls=%async_computation.1 | async-start | bytes 2097152 | tf_op jit(solution)/shard_map/all_to_all | solution.py:118
  96.0 3.4 %copy-start = (bf16[2048,2048]{1,0:T(8,128)(2,1)S(1)}, bf16[2048,2048]{1,0:T(8,128)(2,1)}, u32[]{:S(2)}) copy-start(bf16[2048,2048]{1,0:T(8,128)(2,1)} %all-gather.3.cloned.1.call-done.g_ref) | copy-start | bytes 25165828
  99.4 13.2 %copy-start.3 = (f32[16]{0:T(128)S(1)}, f32[16]{0:T(128)}, u32[]{:S(2)}) copy-start(f32[16]{0:T(128)} %param.13) | copy-start | bytes 196
  106.2 24.5 %all-to-all-start.3 = ((bf16[8,256,256]{2,1,0:T(8,128)(2,1)}), bf16[8,256,256]{2,1,0:T(8,128)(2,1)S(1)}, u32[]{:S(2)}, u32[]{:S(2)}) async-start(bf16[8,256,256]{2,1,0:T(8,128)(2,1)} %grid_two_pass.1), calls=%async_computation.3 | async-start | bytes 2097152 | tf_op jit(solution)/shard_map/all_to_all | solution.py:120
  130.7 22.2 %all-to-all-start.5 = ((bf16[8,256,256]{2,1,0:T(8,128)(2,1)}), bf16[8,256,256]{2,1,0:T(8,128)(2,1)}, u32[]{:S(2)}, u32[]{:S(2)}) async-start(bf16[8,256,256]{2,1,0:T(8,128)(2,1)} %bitcast.13), calls=%async_computation.5 | async-start | bytes 2097152 | tf_op jit(solution)/shard_map/all_to_all | solution.py:101
  152.9 38.6 %all-to-all-start.4 = ((bf16[128,16,256]{2,1,0:T(8,128)(2,1)}), bf16[128,16,256]{2,1,0:T(8,128)(2,1)S(1)}, u32[]{:S(2)}, u32[]{:S(2)}) async-start(bf16[128,16,256]{2,1,0:T(8,128)(2,1)} %bitcast.11), calls=%async_computation.4 | async-start | bytes 2097152 | tf_op jit(solution)/shard_map/all_to_all | solution.py:123
  191.5 1.0 copy-start.2
Sparse Core Ops, SparseCore 0:
  9.1 86.8 all-gather.2
  97.7 86.5 all-gather.4

commit v2 on v1

v2 whole, which is shorter than its diff:
```python
import functools

import jax
import jax.numpy as jnp
from jax import lax
from jax.experimental import pallas as pl
from jax.experimental.pallas import tpu as pltpu
from jax.sharding import PartitionSpec as P

MIB = 1 << 20
NN = ((1,), (0,))
NT = ((1,), (1,))
TN = ((0,), (0,))


def dot_f32(left, right, contract):
    return lax.dot_general(
        left, right, (contract, ((), ())), preferred_element_type=jnp.float32
    )


def params(mib):
    return pltpu.CompilerParams(vmem_limit_bytes=mib * MIB)


def cost(flops, moved):
    return pl.CostEstimate(flops=flops, bytes_accessed=moved, transcendentals=0)


def by_blocks(rows_ref, right_ref):
    width = rows_ref.shape[2]
    right = right_ref[...].reshape(-1, right_ref.shape[-1])
    total = dot_f32(rows_ref[0], right[:, :width], NT)
    for part in range(1, rows_ref.shape[0]):
        total += dot_f32(rows_ref[part], right[:, part * width : (part + 1) * width], NT)
    return total


def forward_step(rows_ref, grid_ref, out_ref):
    out_ref[...] = by_blocks(rows_ref, grid_ref).astype(out_ref.dtype).reshape(out_ref.shape)


def forward_pass(rows, gathered, n_wide, count):
    n_narrow, height, width = rows.shape
    inner = height // n_wide
    points = gathered.shape[0] * count
    cols = gathered.shape[2]
    return pl.pallas_call(
        forward_step,
        grid=(n_narrow,),
        in_specs=[
            pl.BlockSpec(rows.shape, lambda n: (0, 0, 0)),
            pl.BlockSpec((gathered.shape[0], count, cols), lambda n: (0, n, 0)),
        ],
        out_specs=pl.BlockSpec((n_wide, 1, inner, points), lambda n: (0, n, 0, 0)),
        out_shape=jax.ShapeDtypeStruct((n_wide, n_narrow, inner, points), jnp.bfloat16),
        compiler_params=params(48),
        cost_estimate=cost(2 * height * cols * points * n_narrow, 10 * MIB),
        name="forward_pass",
    )(rows, gathered)


def middle_step(values_ref, grid_ref, potential_ref, across_ref, out_ref, acc_ref):
    step = pl.program_id(0)
    width = values_ref.shape[1]

    @pl.when(step == 0)
    def _():
        acc_ref[...] = jnp.zeros_like(acc_ref)

    vals = dot_f32(grid_ref[...], values_ref[...], NN)
    weighted = (vals * potential_ref[...].astype(jnp.float32)).astype(jnp.bfloat16)
    acc_ref[...] += dot_f32(weighted, grid_ref[...], TN)

    @pl.when(step == pl.num_programs(0) - 1)
    def _():
        out_ref[:, :width] = acc_ref[...].T.astype(out_ref.dtype)
        out_ref[:, width:] = across_ref[...]


def middle_pass(values, grid_one, potential, across, tile=256):
    n_one, width = values.shape
    return pl.pallas_call(
        middle_step,
        grid=(n_one // tile,),
        in_specs=[
            pl.BlockSpec((n_one, width), lambda a: (0, 0)),
            pl.BlockSpec((tile, n_one), lambda a: (a, 0)),
            pl.BlockSpec((tile, width), lambda a: (a, 0)),
            pl.BlockSpec((n_one, width), lambda a: (0, 0)),
        ],
        out_specs=pl.BlockSpec((n_one, 2 * width), lambda a: (0, 0)),
        out_shape=jax.ShapeDtypeStruct((n_one, 2 * width), jnp.bfloat16),
        scratch_shapes=[pltpu.VMEM((width, n_one), jnp.float32)],
        compiler_params=params(48),
        cost_estimate=cost(4 * n_one * n_one * width, 13 * MIB),
        name="middle_pass",
    )(values, grid_one, potential, across)


def applied_step(rows_ref, ham_ref, energy_ref, out_ref):
    own = rows_ref[pl.program_id(0)].astype(jnp.float32)
    out_ref[...] = by_blocks(rows_ref, ham_ref) + energy_ref[...] * own


def applied_pass(rows, full_ham, energy):
    n_narrow, height, width = rows.shape
    cols = n_narrow * width
    return pl.pallas_call(
        applied_step,
        grid=(n_narrow,),
        in_specs=[
            pl.BlockSpec(rows.shape, lambda n: (0, 0, 0)),
            pl.BlockSpec((width, cols), lambda n: (n, 0)),
            pl.BlockSpec((height, 1), lambda n: (0, 0)),
        ],
        out_specs=pl.BlockSpec((height, width), lambda n: (0, n)),
        out_shape=jax.ShapeDtypeStruct((height, cols), jnp.float32),
        compiler_params=params(48),
        cost_estimate=cost(2 * height * cols * cols, 11 * MIB),
        name="applied_pass",
    )(rows, full_ham, energy)


def final_step(back_ref, grid_ref, across_ref, applied_ref, swap_ref, out_ref):
    states, blocks, rows, width = back_ref.shape
    total = applied_ref[...] + across_ref[...].astype(jnp.float32).reshape(applied_ref.shape)
    for part in range(blocks):
        left = back_ref[:, part].reshape(states * rows, width)
        right = grid_ref[:, part * rows : (part + 1) * rows].reshape(width, -1)
        total += dot_f32(left, right, NN)
    swapped = dot_f32(swap_ref[...], total.astype(jnp.bfloat16), NN)
    out_ref[...] = swapped.astype(out_ref.dtype).reshape(out_ref.shape)


def final_pass(received, gathered, applied, swap):
    states, blocks, rows, double = received.shape
    width = double // 2
    height = states * rows
    cols = applied.shape[1]
    shards = gathered.shape[0]
    return pl.pallas_call(
        final_step,
        grid=(blocks,),
        in_specs=[
            pl.BlockSpec((states, blocks, rows, width), lambda n: (0, 0, 0, 0)),
            pl.BlockSpec((shards, blocks * rows, width), lambda n: (0, 0, n)),
            pl.BlockSpec((states, 1, rows, width), lambda n: (0, n, 0, 1)),
            pl.BlockSpec((height, width), lambda n: (0, n)),
            pl.BlockSpec((height, height), lambda n: (0, 0)),
        ],
        out_specs=pl.BlockSpec((rows, states, width), lambda n: (0, 0, n)),
        out_shape=jax.ShapeDtypeStruct((rows, states, cols), jnp.bfloat16),
        compiler_params=params(48),
        cost_estimate=cost(2 * height * cols * (cols + height), 14 * MIB),
        name="final_pass",
    )(received, gathered, received, applied, swap)


def on_device(coeffs, ham_one, grid_one, ham_two, grid_two, pair_potential, third_energy):
    n_wide = lax.axis_size("wide")
    n_narrow = lax.axis_size("narrow")
    both = ("wide", "narrow")
    local = coeffs[0]
    rows, states, width = local.shape
    n_one, count = pair_potential.shape
    inner = rows // n_narrow
    height = inner * states
    assert states == n_wide and inner == count and n_wide * count == width

    slim = pair_potential.T.astype(jnp.bfloat16)
    gathered = lax.all_gather(jnp.concatenate([grid_two, slim], 0), "wide", axis=0, tiled=False)
    full_ham = lax.all_gather(ham_two, "wide", axis=0, tiled=True)

    own = local.reshape(n_narrow, inner, states, width).swapaxes(1, 2)
    own = lax.all_to_all(own.reshape(n_narrow, height, width), "narrow", 0, 0, tiled=True)
    by_state = lax.all_to_all(jnp.swapaxes(local, 0, 1), "wide", 0, 0, tiled=True)
    across = dot_f32(ham_one, by_state.reshape(n_one, width), NN).astype(jnp.bfloat16)
    own, across = lax.optimization_barrier((own, across))

    values = forward_pass(own, gathered, n_wide, count)
    values = lax.all_to_all(
        values.reshape(n_wide * n_narrow, inner, width), both, 0, 0, tiled=True
    )
    potential = gathered[:, -count:].reshape(width, n_one).T
    pair = middle_pass(values.reshape(n_one, width), grid_one, potential, across)
    pair = lax.all_to_all(
        pair.reshape(n_wide * n_narrow, inner, 2 * width), both, 0, 0, tiled=True
    )

    energy = jnp.repeat(third_energy, inner)[:, None]
    applied = applied_pass(own, full_ham, energy)
    target = jnp.arange(height)
    source = target % states * inner + target // states
    swap = (source[:, None] == jnp.arange(height)[None, :]).astype(jnp.bfloat16)
    out = final_pass(
        pair.reshape(n_wide, n_narrow, inner, 2 * width), gathered, applied, swap
    )
    return out[None]


def solution(mesh):
    return jax.shard_map(
        on_device,
        mesh=mesh,
        in_specs=(
            P(None, "wide", None, "narrow"),
            P(),
            P(),
            P("wide", None),
            P("wide", None),
            P(None, ("wide", "narrow")),
            P(),
        ),
        out_specs=P(None, ("wide", "narrow"), None, None),
        check_vma=False,
    )
```

time: 206 us -> 208 us (level)
  Pallas kernels: 12.7 us -> 38.6 us
  matrix products: 26.2 us -> 6.86 us
  starting transfers between devices: 40.7 us -> 30.3 us
  waiting for transfers between devices: 97.7 us -> 99.9 us
    pallas_call x2 -> x4, Pallas kernels: 12.7 us -> 38.6 us  [the longest x1 13 us: middle_pass(): pl.pallas_call(middle_step, grid=(n_one // tile,), in_specs=[pl.BlockSpec...]
    all_to_all x5 -> x3, waiting for transfers between devices: 49.2 us -> 24.9 us  [the longest x1 14.5 us: on_device(): lax.all_to_all(values.reshape(n_wide * n_narrow, inner, width), both, 0,...]
    all_gather x1, waiting for transfers between devices: 1.52 us -> 21.9 us  [on_device(): lax.all_gather(jnp.concatenate([grid_two, slim], 0), 'wide', axis=0, tile...]
    dot_general x4 -> x1, matrix products: 26.2 us -> 6.86 us  [dot_f32(): lax.dot_general(left, right, (contract, ((), ())), preferred_element_type...]
    all_to_all x5 -> x3, starting transfers between devices: 32.8 us -> 22.4 us  [the longest x1 8.67 us: on_device(): lax.all_to_all(values.reshape(n_wide * n_narrow, inner, width), both, 0,...]
    all_gather x1, waiting for transfers between devices: 22.7 us -> 29.4 us  [on_device(): full_ham = lax.all_gather(ham_two, 'wide', axis=0, tiled=True)]
    another operation x0 -> x2, local copies, waits for them, and re-layouts: none -> 2.68 us  [the longest x1 2.58 us: on_device(): own = local.reshape(n_narrow, inner, states, width).swapaxes(1, 2)]
    slice x0 -> x1, local copies, waits for them, and re-layouts: none -> 2.32 us  [on_device(): potential = gathered[:, -count:].reshape(width, n_one).T]
  transfers between devices with their start and end apart: 8 -> 6, of which waited for: 7 -> 5; matrix products, arithmetic and copies ran while one was open for 18% -> 8% of each run, Pallas kernels for 3% -> 14%
where the time goes in v2:
time: 208 us; the launch traced here: 207 us
  waiting for transfers between devices  99.9 us (48%)
  Pallas kernels  38.6 us (19%)
  starting transfers between devices  30.3 us (15%)
  local copies, waits for them, and re-layouts  14.6 us (7%)
  between operations  13.5 us (6%)
  matrix products  6.86 us (3%)
  other arithmetic  2.92 us (1%)
    all_gather x1, waiting for transfers between devices, on_device(): full_ham = lax.all_gather(ham_two, 'wide', axis=0, tiled=True)  29.4 us
    all_to_all x1, waiting for transfers between devices, on_device(): lax.all_to_all(jnp.swapaxes(local, 0, 1), 'wide', 0, 0, tiled=True)  23 us
    all_gather x1, waiting for transfers between devices, on_device(): lax.all_gather(jnp.concatenate([grid_two, slim], 0), 'wide', axis=0, tile...  21.9 us
    all_to_all x1, waiting for transfers between devices, on_device(): lax.all_to_all(values.reshape(n_wide * n_narrow, inner, width), both, 0,...  14.5 us
    pallas_call x1, Pallas kernels, middle_pass(): pl.pallas_call(middle_step, grid=(n_one // tile,), in_specs=[pl.BlockSpec...  13 us
    all_to_all x1, waiting for transfers between devices, on_device(): lax.all_to_all(own.reshape(n_narrow, height, width), 'narrow', 0, 0, tile...  10.4 us
    pallas_call x1, Pallas kernels, final_pass(): pl.pallas_call(final_step, grid=(blocks,), in_specs=[pl.BlockSpec((states...  9.51 us
    all_to_all x1, starting transfers between devices, on_device(): lax.all_to_all(values.reshape(n_wide * n_narrow, inner, width), both, 0,...  8.67 us
  transfers between devices with their start and end apart: 6, of which 5 were waited for; matrix products, arithmetic and copies ran while one was open for 8% of the time, Pallas kernels for 14%

profile of v2, /device:TPU:1, one launch (start us, length us, event | category | flops | bytes accessed | tf_op | source)
XLA Modules:
  0.0 206.6 jit_solution(7825863849507796821)
XLA Ops:
  6.5 0.0 all-gather.6.cloned.1.call-start
  6.5 0.9 convert_bitcast_fusion
  7.4 1.9 pad_maximum_fusion
  9.4 0.0 all-gather.6.cloned.1.call-update
  9.4 0.0 all-gather.4.cloned.1.call-start
  9.4 0.7 all-gather.4.cloned.1.call-update
  10.1 2.6 %copy.15 = bf16[1,128,16,256]{3,1,2,0:T(8,128)(2,1)} copy(bf16[1,128,16,256]{3,2,1,0:T(8,128)(2,1)} %param.7) | data formatting | bytes 2097152 | tf_op args[0]
  12.7 7.8 %all-to-all-start.1 = ((bf16[16,128,256]{2,1,0:T(8,128)(2,1)}), bf16[16,128,256]{2,1,0:T(8,128)(2,1)S(1)}, u32[]{:S(2)}, u32[]{:S(2)}) async-start(bf16[16,128,256]{2,1,0:T(8,128)(2,1)} %bitcast.21), calls=%async_computation.1 | async-start | bytes 2097152 | tf_op jit(solution)/shard_map/all_to_all | solution.py:177
  20.5 2.6 %copy.10 = bf16[8,16,16,256]{3,1,2,0:T(8,128)(2,1)} copy(bf16[8,16,16,256]{3,2,1,0:T(8,128)(2,1)} %bitcast.30) | data formatting | bytes 2097152 | tf_op jit(solution)/shard_map/reshape;squeeze | solution.py:175
  23.1 23.0 %all-to-all-done.1 = bf16[16,128,256]{2,1,0:T(8,128)(2,1)S(1)} async-done(((bf16[16,128,256]{2,1,0:T(8,128)(2,1)}), bf16[16,128,256]{2,1,0:T(8,128)(2,1)S(1)}, u32[]{:S(2)}, u32[]{:S(2)}) %all-to-all-start.1) | async-done | bytes 1048608 | tf_op jit(solution)/shard_map/all_to_all | solution.py:177
  46.1 6.6 %all-to-all-start = ((bf16[8,256,256]{2,1,0:T(8,128)(2,1)}), bf16[8,256,256]{2,1,0:T(8,128)(2,1)S(1)}, u32[]{:S(2)}, u32[]{:S(2)}) async-start(bf16[8,256,256]{2,1,0:T(8,128)(2,1)} %bitcast.2), calls=%async_computation | async-start | bytes 2097152 | tf_op jit(solution)/shard_map/all_to_all | solution.py:176
  52.7 6.9 %convolution_convert_fusion.across_ref = bf16[2048,256]{1,0:T(8,128)(2,1)} fusion(bf16[2048,2048]{1,0:T(8,128)(2,1)} %param.8, bf16[2048,256]{1,0:T(8,128)(2,1)S(1)} %bitcast.32), kind=kOutput, calls=%fused_computation | convolution fusion | flops 2148007936 | bytes 10485760 | tf_op jit(solution)/shard_map/dot_general | solution.py:17
  59.5 10.4 %all-to-all-done.rows_ref = bf16[8,256,256]{2,1,0:T(8,128)(2,1)S(1)} async-done(((bf16[8,256,256]{2,1,0:T(8,128)(2,1)}), bf16[8,256,256]{2,1,0:T(8,128)(2,1)S(1)}, u32[]{:S(2)}, u32[]{:S(2)}) %all-to-all-start) | async-done | bytes 1048608 | tf_op jit(solution)/shard_map/all_to_all | solution.py:176
  70.0 21.9 %all-gather.6.cloned.1.call-done = bf16[2304,2048]{1,0:T(8,128)(2,1)} async-done(((bf16[144,2048]{1,0:T(8,128)(2,1)}), bf16[2304,2048]{1,0:T(8,128)(2,1)}) %all-gather.6.cloned.1.call-update) | async-done | bytes 9437200 | tf_op jit(solution)/shard_map/all_gather | solution.py:172
  91.9 8.5 %forward_pass.1 = bf16[16,8,16,256]{3,2,1,0:T(8,128)(2,1)} custom-call(bf16[8,256,256]{2,1,0:T(8,128)(2,1)S(1)} %all-to-all-done.rows_ref, bf16[16,144,2048]{2,1,0:T(8,128)(2,1)} %bitcast.27), custom_call_target="tpu_custom_call" | custom-call | flops 2147483648 | bytes 10485760 | tf_op jit(solution)/shard_map/forward_pass/pallas_call | solution.py:48
  100.3 8.7 %all-to-all-start.2 = ((bf16[128,16,256]{2,1,0:T(8,128)(2,1)}), bf16[128,16,256]{2,1,0:T(8,128)(2,1)S(1)}, u32[]{:S(2)}, u32[]{:S(2)}) async-start(bf16[128,16,256]{2,1,0:T(8,128)(2,1)} %bitcast.8), calls=%async_computation.2 | async-start | bytes 2097152 | tf_op jit(solution)/shard_map/all_to_all | solution.py:182
  109.0 2.3 %slice.4 = bf16[16,16,2048]{2,1,0:T(8,128)(2,1)} slice(bf16[16,144,2048]{2,1,0:T(8,128)(2,1)} %bitcast.28), slice={[0:16], [128:144], [0:2048]} | slice | bytes 2097152 | tf_op jit(solution)/shard_map/slice | solution.py:185
  111.3 1.5 copy.12
  112.8 14.5 %all-to-all-done.2 = bf16[128,16,256]{2,1,0:T(8,128)(2,1)S(1)} async-done(((bf16[128,16,256]{2,1,0:T(8,128)(2,1)}), bf16[128,16,256]{2,1,0:T(8,128)(2,1)S(1)}, u32[]{:S(2)}, u32[]{:S(2)}) %all-to-all-start.2) | async-done | bytes 1048608 | tf_op jit(solution)/shard_map/all_to_all | solution.py:182
  127.3 0.0 copy-start.3
  127.3 1.2 copy-done.3
  128.5 0.0 copy-start.4
  128.5 13.0 %middle_pass.1 = bf16[2048,512]{1,0:T(8,128)(2,1)S(1)} custom-call(bf16[2048,256]{1,0:T(8,128)(2,1)S(1)} %bitcast.25, bf16[2048,2048]{1,0:T(8,128)(2,1)} %grid_ref.1, bf16[2048,256]{1,0:T(8,128)(2,1)S(1)} %bitcast.26, bf16[2048,256]{1,0:T(8,128)(2,1)S(1)} %copy-done.3), custom_call_target="tpu_custom_call" | custom-call | flops 4294967296 | bytes 13631488 | tf_op jit(solution)/shard_map/middle_pass/pallas_call | solution.py:83
  141.6 0.0 copy-start.2
  141.6 1.3 copy-done.2
  142.9 7.1 %all-to-all-start.3 = ((bf16[128,16,512]{2,1,0:T(8,128)(2,1)}), bf16[128,16,512]{2,1,0:T(8,128)(2,1)S(1)}, u32[]{:S(2)}, u32[]{:S(2)}) async-start(bf16[128,16,512]{2,1,0:T(8,128)(2,1)} %bitcast.24), calls=%async_computation.3 | async-start | bytes 4194304 | tf_op jit(solution)/shard_map/all_to_all | solution.py:187
  150.0 0.0 copy-done.4
  150.0 0.1 broadcast_in_dim.8
  150.1 0.1 broadcast_in_dim_reshape.4.energy_ref
  150.2 0.1 fusion.swap_ref
  150.3 29.4 %all-gather.4.cloned.1.call-done.ham_ref = bf16[2048,2048]{1,0:T(8,128)(2,1)} async-done(((bf16[128,2048]{1,0:T(8,128)(2,1)}), bf16[2048,2048]{1,0:T(8,128)(2,1)}) %all-gather.4.cloned.1.call-update) | async-done | bytes 8388624 | tf_op jit(solution)/shard_map/all_gather | solution.py:173
  179.8 7.6 %applied_pass.1.applied_ref = f32[256,2048]{1,0:T(8,128)S(1)} custom-call(bf16[8,256,256]{2,1,0:T(8,128)(2,1)S(1)} %all-to-all-done.rows_ref, bf16[2048,2048]{1,0:T(8,128)(2,1)} %all-gather.4.cloned.1.call-done.ham_ref, f32[256,1]{1,0:T(8,128)S(1)} %broadcast_in_dim_reshape.4.energy_ref), custom_call_target="tpu_custom_call" | custom-call | flops 2147483648 | bytes 11534336 | tf_op jit(solution)/shard_map/applied_pass/pallas_call | solution.py:109
  187.3 0.0 copy-start
  187.3 1.3 copy-done
  188.7 0.0 all-to-all-done.3
  188.7 0.0 copy-start.1
  188.7 1.6 copy-done.1
  190.3 9.5 %final_pass.1 = bf16[16,16,2048]{2,1,0:T(8,128)(2,1)} custom-call(bf16[16,8,16,512]{3,2,1,0:T(8,128)(2,1)S(1)} %bitcast.22, bf16[16,144,2048]{2,1,0:T(8,128)(2,1)} %bitcast.29, bf16[16,8,16,512]{3,2,1,0:T(8,128)(2,1)S(1)} %bitcast.23, f32[256,2048]{1,0:T(8,128)S(1)} %copy-done.1, bf16[256,256]{1,0:T(8,128)(2,1)S(1)} %fusion.swap_ref), custom_call_target="tpu_custom_call" | custom-call | flops 2415919104 | bytes 14680064 | tf_op jit(solution)/shard_map/final_pass/pallas_call | solution.py:142
  (1 shorter events, 0.0 us)
Async XLA Ops:
  6.5 85.3 %all-gather.6.cloned.1.call-start = ((), (), s32[]{:S(2)}) async-start(), calls=%async_computation.5 | async-start | bytes 10027008 | tf_op jit(solution)/shard_map/all_gather | solution.py:172
  9.4 170.4 %all-gather.4.cloned.1.call-start = ((), (), s32[]{:S(2)}) async-start(), calls=%async_computation.4 | async-start | bytes 8912896 | tf_op jit(solution)/shard_map/all_gather | solution.py:173
  12.7 33.4 %all-to-all-start.1 = ((bf16[16,128,256]{2,1,0:T(8,128)(2,1)}), bf16[16,128,256]{2,1,0:T(8,128)(2,1)S(1)}, u32[]{:S(2)}, u32[]{:S(2)}) async-start(bf16[16,128,256]{2,1,0:T(8,128)(2,1)} %bitcast.21), calls=%async_computation.1 | async-start | bytes 2097152 | tf_op jit(solution)/shard_map/all_to_all | solution.py:177
  46.1 23.9 %all-to-all-start = ((bf16[8,256,256]{2,1,0:T(8,128)(2,1)}), bf16[8,256,256]{2,1,0:T(8,128)(2,1)S(1)}, u32[]{:S(2)}, u32[]{:S(2)}) async-start(bf16[8,256,256]{2,1,0:T(8,128)(2,1)} %bitcast.2), calls=%async_computation | async-start | bytes 2097152 | tf_op jit(solution)/shard_map/all_to_all | solution.py:176
  100.3 27.0 %all-to-all-start.2 = ((bf16[128,16,256]{2,1,0:T(8,128)(2,1)}), bf16[128,16,256]{2,1,0:T(8,128)(2,1)S(1)}, u32[]{:S(2)}, u32[]{:S(2)}) async-start(bf16[128,16,256]{2,1,0:T(8,128)(2,1)} %bitcast.8), calls=%async_computation.2 | async-start | bytes 2097152 | tf_op jit(solution)/shard_map/all_to_all | solution.py:182
  127.3 1.2 copy-start.3
  128.5 21.5 %copy-start.4 = (f32[16]{0:T(128)S(1)}, f32[16]{0:T(128)}, u32[]{:S(2)}) copy-start(f32[16]{0:T(128)} %param.13) | copy-start | bytes 196
  141.6 1.3 copy-start.2
  142.9 45.8 %all-to-all-start.3 = ((bf16[128,16,512]{2,1,0:T(8,128)(2,1)}), bf16[128,16,512]{2,1,0:T(8,128)(2,1)S(1)}, u32[]{:S(2)}, u32[]{:S(2)}) async-start(bf16[128,16,512]{2,1,0:T(8,128)(2,1)} %bitcast.24), calls=%async_computation.3 | async-start | bytes 4194304 | tf_op jit(solution)/shard_map/all_to_all | solution.py:187
  187.3 1.3 copy-start
  188.7 1.6 copy-start.1
Sparse Core Ops, SparseCore 0:
  9.5 82.3 all-gather.5
  93.6 86.1 all-gather.3

commit v3 on v2

v3 whole, which is shorter than its diff:
```python
import jax
import jax.numpy as jnp
from jax import lax
from jax.experimental import pallas as pl
from jax.experimental.pallas import tpu as pltpu
from jax.sharding import PartitionSpec as P

MIB = 1 << 20
NN = ((1,), (0,))
NT = ((1,), (1,))


def dot_f32(left, right, contract):
    return lax.dot_general(
        left, right, (contract, ((), ())), preferred_element_type=jnp.float32
    )


def params():
    return pltpu.CompilerParams(vmem_limit_bytes=56 * MIB)


def cost(flops, moved):
    return pl.CostEstimate(flops=flops, bytes_accessed=moved, transcendentals=0)


def flatten(ref):
    return ref[...].reshape(-1, ref.shape[-1])


def side_by_side(refs, out_ref):
    height, width = refs[0].shape[1:]
    for slot, ref in enumerate(refs):
        for part in range(ref.shape[0]):
            rows = slice(slot * height, (slot + 1) * height)
            out_ref[rows, part * width : (part + 1) * width] = ref[part]


def forward_step(own_ref, mate_ref, first_ref, second_ref, out_ref, rows_ref):
    @pl.when(pl.program_id(0) == 0)
    def _():
        side_by_side((own_ref, mate_ref), rows_ref)

    right = jnp.concatenate([flatten(first_ref), flatten(second_ref)], 0)
    vals = dot_f32(rows_ref[...], right, NT).astype(out_ref.dtype)
    states, _, _, inner, points = out_ref.shape
    vals = vals.reshape(2, states, inner, 2 * points)
    for block in range(2):
        for slot in range(2):
            out_ref[:, block, slot] = vals[slot, :, :, block * points : (block + 1) * points]


def forward_pass(own, mate, gathered, states, piece):
    n_narrow, height, width = own.shape
    shards, _, cols = gathered.shape
    inner = height // states
    points = shards * piece
    resident = pl.BlockSpec(own.shape, lambda s: (0, 0, 0))
    return pl.pallas_call(
        forward_step,
        grid=(n_narrow // 2,),
        in_specs=[
            resident,
            resident,
            pl.BlockSpec((shards, piece, cols), lambda s: (0, 2 * s, 0)),
            pl.BlockSpec((shards, piece, cols), lambda s: (0, 2 * s + 1, 0)),
        ],
        out_specs=pl.BlockSpec((states, 2, 2, inner, points), lambda s: (0, s, 0, 0, 0)),
        out_shape=jax.ShapeDtypeStruct((states, n_narrow, 2, inner, points), jnp.bfloat16),
        scratch_shapes=[pltpu.VMEM((2 * height, cols), jnp.bfloat16)],
        compiler_params=params(),
        cost_estimate=cost(4 * height * cols * points * n_narrow, 8 * MIB),
        name="forward_pass",
    )(own, mate, gathered, gathered)


def middle_step(
    values_ref, grid_ref, turned_ref, potential_ref, across_ref, out_ref, rows_ref, kept_ref
):
    step = pl.program_id(0)
    half = pl.num_programs(0) // 2
    tile = grid_ref.shape[0]
    points = values_ref.shape[-1]
    width = 2 * points

    @pl.when(step == 0)
    def _():
        rows_ref[:, :, :, :points] = values_ref[:, 0]
        for slot in range(2):
            rows_ref[:, slot, :, points:] = values_ref[:, 1, 1 - slot]

    @pl.when(step < half)
    def _():
        vals = dot_f32(grid_ref[...], rows_ref[...].reshape(-1, width), NN)
        weighted = vals * potential_ref[...].astype(jnp.float32)
        kept_ref[pl.ds(pl.multiple_of(step * tile, tile), tile)] = weighted.astype(jnp.bfloat16)

    @pl.when(step >= half)
    def _():
        out_ref[:, :width] = dot_f32(turned_ref[...], kept_ref[...], NN).astype(out_ref.dtype)
        out_ref[:, width:] = across_ref[...]


def middle_pass(values, grid_one, turned, potential, across, tile=512):
    n_one, width = across.shape
    half = n_one // tile
    early = lambda s: (jnp.minimum(s, half - 1), 0)
    late = lambda s: (jnp.maximum(s - half, 0), 0)
    groups, _, _, inner, points = values.shape
    return pl.pallas_call(
        middle_step,
        grid=(2 * half,),
        in_specs=[
            pl.BlockSpec(values.shape, lambda s: (0, 0, 0, 0, 0)),
            pl.BlockSpec((tile, n_one), early),
            pl.BlockSpec((tile, n_one), late),
            pl.BlockSpec((tile, width), early),
            pl.BlockSpec((tile, width), late),
        ],
        out_specs=pl.BlockSpec((tile, 2 * width), late),
        out_shape=jax.ShapeDtypeStruct((n_one, 2 * width), jnp.bfloat16),
        scratch_shapes=[
            pltpu.VMEM((groups, 2, inner, 2 * points), jnp.bfloat16),
            pltpu.VMEM((n_one, width), jnp.bfloat16),
        ],
        compiler_params=params(),
        cost_estimate=cost(4 * n_one * n_one * width, 21 * MIB),
        name="middle_pass",
    )(values, grid_one, turned, potential, across)


def applied_step(own_ref, mate_ref, ham_ref, out_ref, sent_ref, rows_ref):
    @pl.when(pl.program_id(0) == 0)
    def _():
        side_by_side((own_ref, mate_ref), rows_ref)

    vals = dot_f32(rows_ref[...], flatten(ham_ref), NT)
    height = out_ref.shape[0]
    out_ref[...] = vals[:height]
    sent_ref[...] = vals[height:].astype(sent_ref.dtype)


def applied_pass(own, mate, gathered, steps=4):
    n_narrow, height, width = own.shape
    shards, depth, cols = gathered.shape
    depth = depth // 2
    points = shards * depth
    resident = pl.BlockSpec(own.shape, lambda s: (0, 0, 0))
    block = pl.BlockSpec((height, points // steps), lambda s: (0, s))
    return pl.pallas_call(
        applied_step,
        grid=(steps,),
        in_specs=[
            resident,
            resident,
            pl.BlockSpec((shards // steps, depth, cols), lambda s: (s, 1, 0)),
        ],
        out_specs=[block, block],
        out_shape=[
            jax.ShapeDtypeStruct((height, points), jnp.float32),
            jax.ShapeDtypeStruct((height, points), jnp.bfloat16),
        ],
        scratch_shapes=[pltpu.VMEM((2 * height, cols), jnp.bfloat16)],
        compiler_params=params(),
        cost_estimate=cost(4 * height * cols * points, 8 * MIB),
        name="applied_pass",
    )(own, mate, gathered)


def final_step(
    half_ref, near_ref, far_ref, near_a, near_b, far_a, far_b, across_ref, kept_ref, moved_ref,
    own_ref, energy_ref, swap_ref, out_ref, acc_ref,
):
    step = pl.program_id(0)
    states, _, rows, _ = near_ref.shape
    height = states * rows
    lefts = [ref[:, block].reshape(height, -1) for ref in (near_ref, far_ref) for block in range(2)]
    rights = [flatten(ref) for ref in (near_a, near_b, far_a, far_b)]
    total = dot_f32(jnp.concatenate(lefts, 1), jnp.concatenate(rights, 0), NN)

    @pl.when(step == 0)
    def _():
        acc_ref[...] = total

    @pl.when(step > 0)
    def _():
        acc_ref[...] += total

    @pl.when(step == pl.num_programs(0) - 1)
    def _():
        even = half_ref[0] == 0
        blocks, _, width = own_ref.shape
        part = width // 2
        for block in range(blocks):
            cols = slice(block * width, (block + 1) * width)
            kept = kept_ref[:, block * part : (block + 1) * part]
            moved = moved_ref[:, block * part : (block + 1) * part].astype(jnp.float32)
            applied = [jnp.where(even, kept, moved), jnp.where(even, moved, kept)]
            value = acc_ref[:, cols] + jnp.concatenate(applied, 1)
            value += across_ref[:, block].reshape(height, width).astype(jnp.float32)
            value += energy_ref[...] * own_ref[block].astype(jnp.float32)
            swapped = dot_f32(swap_ref[...], value.astype(jnp.bfloat16), NN)
            out_ref[:, :, cols] = swapped.astype(out_ref.dtype).reshape(rows, states, width)


def final_pass(half, received, near, far, kept, moved, own, energy, swap, piece):
    states, blocks, rows, double = received.shape
    width = double // 2
    height = states * rows
    shards, _, cols = near.shape
    points = shards * piece
    weights = [
        pl.BlockSpec((shards, piece, cols), lambda s, h: (0, 2 * s, 0)),
        pl.BlockSpec((shards, piece, cols), lambda s, h: (0, 2 * s + 1, 0)),
    ]
    whole = lambda array: pl.BlockSpec(array.shape, lambda s, h: (0,) * array.ndim)
    return pl.pallas_call(
        final_step,
        grid_spec=pltpu.PrefetchScalarGridSpec(
            num_scalar_prefetch=1,
            grid=(blocks // 2,),
            in_specs=[
                pl.BlockSpec((states, 2, rows, points), lambda s, h: (0, s, 0, h[0])),
                pl.BlockSpec((states, 2, rows, points), lambda s, h: (0, s, 0, 1 - h[0])),
                *weights,
                *weights,
                pl.BlockSpec((states, blocks, rows, width), lambda s, h: (0, 0, 0, 1)),
                whole(kept),
                whole(moved),
                whole(own),
                whole(energy),
                whole(swap),
            ],
            out_specs=pl.BlockSpec((rows, states, cols), lambda s, h: (0, 0, 0)),
            scratch_shapes=[pltpu.VMEM((height, cols), jnp.float32)],
        ),
        out_shape=jax.ShapeDtypeStruct((rows, states, cols), jnp.bfloat16),
        compiler_params=params(),
        cost_estimate=cost(2 * height * cols * (cols + height), 14 * MIB),
        name="final_pass",
    )(
        half, received, received, near, near, far, far, received, kept, moved, own, energy, swap
    )


def on_device(coeffs, ham_one, grid_one, ham_two, grid_two, pair_potential, third_energy):
    n_wide = lax.axis_size("wide")
    n_narrow = lax.axis_size("narrow")
    both = ("wide", "narrow")
    half = lax.axis_index("narrow") % 2
    core = lax.axis_index("wide") % 2
    narrow_pairs = [(n, n ^ 1) for n in range(n_narrow)]
    wide_pairs = [(w, w ^ 1) for w in range(n_wide)]

    local = coeffs[0]
    rows, states, width = local.shape
    n_one, count = pair_potential.shape
    cols = grid_two.shape[1]
    inner = rows // n_narrow
    height = inner * states
    piece = count // 2
    share = rows // 2
    assert states == n_wide and inner == count and n_wide * count == width

    pieces = grid_two.reshape(n_narrow, 2, piece, cols)
    near = lax.dynamic_index_in_dim(pieces, half, 1, False).reshape(share, cols)
    far = lax.dynamic_index_in_dim(pieces, 1 - half, 1, False).reshape(share, cols)
    slim = pair_potential.T.astype(jnp.bfloat16)
    near = lax.all_gather(jnp.concatenate([near, slim], 0), "wide", axis=0, tiled=False)

    away = lax.dynamic_slice_in_dim(ham_two, (1 - core) * share, share, 0)
    stay = lax.dynamic_slice_in_dim(ham_two, core * share, share, 0)
    stay = jnp.where(core == half, stay, lax.ppermute(away, "wide", wide_pairs))
    far = lax.all_gather(jnp.concatenate([far, stay], 0), "wide", axis=0, tiled=False)

    own = local.reshape(n_narrow, inner, states, width).swapaxes(1, 2)
    own = lax.all_to_all(own.reshape(n_narrow, height, width), "narrow", 0, 0, tiled=True)
    mate = lax.ppermute(own, "narrow", narrow_pairs)
    by_state = lax.all_to_all(jnp.swapaxes(local, 0, 1), "wide", 0, 0, tiled=True)
    across = dot_f32(ham_one, by_state.reshape(n_one, width), NN).astype(jnp.bfloat16)
    turned = lax.optimization_barrier(grid_one.T)
    own, mate, across, turned = lax.optimization_barrier((own, mate, across, turned))

    values = forward_pass(own, mate, near, states, piece)
    values = lax.all_to_all(
        values.reshape(n_wide * n_narrow, 2 * inner, width // 2), both, 0, 0, tiled=True
    )
    values = values.reshape(n_wide * n_narrow // 2, 2, 2, inner, width // 2)
    potential = near[:, share:].reshape(n_wide, 2, piece, n_one).swapaxes(0, 1)
    potential = potential.reshape(width, n_one).T
    pair = middle_pass(values, grid_one, turned, potential, across)
    pair = lax.all_to_all(
        pair.reshape(n_wide * n_narrow, inner, 2 * width), both, 0, 0, tiled=True
    )

    kept, moved = applied_pass(own, mate, far)
    moved = lax.ppermute(moved, "narrow", narrow_pairs)
    energy = jnp.repeat(third_energy, inner)[:, None]
    target = jnp.arange(height)
    source = target % states * inner + target // states
    swap = (source[:, None] == jnp.arange(height)[None, :]).astype(jnp.bfloat16)
    out = final_pass(
        half[None],
        pair.reshape(n_wide, n_narrow, inner, 2 * width),
        near, far, kept, moved, own, energy, swap, piece,
    )
    return out[None]


def solution(mesh):
    return jax.shard_map(
        on_device,
        mesh=mesh,
        in_specs=(
            P(None, "wide", None, "narrow"),
            P(),
            P(),
            P("wide", None),
            P("wide", None),
            P(None, ("wide", "narrow")),
            P(),
        ),
        out_specs=P(None, ("wide", "narrow"), None, None),
        check_vma=False,
    )
```

time: 208 us -> 199 us (0.957)
  waiting for transfers between devices: 99.9 us -> 75.9 us
  local copies, waits for them, and re-layouts: 14.6 us -> 24.7 us
  starting transfers between devices: 30.3 us -> 36.9 us
  Pallas kernels: 38.6 us -> 35.3 us
    all_gather x2, waiting for transfers between devices: 51.3 us -> 21.2 us  [the longest x1 21.2 us: on_device(): lax.all_gather(jnp.concatenate([far, stay], 0), 'wide', axis=0, tiled=False)]
    all_to_all x1, waiting for transfers between devices: 23 us -> 10.5 us  [on_device(): lax.all_to_all(jnp.swapaxes(local, 0, 1), 'wide', 0, 0, tiled=True)]
    ppermute x0 -> x3, waiting for transfers between devices: none -> 11.9 us  [the longest x1 10.7 us: on_device(): moved = lax.ppermute(moved, 'narrow', narrow_pairs)]
    ppermute x0 -> x3, starting transfers between devices: none -> 9.86 us  [the longest x1 7.18 us: on_device(): moved = lax.ppermute(moved, 'narrow', narrow_pairs)]
    unnamed x11 -> x16, local copies, waits for them, and re-layouts: 8 us -> 16.5 us
    all_to_all x1, waiting for transfers between devices: 10.4 us -> 16.7 us  [on_device(): lax.all_to_all(own.reshape(n_narrow, height, width), 'narrow', 0, 0, tile...]
    pallas_call x4, Pallas kernels: 38.6 us -> 35.3 us  [the longest x1 12.9 us: middle_pass(): pl.pallas_call(middle_step, grid=(2 * half,), in_specs=[pl.BlockSpec(valu...]
    all_to_all x1, starting transfers between devices: 8.67 us -> 6.2 us  [on_device(): lax.all_to_all(values.reshape(n_wide * n_narrow, 2 * inner, width // 2),...]
  transfers between devices with their start and end apart: 6 -> 9, of which waited for: 5 -> 6; matrix products, arithmetic and copies ran while one was open for 8% -> 15% of each run, Pallas kernels for 14% -> 13%
where the time goes in v3:
time: 199 us; the launch traced here: 197 us
  waiting for transfers between devices  75.9 us (38%)
  starting transfers between devices  36.9 us (19%)
  Pallas kernels  35.3 us (18%)
  local copies, waits for them, and re-layouts  24.7 us (12%)
  between operations  13.5 us (7%)
  matrix products  6.81 us (3%)
  other arithmetic  4.36 us (2%)
    all_gather x1, waiting for transfers between devices, on_device(): lax.all_gather(jnp.concatenate([far, stay], 0), 'wide', axis=0, tiled=False)  21.2 us
    all_to_all x1, waiting for transfers between devices, on_device(): lax.all_to_all(own.reshape(n_narrow, height, width), 'narrow', 0, 0, tile...  16.7 us
    unnamed x16, local copies, waits for them, and re-layouts  16.5 us
    all_to_all x1, waiting for transfers between devices, on_device(): lax.all_to_all(values.reshape(n_wide * n_narrow, 2 * inner, width // 2),...  15.5 us
    pallas_call x1, Pallas kernels, middle_pass(): pl.pallas_call(middle_step, grid=(2 * half,), in_specs=[pl.BlockSpec(valu...  12.9 us
    ppermute x1, waiting for transfers between devices, on_device(): moved = lax.ppermute(moved, 'narrow', narrow_pairs)  10.7 us
    all_to_all x1, waiting for transfers between devices, on_device(): lax.all_to_all(jnp.swapaxes(local, 0, 1), 'wide', 0, 0, tiled=True)  10.5 us
    pallas_call x1, Pallas kernels, final_pass(): pl.pallas_call(final_step, grid_spec=pltpu.PrefetchScalarGridSpec(num_sca...  9.2 us
  transfers between devices with their start and end apart: 9, of which 6 were waited for; matrix products, arithmetic and copies ran while one was open for 15% of the time, Pallas kernels for 13%

profile of v3, /device:TPU:1, one launch (start us, length us, event | category | flops | bytes accessed | tf_op | source)
XLA Modules:
  0.0 197.4 jit_solution(10021588495461261496)
XLA Ops:
  6.5 0.0 copy-start.2
  6.5 0.0 all-gather.5.cloned.1.call-start
  6.5 1.0 convert_bitcast_fusion
  7.5 1.1 dynamic-slice_bitcast_fusion
  8.6 0.7 pad_maximum_fusion.1
  9.4 0.0 all-gather.5.cloned.1.call-update
  9.4 0.0 all-gather.7.cloned.1.call-start
  9.4 1.0 constant_dynamic-slice_fusion
  10.4 1.5 collective-permute-start.1
  11.9 1.2 collective-permute-done.1
  13.1 1.0 dynamic-slice_select_fusion
  14.1 0.8 pad_maximum_fusion
  14.9 0.0 all-gather.7.cloned.1.call-update
  15.0 2.6 %copy.11 = bf16[8,16,16,256]{3,1,2,0:T(8,128)(2,1)} copy(bf16[8,16,16,256]{3,2,1,0:T(8,128)(2,1)} %bitcast.47) | data formatting | bytes 2097152 | tf_op jit(solution)/shard_map/reshape;squeeze | solution.py:276
  17.5 6.7 %all-to-all-start = ((bf16[8,256,256]{2,1,0:T(8,128)(2,1)}), bf16[8,256,256]{2,1,0:T(8,128)(2,1)S(1)}, u32[]{:S(2)}, u32[]{:S(2)}) async-start(bf16[8,256,256]{2,1,0:T(8,128)(2,1)} %bitcast.3), calls=%async_computation | async-start | bytes 2097152 | tf_op jit(solution)/shard_map/all_to_all | solution.py:277
  24.3 0.0 copy-done.2
  24.3 1.3 copy.18
  25.6 16.7 %all-to-all-done.own_ref = bf16[8,256,256]{2,1,0:T(8,128)(2,1)S(1)} async-done(((bf16[8,256,256]{2,1,0:T(8,128)(2,1)}), bf16[8,256,256]{2,1,0:T(8,128)(2,1)S(1)}, u32[]{:S(2)}, u32[]{:S(2)}) %all-to-all-start) | async-done | bytes 1048608 | tf_op jit(solution)/shard_map/all_to_all | solution.py:277
  42.3 0.0 copy-start.1
  42.3 6.9 %all-to-all-start.1 = ((bf16[16,128,256]{2,1,0:T(8,128)(2,1)}), bf16[16,128,256]{2,1,0:T(8,128)(2,1)S(1)}, u32[]{:S(2)}, u32[]{:S(2)}) async-start(bf16[16,128,256]{2,1,0:T(8,128)(2,1)} %bitcast.33), calls=%async_computation.1 | async-start | bytes 2097152 | tf_op jit(solution)/shard_map/all_to_all | solution.py:279
  49.3 1.2 collective-permute-start
  50.5 12.4 %copy.13 = bf16[2048,2048]{0,1:T(8,128)(2,1)} copy(bf16[2048,2048]{1,0:T(8,128)(2,1)} %grid_ref.1) | data formatting | bytes 16777216 | tf_op args[2]
  62.9 0.0 copy-done.1
  62.9 10.5 %all-to-all-done.1 = bf16[16,128,256]{2,1,0:T(8,128)(2,1)S(1)} async-done(((bf16[16,128,256]{2,1,0:T(8,128)(2,1)}), bf16[16,128,256]{2,1,0:T(8,128)(2,1)S(1)}, u32[]{:S(2)}, u32[]{:S(2)}) %all-to-all-start.1) | async-done | bytes 1048608 | tf_op jit(solution)/shard_map/all_to_all | solution.py:279
  73.3 6.8 %convolution_convert_fusion.across_ref = bf16[2048,256]{1,0:T(8,128)(2,1)} fusion(bf16[2048,2048]{1,0:T(8,128)(2,1)} %param.8, bf16[2048,256]{1,0:T(8,128)(2,1)S(1)} %bitcast.52), kind=kOutput, calls=%fused_computation | convolution fusion | flops 2148007936 | bytes 10485760 | tf_op jit(solution)/shard_map/dot_general | solution.py:14
  80.1 0.0 collective-permute-done.mate_ref
  80.1 1.0 copy-done.3
  81.1 6.7 %forward_pass.1 = bf16[16,8,2,16,128]{4,3,2,1,0:T(8,128)(2,1)} custom-call(bf16[8,256,256]{2,1,0:T(8,128)(2,1)} %copy-done.1, bf16[8,256,256]{2,1,0:T(8,128)(2,1)} %copy-done.3, bf16[16,80,2048]{2,1,0:T(8,128)(2,1)} %bitcast.34, bf16[16,80,2048]{2,1,0:T(8,128)(2,1)} %bitcast.35), custom_call_target="tpu_custom_call" | custom-call | flops 2147483648 | bytes 8388608 | tf_op jit(solution)/shard_map/forward_pass/pallas_call | solution.py:59
  87.8 6.2 %all-to-all-start.2 = ((bf16[128,32,128]{2,1,0:T(8,128)(2,1)}), bf16[128,32,128]{2,1,0:T(8,128)(2,1)S(1)}, u32[]{:S(2)}, u32[]{:S(2)}) async-start(bf16[128,32,128]{2,1,0:T(8,128)(2,1)} %bitcast.49), calls=%async_computation.2 | async-start | bytes 2097152 | tf_op jit(solution)/shard_map/all_to_all | solution.py:285
  94.1 1.4 slice_bitcast_fusion
  95.4 0.1 copy.14
  95.5 1.3 copy.15
  96.8 15.5 %all-to-all-done.2 = bf16[128,32,128]{2,1,0:T(8,128)(2,1)S(1)} async-done(((bf16[128,32,128]{2,1,0:T(8,128)(2,1)}), bf16[128,32,128]{2,1,0:T(8,128)(2,1)S(1)}, u32[]{:S(2)}, u32[]{:S(2)}) %all-to-all-start.2) | async-done | bytes 1048608 | tf_op jit(solution)/shard_map/all_to_all | solution.py:285
  112.3 1.0 copy-done.4
  113.3 12.9 %middle_pass.1 = bf16[2048,512]{1,0:T(8,128)(2,1)} custom-call(bf16[64,2,2,16,128]{4,3,2,1,0:T(8,128)(2,1)} %bitcast.50, bf16[2048,2048]{1,0:T(8,128)(2,1)} %grid_ref.1, bf16[2048,2048]{1,0:T(8,128)(2,1)} %bitcast.45, bf16[2048,256]{1,0:T(8,128)(2,1)} %bitcast.51, bf16[2048,256]{1,0:T(8,128)(2,1)} %convolution_convert_fusion.across_ref), custom_call_target="tpu_custom_call" | custom-call | flops 4294967296 | bytes 22020096 | tf_op jit(solution)/shard_map/middle_pass/pallas_call | solution.py:110
  126.3 7.1 %all-to-all-start.3 = ((bf16[128,16,512]{2,1,0:T(8,128)(2,1)}), bf16[128,16,512]{2,1,0:T(8,128)(2,1)S(1)}, u32[]{:S(2)}, u32[]{:S(2)}) async-start(bf16[128,16,512]{2,1,0:T(8,128)(2,1)} %bitcast.46), calls=%async_computation.3 | async-start | bytes 4194304 | tf_op jit(solution)/shard_map/all_to_all | solution.py:292
  133.4 21.2 %all-gather.7.cloned.1.call-done = bf16[2048,2048]{1,0:T(8,128)(2,1)} async-done(((bf16[128,2048]{1,0:T(8,128)(2,1)}), bf16[2048,2048]{1,0:T(8,128)(2,1)}) %all-gather.7.cloned.1.call-update) | async-done | bytes 8388624 | tf_op jit(solution)/shard_map/all_gather | solution.py:274
  154.6 6.5 %applied_pass.1 = (f32[256,1024]{1,0:T(8,128)}, bf16[256,1024]{1,0:T(8,128)(2,1)}) custom-call(bf16[8,256,256]{2,1,0:T(8,128)(2,1)} %copy-done.1, bf16[8,256,256]{2,1,0:T(8,128)(2,1)} %copy-done.3, bf16[16,128,2048]{2,1,0:T(8,128)(2,1)} %bitcast.39), custom_call_target="tpu_custom_call" | custom-call | flops 2147483648 | bytes 8388608 | tf_op jit(solution)/shard_map/applied_pass/pallas_call | solution.py:150
  161.1 7.2 %collective-permute-start.2 = (bf16[256,1024]{1,0:T(8,128)(2,1)}, bf16[256,1024]{1,0:T(8,128)(2,1)S(1)}, u32[]{:S(2)}, u32[]{:S(2)}) collective-permute-start(bf16[256,1024]{1,0:T(8,128)(2,1)} %get-tuple-element.16), channel_id=1, source_target_pairs={{0,1},{1,0},{2,3},{3,2},{4,5},{5,4},{6,7},{7,6},{8,9},{9,8},{10,11... | collective-permute-start | bytes 1572872 | tf_op jit(solution)/shard_map/ppermute | solution.py:297
  168.3 0.0 copy-done.6
  168.3 0.1 broadcast_in_dim.12
  168.4 0.8 broadcast_in_dim_reshape.4.energy_ref
  169.1 0.8 fusion.swap_ref
  169.9 0.0 all-to-all-done.3
  169.9 10.7 %collective-permute-done.2.moved_ref = bf16[256,1024]{1,0:T(8,128)(2,1)S(1)} collective-permute-done((bf16[256,1024]{1,0:T(8,128)(2,1)}, bf16[256,1024]{1,0:T(8,128)(2,1)S(1)}, u32[]{:S(2)}, u32[]{:S(2)}) %collective-permute-start.2) | collective-permute-done | bytes 524320 | tf_op jit(solution)/shard_map/ppermute | solution.py:297
  180.6 0.0 copy-done
  180.6 0.8 copy-done.5
  181.4 9.2 %final_pass.1 = bf16[16,16,2048]{2,1,0:T(8,128)(2,1)} custom-call(s32[1]{0:T(128)} %bitcast.half_ref, bf16[16,8,16,512]{3,2,1,0:T(8,128)(2,1)} %bitcast.42, bf16[16,8,16,512]{3,2,1,0:T(8,128)(2,1)} %bitcast.43, bf16[16,80,2048]{2,1,0:T(8,128)(2,1)} %bitcast.37, bf16[16,80,2048]{2,1,0:T(8,128)(2,1)} %bitcast.38, bf16[16,128,2048]{2,1,0:T(8,128)(2,1)} %bitcast.40, ...), custom_call_target="tpu_custom_call" | custom-call | flops 2415919104 | bytes 14680064 | tf_op jit(solution)/shard_map/final_pass/pallas_call | solution.py:217
  (7 shorter events, 0.0 us)
Async XLA Ops:
  6.5 17.7 %copy-start.2 = (bf16[1,128,16,256]{3,2,1,0:T(8,128)(2,1)S(1)}, bf16[1,128,16,256]{3,2,1,0:T(8,128)(2,1)}, u32[]{:S(2)}) copy-start(bf16[1,128,16,256]{3,2,1,0:T(8,128)(2,1)} %param.7) | copy-start | bytes 3145732
  6.5 73.6 %all-gather.5.cloned.1.call-start = ((), (), s32[]{:S(2)}) async-start(), calls=%async_computation.4 | async-start | bytes 5570560 | tf_op jit(solution)/shard_map/all_gather | solution.py:269
  9.4 145.2 %all-gather.7.cloned.1.call-start = ((), (), s32[]{:S(2)}) async-start(), calls=%async_computation.5 | async-start | bytes 8912896 | tf_op jit(solution)/shard_map/all_gather | solution.py:274
  10.4 2.7 %collective-permute-start.1 = (bf16[64,2048]{1,0:T(8,128)(2,1)S(1)}, bf16[64,2048]{1,0:T(8,128)(2,1)S(1)}, u32[]{:S(2)}, u32[]{:S(2)}) collective-permute-start(bf16[64,2048]{1,0:T(8,128)(2,1)S(1)} %constant_dynamic-slice_fusion), channel_id=1, source_target_pairs={{0,8},{8,0},{16,24},{24,16},{32,40},{40,32},{48,56},{56,48},{64,72... | collective-permute-start | bytes 786440 | tf_op jit(solution)/shard_map/ppermute | solution.py:273
  17.5 24.8 %all-to-all-start = ((bf16[8,256,256]{2,1,0:T(8,128)(2,1)}), bf16[8,256,256]{2,1,0:T(8,128)(2,1)S(1)}, u32[]{:S(2)}, u32[]{:S(2)}) async-start(bf16[8,256,256]{2,1,0:T(8,128)(2,1)} %bitcast.3), calls=%async_computation | async-start | bytes 2097152 | tf_op jit(solution)/shard_map/all_to_all | solution.py:277
  42.3 20.5 %copy-start.1 = (bf16[8,256,256]{2,1,0:T(8,128)(2,1)}, bf16[8,256,256]{2,1,0:T(8,128)(2,1)S(1)}, u32[]{:S(2)}) copy-start(bf16[8,256,256]{2,1,0:T(8,128)(2,1)S(1)} %all-to-all-done.own_ref) | copy-start | bytes 3145732
  42.3 31.0 %all-to-all-start.1 = ((bf16[16,128,256]{2,1,0:T(8,128)(2,1)}), bf16[16,128,256]{2,1,0:T(8,128)(2,1)S(1)}, u32[]{:S(2)}, u32[]{:S(2)}) async-start(bf16[16,128,256]{2,1,0:T(8,128)(2,1)} %bitcast.33), calls=%async_computation.1 | async-start | bytes 2097152 | tf_op jit(solution)/shard_map/all_to_all | solution.py:279
  49.3 30.9 %collective-permute-start = (bf16[8,256,256]{2,1,0:T(8,128)(2,1)S(1)}, bf16[8,256,256]{2,1,0:T(8,128)(2,1)S(1)}, u32[]{:S(2)}, u32[]{:S(2)}) collective-permute-start(bf16[8,256,256]{2,1,0:T(8,128)(2,1)S(1)} %all-to-all-done.own_ref), channel_id=1, source_target_pairs={{0,1},{1,0},{2,3},{3,2},{4,5},{5,4},{6,7},{7,6},{8,9},{9,8},{10,11... | collective-permute-start | bytes 3145736 | tf_op jit(solution)/shard_map/ppermute | solution.py:278
  80.1 1.0 copy-start.3
  87.8 24.5 %all-to-all-start.2 = ((bf16[128,32,128]{2,1,0:T(8,128)(2,1)}), bf16[128,32,128]{2,1,0:T(8,128)(2,1)S(1)}, u32[]{:S(2)}, u32[]{:S(2)}) async-start(bf16[128,32,128]{2,1,0:T(8,128)(2,1)} %bitcast.49), calls=%async_computation.2 | async-start | bytes 2097152 | tf_op jit(solution)/shard_map/all_to_all | solution.py:285
  112.3 1.0 copy-start.4
  126.3 42.0 %copy-start.6 = (f32[16]{0:T(128)S(1)}, f32[16]{0:T(128)}, u32[]{:S(2)}) copy-start(f32[16]{0:T(128)} %param.13) | copy-start | bytes 196
  126.3 43.6 %all-to-all-start.3 = ((bf16[128,16,512]{2,1,0:T(8,128)(2,1)}), bf16[128,16,512]{2,1,0:T(8,128)(2,1)S(1)}, u32[]{:S(2)}, u32[]{:S(2)}) async-start(bf16[128,16,512]{2,1,0:T(8,128)(2,1)} %bitcast.46), calls=%async_computation.3 | async-start | bytes 4194304 | tf_op jit(solution)/shard_map/all_to_all | solution.py:292
  161.1 19.5 %collective-permute-start.2 = (bf16[256,1024]{1,0:T(8,128)(2,1)}, bf16[256,1024]{1,0:T(8,128)(2,1)S(1)}, u32[]{:S(2)}, u32[]{:S(2)}) collective-permute-start(bf16[256,1024]{1,0:T(8,128)(2,1)} %get-tuple-element.16), channel_id=1, source_target_pairs={{0,1},{1,0},{2,3},{3,2},{4,5},{5,4},{6,7},{7,6},{8,9},{9,8},{10,11... | collective-permute-start | bytes 1572872 | tf_op jit(solution)/shard_map/ppermute | solution.py:297
  169.9 10.7 %copy-start = (bf16[128,16,512]{2,1,0:T(8,128)(2,1)}, bf16[128,16,512]{2,1,0:T(8,128)(2,1)S(1)}, u32[]{:S(2)}) copy-start(bf16[128,16,512]{2,1,0:T(8,128)(2,1)S(1)} %all-to-all-done.3) | copy-start | bytes 6291460
  180.6 0.8 copy-start.5
Sparse Core Ops, SparseCore 0:
  9.5 64.9 all-gather.4
  76.2 78.3 all-gather.6

commit v4 on v3

--- a/solution.py
+++ b/solution.py
@@ -101,7 +101,7 @@
         out_ref[:, width:] = across_ref[...]
 
 
-def middle_pass(values, grid_one, turned, potential, across, tile=512):
+def middle_pass(values, grid_one, turned, potential, across, tile=1024):
     n_one, width = across.shape
     half = n_one // tile
     early = lambda s: (jnp.minimum(s, half - 1), 0)
@@ -143,7 +143,6 @@
 def applied_pass(own, mate, gathered, steps=4):
     n_narrow, height, width = own.shape
     shards, depth, cols = gathered.shape
-    depth = depth // 2
     points = shards * depth
     resident = pl.BlockSpec(own.shape, lambda s: (0, 0, 0))
     block = pl.BlockSpec((height, points // steps), lambda s: (0, s))
@@ -153,7 +152,7 @@
         in_specs=[
             resident,
             resident,
-            pl.BlockSpec((shards // steps, depth, cols), lambda s: (s, 1, 0)),
+            pl.BlockSpec((shards // steps, depth, cols), lambda s: (s, 0, 0)),
         ],
         out_specs=[block, block],
         out_shape=[
@@ -243,6 +242,27 @@
     )
 
 
+def fetch_other_half(near, after, core, share):
+    n_narrow = lax.axis_size("narrow")
+    shards = near.shape[0]
+    quarter = shards // 4
+    ring = 4
+    near, _ = lax.optimization_barrier((near, after))
+    got = []
+    for side in (0, 1):
+        step = 1 - 2 * side
+        pairs = [(n, n // ring * ring + (n + step) % ring) for n in range(n_narrow)]
+        first = 2 * quarter * core + quarter * side
+        part = lax.dynamic_slice(near, (first, 0, 0), (quarter, share, near.shape[2]))
+        got.append(lax.ppermute(part, "narrow", pairs))
+    mine = jnp.concatenate(got, 0)
+    pairs = [(w, w ^ 1) for w in range(lax.axis_size("wide"))]
+    theirs = lax.ppermute(mine, "wide", pairs)
+    return jnp.where(
+        core == 0, jnp.concatenate([mine, theirs], 0), jnp.concatenate([theirs, mine], 0)
+    )
+
+
 def on_device(coeffs, ham_one, grid_one, ham_two, grid_two, pair_potential, third_energy):
     n_wide = lax.axis_size("wide")
     n_narrow = lax.axis_size("narrow")
@@ -264,24 +284,24 @@
 
     pieces = grid_two.reshape(n_narrow, 2, piece, cols)
     near = lax.dynamic_index_in_dim(pieces, half, 1, False).reshape(share, cols)
-    far = lax.dynamic_index_in_dim(pieces, 1 - half, 1, False).reshape(share, cols)
     slim = pair_potential.T.astype(jnp.bfloat16)
     near = lax.all_gather(jnp.concatenate([near, slim], 0), "wide", axis=0, tiled=False)
 
     away = lax.dynamic_slice_in_dim(ham_two, (1 - core) * share, share, 0)
     stay = lax.dynamic_slice_in_dim(ham_two, core * share, share, 0)
     stay = jnp.where(core == half, stay, lax.ppermute(away, "wide", wide_pairs))
-    far = lax.all_gather(jnp.concatenate([far, stay], 0), "wide", axis=0, tiled=False)
+    half_ham = lax.all_gather(stay, "wide", axis=0, tiled=False)
 
     own = local.reshape(n_narrow, inner, states, width).swapaxes(1, 2)
     own = lax.all_to_all(own.reshape(n_narrow, height, width), "narrow", 0, 0, tiled=True)
     mate = lax.ppermute(own, "narrow", narrow_pairs)
     by_state = lax.all_to_all(jnp.swapaxes(local, 0, 1), "wide", 0, 0, tiled=True)
+    turned = lax.optimization_barrier(grid_one.T)
+    own, mate, by_state, turned = lax.optimization_barrier((own, mate, by_state, turned))
+
+    values = forward_pass(own, mate, near, states, piece)
     across = dot_f32(ham_one, by_state.reshape(n_one, width), NN).astype(jnp.bfloat16)
-    turned = lax.optimization_barrier(grid_one.T)
-    own, mate, across, turned = lax.optimization_barrier((own, mate, across, turned))
-
-    values = forward_pass(own, mate, near, states, piece)
+    far = fetch_other_half(near, values, core, share)
     values = lax.all_to_all(
         values.reshape(n_wide * n_narrow, 2 * inner, width // 2), both, 0, 0, tiled=True
     )
@@ -293,7 +313,7 @@
         pair.reshape(n_wide * n_narrow, inner, 2 * width), both, 0, 0, tiled=True
     )
 
-    kept, moved = applied_pass(own, mate, far)
+    kept, moved = applied_pass(own, mate, half_ham)
     moved = lax.ppermute(moved, "narrow", narrow_pairs)
     energy = jnp.repeat(third_energy, inner)[:, None]
     target = jnp.arange(height)

time: 199 us -> 197 us (0.990)
  waiting for transfers between devices: 75.9 us -> 47.5 us
  blocking collectives: 0 us -> 24.3 us
  other arithmetic: 4.36 us -> 11.1 us
  starting transfers between devices: 36.9 us -> 31.7 us
    all_to_all x0 -> x1, blocking collectives: none -> 24.3 us  [on_device(): lax.all_to_all(own.reshape(n_narrow, height, width), 'narrow', 0, 0, tile...]
    all_gather x1, waiting for transfers between devices: 21.2 us -> 0.01 us  [on_device(): half_ham = lax.all_gather(stay, 'wide', axis=0, tiled=False)]
    all_to_all x1 -> x0, waiting for transfers between devices: 16.7 us -> none  [on_device(): lax.all_to_all(own.reshape(n_narrow, height, width), 'narrow', 0, 0, tile...]
    all_to_all x1, waiting for transfers between devices: 15.5 us -> 3.34 us  [on_device(): lax.all_to_all(values.reshape(n_wide * n_narrow, 2 * inner, width // 2),...]
    ppermute x0 -> x3, waiting for transfers between devices: none -> 10.2 us  [the longest x2 10.2 us: fetch_other_half(): got.append(lax.ppermute(part, 'narrow', pairs))]
    ppermute x1, waiting for transfers between devices: 10.7 us -> 20.6 us  [on_device(): moved = lax.ppermute(moved, 'narrow', narrow_pairs)]
    all_to_all x1 -> x0, starting transfers between devices: 6.73 us -> none  [on_device(): lax.all_to_all(own.reshape(n_narrow, height, width), 'narrow', 0, 0, tile...]
    ppermute x0 -> x3, starting transfers between devices: none -> 6.34 us  [the longest x1 3.89 us: fetch_other_half(): theirs = lax.ppermute(mine, 'wide', pairs)]
  transfers between devices with their start and end apart: 9 -> 11, of which waited for: 6 -> 7; matrix products, arithmetic and copies ran while one was open for 15% -> 21% of each run, Pallas kernels for 13% -> 13%
where the time goes in v4:
time: 197 us; the launch traced here: 196 us
  waiting for transfers between devices  47.5 us (24%)
  Pallas kernels  33.8 us (17%)
  starting transfers between devices  31.7 us (16%)
  local copies, waits for them, and re-layouts  26.5 us (13%)
  blocking collectives  24.3 us (12%)
  between operations  13.5 us (7%)
  other arithmetic  11.1 us (6%)
  matrix products  7.12 us (4%)
    all_to_all x1, blocking collectives, on_device(): lax.all_to_all(own.reshape(n_narrow, height, width), 'narrow', 0, 0, tile...  24.3 us
    ppermute x1, waiting for transfers between devices, on_device(): moved = lax.ppermute(moved, 'narrow', narrow_pairs)  20.6 us
    unnamed x22, local copies, waits for them, and re-layouts  15.3 us
    pallas_call x1, Pallas kernels, middle_pass(): pl.pallas_call(middle_step, grid=(2 * half,), in_specs=[pl.BlockSpec(valu...  11.6 us
    all_to_all x1, waiting for transfers between devices, on_device(): lax.all_to_all(jnp.swapaxes(local, 0, 1), 'wide', 0, 0, tiled=True)  10.9 us
    ppermute x2, waiting for transfers between devices, fetch_other_half(): got.append(lax.ppermute(part, 'narrow', pairs))  10.2 us
    pallas_call x1, Pallas kernels, final_pass(): pl.pallas_call(final_step, grid_spec=pltpu.PrefetchScalarGridSpec(num_sca...  9.28 us
    all_to_all x1, starting transfers between devices, on_device(): lax.all_to_all(values.reshape(n_wide * n_narrow, 2 * inner, width // 2),...  8.74 us
  transfers between devices with their start and end apart: 11, of which 7 were waited for; matrix products, arithmetic and copies ran while one was open for 21% of the time, Pallas kernels for 13%

profile of v4, /device:TPU:1, one launch (start us, length us, event | category | flops | bytes accessed | tf_op | source)
XLA Modules:
  0.0 195.6 jit_solution(5626472129292682735)
XLA Ops:
  6.5 1.0 convert_bitcast_fusion
  7.6 0.1 copy-done
  7.7 0.7 pad_maximum_fusion.1
  8.4 0.0 all-gather.5.cloned.1.call-update
  8.4 0.0 all-gather.7.cloned.1.call-start
  8.5 1.0 constant_dynamic-slice_fusion
  9.5 1.5 collective-permute-start.4
  11.0 1.2 collective-permute-done.4
  12.1 1.7 dynamic-slice_select_fusion
  13.9 0.0 all-gather.7.cloned.1.call-update
  13.9 1.6 copy.12
  15.5 24.3 %all_to_all.20.own_ref = bf16[8,256,256]{2,1,0:T(8,128)(2,1)S(1)} all-to-all(bf16[8,256,256]{2,1,0:T(8,128)(2,1)S(1)} %bitcast.49), channel_id=1, replica_groups=mesh['wide'=16,'narrow'=8] {'narrow'}, dimensions={0} | all-to-all | bytes 2097152 | tf_op jit(solution)/shard_map/all_to_all | solution.py:296
  39.8 1.3 collective-permute-start
  41.1 0.0 copy-done.4
  41.1 1.3 copy.21
  42.4 7.2 %all-to-all-start.1 = ((bf16[16,128,256]{2,1,0:T(8,128)(2,1)}), bf16[16,128,256]{2,1,0:T(8,128)(2,1)S(1)}, u32[]{:S(2)}, u32[]{:S(2)}) async-start(bf16[16,128,256]{2,1,0:T(8,128)(2,1)} %bitcast.47), calls=%async_computation.1 | async-start | bytes 2097152 | tf_op jit(solution)/shard_map/all_to_all | solution.py:298
  49.6 12.4 %copy.14 = bf16[2048,2048]{0,1:T(8,128)(2,1)} copy(bf16[2048,2048]{1,0:T(8,128)(2,1)} %grid_ref.1) | data formatting | bytes 16777216 | tf_op args[2]
  62.0 10.9 %all-to-all-done.1 = bf16[16,128,256]{2,1,0:T(8,128)(2,1)S(1)} async-done(((bf16[16,128,256]{2,1,0:T(8,128)(2,1)}), bf16[16,128,256]{2,1,0:T(8,128)(2,1)S(1)}, u32[]{:S(2)}, u32[]{:S(2)}) %all-to-all-start.1) | async-done | bytes 1048608 | tf_op jit(solution)/shard_map/all_to_all | solution.py:298
  72.9 0.0 collective-permute-done.mate_ref
  72.9 1.3 all-gather.5.cloned.1.call-done
  74.2 6.5 %forward_pass.1 = bf16[16,8,2,16,128]{4,3,2,1,0:T(8,128)(2,1)} custom-call(bf16[8,256,256]{2,1,0:T(8,128)(2,1)} %copy-done.3, bf16[8,256,256]{2,1,0:T(8,128)(2,1)} %collective-permute-done.mate_ref, bf16[16,80,2048]{2,1,0:T(8,128)(2,1)} %bitcast.35, bf16[16,80,2048]{2,1,0:T(8,128)(2,1)} %bitcast.36), custom_call_target="tpu_custom_call" | custom-call | flops 2147483648 | bytes 8388608 | tf_op jit(solution)/shard_map/forward_pass/pallas_call | solution.py:59
  80.7 3.1 %constant_dynamic-slice_fusion.2 = (bf16[4,64,2048]{2,1,0:T(8,128)(2,1)}, bf16[4,64,2048]{2,1,0:T(8,128)(2,1)}) fusion(bf16[16,80,2048]{2,1,0:T(8,128)(2,1)} %bitcast.37, s32[]{:T(128)S(6)} %select_n.66, s32[]{:T(128)S(6)} %select_n.67), kind=kLoop, calls=%fused_computation.21 | loop fusion | bytes 4194312 | tf_op jit(solution)/shard_map/dynamic_slice | solution.py:256
  83.9 2.4 %collective-permute-start.2 = (bf16[4,64,2048]{2,1,0:T(8,128)(2,1)}, bf16[4,64,2048]{2,1,0:T(8,128)(2,1)S(1)}, u32[]{:S(2)}, u32[]{:S(2)}) collective-permute-start(bf16[4,64,2048]{2,1,0:T(8,128)(2,1)} %get-tuple-element.20), channel_id=1, source_target_pairs={{0,3},{1,0},{2,1},{3,2},{4,7},{5,4},{6,5},{7,6},{8,11},{9,8},{10,9... | collective-permute-start | bytes 3145736 | tf_op jit(solution)/shard_map/ppermute | solution.py:257
  86.3 0.0 collective-permute-start.1
  86.3 8.7 %all-to-all-start.2 = ((bf16[128,32,128]{2,1,0:T(8,128)(2,1)}), bf16[128,32,128]{2,1,0:T(8,128)(2,1)}, u32[]{:S(2)}, u32[]{:S(2)}) async-start(bf16[128,32,128]{2,1,0:T(8,128)(2,1)} %bitcast.50), calls=%async_computation.2 | async-start | bytes 2097152 | tf_op jit(solution)/shard_map/all_to_all | solution.py:305
  95.1 7.1 %fusion.across_ref = bf16[2048,256]{1,0:T(8,128)(2,1)} fusion(bf16[2048,2048]{1,0:T(8,128)(2,1)} %param.8, bf16[2048,256]{1,0:T(8,128)(2,1)} %bitcast.52), kind=kOutput, calls=%fused_computation.2 | convolution fusion | flops 2148007936 | bytes 10485760 | tf_op jit(solution)/shard_map/dot_general | solution.py:14
  102.2 6.9 %collective-permute-done.2 = bf16[4,64,2048]{2,1,0:T(8,128)(2,1)S(1)} collective-permute-done((bf16[4,64,2048]{2,1,0:T(8,128)(2,1)}, bf16[4,64,2048]{2,1,0:T(8,128)(2,1)S(1)}, u32[]{:S(2)}, u32[]{:S(2)}) %collective-permute-start.2) | collective-permute-done | bytes 1048608 | tf_op jit(solution)/shard_map/ppermute | solution.py:257
  109.1 3.2 %collective-permute-done.1 = bf16[4,64,2048]{2,1,0:T(8,128)(2,1)S(1)} collective-permute-done((bf16[4,64,2048]{2,1,0:T(8,128)(2,1)}, bf16[4,64,2048]{2,1,0:T(8,128)(2,1)S(1)}, u32[]{:S(2)}, u32[]{:S(2)}) %collective-permute-start.1) | collective-permute-done | bytes 1048608 | tf_op jit(solution)/shard_map/ppermute | solution.py:257
  112.3 1.7 pad_maximum_fusion
  114.0 3.9 %collective-permute-start.3 = (bf16[8,64,2048]{2,1,0:T(8,128)(2,1)}, bf16[8,64,2048]{2,1,0:T(8,128)(2,1)}, u32[]{:S(2)}, u32[]{:S(2)}) collective-permute-start(bf16[8,64,2048]{2,1,0:T(8,128)(2,1)} %pad_maximum_fusion), channel_id=1, source_target_pairs={{0,8},{8,0},{16,24},{24,16},{32,40},{40,32},{48,56},{56,48},{64,72... | collective-permute-start | bytes 6291464 | tf_op jit(solution)/shard_map/ppermute | solution.py:260
  117.9 1.3 slice_bitcast_fusion
  119.2 1.0 copy.15
  120.3 2.3 %copy.16 = bf16[256,2048]{0,1:T(8,128)(2,1)} copy(bf16[256,2048]{1,0:T(8,128)(2,1)} %bitcast.48) | data formatting | bytes 2097152 | tf_op jit(solution)/shard_map/reshape | solution.py:310
  122.6 3.3 %all-to-all-done.2 = bf16[128,32,128]{2,1,0:T(8,128)(2,1)} async-done(((bf16[128,32,128]{2,1,0:T(8,128)(2,1)}), bf16[128,32,128]{2,1,0:T(8,128)(2,1)}, u32[]{:S(2)}, u32[]{:S(2)}) %all-to-all-start.2) | async-done | bytes 1048608 | tf_op jit(solution)/shard_map/all_to_all | solution.py:305
  125.9 11.6 %middle_pass.1 = bf16[2048,512]{1,0:T(8,128)(2,1)} custom-call(bf16[64,2,2,16,128]{4,3,2,1,0:T(8,128)(2,1)} %bitcast.12.values_ref, bf16[2048,2048]{1,0:T(8,128)(2,1)} %grid_ref.1, bf16[2048,2048]{1,0:T(8,128)(2,1)} %bitcast.41, bf16[2048,256]{1,0:T(8,128)(2,1)} %bitcast.51, bf16[2048,256]{1,0:T(8,128)(2,1)} %fusion.across_ref), custom_call_target="tpu_custom_call" | custom-call | flops 4294967296 | bytes 22020096 | tf_op jit(solution)/shard_map/middle_pass/pallas_call | solution.py:110
  137.5 5.2 %all-to-all-start.3 = ((bf16[128,16,512]{2,1,0:T(8,128)(2,1)}), bf16[128,16,512]{2,1,0:T(8,128)(2,1)S(1)}, u32[]{:S(2)}, u32[]{:S(2)}) async-start(bf16[128,16,512]{2,1,0:T(8,128)(2,1)} %bitcast.45), calls=%async_computation.3 | async-start | bytes 4194304 | tf_op jit(solution)/shard_map/all_to_all | solution.py:312
  142.7 0.1 broadcast_in_dim.12
  142.8 0.8 broadcast_in_dim_reshape.4.energy_ref
  143.6 0.7 fusion.1.swap_ref
  144.3 6.4 %applied_pass.1 = (f32[256,1024]{1,0:T(8,128)}, bf16[256,1024]{1,0:T(8,128)(2,1)}) custom-call(bf16[8,256,256]{2,1,0:T(8,128)(2,1)} %copy-done.3, bf16[8,256,256]{2,1,0:T(8,128)(2,1)} %collective-permute-done.mate_ref, bf16[16,64,2048]{2,1,0:T(8,128)(2,1)} %bitcast.53), custom_call_target="tpu_custom_call" | custom-call | flops 2147483648 | bytes 8388608 | tf_op jit(solution)/shard_map/applied_pass/pallas_call | solution.py:149
  150.7 1.4 collective-permute-start.5
  152.1 0.0 collective-permute-done.3
  152.1 5.2 %maximum_select_fusion.far_a.far_b = bf16[16,64,2048]{2,1,0:T(8,128)(2,1)} fusion(bf16[8,64,2048]{2,1,0:T(8,128)(2,1)} %collective-permute-done.3, bf16[4,64,2048]{2,1,0:T(8,128)(2,1)} %copy-done.5, bf16[4,64,2048]{2,1,0:T(8,128)(2,1)} %copy-done.6, pred[]{:T(512)S(6)} %eq.24), kind=kLoop, calls=%fused_computation | loop fusion | flops 10485760 | bytes 8388609 | tf_op jit(solution)/shard_map/jit(_where)/select_n | solution.py:261
  157.3 20.6 %collective-permute-done.5.moved_ref = bf16[256,1024]{1,0:T(8,128)(2,1)S(1)} collective-permute-done((bf16[256,1024]{1,0:T(8,128)(2,1)}, bf16[256,1024]{1,0:T(8,128)(2,1)S(1)}, u32[]{:S(2)}, u32[]{:S(2)}) %collective-permute-start.5) | collective-permute-done | bytes 524320 | tf_op jit(solution)/shard_map/ppermute | solution.py:317
  177.9 0.0 all-to-all-done.3
  177.9 0.8 copy-done.8
  178.7 0.7 copy-done.2
  179.4 9.3 %final_pass.1 = bf16[16,16,2048]{2,1,0:T(8,128)(2,1)} custom-call(s32[1]{0:T(128)} %bitcast.half_ref, bf16[16,8,16,512]{3,2,1,0:T(8,128)(2,1)} %bitcast.42, bf16[16,8,16,512]{3,2,1,0:T(8,128)(2,1)} %bitcast.43, bf16[16,80,2048]{2,1,0:T(8,128)(2,1)} %bitcast.39, bf16[16,80,2048]{2,1,0:T(8,128)(2,1)} %bitcast.40, ...), custom_call_target="tpu_custom_call" | custom-call | flops 2415919104 | bytes 14680064 | tf_op jit(solution)/shard_map/final_pass/pallas_call | solution.py:216
  (20 shorter events, 0.1 us)
Async XLA Ops:
  6.5 1.1 copy-start
  6.5 34.6 %copy-start.4 = (bf16[1,128,16,256]{3,2,1,0:T(8,128)(2,1)S(1)}, bf16[1,128,16,256]{3,2,1,0:T(8,128)(2,1)}, u32[]{:S(2)}) copy-start(bf16[1,128,16,256]{3,2,1,0:T(8,128)(2,1)} %param.7) | copy-start | bytes 3145732
  6.5 67.7 %all-gather.5.cloned.1.call-start = ((), (), s32[]{:S(2)}) async-start(), calls=%async_computation.4 | async-start | bytes 5570560 | tf_op jit(solution)/shard_map/all_gather | solution.py:288
  8.4 135.9 %all-gather.7.cloned.1.call-start = ((), (), s32[]{:S(2)}) async-start(), calls=%async_computation.5 | async-start | bytes 4456448 | tf_op jit(solution)/shard_map/all_gather | solution.py:293
  9.5 2.7 %collective-permute-start.4 = (bf16[64,2048]{1,0:T(8,128)(2,1)S(1)}, bf16[64,2048]{1,0:T(8,128)(2,1)S(1)}, u32[]{:S(2)}, u32[]{:S(2)}) collective-permute-start(bf16[64,2048]{1,0:T(8,128)(2,1)S(1)} %constant_dynamic-slice_fusion), channel_id=1, source_target_pairs={{0,8},{8,0},{16,24},{24,16},{32,40},{40,32},{48,56},{56,48},{64,72... | collective-permute-start | bytes 786440 | tf_op jit(solution)/shard_map/ppermute | solution.py:292
  39.8 22.2 %copy-start.3 = (bf16[8,256,256]{2,1,0:T(8,128)(2,1)}, bf16[8,256,256]{2,1,0:T(8,128)(2,1)S(1)}, u32[]{:S(2)}) copy-start(bf16[8,256,256]{2,1,0:T(8,128)(2,1)S(1)} %all_to_all.20.own_ref) | copy-start | bytes 3145732
  39.8 33.1 %collective-permute-start = (bf16[8,256,256]{2,1,0:T(8,128)(2,1)S(1)}, bf16[8,256,256]{2,1,0:T(8,128)(2,1)}, u32[]{:S(2)}, u32[]{:S(2)}) collective-permute-start(bf16[8,256,256]{2,1,0:T(8,128)(2,1)S(1)} %all_to_all.20.own_ref), channel_id=1, source_target_pairs={{0,1},{1,0},{2,3},{3,2},{4,5},{5,4},{6,7},{7,6},{8,9},{9,8},{10,11... | collective-permute-start | bytes 3145736 | tf_op jit(solution)/shard_map/ppermute | solution.py:297
  42.4 30.5 %all-to-all-start.1 = ((bf16[16,128,256]{2,1,0:T(8,128)(2,1)}), bf16[16,128,256]{2,1,0:T(8,128)(2,1)S(1)}, u32[]{:S(2)}, u32[]{:S(2)}) async-start(bf16[16,128,256]{2,1,0:T(8,128)(2,1)} %bitcast.47), calls=%async_computation.1 | async-start | bytes 2097152 | tf_op jit(solution)/shard_map/all_to_all | solution.py:298
  72.9 7.9 %copy-start.7 = (bf16[16,128,256]{2,1,0:T(8,128)(2,1)}, bf16[16,128,256]{2,1,0:T(8,128)(2,1)S(1)}, u32[]{:S(2)}) copy-start(bf16[16,128,256]{2,1,0:T(8,128)(2,1)S(1)} %all-to-all-done.1) | copy-start | bytes 3145732
  83.9 25.3 %collective-permute-start.2 = (bf16[4,64,2048]{2,1,0:T(8,128)(2,1)}, bf16[4,64,2048]{2,1,0:T(8,128)(2,1)S(1)}, u32[]{:S(2)}, u32[]{:S(2)}) collective-permute-start(bf16[4,64,2048]{2,1,0:T(8,128)(2,1)} %get-tuple-element.20), channel_id=1, source_target_pairs={{0,3},{1,0},{2,1},{3,2},{4,7},{5,4},{6,5},{7,6},{8,11},{9,8},{10,9... | collective-permute-start | bytes 3145736 | tf_op jit(solution)/shard_map/ppermute | solution.py:257
  86.3 26.0 %collective-permute-start.1 = (bf16[4,64,2048]{2,1,0:T(8,128)(2,1)}, bf16[4,64,2048]{2,1,0:T(8,128)(2,1)S(1)}, u32[]{:S(2)}, u32[]{:S(2)}) collective-permute-start(bf16[4,64,2048]{2,1,0:T(8,128)(2,1)} %get-tuple-element.19), channel_id=1, source_target_pairs={{0,1},{1,2},{2,3},{3,0},{4,5},{5,6},{6,7},{7,4},{8,9},{9,10},{10,1... | collective-permute-start | bytes 3145736 | tf_op jit(solution)/shard_map/ppermute | solution.py:257
  86.3 39.6 %all-to-all-start.2 = ((bf16[128,32,128]{2,1,0:T(8,128)(2,1)}), bf16[128,32,128]{2,1,0:T(8,128)(2,1)}, u32[]{:S(2)}, u32[]{:S(2)}) async-start(bf16[128,32,128]{2,1,0:T(8,128)(2,1)} %bitcast.50), calls=%async_computation.2 | async-start | bytes 2097152 | tf_op jit(solution)/shard_map/all_to_all | solution.py:305
  109.1 11.1 %copy-start.5 = (bf16[4,64,2048]{2,1,0:T(8,128)(2,1)}, bf16[4,64,2048]{2,1,0:T(8,128)(2,1)S(1)}, u32[]{:S(2)}) copy-start(bf16[4,64,2048]{2,1,0:T(8,128)(2,1)S(1)} %collective-permute-done.2) | copy-start | bytes 3145732
  112.3 7.9 %copy-start.6 = (bf16[4,64,2048]{2,1,0:T(8,128)(2,1)}, bf16[4,64,2048]{2,1,0:T(8,128)(2,1)S(1)}, u32[]{:S(2)}) copy-start(bf16[4,64,2048]{2,1,0:T(8,128)(2,1)S(1)} %collective-permute-done.1) | copy-start | bytes 3145732
  114.0 38.1 %collective-permute-start.3 = (bf16[8,64,2048]{2,1,0:T(8,128)(2,1)}, bf16[8,64,2048]{2,1,0:T(8,128)(2,1)}, u32[]{:S(2)}, u32[]{:S(2)}) collective-permute-start(bf16[8,64,2048]{2,1,0:T(8,128)(2,1)} %pad_maximum_fusion), channel_id=1, source_target_pairs={{0,8},{8,0},{16,24},{24,16},{32,40},{40,32},{48,56},{56,48},{64,72... | collective-permute-start | bytes 6291464 | tf_op jit(solution)/shard_map/ppermute | solution.py:260
  137.5 5.2 %copy-start.9 = (f32[16]{0:T(128)S(1)}, f32[16]{0:T(128)}, u32[]{:S(2)}) copy-start(f32[16]{0:T(128)} %param.13) | copy-start | bytes 196
  137.5 40.4 %all-to-all-start.3 = ((bf16[128,16,512]{2,1,0:T(8,128)(2,1)}), bf16[128,16,512]{2,1,0:T(8,128)(2,1)S(1)}, u32[]{:S(2)}, u32[]{:S(2)}) async-start(bf16[128,16,512]{2,1,0:T(8,128)(2,1)} %bitcast.45), calls=%async_computation.3 | async-start | bytes 4194304 | tf_op jit(solution)/shard_map/all_to_all | solution.py:312
  150.7 27.2 %collective-permute-start.5 = (bf16[256,1024]{1,0:T(8,128)(2,1)}, bf16[256,1024]{1,0:T(8,128)(2,1)S(1)}, u32[]{:S(2)}, u32[]{:S(2)}) collective-permute-start(bf16[256,1024]{1,0:T(8,128)(2,1)} %get-tuple-element.18), channel_id=1, source_target_pairs={{0,1},{1,0},{2,3},{3,2},{4,5},{5,4},{6,7},{7,6},{8,9},{9,8},{10,11... | collective-permute-start | bytes 1572872 | tf_op jit(solution)/shard_map/ppermute | solution.py:317
  177.9 0.8 copy-start.8
  177.9 1.5 copy-start.2
  179.4 9.3 %copy-start.1 = (bf16[128,2048]{1,0:T(8,128)(2,1)S(1)}, bf16[128,2048]{1,0:T(8,128)(2,1)}, u32[]{:S(2)}) copy-start(bf16[128,2048]{1,0:T(8,128)(2,1)} %param.11) | copy-start | bytes 1572868
Sparse Core Ops, SparseCore 0:
  9.1 65.1 all-gather.4
  75.9 41.3 all-gather.6

commit v5 on v3

--- a/solution.py
+++ b/solution.py
@@ -101,7 +101,7 @@
         out_ref[:, width:] = across_ref[...]
 
 
-def middle_pass(values, grid_one, turned, potential, across, tile=512):
+def middle_pass(values, grid_one, turned, potential, across, tile=1024):
     n_one, width = across.shape
     half = n_one // tile
     early = lambda s: (jnp.minimum(s, half - 1), 0)
@@ -143,7 +143,6 @@
 def applied_pass(own, mate, gathered, steps=4):
     n_narrow, height, width = own.shape
     shards, depth, cols = gathered.shape
-    depth = depth // 2
     points = shards * depth
     resident = pl.BlockSpec(own.shape, lambda s: (0, 0, 0))
     block = pl.BlockSpec((height, points // steps), lambda s: (0, s))
@@ -153,7 +152,7 @@
         in_specs=[
             resident,
             resident,
-            pl.BlockSpec((shards // steps, depth, cols), lambda s: (s, 1, 0)),
+            pl.BlockSpec((shards // steps, depth, cols), lambda s: (s, 0, 0)),
         ],
         out_specs=[block, block],
         out_shape=[
@@ -271,17 +270,19 @@
     away = lax.dynamic_slice_in_dim(ham_two, (1 - core) * share, share, 0)
     stay = lax.dynamic_slice_in_dim(ham_two, core * share, share, 0)
     stay = jnp.where(core == half, stay, lax.ppermute(away, "wide", wide_pairs))
-    far = lax.all_gather(jnp.concatenate([far, stay], 0), "wide", axis=0, tiled=False)
+    half_ham = lax.all_gather(stay, "wide", axis=0, tiled=False)
 
     own = local.reshape(n_narrow, inner, states, width).swapaxes(1, 2)
     own = lax.all_to_all(own.reshape(n_narrow, height, width), "narrow", 0, 0, tiled=True)
+    own, far = lax.optimization_barrier((own, far))
+    far = lax.all_gather(far, "wide", axis=0, tiled=False)
     mate = lax.ppermute(own, "narrow", narrow_pairs)
     by_state = lax.all_to_all(jnp.swapaxes(local, 0, 1), "wide", 0, 0, tiled=True)
+    turned = lax.optimization_barrier(grid_one.T)
+    own, mate, by_state, turned = lax.optimization_barrier((own, mate, by_state, turned))
+
+    values = forward_pass(own, mate, near, states, piece)
     across = dot_f32(ham_one, by_state.reshape(n_one, width), NN).astype(jnp.bfloat16)
-    turned = lax.optimization_barrier(grid_one.T)
-    own, mate, across, turned = lax.optimization_barrier((own, mate, across, turned))
-
-    values = forward_pass(own, mate, near, states, piece)
     values = lax.all_to_all(
         values.reshape(n_wide * n_narrow, 2 * inner, width // 2), both, 0, 0, tiled=True
     )
@@ -293,7 +294,7 @@
         pair.reshape(n_wide * n_narrow, inner, 2 * width), both, 0, 0, tiled=True
     )
 
-    kept, moved = applied_pass(own, mate, far)
+    kept, moved = applied_pass(own, mate, half_ham)
     moved = lax.ppermute(moved, "narrow", narrow_pairs)
     energy = jnp.repeat(third_energy, inner)[:, None]
     target = jnp.arange(height)

time: 199 us -> 197 us (0.990)
  blocking collectives: 0 us -> 24.5 us
  waiting for transfers between devices: 75.9 us -> 63.4 us
  starting transfers between devices: 36.9 us -> 26.1 us
    all_to_all x0 -> x1, blocking collectives: none -> 24.5 us  [on_device(): lax.all_to_all(own.reshape(n_narrow, height, width), 'narrow', 0, 0, tile...]
    all_to_all x1 -> x0, waiting for transfers between devices: 16.7 us -> none  [on_device(): lax.all_to_all(own.reshape(n_narrow, height, width), 'narrow', 0, 0, tile...]
    ppermute x1, waiting for transfers between devices: 10.7 us -> 25.8 us  [on_device(): moved = lax.ppermute(moved, 'narrow', narrow_pairs)]
    all_to_all x1, waiting for transfers between devices: 15.5 us -> 8.58 us  [on_device(): lax.all_to_all(values.reshape(n_wide * n_narrow, 2 * inner, width // 2),...]
    all_to_all x1 -> x0, starting transfers between devices: 6.73 us -> none  [on_device(): lax.all_to_all(own.reshape(n_narrow, height, width), 'narrow', 0, 0, tile...]
    ppermute x1, starting transfers between devices: 7.18 us -> 1.39 us  [on_device(): moved = lax.ppermute(moved, 'narrow', narrow_pairs)]
    all_gather x1 -> x2, waiting for transfers between devices: 21.2 us -> 16.2 us  [the longest x1 16.2 us: on_device(): far = lax.all_gather(far, 'wide', axis=0, tiled=False)]
where the time goes in v5:
time: 197 us; the launch traced here: 196 us
  waiting for transfers between devices  63.4 us (32%)
  Pallas kernels  34.1 us (17%)
  starting transfers between devices  26.1 us (13%)
  blocking collectives  24.5 us (12%)
  local copies, waits for them, and re-layouts  23.9 us (12%)
  between operations  13.2 us (7%)
  matrix products  6.88 us (3%)
  other arithmetic  4.24 us (2%)
    ppermute x1, waiting for transfers between devices, on_device(): moved = lax.ppermute(moved, 'narrow', narrow_pairs)  25.8 us
    all_to_all x1, blocking collectives, on_device(): lax.all_to_all(own.reshape(n_narrow, height, width), 'narrow', 0, 0, tile...  24.5 us
    all_gather x1, waiting for transfers between devices, on_device(): far = lax.all_gather(far, 'wide', axis=0, tiled=False)  16.2 us
    unnamed x16, local copies, waits for them, and re-layouts  16 us
    pallas_call x1, Pallas kernels, middle_pass(): pl.pallas_call(middle_step, grid=(2 * half,), in_specs=[pl.BlockSpec(valu...  11.9 us
    all_to_all x1, waiting for transfers between devices, on_device(): lax.all_to_all(jnp.swapaxes(local, 0, 1), 'wide', 0, 0, tiled=True)  10.2 us
    pallas_call x1, Pallas kernels, final_pass(): pl.pallas_call(final_step, grid_spec=pltpu.PrefetchScalarGridSpec(num_sca...  9.2 us
    all_to_all x1, waiting for transfers between devices, on_device(): lax.all_to_all(values.reshape(n_wide * n_narrow, 2 * inner, width // 2),...  8.58 us
  transfers between devices with their start and end apart: 9, of which 6 were waited for; matrix products, arithmetic and copies ran while one was open for 15% of the time, Pallas kernels for 13%

profile of v5, /device:TPU:1, one launch (start us, length us, event | category | flops | bytes accessed | tf_op | source)
XLA Modules:
  0.0 196.4 jit_solution(7443356368679695356)
XLA Ops:
  6.5 0.0 all-gather.7.cloned.1.call-start
  6.5 1.0 convert_bitcast_fusion
  7.5 1.8 dynamic-slice_bitcast_fusion
  9.3 0.8 pad_maximum_fusion
  10.1 0.0 all-gather.7.cloned.1.call-update
  10.1 0.0 all-gather.11.cloned.1.call-start
  10.2 1.0 constant_dynamic-slice_fusion
  11.1 1.5 collective-permute-start.1
  12.6 1.2 collective-permute-done.1
  13.8 1.7 dynamic-slice_select_fusion
  15.5 0.0 all-gather.11.cloned.1.call-update
  15.5 0.0 all-gather.9.cloned.1.call-start
  15.6 1.6 copy.12
  17.2 24.5 %all_to_all.20.own_ref = bf16[8,256,256]{2,1,0:T(8,128)(2,1)S(1)} all-to-all(bf16[8,256,256]{2,1,0:T(8,128)(2,1)S(1)} %bitcast.51), channel_id=1, replica_groups=mesh['wide'=16,'narrow'=8] {'narrow'}, dimensions={0} | all-to-all | bytes 2097152 | tf_op jit(solution)/shard_map/all_to_all | solution.py:276
  41.7 0.0 all-gather.9.cloned.1.call-update
  41.8 1.4 collective-permute-start
  43.1 0.0 copy-done.2
  43.1 1.3 copy.21
  44.4 7.0 %all-to-all-start.1 = ((bf16[16,128,256]{2,1,0:T(8,128)(2,1)}), bf16[16,128,256]{2,1,0:T(8,128)(2,1)S(1)}, u32[]{:S(2)}, u32[]{:S(2)}) async-start(bf16[16,128,256]{2,1,0:T(8,128)(2,1)} %bitcast.36), calls=%async_computation.1 | async-start | bytes 2097152 | tf_op jit(solution)/shard_map/all_to_all | solution.py:280
  51.4 12.4 %copy.14 = bf16[2048,2048]{0,1:T(8,128)(2,1)} copy(bf16[2048,2048]{1,0:T(8,128)(2,1)} %grid_ref.1) | data formatting | bytes 16777216 | tf_op args[2]
  63.8 0.0 copy-done.1
  63.8 10.2 %all-to-all-done.1 = bf16[16,128,256]{2,1,0:T(8,128)(2,1)S(1)} async-done(((bf16[16,128,256]{2,1,0:T(8,128)(2,1)}), bf16[16,128,256]{2,1,0:T(8,128)(2,1)S(1)}, u32[]{:S(2)}, u32[]{:S(2)}) %all-to-all-start.1) | async-done | bytes 1048608 | tf_op jit(solution)/shard_map/all_to_all | solution.py:280
  74.0 0.0 collective-permute-done.mate_ref
  74.0 1.4 all-gather.7.cloned.1.call-done
  75.4 0.0 copy-done.4
  75.4 6.5 %forward_pass.1 = bf16[16,8,2,16,128]{4,3,2,1,0:T(8,128)(2,1)} custom-call(bf16[8,256,256]{2,1,0:T(8,128)(2,1)} %copy-done.1, bf16[8,256,256]{2,1,0:T(8,128)(2,1)} %copy-done.4, bf16[16,80,2048]{2,1,0:T(8,128)(2,1)} %bitcast.37, bf16[16,80,2048]{2,1,0:T(8,128)(2,1)} %bitcast.38), custom_call_target="tpu_custom_call" | custom-call | flops 2147483648 | bytes 8388608 | tf_op jit(solution)/shard_map/forward_pass/pallas_call | solution.py:59
  82.0 7.7 %all-to-all-start.2 = ((bf16[128,32,128]{2,1,0:T(8,128)(2,1)}), bf16[128,32,128]{2,1,0:T(8,128)(2,1)S(1)}, u32[]{:S(2)}, u32[]{:S(2)}) async-start(bf16[128,32,128]{2,1,0:T(8,128)(2,1)} %bitcast.52), calls=%async_computation.2 | async-start | bytes 2097152 | tf_op jit(solution)/shard_map/all_to_all | solution.py:286
  89.7 6.9 %fusion.across_ref = bf16[2048,256]{1,0:T(8,128)(2,1)} fusion(bf16[2048,2048]{1,0:T(8,128)(2,1)} %param.8, bf16[2048,256]{1,0:T(8,128)(2,1)S(1)} %bitcast.55), kind=kOutput, calls=%fused_computation.1 | convolution fusion | flops 2148007936 | bytes 10485760 | tf_op jit(solution)/shard_map/dot_general | solution.py:14
  96.6 1.3 slice_bitcast_fusion
  97.9 0.1 copy.15
  97.9 1.4 copy.16
  99.3 8.6 %all-to-all-done.2 = bf16[128,32,128]{2,1,0:T(8,128)(2,1)S(1)} async-done(((bf16[128,32,128]{2,1,0:T(8,128)(2,1)}), bf16[128,32,128]{2,1,0:T(8,128)(2,1)S(1)}, u32[]{:S(2)}, u32[]{:S(2)}) %all-to-all-start.2) | async-done | bytes 1048608 | tf_op jit(solution)/shard_map/all_to_all | solution.py:286
  107.9 1.0 copy-done.3
  108.9 11.9 %middle_pass.1 = bf16[2048,512]{1,0:T(8,128)(2,1)} custom-call(bf16[64,2,2,16,128]{4,3,2,1,0:T(8,128)(2,1)} %bitcast.53, bf16[2048,2048]{1,0:T(8,128)(2,1)} %grid_ref.1, bf16[2048,2048]{1,0:T(8,128)(2,1)} %bitcast.42, bf16[2048,256]{1,0:T(8,128)(2,1)} %bitcast.54, bf16[2048,256]{1,0:T(8,128)(2,1)} %fusion.across_ref), custom_call_target="tpu_custom_call" | custom-call | flops 4294967296 | bytes 22020096 | tf_op jit(solution)/shard_map/middle_pass/pallas_call | solution.py:110
  120.7 7.1 %all-to-all-start.3 = ((bf16[128,16,512]{2,1,0:T(8,128)(2,1)}), bf16[128,16,512]{2,1,0:T(8,128)(2,1)S(1)}, u32[]{:S(2)}, u32[]{:S(2)}) async-start(bf16[128,16,512]{2,1,0:T(8,128)(2,1)} %bitcast.48), calls=%async_computation.3 | async-start | bytes 4194304 | tf_op jit(solution)/shard_map/all_to_all | solution.py:293
  127.9 0.0 all-gather.11.cloned.1.call-done
  127.9 6.5 %applied_pass.1 = (f32[256,1024]{1,0:T(8,128)}, bf16[256,1024]{1,0:T(8,128)(2,1)}) custom-call(bf16[8,256,256]{2,1,0:T(8,128)(2,1)} %copy-done.1, bf16[8,256,256]{2,1,0:T(8,128)(2,1)} %copy-done.4, bf16[16,64,2048]{2,1,0:T(8,128)(2,1)} %bitcast.57), custom_call_target="tpu_custom_call" | custom-call | flops 2147483648 | bytes 8388608 | tf_op jit(solution)/shard_map/applied_pass/pallas_call | solution.py:149
  134.4 1.4 collective-permute-start.2
  135.7 0.0 copy-done.6
  135.7 0.1 broadcast_in_dim.12
  135.8 0.8 broadcast_in_dim_reshape.4.energy_ref
  136.6 0.8 fusion.1.swap_ref
  137.3 25.8 %collective-permute-done.2.moved_ref = bf16[256,1024]{1,0:T(8,128)(2,1)S(1)} collective-permute-done((bf16[256,1024]{1,0:T(8,128)(2,1)}, bf16[256,1024]{1,0:T(8,128)(2,1)S(1)}, u32[]{:S(2)}, u32[]{:S(2)}) %collective-permute-start.2) | collective-permute-done | bytes 524320 | tf_op jit(solution)/shard_map/ppermute | solution.py:298
  163.2 16.2 %all-gather.9.cloned.1.call-done = bf16[1024,2048]{1,0:T(8,128)(2,1)} async-done(((bf16[64,2048]{1,0:T(8,128)(2,1)}), bf16[1024,2048]{1,0:T(8,128)(2,1)}) %all-gather.9.cloned.1.call-update) | async-done | bytes 4194320 | tf_op jit(solution)/shard_map/all_gather | solution.py:278
  179.3 0.0 all-to-all-done.3
  179.3 0.0 copy-done.5
  179.3 1.3 copy-done
  180.7 9.2 %final_pass.1 = bf16[16,16,2048]{2,1,0:T(8,128)(2,1)} custom-call(s32[1]{0:T(128)} %bitcast.half_ref, bf16[16,8,16,512]{3,2,1,0:T(8,128)(2,1)} %bitcast.43, bf16[16,8,16,512]{3,2,1,0:T(8,128)(2,1)} %bitcast.44, bf16[16,80,2048]{2,1,0:T(8,128)(2,1)} %bitcast.40, bf16[16,80,2048]{2,1,0:T(8,128)(2,1)} %bitcast.41, bf16[16,64,2048]{2,1,0:T(8,128)(2,1)} %bitcast.46, ...), custom_call_target="tpu_custom_call" | custom-call | flops 2415919104 | bytes 14680064 | tf_op jit(solution)/shard_map/final_pass/pallas_call | solution.py:216
  (8 shorter events, 0.0 us)
Async XLA Ops:
  6.5 36.6 %copy-start.2 = (bf16[1,128,16,256]{3,2,1,0:T(8,128)(2,1)S(1)}, bf16[1,128,16,256]{3,2,1,0:T(8,128)(2,1)}, u32[]{:S(2)}) copy-start(bf16[1,128,16,256]{3,2,1,0:T(8,128)(2,1)} %param.7) | copy-start | bytes 3145732
  6.5 68.9 %all-gather.7.cloned.1.call-start = ((), (), s32[]{:S(2)}) async-start(), calls=%async_computation.4 | async-start | bytes 5570560 | tf_op jit(solution)/shard_map/all_gather | solution.py:268
  10.1 117.8 %all-gather.11.cloned.1.call-start = ((), (), s32[]{:S(2)}) async-start(), calls=%async_computation.6 | async-start | bytes 4456448 | tf_op jit(solution)/shard_map/all_gather | solution.py:273
  11.1 2.7 %collective-permute-start.1 = (bf16[64,2048]{1,0:T(8,128)(2,1)S(1)}, bf16[64,2048]{1,0:T(8,128)(2,1)S(1)}, u32[]{:S(2)}, u32[]{:S(2)}) collective-permute-start(bf16[64,2048]{1,0:T(8,128)(2,1)S(1)} %constant_dynamic-slice_fusion), channel_id=1, source_target_pairs={{0,8},{8,0},{16,24},{24,16},{32,40},{40,32},{48,56},{56,48},{64,72... | collective-permute-start | bytes 786440 | tf_op jit(solution)/shard_map/ppermute | solution.py:272
  15.5 163.8 %all-gather.9.cloned.1.call-start = ((), (), s32[]{:S(2)}) async-start(), calls=%async_computation.5 | async-start | bytes 4456448 | tf_op jit(solution)/shard_map/all_gather | solution.py:278
  41.7 22.1 %copy-start.1 = (bf16[8,256,256]{2,1,0:T(8,128)(2,1)}, bf16[8,256,256]{2,1,0:T(8,128)(2,1)S(1)}, u32[]{:S(2)}) copy-start(bf16[8,256,256]{2,1,0:T(8,128)(2,1)S(1)} %all_to_all.20.own_ref) | copy-start | bytes 3145732
  41.8 32.3 %collective-permute-start = (bf16[8,256,256]{2,1,0:T(8,128)(2,1)S(1)}, bf16[8,256,256]{2,1,0:T(8,128)(2,1)S(1)}, u32[]{:S(2)}, u32[]{:S(2)}) collective-permute-start(bf16[8,256,256]{2,1,0:T(8,128)(2,1)S(1)} %all_to_all.20.own_ref), channel_id=1, source_target_pairs={{0,1},{1,0},{2,3},{3,2},{4,5},{5,4},{6,7},{7,6},{8,9},{9,8},{10,11... | collective-permute-start | bytes 3145736 | tf_op jit(solution)/shard_map/ppermute | solution.py:279
  44.4 29.6 %all-to-all-start.1 = ((bf16[16,128,256]{2,1,0:T(8,128)(2,1)}), bf16[16,128,256]{2,1,0:T(8,128)(2,1)S(1)}, u32[]{:S(2)}, u32[]{:S(2)}) async-start(bf16[16,128,256]{2,1,0:T(8,128)(2,1)} %bitcast.36), calls=%async_computation.1 | async-start | bytes 2097152 | tf_op jit(solution)/shard_map/all_to_all | solution.py:280
  74.0 1.4 copy-start.4
  82.0 25.9 %all-to-all-start.2 = ((bf16[128,32,128]{2,1,0:T(8,128)(2,1)}), bf16[128,32,128]{2,1,0:T(8,128)(2,1)S(1)}, u32[]{:S(2)}, u32[]{:S(2)}) async-start(bf16[128,32,128]{2,1,0:T(8,128)(2,1)} %bitcast.52), calls=%async_computation.2 | async-start | bytes 2097152 | tf_op jit(solution)/shard_map/all_to_all | solution.py:286
  107.9 1.0 copy-start.3
  120.7 15.0 %copy-start.6 = (f32[16]{0:T(128)S(1)}, f32[16]{0:T(128)}, u32[]{:S(2)}) copy-start(f32[16]{0:T(128)} %param.13) | copy-start | bytes 196
  120.7 58.6 %all-to-all-start.3 = ((bf16[128,16,512]{2,1,0:T(8,128)(2,1)}), bf16[128,16,512]{2,1,0:T(8,128)(2,1)S(1)}, u32[]{:S(2)}, u32[]{:S(2)}) async-start(bf16[128,16,512]{2,1,0:T(8,128)(2,1)} %bitcast.48), calls=%async_computation.3 | async-start | bytes 4194304 | tf_op jit(solution)/shard_map/all_to_all | solution.py:293
  134.4 28.8 %collective-permute-start.2 = (bf16[256,1024]{1,0:T(8,128)(2,1)}, bf16[256,1024]{1,0:T(8,128)(2,1)S(1)}, u32[]{:S(2)}, u32[]{:S(2)}) collective-permute-start(bf16[256,1024]{1,0:T(8,128)(2,1)} %get-tuple-element.20), channel_id=1, source_target_pairs={{0,1},{1,0},{2,3},{3,2},{4,5},{5,4},{6,7},{7,6},{8,9},{9,8},{10,11... | collective-permute-start | bytes 1572872 | tf_op jit(solution)/shard_map/ppermute | solution.py:298
  163.2 16.2 %copy-start.5 = (bf16[256,1024]{1,0:T(8,128)(2,1)}, bf16[256,1024]{1,0:T(8,128)(2,1)S(1)}, u32[]{:S(2)}) copy-start(bf16[256,1024]{1,0:T(8,128)(2,1)S(1)} %collective-permute-done.2.moved_ref) | copy-start | bytes 1572868
  179.3 1.3 copy-start
Sparse Core Ops, SparseCore 0:
  10.2 65.1 all-gather.6
  77.1 48.2 all-gather.10
  127.2 52.1 all-gather.8

commit v6 on v5

--- a/solution.py
+++ b/solution.py
@@ -142,8 +142,9 @@
 
 def applied_pass(own, mate, gathered, steps=4):
     n_narrow, height, width = own.shape
-    shards, depth, cols = gathered.shape
-    points = shards * depth
+    shards, sides, depth, cols = gathered.shape
+    points = shards * sides * depth
+    parts = steps // sides
     resident = pl.BlockSpec(own.shape, lambda s: (0, 0, 0))
     block = pl.BlockSpec((height, points // steps), lambda s: (0, s))
     return pl.pallas_call(
@@ -152,7 +153,7 @@
         in_specs=[
             resident,
             resident,
-            pl.BlockSpec((shards // steps, depth, cols), lambda s: (s, 0, 0)),
+            pl.BlockSpec((shards // parts, 1, depth, cols), lambda s: (s % parts, s // parts, 0, 0)),
         ],
         out_specs=[block, block],
         out_shape=[
@@ -167,14 +168,14 @@
 
 
 def final_step(
-    half_ref, near_ref, far_ref, near_a, near_b, far_a, far_b, across_ref, kept_ref, moved_ref,
-    own_ref, energy_ref, swap_ref, out_ref, acc_ref,
+    half_ref, near_ref, far_ref, near_a, near_b, far_a0, far_a1, far_b0, far_b1, across_ref,
+    kept_ref, moved_ref, own_ref, energy_ref, swap_ref, out_ref, acc_ref,
 ):
     step = pl.program_id(0)
     states, _, rows, _ = near_ref.shape
     height = states * rows
     lefts = [ref[:, block].reshape(height, -1) for ref in (near_ref, far_ref) for block in range(2)]
-    rights = [flatten(ref) for ref in (near_a, near_b, far_a, far_b)]
+    rights = [flatten(ref) for ref in (near_a, near_b, far_a0, far_a1, far_b0, far_b1)]
     total = dot_f32(jnp.concatenate(lefts, 1), jnp.concatenate(rights, 0), NN)
 
     @pl.when(step == 0)
@@ -212,6 +213,13 @@
         pl.BlockSpec((shards, piece, cols), lambda s, h: (0, 2 * s, 0)),
         pl.BlockSpec((shards, piece, cols), lambda s, h: (0, 2 * s + 1, 0)),
     ]
+    part = (far.shape[0], 1, piece, cols)
+    others = [
+        pl.BlockSpec(part, lambda s, h: (0, 0, 2 * s, 0)),
+        pl.BlockSpec(part, lambda s, h: (0, 1, 2 * s, 0)),
+        pl.BlockSpec(part, lambda s, h: (0, 0, 2 * s + 1, 0)),
+        pl.BlockSpec(part, lambda s, h: (0, 1, 2 * s + 1, 0)),
+    ]
     whole = lambda array: pl.BlockSpec(array.shape, lambda s, h: (0,) * array.ndim)
     return pl.pallas_call(
         final_step,
@@ -222,7 +230,7 @@
                 pl.BlockSpec((states, 2, rows, points), lambda s, h: (0, s, 0, h[0])),
                 pl.BlockSpec((states, 2, rows, points), lambda s, h: (0, s, 0, 1 - h[0])),
                 *weights,
-                *weights,
+                *others,
                 pl.BlockSpec((states, blocks, rows, width), lambda s, h: (0, 0, 0, 1)),
                 whole(kept),
                 whole(moved),
@@ -238,7 +246,7 @@
         cost_estimate=cost(2 * height * cols * (cols + height), 14 * MIB),
         name="final_pass",
     )(
-        half, received, received, near, near, far, far, received, kept, moved, own, energy, swap
+        half, received, received, near, near, far, far, far, far, received, kept, moved, own, energy, swap
     )
 
 
@@ -264,18 +272,26 @@
     pieces = grid_two.reshape(n_narrow, 2, piece, cols)
     near = lax.dynamic_index_in_dim(pieces, half, 1, False).reshape(share, cols)
     far = lax.dynamic_index_in_dim(pieces, 1 - half, 1, False).reshape(share, cols)
+    groups = n_wide // 2
+    side = lax.axis_index("wide") // groups
+    across_y = [(w, (w + groups) % n_wide) for w in range(n_wide)]
+    members = [list(range(groups)), list(range(groups, n_wide))]
     slim = pair_potential.T.astype(jnp.bfloat16)
     near = lax.all_gather(jnp.concatenate([near, slim], 0), "wide", axis=0, tiled=False)
 
     away = lax.dynamic_slice_in_dim(ham_two, (1 - core) * share, share, 0)
     stay = lax.dynamic_slice_in_dim(ham_two, core * share, share, 0)
     stay = jnp.where(core == half, stay, lax.ppermute(away, "wide", wide_pairs))
-    half_ham = lax.all_gather(stay, "wide", axis=0, tiled=False)
 
     own = local.reshape(n_narrow, inner, states, width).swapaxes(1, 2)
     own = lax.all_to_all(own.reshape(n_narrow, height, width), "narrow", 0, 0, tiled=True)
-    own, far = lax.optimization_barrier((own, far))
-    far = lax.all_gather(far, "wide", axis=0, tiled=False)
+    mine = jnp.stack([stay, far])
+    theirs = lax.ppermute(mine, "wide", across_y)
+    own, theirs, mine = lax.optimization_barrier((own, theirs, mine))
+    joined = jnp.where(side == 0, jnp.stack([mine, theirs]), jnp.stack([theirs, mine]))
+    stay, far = joined[:, 0], joined[:, 1]
+    half_ham = lax.all_gather(stay, "wide", axis=0, tiled=False, axis_index_groups=members)
+    far = lax.all_gather(far, "wide", axis=0, tiled=False, axis_index_groups=members)
     mate = lax.ppermute(own, "narrow", narrow_pairs)
     by_state = lax.all_to_all(jnp.swapaxes(local, 0, 1), "wide", 0, 0, tiled=True)
     turned = lax.optimization_barrier(grid_one.T)

time: 197 us -> 194 us (0.985)
  blocking collectives: 24.5 us -> 0 us
  waiting for transfers between devices: 63.4 us -> 74.2 us
  starting transfers between devices: 26.1 us -> 36.8 us
    ppermute x0 -> x1, waiting for transfers between devices: none -> 36.2 us  [on_device(): theirs = lax.ppermute(mine, 'wide', across_y)]
    all_to_all x1 -> x0, blocking collectives: 24.5 us -> none  [on_device(): lax.all_to_all(own.reshape(n_narrow, height, width), 'narrow', 0, 0, tile...]
    all_gather x2, waiting for transfers between devices: 16.2 us -> 0.02 us  [the longest x1 0.02 us: on_device(): lax.all_gather(stay, 'wide', axis=0, tiled=False, axis_index_groups=members)]
    all_to_all x1, waiting for transfers between devices: 10.2 us -> 3.48 us  [on_device(): lax.all_to_all(jnp.swapaxes(local, 0, 1), 'wide', 0, 0, tiled=True)]
    all_to_all x0 -> x1, starting transfers between devices: none -> 6.73 us  [on_device(): lax.all_to_all(own.reshape(n_narrow, height, width), 'narrow', 0, 0, tile...]
    all_to_all x1, starting transfers between devices: 7.69 us -> 10.3 us  [on_device(): lax.all_to_all(values.reshape(n_wide * n_narrow, 2 * inner, width // 2),...]
  transfers between devices with their start and end apart: 9 -> 11, of which waited for: 6 -> 4; matrix products, arithmetic and copies ran while one was open for 15% -> 15% of each run, Pallas kernels for 13% -> 13%
where the time goes in v6:
time: 194 us; the launch traced here: 193 us
  waiting for transfers between devices  74.2 us (38%)
  starting transfers between devices  36.8 us (19%)
  Pallas kernels  34.1 us (18%)
  local copies, waits for them, and re-layouts  25.6 us (13%)
  between operations  13.2 us (7%)
  matrix products  6.8 us (4%)
  other arithmetic  2.79 us (1%)
    ppermute x1, waiting for transfers between devices, on_device(): theirs = lax.ppermute(mine, 'wide', across_y)  36.2 us
    ppermute x1, waiting for transfers between devices, on_device(): moved = lax.ppermute(moved, 'narrow', narrow_pairs)  25.7 us
    unnamed x16, local copies, waits for them, and re-layouts  16.1 us
    pallas_call x1, Pallas kernels, middle_pass(): pl.pallas_call(middle_step, grid=(2 * half,), in_specs=[pl.BlockSpec(valu...  11.8 us
    all_to_all x1, starting transfers between devices, on_device(): lax.all_to_all(values.reshape(n_wide * n_narrow, 2 * inner, width // 2),...  10.3 us
    pallas_call x1, Pallas kernels, final_pass(): pl.pallas_call(final_step, grid_spec=pltpu.PrefetchScalarGridSpec(num_sca...  9.23 us
    all_to_all x1, starting transfers between devices, on_device(): lax.all_to_all(jnp.swapaxes(local, 0, 1), 'wide', 0, 0, tiled=True)  8.58 us
    all_to_all x1, waiting for transfers between devices, on_device(): lax.all_to_all(values.reshape(n_wide * n_narrow, 2 * inner, width // 2),...  8.04 us
  transfers between devices with their start and end apart: 11, of which 4 were waited for; matrix products, arithmetic and copies ran while one was open for 15% of the time, Pallas kernels for 13%

profile of v6, /device:TPU:1, one launch (start us, length us, event | category | flops | bytes accessed | tf_op | source)
XLA Modules:
  0.0 193.5 jit_solution(2895091827685307497)
XLA Ops:
  6.5 1.0 convert_bitcast_fusion
  7.5 1.1 dynamic-slice_bitcast_fusion
  8.6 0.8 pad_maximum_fusion.1
  9.3 0.0 all-gather.7.cloned.1.call-update
  9.4 1.0 constant_dynamic-slice_fusion
  10.4 1.5 collective-permute-start
  11.9 2.7 %copy.19 = bf16[8,16,16,256]{3,1,2,0:T(8,128)(2,1)} copy(bf16[8,16,16,256]{3,2,1,0:T(8,128)(2,1)} %bitcast.57) | data formatting | bytes 2097152 | tf_op jit(solution)/shard_map/reshape;squeeze | solution.py:286
  14.5 6.7 %all-to-all-start = ((bf16[8,256,256]{2,1,0:T(8,128)(2,1)}), bf16[8,256,256]{2,1,0:T(8,128)(2,1)S(1)}, u32[]{:S(2)}, u32[]{:S(2)}) async-start(bf16[8,256,256]{2,1,0:T(8,128)(2,1)} %bitcast.3), calls=%async_computation | async-start | bytes 2097152 | tf_op jit(solution)/shard_map/all_to_all | solution.py:287
  21.3 0.0 all-gather.11.cloned.1.call-start
  21.3 0.0 collective-permute-done
  21.3 0.1 select_bitcast_fusion
  21.4 0.1 pad_maximum_fusion
  21.5 0.5 collective-permute-start.1
  21.9 36.2 %collective-permute-done.1 = bf16[2,64,2048]{2,1,0:T(8,128)(2,1)S(1)} collective-permute-done((bf16[2,64,2048]{2,1,0:T(8,128)(2,1)S(1)}, bf16[2,64,2048]{2,1,0:T(8,128)(2,1)S(1)}, u32[]{:S(2)}, u32[]{:S(2)}) %collective-permute-start.1) | collective-permute-done | bytes 524320 | tf_op jit(solution)/shard_map/ppermute | solution.py:289
  58.2 0.0 all-to-all-done.own_ref
  58.2 0.2 maximum_select_fusion
  58.4 1.2 fusion.6
  59.5 0.0 all-gather.11.cloned.1.call-update
  59.5 0.0 all-gather.9.cloned.1.call-start
  59.6 0.7 all-gather.9.cloned.1.call-update
  60.3 1.6 collective-permute-start.2
  61.9 1.3 copy.30
  63.2 8.6 %all-to-all-start.1 = ((bf16[16,128,256]{2,1,0:T(8,128)(2,1)}), bf16[16,128,256]{2,1,0:T(8,128)(2,1)S(1)}, u32[]{:S(2)}, u32[]{:S(2)}) async-start(bf16[16,128,256]{2,1,0:T(8,128)(2,1)} %bitcast.42), calls=%async_computation.1 | async-start | bytes 2097152 | tf_op jit(solution)/shard_map/all_to_all | solution.py:296
  71.7 12.3 %copy.22 = bf16[2048,2048]{0,1:T(8,128)(2,1)} copy(bf16[2048,2048]{1,0:T(8,128)(2,1)} %grid_ref.1) | data formatting | bytes 16777216 | tf_op args[2]
  84.1 3.5 %all-to-all-done.1 = bf16[16,128,256]{2,1,0:T(8,128)(2,1)S(1)} async-done(((bf16[16,128,256]{2,1,0:T(8,128)(2,1)}), bf16[16,128,256]{2,1,0:T(8,128)(2,1)S(1)}, u32[]{:S(2)}, u32[]{:S(2)}) %all-to-all-start.1) | async-done | bytes 1048608 | tf_op jit(solution)/shard_map/all_to_all | solution.py:296
  87.6 0.0 collective-permute-done.2.mate_ref
  87.6 6.5 %forward_pass.1 = bf16[16,8,2,16,128]{4,3,2,1,0:T(8,128)(2,1)} custom-call(bf16[8,256,256]{2,1,0:T(8,128)(2,1)} %copy-done.1, bf16[8,256,256]{2,1,0:T(8,128)(2,1)} %collective-permute-done.2.mate_ref, bf16[16,80,2048]{2,1,0:T(8,128)(2,1)} %bitcast.43, bf16[16,80,2048]{2,1,0:T(8,128)(2,1)} %bitcast.44), custom_call_target="tpu_custom_call" | custom-call | flops 2147483648 | bytes 8388608 | tf_op jit(solution)/shard_map/forward_pass/pallas_call | solution.py:59
  94.1 10.3 %all-to-all-start.2 = ((bf16[128,32,128]{2,1,0:T(8,128)(2,1)}), bf16[128,32,128]{2,1,0:T(8,128)(2,1)S(1)}, u32[]{:S(2)}, u32[]{:S(2)}) async-start(bf16[128,32,128]{2,1,0:T(8,128)(2,1)} %bitcast.59), calls=%async_computation.2 | async-start | bytes 2097152 | tf_op jit(solution)/shard_map/all_to_all | solution.py:302
  104.4 6.8 %fusion.across_ref = bf16[2048,256]{1,0:T(8,128)(2,1)} fusion(bf16[2048,2048]{1,0:T(8,128)(2,1)} %param.8, bf16[2048,256]{1,0:T(8,128)(2,1)S(1)} %bitcast.63), kind=kOutput, calls=%fused_computation.1 | convolution fusion | flops 2148007936 | bytes 10485760 | tf_op jit(solution)/shard_map/dot_general | solution.py:14
  111.3 1.3 slice_bitcast_fusion
  112.5 0.1 copy.23
  112.7 1.3 copy.24
  114.0 8.0 %all-to-all-done.2 = bf16[128,32,128]{2,1,0:T(8,128)(2,1)S(1)} async-done(((bf16[128,32,128]{2,1,0:T(8,128)(2,1)}), bf16[128,32,128]{2,1,0:T(8,128)(2,1)S(1)}, u32[]{:S(2)}, u32[]{:S(2)}) %all-to-all-start.2) | async-done | bytes 1048608 | tf_op jit(solution)/shard_map/all_to_all | solution.py:302
  122.0 1.0 copy-done.3
  123.0 11.8 %middle_pass.1 = bf16[2048,512]{1,0:T(8,128)(2,1)} custom-call(bf16[64,2,2,16,128]{4,3,2,1,0:T(8,128)(2,1)} %bitcast.60, bf16[2048,2048]{1,0:T(8,128)(2,1)} %grid_ref.1, bf16[2048,2048]{1,0:T(8,128)(2,1)} %bitcast.55, bf16[2048,256]{1,0:T(8,128)(2,1)} %bitcast.61, bf16[2048,256]{1,0:T(8,128)(2,1)} %fusion.across_ref), custom_call_target="tpu_custom_call" | custom-call | flops 4294967296 | bytes 22020096 | tf_op jit(solution)/shard_map/middle_pass/pallas_call | solution.py:110
  134.8 6.2 %all-to-all-start.3 = ((bf16[128,16,512]{2,1,0:T(8,128)(2,1)}), bf16[128,16,512]{2,1,0:T(8,128)(2,1)S(1)}, u32[]{:S(2)}, u32[]{:S(2)}) async-start(bf16[128,16,512]{2,1,0:T(8,128)(2,1)} %bitcast.56), calls=%async_computation.3 | async-start | bytes 4194304 | tf_op jit(solution)/shard_map/all_to_all | solution.py:309
  141.0 0.0 all-gather.11.cloned.1.call-done
  141.0 6.5 %applied_pass.1 = (f32[256,1024]{1,0:T(8,128)}, bf16[256,1024]{1,0:T(8,128)(2,1)}) custom-call(bf16[8,256,256]{2,1,0:T(8,128)(2,1)} %copy-done.1, bf16[8,256,256]{2,1,0:T(8,128)(2,1)} %collective-permute-done.2.mate_ref, bf16[8,2,64,2048]{3,2,1,0:T(8,128)(2,1)} %bitcast.66), custom_call_target="tpu_custom_call" | custom-call | flops 2147483648 | bytes 8388608 | tf_op jit(solution)/shard_map/applied_pass/pallas_call | solution.py:150
  147.5 1.4 collective-permute-start.3
  148.9 0.0 copy-done.6
  148.9 0.1 broadcast_in_dim.12
  149.0 0.8 broadcast_in_dim_reshape.4.energy_ref
  149.8 0.8 fusion.1.swap_ref
  150.6 25.7 %collective-permute-done.3.moved_ref = bf16[256,1024]{1,0:T(8,128)(2,1)S(1)} collective-permute-done((bf16[256,1024]{1,0:T(8,128)(2,1)}, bf16[256,1024]{1,0:T(8,128)(2,1)S(1)}, u32[]{:S(2)}, u32[]{:S(2)}) %collective-permute-start.3) | collective-permute-done | bytes 524320 | tf_op jit(solution)/shard_map/ppermute | solution.py:314
  176.2 0.0 all-to-all-done.3
  176.2 0.8 copy-done.4
  177.0 0.7 copy-done
  177.7 9.2 %final_pass.1 = bf16[16,16,2048]{2,1,0:T(8,128)(2,1)} custom-call(s32[1]{0:T(128)} %bitcast.half_ref, bf16[16,8,16,512]{3,2,1,0:T(8,128)(2,1)} %bitcast.52, bf16[16,8,16,512]{3,2,1,0:T(8,128)(2,1)} %bitcast.53, bf16[16,80,2048]{2,1,0:T(8,128)(2,1)} %bitcast.46, bf16[16,80,2048]{2,1,0:T(8,128)(2,1)} %bitcast.47, bf16[8,2,64,2048]{3,2,1,0:T(8,128)(2,1)} %bitcast.48, ...), custom_call_target="tpu_custom_call" | custom-call | flops 2415919104 | bytes 14680064 | tf_op jit(solution)/shard_map/final_pass/pallas_call | solution.py:224
  (14 shorter events, 0.0 us)
Async XLA Ops:
  6.5 14.8 %copy-start.5 = (bf16[128,2048]{1,0:T(8,128)(2,1)S(1)}, bf16[128,2048]{1,0:T(8,128)(2,1)}, u32[]{:S(2)}) copy-start(bf16[128,2048]{1,0:T(8,128)(2,1)} %param.10) | copy-start | bytes 1572868
  6.5 81.0 %all-gather.7.cloned.1.call-start = ((), (), s32[]{:S(2)}) async-start(), calls=%async_computation.4 | async-start | bytes 5570560 | tf_op jit(solution)/shard_map/all_gather | solution.py:280
  10.4 11.0 %collective-permute-start = (bf16[64,2048]{1,0:T(8,128)(2,1)S(1)}, bf16[64,2048]{1,0:T(8,128)(2,1)S(1)}, u32[]{:S(2)}, u32[]{:S(2)}) collective-permute-start(bf16[64,2048]{1,0:T(8,128)(2,1)S(1)} %constant_dynamic-slice_fusion), channel_id=1, source_target_pairs={{0,8},{8,0},{16,24},{24,16},{32,40},{40,32},{48,56},{56,48},{64,72... | collective-permute-start | bytes 786440 | tf_op jit(solution)/shard_map/ppermute | solution.py:284
  11.9 50.0 %copy-start.2 = (bf16[1,128,16,256]{3,2,1,0:T(8,128)(2,1)S(1)}, bf16[1,128,16,256]{3,2,1,0:T(8,128)(2,1)}, u32[]{:S(2)}) copy-start(bf16[1,128,16,256]{3,2,1,0:T(8,128)(2,1)} %param.7) | copy-start | bytes 3145732
  14.5 43.7 %all-to-all-start = ((bf16[8,256,256]{2,1,0:T(8,128)(2,1)}), bf16[8,256,256]{2,1,0:T(8,128)(2,1)S(1)}, u32[]{:S(2)}, u32[]{:S(2)}) async-start(bf16[8,256,256]{2,1,0:T(8,128)(2,1)} %bitcast.3), calls=%async_computation | async-start | bytes 2097152 | tf_op jit(solution)/shard_map/all_to_all | solution.py:287
  21.3 119.8 %all-gather.11.cloned.1.call-start = ((), (), s32[]{:S(2)}) async-start(), calls=%async_computation.6 | async-start | bytes 4718592 | tf_op jit(solution)/shard_map/all_gather | solution.py:293
  21.5 36.7 %collective-permute-start.1 = (bf16[2,64,2048]{2,1,0:T(8,128)(2,1)S(1)}, bf16[2,64,2048]{2,1,0:T(8,128)(2,1)S(1)}, u32[]{:S(2)}, u32[]{:S(2)}) collective-permute-start(bf16[2,64,2048]{2,1,0:T(8,128)(2,1)S(1)} %pad_maximum_fusion), channel_id=1, source_target_pairs={{0,64},{8,72},{16,80},{24,88},{32,96},{40,104},{48,112},{56,120},{... | collective-permute-start | bytes 1572872 | tf_op jit(solution)/shard_map/ppermute | solution.py:289
  58.2 25.9 %copy-start.1 = (bf16[8,256,256]{2,1,0:T(8,128)(2,1)}, bf16[8,256,256]{2,1,0:T(8,128)(2,1)S(1)}, u32[]{:S(2)}) copy-start(bf16[8,256,256]{2,1,0:T(8,128)(2,1)S(1)} %all-to-all-done.own_ref) | copy-start | bytes 3145732
  59.5 91.0 %all-gather.9.cloned.1.call-start = ((), (), s32[]{:S(2)}) async-start(), calls=%async_computation.5 | async-start | bytes 4718592 | tf_op jit(solution)/shard_map/all_gather | solution.py:294
  60.3 27.3 %collective-permute-start.2 = (bf16[8,256,256]{2,1,0:T(8,128)(2,1)S(1)}, bf16[8,256,256]{2,1,0:T(8,128)(2,1)}, u32[]{:S(2)}, u32[]{:S(2)}) collective-permute-start(bf16[8,256,256]{2,1,0:T(8,128)(2,1)S(1)} %all-to-all-done.own_ref), channel_id=1, source_target_pairs={{0,1},{1,0},{2,3},{3,2},{4,5},{5,4},{6,7},{7,6},{8,9},{9,8},{10,11... | collective-permute-start | bytes 3145736 | tf_op jit(solution)/shard_map/ppermute | solution.py:295
  63.2 24.4 %all-to-all-start.1 = ((bf16[16,128,256]{2,1,0:T(8,128)(2,1)}), bf16[16,128,256]{2,1,0:T(8,128)(2,1)S(1)}, u32[]{:S(2)}, u32[]{:S(2)}) async-start(bf16[16,128,256]{2,1,0:T(8,128)(2,1)} %bitcast.42), calls=%async_computation.1 | async-start | bytes 2097152 | tf_op jit(solution)/shard_map/all_to_all | solution.py:296
  94.1 27.9 %all-to-all-start.2 = ((bf16[128,32,128]{2,1,0:T(8,128)(2,1)}), bf16[128,32,128]{2,1,0:T(8,128)(2,1)S(1)}, u32[]{:S(2)}, u32[]{:S(2)}) async-start(bf16[128,32,128]{2,1,0:T(8,128)(2,1)} %bitcast.59), calls=%async_computation.2 | async-start | bytes 2097152 | tf_op jit(solution)/shard_map/all_to_all | solution.py:302
  122.0 1.0 copy-start.3
  134.8 14.1 %copy-start.6 = (f32[16]{0:T(128)S(1)}, f32[16]{0:T(128)}, u32[]{:S(2)}) copy-start(f32[16]{0:T(128)} %param.13) | copy-start | bytes 196
  134.8 41.4 %all-to-all-start.3 = ((bf16[128,16,512]{2,1,0:T(8,128)(2,1)}), bf16[128,16,512]{2,1,0:T(8,128)(2,1)S(1)}, u32[]{:S(2)}, u32[]{:S(2)}) async-start(bf16[128,16,512]{2,1,0:T(8,128)(2,1)} %bitcast.56), calls=%async_computation.3 | async-start | bytes 4194304 | tf_op jit(solution)/shard_map/all_to_all | solution.py:309
  147.5 28.7 %collective-permute-start.3 = (bf16[256,1024]{1,0:T(8,128)(2,1)}, bf16[256,1024]{1,0:T(8,128)(2,1)S(1)}, u32[]{:S(2)}, u32[]{:S(2)}) collective-permute-start(bf16[256,1024]{1,0:T(8,128)(2,1)} %get-tuple-element.22), channel_id=1, source_target_pairs={{0,1},{1,0},{2,3},{3,2},{4,5},{5,4},{6,7},{7,6},{8,9},{9,8},{10,11... | collective-permute-start | bytes 1572872 | tf_op jit(solution)/shard_map/ppermute | solution.py:314
  176.2 0.8 copy-start.4
  176.2 1.5 copy-start
Sparse Core Ops, SparseCore 0:
  9.5 64.5 all-gather.6
  75.8 32.4 all-gather.10
  110.0 32.1 all-gather.8

commit v7 on v6

--- a/solution.py
+++ b/solution.py
@@ -36,12 +36,12 @@
             out_ref[rows, part * width : (part + 1) * width] = ref[part]
 
 
-def forward_step(own_ref, mate_ref, first_ref, second_ref, out_ref, rows_ref):
+def forward_step(own_ref, mate_ref, a0_ref, a1_ref, b0_ref, b1_ref, out_ref, rows_ref):
     @pl.when(pl.program_id(0) == 0)
     def _():
         side_by_side((own_ref, mate_ref), rows_ref)
 
-    right = jnp.concatenate([flatten(first_ref), flatten(second_ref)], 0)
+    right = jnp.concatenate([flatten(ref) for ref in (a0_ref, a1_ref, b0_ref, b1_ref)], 0)
     vals = dot_f32(rows_ref[...], right, NT).astype(out_ref.dtype)
     states, _, _, inner, points = out_ref.shape
     vals = vals.reshape(2, states, inner, 2 * points)
@@ -50,9 +50,21 @@
             out_ref[:, block, slot] = vals[slot, :, :, block * points : (block + 1) * points]
 
 
+def piece_specs(gathered, piece):
+    shards, _, _, cols = gathered.shape
+    block = (shards, 1, piece, cols)
+    return [
+        pl.BlockSpec(block, lambda s, *_: (0, 0, 2 * s, 0)),
+        pl.BlockSpec(block, lambda s, *_: (0, 1, 2 * s, 0)),
+        pl.BlockSpec(block, lambda s, *_: (0, 0, 2 * s + 1, 0)),
+        pl.BlockSpec(block, lambda s, *_: (0, 1, 2 * s + 1, 0)),
+    ]
+
+
 def forward_pass(own, mate, gathered, states, piece):
     n_narrow, height, width = own.shape
-    shards, _, cols = gathered.shape
+    shards, sides, _, cols = gathered.shape
+    shards = shards * sides
     inner = height // states
     points = shards * piece
     resident = pl.BlockSpec(own.shape, lambda s: (0, 0, 0))
@@ -62,8 +74,7 @@
         in_specs=[
             resident,
             resident,
-            pl.BlockSpec((shards, piece, cols), lambda s: (0, 2 * s, 0)),
-            pl.BlockSpec((shards, piece, cols), lambda s: (0, 2 * s + 1, 0)),
+            *piece_specs(gathered, piece),
         ],
         out_specs=pl.BlockSpec((states, 2, 2, inner, points), lambda s: (0, s, 0, 0, 0)),
         out_shape=jax.ShapeDtypeStruct((states, n_narrow, 2, inner, points), jnp.bfloat16),
@@ -71,7 +82,7 @@
         compiler_params=params(),
         cost_estimate=cost(4 * height * cols * points * n_narrow, 8 * MIB),
         name="forward_pass",
-    )(own, mate, gathered, gathered)
+    )(own, mate, gathered, gathered, gathered, gathered)
 
 
 def middle_step(
@@ -168,14 +179,15 @@
 
 
 def final_step(
-    half_ref, near_ref, far_ref, near_a, near_b, far_a0, far_a1, far_b0, far_b1, across_ref,
-    kept_ref, moved_ref, own_ref, energy_ref, swap_ref, out_ref, acc_ref,
+    half_ref, near_ref, far_ref, near_a0, near_a1, near_b0, near_b1, far_a0, far_a1, far_b0,
+    far_b1, across_ref, kept_ref, moved_ref, own_ref, energy_ref, swap_ref, out_ref, acc_ref,
 ):
     step = pl.program_id(0)
     states, _, rows, _ = near_ref.shape
     height = states * rows
     lefts = [ref[:, block].reshape(height, -1) for ref in (near_ref, far_ref) for block in range(2)]
-    rights = [flatten(ref) for ref in (near_a, near_b, far_a0, far_a1, far_b0, far_b1)]
+    rights = (near_a0, near_a1, near_b0, near_b1, far_a0, far_a1, far_b0, far_b1)
+    rights = [flatten(ref) for ref in rights]
     total = dot_f32(jnp.concatenate(lefts, 1), jnp.concatenate(rights, 0), NN)
 
     @pl.when(step == 0)
@@ -207,19 +219,8 @@
     states, blocks, rows, double = received.shape
     width = double // 2
     height = states * rows
-    shards, _, cols = near.shape
-    points = shards * piece
-    weights = [
-        pl.BlockSpec((shards, piece, cols), lambda s, h: (0, 2 * s, 0)),
-        pl.BlockSpec((shards, piece, cols), lambda s, h: (0, 2 * s + 1, 0)),
-    ]
-    part = (far.shape[0], 1, piece, cols)
-    others = [
-        pl.BlockSpec(part, lambda s, h: (0, 0, 2 * s, 0)),
-        pl.BlockSpec(part, lambda s, h: (0, 1, 2 * s, 0)),
-        pl.BlockSpec(part, lambda s, h: (0, 0, 2 * s + 1, 0)),
-        pl.BlockSpec(part, lambda s, h: (0, 1, 2 * s + 1, 0)),
-    ]
+    shards, sides, _, cols = near.shape
+    points = shards * sides * piece
     whole = lambda array: pl.BlockSpec(array.shape, lambda s, h: (0,) * array.ndim)
     return pl.pallas_call(
         final_step,
@@ -229,8 +230,8 @@
             in_specs=[
                 pl.BlockSpec((states, 2, rows, points), lambda s, h: (0, s, 0, h[0])),
                 pl.BlockSpec((states, 2, rows, points), lambda s, h: (0, s, 0, 1 - h[0])),
-                *weights,
-                *others,
+                *piece_specs(near, piece),
+                *piece_specs(far, piece),
                 pl.BlockSpec((states, blocks, rows, width), lambda s, h: (0, 0, 0, 1)),
                 whole(kept),
                 whole(moved),
@@ -246,7 +247,7 @@
         cost_estimate=cost(2 * height * cols * (cols + height), 14 * MIB),
         name="final_pass",
     )(
-        half, received, received, near, near, far, far, far, far, received, kept, moved, own, energy, swap
+        half, received, received, *[near] * 4, *[far] * 4, received, kept, moved, own, energy, swap
     )
 
 
@@ -269,16 +270,23 @@
     share = rows // 2
     assert states == n_wide and inner == count and n_wide * count == width
 
-    pieces = grid_two.reshape(n_narrow, 2, piece, cols)
-    near = lax.dynamic_index_in_dim(pieces, half, 1, False).reshape(share, cols)
-    far = lax.dynamic_index_in_dim(pieces, 1 - half, 1, False).reshape(share, cols)
     groups = n_wide // 2
     side = lax.axis_index("wide") // groups
     across_y = [(w, (w + groups) % n_wide) for w in range(n_wide)]
     members = [list(range(groups)), list(range(groups, n_wide))]
-    slim = pair_potential.T.astype(jnp.bfloat16)
-    near = lax.all_gather(jnp.concatenate([near, slim], 0), "wide", axis=0, tiled=False)
-
+
+    def both_sides(mine, theirs):
+        return jnp.where(side == 0, jnp.stack([mine, theirs]), jnp.stack([theirs, mine]))
+
+    def gather(value):
+        return lax.all_gather(value, "wide", axis=0, tiled=False, axis_index_groups=members)
+
+    pieces = grid_two.reshape(n_narrow, 2, piece, cols)
+    near = lax.dynamic_index_in_dim(pieces, half, 1, False).reshape(share, cols)
+    near = jnp.concatenate([near, pair_potential.T.astype(jnp.bfloat16)], 0)
+    near = gather(both_sides(near, lax.ppermute(near, "wide", across_y)))
+
+    far = lax.dynamic_index_in_dim(pieces, 1 - half, 1, False).reshape(share, cols)
     away = lax.dynamic_slice_in_dim(ham_two, (1 - core) * share, share, 0)
     stay = lax.dynamic_slice_in_dim(ham_two, core * share, share, 0)
     stay = jnp.where(core == half, stay, lax.ppermute(away, "wide", wide_pairs))
@@ -288,10 +296,10 @@
     mine = jnp.stack([stay, far])
     theirs = lax.ppermute(mine, "wide", across_y)
     own, theirs, mine = lax.optimization_barrier((own, theirs, mine))
-    joined = jnp.where(side == 0, jnp.stack([mine, theirs]), jnp.stack([theirs, mine]))
+    joined = both_sides(mine, theirs)
     stay, far = joined[:, 0], joined[:, 1]
-    half_ham = lax.all_gather(stay, "wide", axis=0, tiled=False, axis_index_groups=members)
-    far = lax.all_gather(far, "wide", axis=0, tiled=False, axis_index_groups=members)
+    half_ham = gather(stay)
+    far = gather(far)
     mate = lax.ppermute(own, "narrow", narrow_pairs)
     by_state = lax.all_to_all(jnp.swapaxes(local, 0, 1), "wide", 0, 0, tiled=True)
     turned = lax.optimization_barrier(grid_one.T)
@@ -303,7 +311,7 @@
         values.reshape(n_wide * n_narrow, 2 * inner, width // 2), both, 0, 0, tiled=True
     )
     values = values.reshape(n_wide * n_narrow // 2, 2, 2, inner, width // 2)
-    potential = near[:, share:].reshape(n_wide, 2, piece, n_one).swapaxes(0, 1)
+    potential = near[:, :, share:].reshape(groups, 2, 2, piece, n_one).transpose(2, 1, 0, 3, 4)
     potential = potential.reshape(width, n_one).T
     pair = middle_pass(values, grid_one, turned, potential, across)
     pair = lax.all_to_all(

time: 194 us -> 190 us (0.979)
  waiting for transfers between devices: 74.2 us -> 69.1 us
    ppermute x1, waiting for transfers between devices: 36.2 us -> 23.3 us  [on_device(): theirs = lax.ppermute(mine, 'wide', across_y)]
    ppermute x0 -> x1, waiting for transfers between devices: none -> 7.02 us  [on_device(): near = gather(both_sides(near, lax.ppermute(near, 'wide', across_y)))]
    ppermute x0 -> x1, starting transfers between devices: none -> 2.21 us  [on_device(): near = gather(both_sides(near, lax.ppermute(near, 'wide', across_y)))]
    unnamed x16 -> x20, local copies, waits for them, and re-layouts: 16.1 us -> 17.2 us
  transfers between devices with their start and end apart: 11 -> 12, of which waited for: 4 -> 5; matrix products, arithmetic and copies ran while one was open for 15% -> 15% of each run, Pallas kernels for 13% -> 13%
where the time goes in v7:
time: 190 us; the launch traced here: 189 us
  waiting for transfers between devices  69.1 us (36%)
  starting transfers between devices  37.2 us (20%)
  Pallas kernels  34.4 us (18%)
  local copies, waits for them, and re-layouts  25.2 us (13%)
  between operations  13.3 us (7%)
  matrix products  7 us (4%)
  other arithmetic  3.09 us (2%)
    ppermute x1, waiting for transfers between devices, on_device(): moved = lax.ppermute(moved, 'narrow', narrow_pairs)  25.6 us
    ppermute x1, waiting for transfers between devices, on_device(): theirs = lax.ppermute(mine, 'wide', across_y)  23.3 us
    unnamed x20, local copies, waits for them, and re-layouts  17.2 us
    pallas_call x1, Pallas kernels, middle_pass(): pl.pallas_call(middle_step, grid=(2 * half,), in_specs=[pl.BlockSpec(valu...  11.9 us
    all_to_all x1, starting transfers between devices, on_device(): lax.all_to_all(values.reshape(n_wide * n_narrow, 2 * inner, width // 2),...  9.61 us
    pallas_call x1, Pallas kernels, final_pass(): pl.pallas_call(final_step, grid_spec=pltpu.PrefetchScalarGridSpec(num_sca...  9.26 us
    all_to_all x1, waiting for transfers between devices, on_device(): lax.all_to_all(values.reshape(n_wide * n_narrow, 2 * inner, width // 2),...  7.86 us
    all_to_all x1, starting transfers between devices, on_device(): lax.all_to_all(jnp.swapaxes(local, 0, 1), 'wide', 0, 0, tiled=True)  7.41 us
  transfers between devices with their start and end apart: 12, of which 5 were waited for; matrix products, arithmetic and copies ran while one was open for 15% of the time, Pallas kernels for 13%

profile of v7, /device:TPU:1, one launch (start us, length us, event | category | flops | bytes accessed | tf_op | source)
XLA Modules:
  0.0 189.3 jit_solution(11492877437663237195)
XLA Ops:
  6.5 1.0 convert_bitcast_fusion
  7.6 1.1 dynamic-slice_bitcast_fusion
  8.6 0.1 fusion.6
  8.7 2.2 %collective-permute-start.3 = (bf16[80,2048]{1,0:T(8,128)(2,1)S(1)}, bf16[80,2048]{1,0:T(8,128)(2,1)S(1)}, u32[]{:S(2)}, u32[]{:S(2)}) collective-permute-start(bf16[80,2048]{1,0:T(8,128)(2,1)S(1)} %get-tuple-element.28), channel_id=1, source_target_pairs={{0,64},{8,72},{16,80},{24,88},{32,96},{40,104},{48,112},{56,120},{... | collective-permute-start | bytes 983048 | tf_op jit(solution)/shard_map/ppermute | solution.py:287
  10.9 7.0 %collective-permute-done.3 = bf16[80,2048]{1,0:T(8,128)(2,1)S(1)} collective-permute-done((bf16[80,2048]{1,0:T(8,128)(2,1)S(1)}, bf16[80,2048]{1,0:T(8,128)(2,1)S(1)}, u32[]{:S(2)}, u32[]{:S(2)}) %collective-permute-start.3) | collective-permute-done | bytes 327712 | tf_op jit(solution)/shard_map/ppermute | solution.py:287
  17.9 0.9 maximum_select_fusion.1
  18.9 0.0 all-gather.6.cloned.1.call-update
  18.9 1.0 constant_dynamic-slice_fusion
  19.9 1.7 collective-permute-start
  21.6 1.3 copy.29
  23.0 6.8 %all-to-all-start = ((bf16[8,256,256]{2,1,0:T(8,128)(2,1)}), bf16[8,256,256]{2,1,0:T(8,128)(2,1)S(1)}, u32[]{:S(2)}, u32[]{:S(2)}) async-start(bf16[8,256,256]{2,1,0:T(8,128)(2,1)} %bitcast.3), calls=%async_computation | async-start | bytes 2097152 | tf_op jit(solution)/shard_map/all_to_all | solution.py:295
  29.8 0.0 all-gather.10.cloned.1.call-start
  29.9 0.1 select_bitcast_fusion
  29.9 0.1 pad_maximum_fusion
  30.0 0.5 collective-permute-start.1
  30.5 23.3 %collective-permute-done.1 = bf16[2,64,2048]{2,1,0:T(8,128)(2,1)S(1)} collective-permute-done((bf16[2,64,2048]{2,1,0:T(8,128)(2,1)S(1)}, bf16[2,64,2048]{2,1,0:T(8,128)(2,1)S(1)}, u32[]{:S(2)}, u32[]{:S(2)}) %collective-permute-start.1) | collective-permute-done | bytes 524320 | tf_op jit(solution)/shard_map/ppermute | solution.py:297
  53.8 0.2 maximum_select_fusion
  54.0 1.1 fusion.7
  55.1 0.0 all-gather.10.cloned.1.call-update
  55.1 0.0 all-gather.8.cloned.1.call-start
  55.2 0.7 all-gather.8.cloned.1.call-update
  55.9 1.2 collective-permute-start.2
  57.1 1.3 copy.42
  58.4 7.4 %all-to-all-start.1 = ((bf16[16,128,256]{2,1,0:T(8,128)(2,1)}), bf16[16,128,256]{2,1,0:T(8,128)(2,1)S(1)}, u32[]{:S(2)}, u32[]{:S(2)}) async-start(bf16[16,128,256]{2,1,0:T(8,128)(2,1)} %bitcast.46), calls=%async_computation.1 | async-start | bytes 2097152 | tf_op jit(solution)/shard_map/all_to_all | solution.py:304
  65.8 12.4 %copy.32 = bf16[2048,2048]{0,1:T(8,128)(2,1)} copy(bf16[2048,2048]{1,0:T(8,128)(2,1)} %grid_ref.1) | data formatting | bytes 16777216 | tf_op args[2]
  78.2 4.5 %all-to-all-done.1 = bf16[16,128,256]{2,1,0:T(8,128)(2,1)S(1)} async-done(((bf16[16,128,256]{2,1,0:T(8,128)(2,1)}), bf16[16,128,256]{2,1,0:T(8,128)(2,1)S(1)}, u32[]{:S(2)}, u32[]{:S(2)}) %all-to-all-start.1) | async-done | bytes 1048608 | tf_op jit(solution)/shard_map/all_to_all | solution.py:304
  82.7 0.0 all-gather.6.cloned.1.call-done.a0_ref.a1_ref.b0_ref.b1_ref.near_a0.near_a1.near_b0.near_b1
  82.7 1.0 copy-done.4
  83.7 6.7 %forward_pass.1 = bf16[16,8,2,16,128]{4,3,2,1,0:T(8,128)(2,1)} custom-call(bf16[8,256,256]{2,1,0:T(8,128)(2,1)} %copy-done.1, bf16[8,256,256]{2,1,0:T(8,128)(2,1)} %copy-done.4, bf16[8,2,80,2048]{3,2,1,0:T(8,128)(2,1)} %all-gather.6.cloned.1.call-done.a0_ref.a1_ref.b0_ref.b1_ref.near_a0.near_a1.near_b0.near_b1, ...), custom_call_target="tpu_custom_call" | custom-call | flops 2147483648 | bytes 8388608 | tf_op jit(solution)/shard_map/forward_pass/pallas_call | solution.py:71
  90.4 9.6 %all-to-all-start.2 = ((bf16[128,32,128]{2,1,0:T(8,128)(2,1)}), bf16[128,32,128]{2,1,0:T(8,128)(2,1)S(1)}, u32[]{:S(2)}, u32[]{:S(2)}) async-start(bf16[128,32,128]{2,1,0:T(8,128)(2,1)} %bitcast.56), calls=%async_computation.2 | async-start | bytes 2097152 | tf_op jit(solution)/shard_map/all_to_all | solution.py:310
  100.0 7.0 %fusion.across_ref = bf16[2048,256]{1,0:T(8,128)(2,1)} fusion(bf16[2048,2048]{1,0:T(8,128)(2,1)} %param.8, bf16[2048,256]{1,0:T(8,128)(2,1)} %bitcast.62), kind=kOutput, calls=%fused_computation.1 | convolution fusion | flops 2148007936 | bytes 10485760 | tf_op jit(solution)/shard_map/dot_general | solution.py:14
  107.0 1.3 slice_bitcast_fusion
  108.3 0.1 copy.34
  108.5 1.3 copy.35
  109.8 7.9 %all-to-all-done.2 = bf16[128,32,128]{2,1,0:T(8,128)(2,1)S(1)} async-done(((bf16[128,32,128]{2,1,0:T(8,128)(2,1)}), bf16[128,32,128]{2,1,0:T(8,128)(2,1)S(1)}, u32[]{:S(2)}, u32[]{:S(2)}) %all-to-all-start.2) | async-done | bytes 1048608 | tf_op jit(solution)/shard_map/all_to_all | solution.py:310
  117.6 1.0 copy-done.3
  118.6 11.9 %middle_pass.1 = bf16[2048,512]{1,0:T(8,128)(2,1)} custom-call(bf16[64,2,2,16,128]{4,3,2,1,0:T(8,128)(2,1)} %bitcast.59, bf16[2048,2048]{1,0:T(8,128)(2,1)} %grid_ref.1, bf16[2048,2048]{1,0:T(8,128)(2,1)} %bitcast.54, bf16[2048,256]{1,0:T(8,128)(2,1)} %bitcast.60, bf16[2048,256]{1,0:T(8,128)(2,1)} %fusion.across_ref), custom_call_target="tpu_custom_call" | custom-call | flops 4294967296 | bytes 22020096 | tf_op jit(solution)/shard_map/middle_pass/pallas_call | solution.py:121
  130.5 6.2 %all-to-all-start.3 = ((bf16[128,16,512]{2,1,0:T(8,128)(2,1)}), bf16[128,16,512]{2,1,0:T(8,128)(2,1)S(1)}, u32[]{:S(2)}, u32[]{:S(2)}) async-start(bf16[128,16,512]{2,1,0:T(8,128)(2,1)} %bitcast.55), calls=%async_computation.3 | async-start | bytes 4194304 | tf_op jit(solution)/shard_map/all_to_all | solution.py:317
  136.8 0.0 all-gather.10.cloned.1.call-done
  136.8 6.6 %applied_pass.1 = (f32[256,1024]{1,0:T(8,128)}, bf16[256,1024]{1,0:T(8,128)(2,1)}) custom-call(bf16[8,256,256]{2,1,0:T(8,128)(2,1)} %copy-done.1, bf16[8,256,256]{2,1,0:T(8,128)(2,1)} %copy-done.4, bf16[8,2,64,2048]{3,2,1,0:T(8,128)(2,1)} %bitcast.66), custom_call_target="tpu_custom_call" | custom-call | flops 2147483648 | bytes 8388608 | tf_op jit(solution)/shard_map/applied_pass/pallas_call | solution.py:161
  143.4 1.4 collective-permute-start.4
  144.8 0.1 broadcast_in_dim.12
  144.8 0.8 broadcast_in_dim_reshape.4.energy_ref
  145.6 0.8 fusion.1.swap_ref
  146.4 25.6 %collective-permute-done.4.moved_ref = bf16[256,1024]{1,0:T(8,128)(2,1)S(1)} collective-permute-done((bf16[256,1024]{1,0:T(8,128)(2,1)}, bf16[256,1024]{1,0:T(8,128)(2,1)S(1)}, u32[]{:S(2)}, u32[]{:S(2)}) %collective-permute-start.4) | collective-permute-done | bytes 524320 | tf_op jit(solution)/shard_map/ppermute | solution.py:322
  172.0 0.8 copy-done.6
  172.8 0.7 copy-done
  173.5 9.3 %final_pass.1 = bf16[16,16,2048]{2,1,0:T(8,128)(2,1)} custom-call(s32[1]{0:T(128)} %bitcast.half_ref, bf16[16,8,16,512]{3,2,1,0:T(8,128)(2,1)} %bitcast.51, bf16[16,8,16,512]{3,2,1,0:T(8,128)(2,1)} %bitcast.52, bf16[8,2,80,2048]{3,2,1,0:T(8,128)(2,1)} %all-gather.6.cloned.1.call-done.a0_ref.a1_ref.b0_ref.b1_ref.near_a0.near_a1.near_b0.near_b1, ...), custom_call_target="tpu_custom_call" | custom-call | flops 2415919104 | bytes 14680064 | tf_op jit(solution)/shard_map/final_pass/pallas_call | solution.py:225
  (21 shorter events, 0.0 us)
Async XLA Ops:
  6.5 23.3 %copy-start.7 = (bf16[128,2048]{1,0:T(8,128)(2,1)S(1)}, bf16[128,2048]{1,0:T(8,128)(2,1)}, u32[]{:S(2)}) copy-start(bf16[128,2048]{1,0:T(8,128)(2,1)} %param.10) | copy-start | bytes 1572868
  6.5 15.1 %copy-start.2 = (bf16[1,128,16,256]{3,2,1,0:T(8,128)(2,1)S(1)}, bf16[1,128,16,256]{3,2,1,0:T(8,128)(2,1)}, u32[]{:S(2)}) copy-start(bf16[1,128,16,256]{3,2,1,0:T(8,128)(2,1)} %param.7) | copy-start | bytes 3145732
  6.5 76.2 %all-gather.6.cloned.1.call-start = ((), (), s32[]{:S(2)}) async-start(), calls=%async_computation.4 | async-start | bytes 5898240 | tf_op jit(solution)/shard_map/all_gather | solution.py:282
  8.7 9.2 %collective-permute-start.3 = (bf16[80,2048]{1,0:T(8,128)(2,1)S(1)}, bf16[80,2048]{1,0:T(8,128)(2,1)S(1)}, u32[]{:S(2)}, u32[]{:S(2)}) collective-permute-start(bf16[80,2048]{1,0:T(8,128)(2,1)S(1)} %get-tuple-element.28), channel_id=1, source_target_pairs={{0,64},{8,72},{16,80},{24,88},{32,96},{40,104},{48,112},{56,120},{... | collective-permute-start | bytes 983048 | tf_op jit(solution)/shard_map/ppermute | solution.py:287
  19.9 9.9 %collective-permute-start = (bf16[64,2048]{1,0:T(8,128)(2,1)S(1)}, bf16[64,2048]{1,0:T(8,128)(2,1)S(1)}, u32[]{:S(2)}, u32[]{:S(2)}) collective-permute-start(bf16[64,2048]{1,0:T(8,128)(2,1)S(1)} %constant_dynamic-slice_fusion), channel_id=1, source_target_pairs={{0,8},{8,0},{16,24},{24,16},{32,40},{40,32},{48,56},{56,48},{64,72... | collective-permute-start | bytes 786440 | tf_op jit(solution)/shard_map/ppermute | solution.py:292
  23.0 30.8 %all-to-all-start = ((bf16[8,256,256]{2,1,0:T(8,128)(2,1)}), bf16[8,256,256]{2,1,0:T(8,128)(2,1)S(1)}, u32[]{:S(2)}, u32[]{:S(2)}) async-start(bf16[8,256,256]{2,1,0:T(8,128)(2,1)} %bitcast.3), calls=%async_computation | async-start | bytes 2097152 | tf_op jit(solution)/shard_map/all_to_all | solution.py:295
  29.8 107.0 %all-gather.10.cloned.1.call-start = ((), (), s32[]{:S(2)}) async-start(), calls=%async_computation.6 | async-start | bytes 4718592 | tf_op jit(solution)/shard_map/all_gather | solution.py:282
  30.0 23.8 %collective-permute-start.1 = (bf16[2,64,2048]{2,1,0:T(8,128)(2,1)S(1)}, bf16[2,64,2048]{2,1,0:T(8,128)(2,1)S(1)}, u32[]{:S(2)}, u32[]{:S(2)}) collective-permute-start(bf16[2,64,2048]{2,1,0:T(8,128)(2,1)S(1)} %pad_maximum_fusion), channel_id=1, source_target_pairs={{0,64},{8,72},{16,80},{24,88},{32,96},{40,104},{48,112},{56,120},{... | collective-permute-start | bytes 1572872 | tf_op jit(solution)/shard_map/ppermute | solution.py:297
  53.8 24.4 %copy-start.1 = (bf16[8,256,256]{2,1,0:T(8,128)(2,1)}, bf16[8,256,256]{2,1,0:T(8,128)(2,1)S(1)}, u32[]{:S(2)}) copy-start(bf16[8,256,256]{2,1,0:T(8,128)(2,1)S(1)} %all-to-all-done.own_ref) | copy-start | bytes 3145732
  55.1 91.2 %all-gather.8.cloned.1.call-start = ((), (), s32[]{:S(2)}) async-start(), calls=%async_computation.5 | async-start | bytes 4718592 | tf_op jit(solution)/shard_map/all_gather | solution.py:282
  55.9 26.8 %collective-permute-start.2 = (bf16[8,256,256]{2,1,0:T(8,128)(2,1)S(1)}, bf16[8,256,256]{2,1,0:T(8,128)(2,1)S(1)}, u32[]{:S(2)}, u32[]{:S(2)}) collective-permute-start(bf16[8,256,256]{2,1,0:T(8,128)(2,1)S(1)} %all-to-all-done.own_ref), channel_id=1, source_target_pairs={{0,1},{1,0},{2,3},{3,2},{4,5},{5,4},{6,7},{7,6},{8,9},{9,8},{10,11... | collective-permute-start | bytes 3145736 | tf_op jit(solution)/shard_map/ppermute | solution.py:303
  58.4 24.3 %all-to-all-start.1 = ((bf16[16,128,256]{2,1,0:T(8,128)(2,1)}), bf16[16,128,256]{2,1,0:T(8,128)(2,1)S(1)}, u32[]{:S(2)}, u32[]{:S(2)}) async-start(bf16[16,128,256]{2,1,0:T(8,128)(2,1)} %bitcast.46), calls=%async_computation.1 | async-start | bytes 2097152 | tf_op jit(solution)/shard_map/all_to_all | solution.py:304
  82.7 7.7 %copy-start.5 = (bf16[16,128,256]{2,1,0:T(8,128)(2,1)}, bf16[16,128,256]{2,1,0:T(8,128)(2,1)S(1)}, u32[]{:S(2)}) copy-start(bf16[16,128,256]{2,1,0:T(8,128)(2,1)S(1)} %all-to-all-done.1) | copy-start | bytes 3145732
  82.7 1.0 copy-start.4
  90.4 27.2 %all-to-all-start.2 = ((bf16[128,32,128]{2,1,0:T(8,128)(2,1)}), bf16[128,32,128]{2,1,0:T(8,128)(2,1)S(1)}, u32[]{:S(2)}, u32[]{:S(2)}) async-start(bf16[128,32,128]{2,1,0:T(8,128)(2,1)} %bitcast.56), calls=%async_computation.2 | async-start | bytes 2097152 | tf_op jit(solution)/shard_map/all_to_all | solution.py:310
  117.6 1.0 copy-start.3
  130.5 14.2 %copy-start.8 = (f32[16]{0:T(128)S(1)}, f32[16]{0:T(128)}, u32[]{:S(2)}) copy-start(f32[16]{0:T(128)} %param.13) | copy-start | bytes 196
  130.5 41.5 %all-to-all-start.3 = ((bf16[128,16,512]{2,1,0:T(8,128)(2,1)}), bf16[128,16,512]{2,1,0:T(8,128)(2,1)S(1)}, u32[]{:S(2)}, u32[]{:S(2)}) async-start(bf16[128,16,512]{2,1,0:T(8,128)(2,1)} %bitcast.55), calls=%async_computation.3 | async-start | bytes 4194304 | tf_op jit(solution)/shard_map/all_to_all | solution.py:317
  143.4 28.6 %collective-permute-start.4 = (bf16[256,1024]{1,0:T(8,128)(2,1)}, bf16[256,1024]{1,0:T(8,128)(2,1)S(1)}, u32[]{:S(2)}, u32[]{:S(2)}) collective-permute-start(bf16[256,1024]{1,0:T(8,128)(2,1)} %get-tuple-element.22), channel_id=1, source_target_pairs={{0,1},{1,0},{2,3},{3,2},{4,5},{5,4},{6,7},{7,6},{8,9},{9,8},{10,11... | collective-permute-start | bytes 1572872 | tf_op jit(solution)/shard_map/ppermute | solution.py:322
  172.0 0.8 copy-start.6
  172.0 1.5 copy-start
Sparse Core Ops, SparseCore 0:
  19.0 40.6 all-gather.5
  61.4 38.2 all-gather.9
  101.5 34.8 all-gather.7

commit v8 on v7

--- a/solution.py
+++ b/solution.py
@@ -295,17 +295,17 @@
     own = lax.all_to_all(own.reshape(n_narrow, height, width), "narrow", 0, 0, tiled=True)
     mine = jnp.stack([stay, far])
     theirs = lax.ppermute(mine, "wide", across_y)
-    own, theirs, mine = lax.optimization_barrier((own, theirs, mine))
+    mate = lax.ppermute(own, "narrow", narrow_pairs)
+    by_state = lax.all_to_all(jnp.swapaxes(local, 0, 1), "wide", 0, 0, tiled=True)
+
+    turned = lax.optimization_barrier(grid_one.T)
+    values = forward_pass(own, mate, near, states, piece)
+    values, by_state, turned = lax.optimization_barrier((values, by_state, turned))
+    by_state, theirs, mine = lax.optimization_barrier((by_state, theirs, mine))
     joined = both_sides(mine, theirs)
     stay, far = joined[:, 0], joined[:, 1]
     half_ham = gather(stay)
     far = gather(far)
-    mate = lax.ppermute(own, "narrow", narrow_pairs)
-    by_state = lax.all_to_all(jnp.swapaxes(local, 0, 1), "wide", 0, 0, tiled=True)
-    turned = lax.optimization_barrier(grid_one.T)
-    own, mate, by_state, turned = lax.optimization_barrier((own, mate, by_state, turned))
-
-    values = forward_pass(own, mate, near, states, piece)
     across = dot_f32(ham_one, by_state.reshape(n_one, width), NN).astype(jnp.bfloat16)
     values = lax.all_to_all(
         values.reshape(n_wide * n_narrow, 2 * inner, width // 2), both, 0, 0, tiled=True

time: 190 us -> 188 us (0.989)
  starting transfers between devices: 37.2 us -> 34 us
    ppermute x1, waiting for transfers between devices: 25.6 us -> 0.01 us  [on_device(): moved = lax.ppermute(moved, 'narrow', narrow_pairs)]
    ppermute x1, waiting for transfers between devices: 23.3 us -> 1.98 us  [on_device(): theirs = lax.ppermute(mine, 'wide', across_y)]
    all_to_all x1, waiting for transfers between devices: 0.01 us -> 19.2 us  [on_device(): lax.all_to_all(pair.reshape(n_wide * n_narrow, inner, 2 * width), both, 0...]
    all_gather x3, waiting for transfers between devices: 0.04 us -> 17.1 us  [gather(): lax.all_gather(value, 'wide', axis=0, tiled=False, axis_index_groups=memb...]
    all_to_all x1, waiting for transfers between devices: 0.01 us -> 14.8 us  [on_device(): lax.all_to_all(own.reshape(n_narrow, height, width), 'narrow', 0, 0, tile...]
    all_to_all x1, waiting for transfers between devices: 4.49 us -> 0.01 us  [on_device(): lax.all_to_all(jnp.swapaxes(local, 0, 1), 'wide', 0, 0, tiled=True)]
    all_to_all x1, starting transfers between devices: 9.61 us -> 6.8 us  [on_device(): lax.all_to_all(values.reshape(n_wide * n_narrow, 2 * inner, width // 2),...]
    unnamed x20 -> x18, local copies, waits for them, and re-layouts: 17.2 us -> 16.4 us
  transfers between devices with their start and end apart: 12 -> 12, of which waited for: 5 -> 7; matrix products, arithmetic and copies ran while one was open for 15% -> 16% of each run, Pallas kernels for 13% -> 13%
where the time goes in v8:
time: 188 us; the launch traced here: 187 us
  waiting for transfers between devices  68.9 us (37%)
  Pallas kernels  34.5 us (18%)
  starting transfers between devices  34 us (18%)
  local copies, waits for them, and re-layouts  25.5 us (14%)
  between operations  13.2 us (7%)
  matrix products  6.98 us (4%)
  other arithmetic  4.12 us (2%)
    all_to_all x1, waiting for transfers between devices, on_device(): lax.all_to_all(pair.reshape(n_wide * n_narrow, inner, 2 * width), both, 0...  19.2 us
    all_gather x3, waiting for transfers between devices, gather(): lax.all_gather(value, 'wide', axis=0, tiled=False, axis_index_groups=memb...  17.1 us
    unnamed x18, local copies, waits for them, and re-layouts  16.4 us
    all_to_all x1, waiting for transfers between devices, on_device(): lax.all_to_all(own.reshape(n_narrow, height, width), 'narrow', 0, 0, tile...  14.8 us
    pallas_call x1, Pallas kernels, middle_pass(): pl.pallas_call(middle_step, grid=(2 * half,), in_specs=[pl.BlockSpec(valu...  12 us
    pallas_call x1, Pallas kernels, final_pass(): pl.pallas_call(final_step, grid_spec=pltpu.PrefetchScalarGridSpec(num_sca...  9.26 us
    all_to_all x1, waiting for transfers between devices, on_device(): lax.all_to_all(values.reshape(n_wide * n_narrow, 2 * inner, width // 2),...  7.8 us
    all_to_all x1, starting transfers between devices, on_device(): lax.all_to_all(jnp.swapaxes(local, 0, 1), 'wide', 0, 0, tiled=True)  7.14 us
  transfers between devices with their start and end apart: 12, of which 7 were waited for; matrix products, arithmetic and copies ran while one was open for 16% of the time, Pallas kernels for 13%

profile of v8, /device:TPU:1, one launch (start us, length us, event | category | flops | bytes accessed | tf_op | source)
XLA Modules:
  0.0 187.2 jit_solution(3569905473138536221)
XLA Ops:
  6.5 1.0 convert_bitcast_fusion
  7.6 1.1 dynamic-slice_bitcast_fusion
  8.6 0.1 fusion.6
  8.7 2.2 %collective-permute-start.1 = (bf16[80,2048]{1,0:T(8,128)(2,1)S(1)}, bf16[80,2048]{1,0:T(8,128)(2,1)S(1)}, u32[]{:S(2)}, u32[]{:S(2)}) collective-permute-start(bf16[80,2048]{1,0:T(8,128)(2,1)S(1)} %get-tuple-element.26), channel_id=1, source_target_pairs={{0,64},{8,72},{16,80},{24,88},{32,96},{40,104},{48,112},{56,120},{... | collective-permute-start | bytes 983048 | tf_op jit(solution)/shard_map/ppermute | solution.py:287
  10.9 7.0 %collective-permute-done.1 = bf16[80,2048]{1,0:T(8,128)(2,1)S(1)} collective-permute-done((bf16[80,2048]{1,0:T(8,128)(2,1)S(1)}, bf16[80,2048]{1,0:T(8,128)(2,1)S(1)}, u32[]{:S(2)}, u32[]{:S(2)}) %collective-permute-start.1) | collective-permute-done | bytes 327712 | tf_op jit(solution)/shard_map/ppermute | solution.py:287
  17.9 0.9 maximum_select_fusion.1
  18.9 0.0 all-gather.6.cloned.1.call-update
  18.9 2.6 %copy.29 = bf16[8,16,16,256]{3,1,2,0:T(8,128)(2,1)} copy(bf16[8,16,16,256]{3,2,1,0:T(8,128)(2,1)} %bitcast.56) | data formatting | bytes 2097152 | tf_op jit(solution)/shard_map/reshape;squeeze | solution.py:294
  21.5 6.9 %all-to-all-start = ((bf16[8,256,256]{2,1,0:T(8,128)(2,1)}), bf16[8,256,256]{2,1,0:T(8,128)(2,1)S(1)}, u32[]{:S(2)}, u32[]{:S(2)}) async-start(bf16[8,256,256]{2,1,0:T(8,128)(2,1)} %bitcast.3), calls=%async_computation | async-start | bytes 2097152 | tf_op jit(solution)/shard_map/all_to_all | solution.py:295
  28.4 0.7 constant_dynamic-slice_fusion
  29.1 1.8 collective-permute-start.2
  30.9 14.8 %all-to-all-done.own_ref = bf16[8,256,256]{2,1,0:T(8,128)(2,1)S(1)} async-done(((bf16[8,256,256]{2,1,0:T(8,128)(2,1)}), bf16[8,256,256]{2,1,0:T(8,128)(2,1)S(1)}, u32[]{:S(2)}, u32[]{:S(2)}) %all-to-all-start) | async-done | bytes 1048608 | tf_op jit(solution)/shard_map/all_to_all | solution.py:295
  45.7 0.0 collective-permute-start
  45.7 1.3 copy.42
  47.0 7.1 %all-to-all-start.1 = ((bf16[16,128,256]{2,1,0:T(8,128)(2,1)}), bf16[16,128,256]{2,1,0:T(8,128)(2,1)}, u32[]{:S(2)}, u32[]{:S(2)}) async-start(bf16[16,128,256]{2,1,0:T(8,128)(2,1)} %bitcast.46), calls=%async_computation.1 | async-start | bytes 2097152 | tf_op jit(solution)/shard_map/all_to_all | solution.py:299
  54.2 0.0 all-gather.10.cloned.1.call-start
  54.2 1.1 select_bitcast_fusion
  55.4 0.1 pad_maximum_fusion
  55.4 1.5 collective-permute-start.3
  56.9 12.3 %copy.32 = bf16[2048,2048]{0,1:T(8,128)(2,1)} copy(bf16[2048,2048]{1,0:T(8,128)(2,1)} %grid_ref.1) | data formatting | bytes 16777216 | tf_op args[2]
  69.3 0.2 collective-permute-done.mate_ref
  69.5 1.0 copy-done.4
  70.5 6.6 %forward_pass.1 = bf16[16,8,2,16,128]{4,3,2,1,0:T(8,128)(2,1)} custom-call(bf16[8,256,256]{2,1,0:T(8,128)(2,1)} %copy-done.1, bf16[8,256,256]{2,1,0:T(8,128)(2,1)} %copy-done.4, bf16[8,2,80,2048]{3,2,1,0:T(8,128)(2,1)} %all-gather.6.cloned.1.call-done.a0_ref.a1_ref.b0_ref.b1_ref.near_a0.near_a1.near_b0.near_b1, ...), custom_call_target="tpu_custom_call" | custom-call | flops 2147483648 | bytes 8388608 | tf_op jit(solution)/shard_map/forward_pass/pallas_call | solution.py:71
  77.1 2.0 %collective-permute-done.3 = bf16[2,64,2048]{2,1,0:T(8,128)(2,1)S(1)} collective-permute-done((bf16[2,64,2048]{2,1,0:T(8,128)(2,1)S(1)}, bf16[2,64,2048]{2,1,0:T(8,128)(2,1)S(1)}, u32[]{:S(2)}, u32[]{:S(2)}) %collective-permute-start.3) | collective-permute-done | bytes 524320 | tf_op jit(solution)/shard_map/ppermute | solution.py:297
  79.1 0.2 maximum_select_fusion
  79.3 1.1 fusion.7
  80.3 0.0 all-gather.10.cloned.1.call-update
  80.4 0.0 all-gather.8.cloned.1.call-start
  80.4 0.7 all-gather.8.cloned.1.call-update
  81.1 6.8 %all-to-all-start.2 = ((bf16[128,32,128]{2,1,0:T(8,128)(2,1)}), bf16[128,32,128]{2,1,0:T(8,128)(2,1)S(1)}, u32[]{:S(2)}, u32[]{:S(2)}) async-start(bf16[128,32,128]{2,1,0:T(8,128)(2,1)} %bitcast.12), calls=%async_computation.2 | async-start | bytes 2097152 | tf_op jit(solution)/shard_map/all_to_all | solution.py:310
  87.9 1.4 slice_bitcast_fusion
  89.3 0.1 copy.33
  89.4 1.3 copy.34
  90.7 7.0 %fusion.across_ref = bf16[2048,256]{1,0:T(8,128)(2,1)} fusion(bf16[2048,2048]{1,0:T(8,128)(2,1)} %param.8, bf16[2048,256]{1,0:T(8,128)(2,1)} %bitcast.20), kind=kOutput, calls=%fused_computation.1 | convolution fusion | flops 2148007936 | bytes 10485760 | tf_op jit(solution)/shard_map/dot_general | solution.py:14
  97.7 7.8 %all-to-all-done.2 = bf16[128,32,128]{2,1,0:T(8,128)(2,1)S(1)} async-done(((bf16[128,32,128]{2,1,0:T(8,128)(2,1)}), bf16[128,32,128]{2,1,0:T(8,128)(2,1)S(1)}, u32[]{:S(2)}, u32[]{:S(2)}) %all-to-all-start.2) | async-done | bytes 1048608 | tf_op jit(solution)/shard_map/all_to_all | solution.py:310
  105.5 1.0 copy-done.3
  106.5 12.0 %middle_pass.1 = bf16[2048,512]{1,0:T(8,128)(2,1)} custom-call(bf16[64,2,2,16,128]{4,3,2,1,0:T(8,128)(2,1)} %bitcast.58, bf16[2048,2048]{1,0:T(8,128)(2,1)} %grid_ref.1, bf16[2048,2048]{1,0:T(8,128)(2,1)} %bitcast.54, bf16[2048,256]{1,0:T(8,128)(2,1)} %bitcast.59, bf16[2048,256]{1,0:T(8,128)(2,1)} %fusion.across_ref), custom_call_target="tpu_custom_call" | custom-call | flops 4294967296 | bytes 22020096 | tf_op jit(solution)/shard_map/middle_pass/pallas_call | solution.py:121
  118.5 6.1 %all-to-all-start.3 = ((bf16[128,16,512]{2,1,0:T(8,128)(2,1)}), bf16[128,16,512]{2,1,0:T(8,128)(2,1)S(1)}, u32[]{:S(2)}, u32[]{:S(2)}) async-start(bf16[128,16,512]{2,1,0:T(8,128)(2,1)} %bitcast.55), calls=%async_computation.3 | async-start | bytes 4194304 | tf_op jit(solution)/shard_map/all_to_all | solution.py:317
  124.7 0.0 all-gather.10.cloned.1.call-done
  124.7 6.6 %applied_pass.1 = (f32[256,1024]{1,0:T(8,128)}, bf16[256,1024]{1,0:T(8,128)(2,1)}) custom-call(bf16[8,256,256]{2,1,0:T(8,128)(2,1)} %copy-done.1, bf16[8,256,256]{2,1,0:T(8,128)(2,1)} %copy-done.4, bf16[8,2,64,2048]{3,2,1,0:T(8,128)(2,1)} %bitcast.64), custom_call_target="tpu_custom_call" | custom-call | flops 2147483648 | bytes 8388608 | tf_op jit(solution)/shard_map/applied_pass/pallas_call | solution.py:161
  131.3 1.4 collective-permute-start.4
  132.7 0.1 broadcast_in_dim.12
  132.7 0.8 broadcast_in_dim_reshape.4.energy_ref
  133.5 0.8 fusion.1.swap_ref
  134.3 19.2 %all-to-all-done.3 = bf16[128,16,512]{2,1,0:T(8,128)(2,1)S(1)} async-done(((bf16[128,16,512]{2,1,0:T(8,128)(2,1)}), bf16[128,16,512]{2,1,0:T(8,128)(2,1)S(1)}, u32[]{:S(2)}, u32[]{:S(2)}) %all-to-all-start.3) | async-done | bytes 2097184 | tf_op jit(solution)/shard_map/all_to_all | solution.py:317
  153.5 17.1 %all-gather.8.cloned.1.call-done = bf16[16,1,64,2048]{3,2,1,0:T(8,128)(2,1)} async-done(((bf16[2,1,64,2048]{3,2,1,0:T(8,128)(2,1)}), bf16[16,1,64,2048]{3,2,1,0:T(8,128)(2,1)}) %all-gather.8.cloned.1.call-update) | async-done | bytes 4194320 | tf_op jit(solution)/shard_map/all_gather | solution.py:282
  170.6 0.8 copy-done.5
  171.4 9.3 %final_pass.1 = bf16[16,16,2048]{2,1,0:T(8,128)(2,1)} custom-call(s32[1]{0:T(128)} %bitcast.half_ref, bf16[16,8,16,512]{3,2,1,0:T(8,128)(2,1)} %bitcast.51, bf16[16,8,16,512]{3,2,1,0:T(8,128)(2,1)} %bitcast.52, bf16[8,2,80,2048]{3,2,1,0:T(8,128)(2,1)} %all-gather.6.cloned.1.call-done.a0_ref.a1_ref.b0_ref.b1_ref.near_a0.near_a1.near_b0.near_b1, ...), custom_call_target="tpu_custom_call" | custom-call | flops 2415919104 | bytes 14680064 | tf_op jit(solution)/shard_map/final_pass/pallas_call | solution.py:225
  (19 shorter events, 0.0 us)
Async XLA Ops:
  6.5 39.2 %copy-start.2 = (bf16[1,128,16,256]{3,2,1,0:T(8,128)(2,1)S(1)}, bf16[1,128,16,256]{3,2,1,0:T(8,128)(2,1)}, u32[]{:S(2)}) copy-start(bf16[1,128,16,256]{3,2,1,0:T(8,128)(2,1)} %param.7) | copy-start | bytes 3145732
  6.5 21.9 %copy-start.6 = (bf16[128,2048]{1,0:T(8,128)(2,1)S(1)}, bf16[128,2048]{1,0:T(8,128)(2,1)}, u32[]{:S(2)}) copy-start(bf16[128,2048]{1,0:T(8,128)(2,1)} %param.10) | copy-start | bytes 1572868
  6.5 63.0 %all-gather.6.cloned.1.call-start = ((), (), s32[]{:S(2)}) async-start(), calls=%async_computation.4 | async-start | bytes 5898240 | tf_op jit(solution)/shard_map/all_gather | solution.py:282
  8.7 9.2 %collective-permute-start.1 = (bf16[80,2048]{1,0:T(8,128)(2,1)S(1)}, bf16[80,2048]{1,0:T(8,128)(2,1)S(1)}, u32[]{:S(2)}, u32[]{:S(2)}) collective-permute-start(bf16[80,2048]{1,0:T(8,128)(2,1)S(1)} %get-tuple-element.26), channel_id=1, source_target_pairs={{0,64},{8,72},{16,80},{24,88},{32,96},{40,104},{48,112},{56,120},{... | collective-permute-start | bytes 983048 | tf_op jit(solution)/shard_map/ppermute | solution.py:287
  21.5 24.2 %all-to-all-start = ((bf16[8,256,256]{2,1,0:T(8,128)(2,1)}), bf16[8,256,256]{2,1,0:T(8,128)(2,1)S(1)}, u32[]{:S(2)}, u32[]{:S(2)}) async-start(bf16[8,256,256]{2,1,0:T(8,128)(2,1)} %bitcast.3), calls=%async_computation | async-start | bytes 2097152 | tf_op jit(solution)/shard_map/all_to_all | solution.py:295
  29.1 25.1 %collective-permute-start.2 = (bf16[64,2048]{1,0:T(8,128)(2,1)}, bf16[64,2048]{1,0:T(8,128)(2,1)}, u32[]{:S(2)}, u32[]{:S(2)}) collective-permute-start(bf16[64,2048]{1,0:T(8,128)(2,1)} %constant_dynamic-slice_fusion), channel_id=1, source_target_pairs={{0,8},{8,0},{16,24},{24,16},{32,40},{40,32},{48,56},{56,48},{64,72... | collective-permute-start | bytes 786440 | tf_op jit(solution)/shard_map/ppermute | solution.py:292
  45.7 23.6 %copy-start.1 = (bf16[8,256,256]{2,1,0:T(8,128)(2,1)}, bf16[8,256,256]{2,1,0:T(8,128)(2,1)S(1)}, u32[]{:S(2)}) copy-start(bf16[8,256,256]{2,1,0:T(8,128)(2,1)S(1)} %all-to-all-done.own_ref) | copy-start | bytes 3145732
  45.7 23.8 %collective-permute-start = (bf16[8,256,256]{2,1,0:T(8,128)(2,1)S(1)}, bf16[8,256,256]{2,1,0:T(8,128)(2,1)S(1)}, u32[]{:S(2)}, u32[]{:S(2)}) collective-permute-start(bf16[8,256,256]{2,1,0:T(8,128)(2,1)S(1)} %all-to-all-done.own_ref), channel_id=1, source_target_pairs={{0,1},{1,0},{2,3},{3,2},{4,5},{5,4},{6,7},{7,6},{8,9},{9,8},{10,11... | collective-permute-start | bytes 3145736 | tf_op jit(solution)/shard_map/ppermute | solution.py:298
  47.0 30.1 %all-to-all-start.1 = ((bf16[16,128,256]{2,1,0:T(8,128)(2,1)}), bf16[16,128,256]{2,1,0:T(8,128)(2,1)}, u32[]{:S(2)}, u32[]{:S(2)}) async-start(bf16[16,128,256]{2,1,0:T(8,128)(2,1)} %bitcast.46), calls=%async_computation.1 | async-start | bytes 2097152 | tf_op jit(solution)/shard_map/all_to_all | solution.py:299
  54.2 70.5 %all-gather.10.cloned.1.call-start = ((), (), s32[]{:S(2)}) async-start(), calls=%async_computation.6 | async-start | bytes 4718592 | tf_op jit(solution)/shard_map/all_gather | solution.py:282
  55.4 23.7 %collective-permute-start.3 = (bf16[2,64,2048]{2,1,0:T(8,128)(2,1)S(1)}, bf16[2,64,2048]{2,1,0:T(8,128)(2,1)S(1)}, u32[]{:S(2)}, u32[]{:S(2)}) collective-permute-start(bf16[2,64,2048]{2,1,0:T(8,128)(2,1)S(1)} %pad_maximum_fusion), channel_id=1, source_target_pairs={{0,64},{8,72},{16,80},{24,88},{32,96},{40,104},{48,112},{56,120},{... | collective-permute-start | bytes 1572872 | tf_op jit(solution)/shard_map/ppermute | solution.py:297
  69.5 1.0 copy-start.4
  80.4 90.2 %all-gather.8.cloned.1.call-start = ((), (), s32[]{:S(2)}) async-start(), calls=%async_computation.5 | async-start | bytes 4718592 | tf_op jit(solution)/shard_map/all_gather | solution.py:282
  81.1 24.4 %all-to-all-start.2 = ((bf16[128,32,128]{2,1,0:T(8,128)(2,1)}), bf16[128,32,128]{2,1,0:T(8,128)(2,1)S(1)}, u32[]{:S(2)}, u32[]{:S(2)}) async-start(bf16[128,32,128]{2,1,0:T(8,128)(2,1)} %bitcast.12), calls=%async_computation.2 | async-start | bytes 2097152 | tf_op jit(solution)/shard_map/all_to_all | solution.py:310
  105.5 1.0 copy-start.3
  118.5 14.2 %copy-start.7 = (f32[16]{0:T(128)S(1)}, f32[16]{0:T(128)}, u32[]{:S(2)}) copy-start(f32[16]{0:T(128)} %param.13) | copy-start | bytes 196
  118.5 35.0 %all-to-all-start.3 = ((bf16[128,16,512]{2,1,0:T(8,128)(2,1)}), bf16[128,16,512]{2,1,0:T(8,128)(2,1)S(1)}, u32[]{:S(2)}, u32[]{:S(2)}) async-start(bf16[128,16,512]{2,1,0:T(8,128)(2,1)} %bitcast.55), calls=%async_computation.3 | async-start | bytes 4194304 | tf_op jit(solution)/shard_map/all_to_all | solution.py:317
  131.3 39.3 %collective-permute-start.4 = (bf16[256,1024]{1,0:T(8,128)(2,1)}, bf16[256,1024]{1,0:T(8,128)(2,1)S(1)}, u32[]{:S(2)}, u32[]{:S(2)}) collective-permute-start(bf16[256,1024]{1,0:T(8,128)(2,1)} %get-tuple-element.20), channel_id=1, source_target_pairs={{0,1},{1,0},{2,3},{3,2},{4,5},{5,4},{6,7},{7,6},{8,9},{9,8},{10,11... | collective-permute-start | bytes 1572872 | tf_op jit(solution)/shard_map/ppermute | solution.py:322
  153.5 17.1 %copy-start = (bf16[128,16,512]{2,1,0:T(8,128)(2,1)}, bf16[128,16,512]{2,1,0:T(8,128)(2,1)S(1)}, u32[]{:S(2)}) copy-start(bf16[128,16,512]{2,1,0:T(8,128)(2,1)S(1)} %all-to-all-done.3) | copy-start | bytes 6291460
  170.6 0.8 copy-start.5
Sparse Core Ops, SparseCore 0:
  19.0 40.6 all-gather.5
  80.5 41.8 all-gather.9
  124.1 46.4 all-gather.7

commit v9 on v8

--- a/solution.py
+++ b/solution.py
@@ -293,19 +293,17 @@
 
     own = local.reshape(n_narrow, inner, states, width).swapaxes(1, 2)
     own = lax.all_to_all(own.reshape(n_narrow, height, width), "narrow", 0, 0, tiled=True)
-    mine = jnp.stack([stay, far])
-    theirs = lax.ppermute(mine, "wide", across_y)
+    own, stay = lax.optimization_barrier((own, stay))
+    half_ham = lax.all_gather(stay, "wide", axis=0, tiled=False)[:, None]
+    theirs = lax.ppermute(far, "wide", across_y)
     mate = lax.ppermute(own, "narrow", narrow_pairs)
     by_state = lax.all_to_all(jnp.swapaxes(local, 0, 1), "wide", 0, 0, tiled=True)
 
     turned = lax.optimization_barrier(grid_one.T)
     values = forward_pass(own, mate, near, states, piece)
     values, by_state, turned = lax.optimization_barrier((values, by_state, turned))
-    by_state, theirs, mine = lax.optimization_barrier((by_state, theirs, mine))
-    joined = both_sides(mine, theirs)
-    stay, far = joined[:, 0], joined[:, 1]
-    half_ham = gather(stay)
-    far = gather(far)
+    by_state, theirs = lax.optimization_barrier((by_state, theirs))
+    far = gather(both_sides(far, theirs))
     across = dot_f32(ham_one, by_state.reshape(n_one, width), NN).astype(jnp.bfloat16)
     values = lax.all_to_all(
         values.reshape(n_wide * n_narrow, 2 * inner, width // 2), both, 0, 0, tiled=True

time: 188 us -> 189 us (level)
  local copies, waits for them, and re-layouts: 25.5 us -> 22.5 us
  starting transfers between devices: 34 us -> 36.7 us
    ppermute x1, waiting for transfers between devices: 0.01 us -> 25.7 us  [on_device(): moved = lax.ppermute(moved, 'narrow', narrow_pairs)]
    all_to_all x1, waiting for transfers between devices: 19.2 us -> 0.01 us  [on_device(): lax.all_to_all(pair.reshape(n_wide * n_narrow, inner, 2 * width), both, 0...]
    all_gather x3 -> x2, waiting for transfers between devices: 17.1 us -> 10.6 us  [gather(): lax.all_gather(value, 'wide', axis=0, tiled=False, axis_index_groups=memb...]
    select_n x2, other arithmetic: 1.11 us -> 3.23 us  [both_sides(): jnp.where(side == 0, jnp.stack([mine, theirs]), jnp.stack([theirs, mine]))]
    ppermute x1, waiting for transfers between devices: 1.98 us -> 0.01 us  [on_device(): theirs = lax.ppermute(far, 'wide', across_y)]
    unnamed x18 -> x22, local copies, waits for them, and re-layouts: 16.4 us -> 15.6 us
where the time goes in v9:
time: 189 us; the launch traced here: 188 us
  waiting for transfers between devices  68.4 us (36%)
  starting transfers between devices  36.7 us (19%)
  Pallas kernels  34.3 us (18%)
  local copies, waits for them, and re-layouts  22.5 us (12%)
  between operations  13.3 us (7%)
  matrix products  6.78 us (4%)
  other arithmetic  5.86 us (3%)
    ppermute x1, waiting for transfers between devices, on_device(): moved = lax.ppermute(moved, 'narrow', narrow_pairs)  25.7 us
    unnamed x22, local copies, waits for them, and re-layouts  15.6 us
    all_to_all x1, waiting for transfers between devices, on_device(): lax.all_to_all(own.reshape(n_narrow, height, width), 'narrow', 0, 0, tile...  13.4 us
    pallas_call x1, Pallas kernels, middle_pass(): pl.pallas_call(middle_step, grid=(2 * half,), in_specs=[pl.BlockSpec(valu...  11.8 us
    all_gather x2, waiting for transfers between devices, gather(): lax.all_gather(value, 'wide', axis=0, tiled=False, axis_index_groups=memb...  10.6 us
    pallas_call x1, Pallas kernels, final_pass(): pl.pallas_call(final_step, grid_spec=pltpu.PrefetchScalarGridSpec(num_sca...  9.26 us
    all_to_all x1, waiting for transfers between devices, on_device(): lax.all_to_all(values.reshape(n_wide * n_narrow, 2 * inner, width // 2),...  8.8 us
    all_to_all x1, starting transfers between devices, on_device(): lax.all_to_all(values.reshape(n_wide * n_narrow, 2 * inner, width // 2),...  8.46 us
  transfers between devices with their start and end apart: 12, of which 7 were waited for; matrix products, arithmetic and copies ran while one was open for 16% of the time, Pallas kernels for 13%

profile of v9, /device:TPU:1, one launch (start us, length us, event | category | flops | bytes accessed | tf_op | source)
XLA Modules:
  0.0 187.7 jit_solution(8049676841023143385)
XLA Ops:
  6.5 1.0 convert_bitcast_fusion
  7.6 1.8 dynamic-slice_bitcast_fusion.2
  9.4 0.1 fusion.6
  9.5 2.2 %collective-permute-start.2 = (bf16[80,2048]{1,0:T(8,128)(2,1)S(1)}, bf16[80,2048]{1,0:T(8,128)(2,1)S(1)}, u32[]{:S(2)}, u32[]{:S(2)}) collective-permute-start(bf16[80,2048]{1,0:T(8,128)(2,1)S(1)} %get-tuple-element.27), channel_id=1, source_target_pairs={{0,64},{8,72},{16,80},{24,88},{32,96},{40,104},{48,112},{56,120},{... | collective-permute-start | bytes 983048 | tf_op jit(solution)/shard_map/ppermute | solution.py:287
  11.7 7.0 %collective-permute-done.2 = bf16[80,2048]{1,0:T(8,128)(2,1)S(1)} collective-permute-done((bf16[80,2048]{1,0:T(8,128)(2,1)S(1)}, bf16[80,2048]{1,0:T(8,128)(2,1)S(1)}, u32[]{:S(2)}, u32[]{:S(2)}) %collective-permute-start.2) | collective-permute-done | bytes 327712 | tf_op jit(solution)/shard_map/ppermute | solution.py:287
  18.7 0.9 maximum_select_fusion
  19.6 0.0 all-gather.5.cloned.1.call-update
  19.7 1.3 copy.31
  21.0 6.9 %all-to-all-start = ((bf16[8,256,256]{2,1,0:T(8,128)(2,1)}), bf16[8,256,256]{2,1,0:T(8,128)(2,1)S(1)}, u32[]{:S(2)}, u32[]{:S(2)}) async-start(bf16[8,256,256]{2,1,0:T(8,128)(2,1)} %bitcast.3), calls=%async_computation | async-start | bytes 2097152 | tf_op jit(solution)/shard_map/all_to_all | solution.py:295
  27.9 0.0 all-gather.9.cloned.1.call-start
  28.0 1.9 %collective-permute-start = (bf16[64,2048]{1,0:T(8,128)(2,1)S(1)}, bf16[64,2048]{1,0:T(8,128)(2,1)S(1)}, u32[]{:S(2)}, u32[]{:S(2)}) collective-permute-start(bf16[64,2048]{1,0:T(8,128)(2,1)S(1)} %constant_dynamic-slice_fusion), channel_id=1, source_target_pairs={{0,8},{8,0},{16,24},{24,16},{32,40},{40,32},{48,56},{56,48},{64,72... | collective-permute-start | bytes 786440 | tf_op jit(solution)/shard_map/ppermute | solution.py:292
  29.9 1.2 collective-permute-done
  31.1 0.8 dynamic-slice_select_fusion
  31.9 13.4 %all-to-all-done.own_ref = bf16[8,256,256]{2,1,0:T(8,128)(2,1)S(1)} async-done(((bf16[8,256,256]{2,1,0:T(8,128)(2,1)}), bf16[8,256,256]{2,1,0:T(8,128)(2,1)S(1)}, u32[]{:S(2)}, u32[]{:S(2)}) %all-to-all-start) | async-done | bytes 1048608 | tf_op jit(solution)/shard_map/all_to_all | solution.py:295
  45.2 0.0 all-gather.9.cloned.1.call-update
  45.3 0.1 collective-permute-start.1
  45.4 1.3 copy.44
  46.7 7.1 %all-to-all-start.1 = ((bf16[16,128,256]{2,1,0:T(8,128)(2,1)}), bf16[16,128,256]{2,1,0:T(8,128)(2,1)S(1)}, u32[]{:S(2)}, u32[]{:S(2)}) async-start(bf16[16,128,256]{2,1,0:T(8,128)(2,1)} %bitcast.45), calls=%async_computation.1 | async-start | bytes 2097152 | tf_op jit(solution)/shard_map/all_to_all | solution.py:300
  53.8 0.0 all-gather.7.cloned.1.call-start
  53.8 1.5 collective-permute-start.3
  55.3 12.4 %copy.34 = bf16[2048,2048]{0,1:T(8,128)(2,1)} copy(bf16[2048,2048]{1,0:T(8,128)(2,1)} %grid_ref.1) | data formatting | bytes 16777216 | tf_op args[2]
  67.7 1.6 collective-permute-done.1.mate_ref
  69.3 1.0 copy-done.4
  70.2 6.6 %forward_pass.1 = bf16[16,8,2,16,128]{4,3,2,1,0:T(8,128)(2,1)} custom-call(bf16[8,256,256]{2,1,0:T(8,128)(2,1)} %copy-done.1, bf16[8,256,256]{2,1,0:T(8,128)(2,1)} %copy-done.4, bf16[8,2,80,2048]{3,2,1,0:T(8,128)(2,1)} %all-gather.5.cloned.1.call-done.a0_ref.a1_ref.b0_ref.b1_ref.near_a0.near_a1.near_b0.near_b1, ...), custom_call_target="tpu_custom_call" | custom-call | flops 2147483648 | bytes 8388608 | tf_op jit(solution)/shard_map/forward_pass/pallas_call | solution.py:71
  76.9 0.0 all-to-all-done.1
  76.9 0.0 collective-permute-done.3
  76.9 2.3 %maximum_select_fusion.1 = bf16[1,2,64,2048]{3,2,1,0:T(8,128)(2,1)} fusion(bf16[1,1,64,2048]{3,2,1,0:T(8,128)(2,1)} %bitcast.24, bf16[1,1,64,2048]{3,2,1,0:T(8,128)(2,1)S(1)} %get-tuple-element.23, pred[]{:T(512)S(6)} %eq.26), kind=kLoop, calls=%fused_computation.5 | loop fusion | flops 786432 | bytes 1048577 | tf_op jit(solution)/shard_map/jit(_where)/select_n | solution.py:279
  79.2 0.0 all-gather.7.cloned.1.call-update
  79.2 8.5 %all-to-all-start.2 = ((bf16[128,32,128]{2,1,0:T(8,128)(2,1)}), bf16[128,32,128]{2,1,0:T(8,128)(2,1)S(1)}, u32[]{:S(2)}, u32[]{:S(2)}) async-start(bf16[128,32,128]{2,1,0:T(8,128)(2,1)} %bitcast.51), calls=%async_computation.2 | async-start | bytes 2097152 | tf_op jit(solution)/shard_map/all_to_all | solution.py:308
  87.7 0.0 copy-start.6
  87.7 1.4 slice_bitcast_fusion
  89.1 0.1 copy.35
  89.2 1.3 copy.36
  90.5 6.8 %fusion.across_ref = bf16[2048,256]{1,0:T(8,128)(2,1)} fusion(bf16[2048,2048]{1,0:T(8,128)(2,1)} %param.8, bf16[2048,256]{1,0:T(8,128)(2,1)S(1)} %bitcast.56), kind=kOutput, calls=%fused_computation.1 | convolution fusion | flops 2148007936 | bytes 10485760 | tf_op jit(solution)/shard_map/dot_general | solution.py:14
  97.3 8.8 %all-to-all-done.2 = bf16[128,32,128]{2,1,0:T(8,128)(2,1)S(1)} async-done(((bf16[128,32,128]{2,1,0:T(8,128)(2,1)}), bf16[128,32,128]{2,1,0:T(8,128)(2,1)S(1)}, u32[]{:S(2)}, u32[]{:S(2)}) %all-to-all-start.2) | async-done | bytes 1048608 | tf_op jit(solution)/shard_map/all_to_all | solution.py:308
  106.1 1.0 copy-done.3
  107.1 11.8 %middle_pass.1 = bf16[2048,512]{1,0:T(8,128)(2,1)} custom-call(bf16[64,2,2,16,128]{4,3,2,1,0:T(8,128)(2,1)} %bitcast.54, bf16[2048,2048]{1,0:T(8,128)(2,1)} %grid_ref.1, bf16[2048,2048]{1,0:T(8,128)(2,1)} %bitcast.49, bf16[2048,256]{1,0:T(8,128)(2,1)} %bitcast.55, bf16[2048,256]{1,0:T(8,128)(2,1)} %fusion.across_ref), custom_call_target="tpu_custom_call" | custom-call | flops 4294967296 | bytes 22020096 | tf_op jit(solution)/shard_map/middle_pass/pallas_call | solution.py:121
  118.9 7.0 %all-to-all-start.3 = ((bf16[128,16,512]{2,1,0:T(8,128)(2,1)}), bf16[128,16,512]{2,1,0:T(8,128)(2,1)S(1)}, u32[]{:S(2)}, u32[]{:S(2)}) async-start(bf16[128,16,512]{2,1,0:T(8,128)(2,1)} %bitcast.50), calls=%async_computation.3 | async-start | bytes 4194304 | tf_op jit(solution)/shard_map/all_to_all | solution.py:315
  126.0 0.0 all-gather.9.cloned.1.call-done
  126.0 6.6 %applied_pass.1 = (f32[256,1024]{1,0:T(8,128)}, bf16[256,1024]{1,0:T(8,128)(2,1)}) custom-call(bf16[8,256,256]{2,1,0:T(8,128)(2,1)} %copy-done.1, bf16[8,256,256]{2,1,0:T(8,128)(2,1)} %copy-done.4, bf16[16,1,64,2048]{3,2,1,0:T(8,128)(2,1)} %bitcast.59), custom_call_target="tpu_custom_call" | custom-call | flops 2147483648 | bytes 8388608 | tf_op jit(solution)/shard_map/applied_pass/pallas_call | solution.py:161
  132.6 1.4 collective-permute-start.4
  134.0 0.1 broadcast_in_dim.16
  134.0 0.8 broadcast_in_dim_reshape.4.energy_ref
  134.8 0.8 fusion.1.swap_ref
  135.6 25.7 %collective-permute-done.4.moved_ref = bf16[256,1024]{1,0:T(8,128)(2,1)S(1)} collective-permute-done((bf16[256,1024]{1,0:T(8,128)(2,1)}, bf16[256,1024]{1,0:T(8,128)(2,1)S(1)}, u32[]{:S(2)}, u32[]{:S(2)}) %collective-permute-start.4) | collective-permute-done | bytes 524320 | tf_op jit(solution)/shard_map/ppermute | solution.py:320
  161.3 0.0 all-to-all-done.3
  161.3 10.6 %all-gather.7.cloned.1.call-done.far_a0.far_a1.far_b0.far_b1 = bf16[8,2,64,2048]{3,2,1,0:T(8,128)(2,1)} async-done(((bf16[1,2,64,2048]{3,2,1,0:T(8,128)(2,1)}), bf16[8,2,64,2048]{3,2,1,0:T(8,128)(2,1)}) %all-gather.7.cloned.1.call-update) | async-done | bytes 4194320 | tf_op jit(solution)/shard_map/all_gather | solution.py:282
  171.9 9.3 %final_pass.1 = bf16[16,16,2048]{2,1,0:T(8,128)(2,1)} custom-call(s32[1]{0:T(128)} %bitcast.half_ref, bf16[16,8,16,512]{3,2,1,0:T(8,128)(2,1)} %bitcast.46, bf16[16,8,16,512]{3,2,1,0:T(8,128)(2,1)} %bitcast.47, bf16[8,2,80,2048]{3,2,1,0:T(8,128)(2,1)} %all-gather.5.cloned.1.call-done.a0_ref.a1_ref.b0_ref.b1_ref.near_a0.near_a1.near_b0.near_b1, ...), custom_call_target="tpu_custom_call" | custom-call | flops 2415919104 | bytes 14680064 | tf_op jit(solution)/shard_map/final_pass/pallas_call | solution.py:225
  (21 shorter events, 0.1 us)
Async XLA Ops:
  6.5 13.1 %copy-start.2 = (bf16[1,128,16,256]{3,2,1,0:T(8,128)(2,1)S(1)}, bf16[1,128,16,256]{3,2,1,0:T(8,128)(2,1)}, u32[]{:S(2)}) copy-start(bf16[1,128,16,256]{3,2,1,0:T(8,128)(2,1)} %param.7) | copy-start | bytes 3145732
  6.5 21.5 %copy-start.8 = (bf16[128,2048]{1,0:T(8,128)(2,1)S(1)}, bf16[128,2048]{1,0:T(8,128)(2,1)}, u32[]{:S(2)}) copy-start(bf16[128,2048]{1,0:T(8,128)(2,1)} %param.10) | copy-start | bytes 1572868
  6.5 62.7 %all-gather.5.cloned.1.call-start = ((), (), s32[]{:S(2)}) async-start(), calls=%async_computation.4 | async-start | bytes 5898240 | tf_op jit(solution)/shard_map/all_gather | solution.py:282
  9.5 9.2 %collective-permute-start.2 = (bf16[80,2048]{1,0:T(8,128)(2,1)S(1)}, bf16[80,2048]{1,0:T(8,128)(2,1)S(1)}, u32[]{:S(2)}, u32[]{:S(2)}) collective-permute-start(bf16[80,2048]{1,0:T(8,128)(2,1)S(1)} %get-tuple-element.27), channel_id=1, source_target_pairs={{0,64},{8,72},{16,80},{24,88},{32,96},{40,104},{48,112},{56,120},{... | collective-permute-start | bytes 983048 | tf_op jit(solution)/shard_map/ppermute | solution.py:287
  21.0 24.2 %all-to-all-start = ((bf16[8,256,256]{2,1,0:T(8,128)(2,1)}), bf16[8,256,256]{2,1,0:T(8,128)(2,1)S(1)}, u32[]{:S(2)}, u32[]{:S(2)}) async-start(bf16[8,256,256]{2,1,0:T(8,128)(2,1)} %bitcast.3), calls=%async_computation | async-start | bytes 2097152 | tf_op jit(solution)/shard_map/all_to_all | solution.py:295
  27.9 98.1 %all-gather.9.cloned.1.call-start = ((), (), s32[]{:S(2)}) async-start(), calls=%async_computation.6 | async-start | bytes 4456448 | tf_op jit(solution)/shard_map/all_gather | solution.py:297
  28.0 3.1 %collective-permute-start = (bf16[64,2048]{1,0:T(8,128)(2,1)S(1)}, bf16[64,2048]{1,0:T(8,128)(2,1)S(1)}, u32[]{:S(2)}, u32[]{:S(2)}) collective-permute-start(bf16[64,2048]{1,0:T(8,128)(2,1)S(1)} %constant_dynamic-slice_fusion), channel_id=1, source_target_pairs={{0,8},{8,0},{16,24},{24,16},{32,40},{40,32},{48,56},{56,48},{64,72... | collective-permute-start | bytes 786440 | tf_op jit(solution)/shard_map/ppermute | solution.py:292
  45.2 22.4 %copy-start.1 = (bf16[8,256,256]{2,1,0:T(8,128)(2,1)}, bf16[8,256,256]{2,1,0:T(8,128)(2,1)S(1)}, u32[]{:S(2)}) copy-start(bf16[8,256,256]{2,1,0:T(8,128)(2,1)S(1)} %all-to-all-done.own_ref) | copy-start | bytes 3145732
  45.3 24.0 %collective-permute-start.1 = (bf16[8,256,256]{2,1,0:T(8,128)(2,1)S(1)}, bf16[8,256,256]{2,1,0:T(8,128)(2,1)S(1)}, u32[]{:S(2)}, u32[]{:S(2)}) collective-permute-start(bf16[8,256,256]{2,1,0:T(8,128)(2,1)S(1)} %all-to-all-done.own_ref), channel_id=1, source_target_pairs={{0,1},{1,0},{2,3},{3,2},{4,5},{5,4},{6,7},{7,6},{8,9},{9,8},{10,11... | collective-permute-start | bytes 3145736 | tf_op jit(solution)/shard_map/ppermute | solution.py:299
  46.7 30.2 %all-to-all-start.1 = ((bf16[16,128,256]{2,1,0:T(8,128)(2,1)}), bf16[16,128,256]{2,1,0:T(8,128)(2,1)S(1)}, u32[]{:S(2)}, u32[]{:S(2)}) async-start(bf16[16,128,256]{2,1,0:T(8,128)(2,1)} %bitcast.45), calls=%async_computation.1 | async-start | bytes 2097152 | tf_op jit(solution)/shard_map/all_to_all | solution.py:300
  53.8 118.1 %all-gather.7.cloned.1.call-start = ((), (), s32[]{:S(2)}) async-start(), calls=%async_computation.5 | async-start | bytes 4718592 | tf_op jit(solution)/shard_map/all_gather | solution.py:282
  53.8 23.0 %collective-permute-start.3 = (bf16[64,2048]{1,0:T(8,128)(2,1)}, bf16[64,2048]{1,0:T(8,128)(2,1)}, u32[]{:S(2)}, u32[]{:S(2)}) collective-permute-start(bf16[64,2048]{1,0:T(8,128)(2,1)} %get-tuple-element.24), channel_id=1, source_target_pairs={{0,64},{8,72},{16,80},{24,88},{32,96},{40,104},{48,112},{56,120},{... | collective-permute-start | bytes 786440 | tf_op jit(solution)/shard_map/ppermute | solution.py:298
  69.3 1.0 copy-start.4
  76.9 2.3 %copy-start.5 = (bf16[16,128,256]{2,1,0:T(8,128)(2,1)}, bf16[16,128,256]{2,1,0:T(8,128)(2,1)S(1)}, u32[]{:S(2)}) copy-start(bf16[16,128,256]{2,1,0:T(8,128)(2,1)S(1)} %all-to-all-done.1) | copy-start | bytes 3145732
  79.2 26.9 %all-to-all-start.2 = ((bf16[128,32,128]{2,1,0:T(8,128)(2,1)}), bf16[128,32,128]{2,1,0:T(8,128)(2,1)S(1)}, u32[]{:S(2)}, u32[]{:S(2)}) async-start(bf16[128,32,128]{2,1,0:T(8,128)(2,1)} %bitcast.51), calls=%async_computation.2 | async-start | bytes 2097152 | tf_op jit(solution)/shard_map/all_to_all | solution.py:308
  87.7 2.8 %copy-start.6 = (bf16[16,128,256]{2,1,0:T(8,128)(2,1)S(1)}, bf16[16,128,256]{2,1,0:T(8,128)(2,1)}, u32[]{:S(2)}) copy-start(bf16[16,128,256]{2,1,0:T(8,128)(2,1)} %copy-done.5) | copy-start | bytes 3145732
  106.1 1.0 copy-start.3
  118.9 15.0 %copy-start.9 = (f32[16]{0:T(128)S(1)}, f32[16]{0:T(128)}, u32[]{:S(2)}) copy-start(f32[16]{0:T(128)} %param.13) | copy-start | bytes 196
  118.9 42.4 %all-to-all-start.3 = ((bf16[128,16,512]{2,1,0:T(8,128)(2,1)}), bf16[128,16,512]{2,1,0:T(8,128)(2,1)S(1)}, u32[]{:S(2)}, u32[]{:S(2)}) async-start(bf16[128,16,512]{2,1,0:T(8,128)(2,1)} %bitcast.50), calls=%async_computation.3 | async-start | bytes 4194304 | tf_op jit(solution)/shard_map/all_to_all | solution.py:315
  132.6 28.7 %collective-permute-start.4 = (bf16[256,1024]{1,0:T(8,128)(2,1)}, bf16[256,1024]{1,0:T(8,128)(2,1)S(1)}, u32[]{:S(2)}, u32[]{:S(2)}) collective-permute-start(bf16[256,1024]{1,0:T(8,128)(2,1)} %get-tuple-element.22), channel_id=1, source_target_pairs={{0,1},{1,0},{2,3},{3,2},{4,5},{5,4},{6,7},{7,6},{8,9},{9,8},{10,11... | collective-permute-start | bytes 1572872 | tf_op jit(solution)/shard_map/ppermute | solution.py:320
  161.3 10.6 %copy-start.7 = (bf16[256,1024]{1,0:T(8,128)(2,1)}, bf16[256,1024]{1,0:T(8,128)(2,1)S(1)}, u32[]{:S(2)}) copy-start(bf16[256,1024]{1,0:T(8,128)(2,1)S(1)} %collective-permute-done.4.moved_ref) | copy-start | bytes 1572868
  161.3 10.6 %copy-start = (bf16[128,16,512]{2,1,0:T(8,128)(2,1)}, bf16[128,16,512]{2,1,0:T(8,128)(2,1)S(1)}, u32[]{:S(2)}) copy-start(bf16[128,16,512]{2,1,0:T(8,128)(2,1)S(1)} %all-to-all-done.3) | copy-start | bytes 6291460
Sparse Core Ops, SparseCore 0:
  19.8 44.3 all-gather.4
  65.9 55.0 all-gather.8
  122.7 49.1 all-gather.6

commit v10 on v7

--- a/solution.py
+++ b/solution.py
@@ -16,8 +16,8 @@
     )
 
 
-def params():
-    return pltpu.CompilerParams(vmem_limit_bytes=56 * MIB)
+def params(mib):
+    return pltpu.CompilerParams(vmem_limit_bytes=mib * MIB)
 
 
 def cost(flops, moved):
@@ -79,7 +79,7 @@
         out_specs=pl.BlockSpec((states, 2, 2, inner, points), lambda s: (0, s, 0, 0, 0)),
         out_shape=jax.ShapeDtypeStruct((states, n_narrow, 2, inner, points), jnp.bfloat16),
         scratch_shapes=[pltpu.VMEM((2 * height, cols), jnp.bfloat16)],
-        compiler_params=params(),
+        compiler_params=params(50),
         cost_estimate=cost(4 * height * cols * points * n_narrow, 8 * MIB),
         name="forward_pass",
     )(own, mate, gathered, gathered, gathered, gathered)
@@ -134,7 +134,7 @@
             pltpu.VMEM((groups, 2, inner, 2 * points), jnp.bfloat16),
             pltpu.VMEM((n_one, width), jnp.bfloat16),
         ],
-        compiler_params=params(),
+        compiler_params=params(52),
         cost_estimate=cost(4 * n_one * n_one * width, 21 * MIB),
         name="middle_pass",
     )(values, grid_one, turned, potential, across)
@@ -172,7 +172,7 @@
             jax.ShapeDtypeStruct((height, points), jnp.bfloat16),
         ],
         scratch_shapes=[pltpu.VMEM((2 * height, cols), jnp.bfloat16)],
-        compiler_params=params(),
+        compiler_params=params(50),
         cost_estimate=cost(4 * height * cols * points, 8 * MIB),
         name="applied_pass",
     )(own, mate, gathered)
@@ -207,7 +207,13 @@
             cols = slice(block * width, (block + 1) * width)
             kept = kept_ref[:, block * part : (block + 1) * part]
             moved = moved_ref[:, block * part : (block + 1) * part].astype(jnp.float32)
-            applied = [jnp.where(even, kept, moved), jnp.where(even, moved, kept)]
+            low = jnp.where(even, kept, moved)
+            high = jnp.where(even, moved, kept)
+            left = lax.broadcasted_iota(jnp.int32, low.shape, 1) < part // 2
+            applied = [
+                jnp.where(left, low, pltpu.roll(high, part // 2, 1)),
+                jnp.where(left, pltpu.roll(low, part // 2, 1), high),
+            ]
             value = acc_ref[:, cols] + jnp.concatenate(applied, 1)
             value += across_ref[:, block].reshape(height, width).astype(jnp.float32)
             value += energy_ref[...] * own_ref[block].astype(jnp.float32)
@@ -243,7 +249,7 @@
             scratch_shapes=[pltpu.VMEM((height, cols), jnp.float32)],
         ),
         out_shape=jax.ShapeDtypeStruct((rows, states, cols), jnp.bfloat16),
-        compiler_params=params(),
+        compiler_params=params(50),
         cost_estimate=cost(2 * height * cols * (cols + height), 14 * MIB),
         name="final_pass",
     )(
@@ -256,9 +262,7 @@
     n_narrow = lax.axis_size("narrow")
     both = ("wide", "narrow")
     half = lax.axis_index("narrow") % 2
-    core = lax.axis_index("wide") % 2
     narrow_pairs = [(n, n ^ 1) for n in range(n_narrow)]
-    wide_pairs = [(w, w ^ 1) for w in range(n_wide)]
 
     local = coeffs[0]
     rows, states, width = local.shape
@@ -287,9 +291,7 @@
     near = gather(both_sides(near, lax.ppermute(near, "wide", across_y)))
 
     far = lax.dynamic_index_in_dim(pieces, 1 - half, 1, False).reshape(share, cols)
-    away = lax.dynamic_slice_in_dim(ham_two, (1 - core) * share, share, 0)
-    stay = lax.dynamic_slice_in_dim(ham_two, core * share, share, 0)
-    stay = jnp.where(core == half, stay, lax.ppermute(away, "wide", wide_pairs))
+    stay = lax.dynamic_slice_in_dim(ham_two, half * share, share, 0)
 
     own = local.reshape(n_narrow, inner, states, width).swapaxes(1, 2)
     own = lax.all_to_all(own.reshape(n_narrow, height, width), "narrow", 0, 0, tiled=True)
@@ -302,10 +304,10 @@
     far = gather(far)
     mate = lax.ppermute(own, "narrow", narrow_pairs)
     by_state = lax.all_to_all(jnp.swapaxes(local, 0, 1), "wide", 0, 0, tiled=True)
+
     turned = lax.optimization_barrier(grid_one.T)
-    own, mate, by_state, turned = lax.optimization_barrier((own, mate, by_state, turned))
-
     values = forward_pass(own, mate, near, states, piece)
+    values, by_state, turned = lax.optimization_barrier((values, by_state, turned))
     across = dot_f32(ham_one, by_state.reshape(n_one, width), NN).astype(jnp.bfloat16)
     values = lax.all_to_all(
         values.reshape(n_wide * n_narrow, 2 * inner, width // 2), both, 0, 0, tiled=True

time: 190 us -> 184 us (0.968)
  waiting for transfers between devices: 69.1 us -> 61.5 us
  starting transfers between devices: 37.2 us -> 40.5 us
  Pallas kernels: 34.4 us -> 32.4 us
    all_to_all x1, waiting for transfers between devices: 4.49 us -> 0.01 us  [on_device(): lax.all_to_all(jnp.swapaxes(local, 0, 1), 'wide', 0, 0, tiled=True)]
    all_to_all x1, starting transfers between devices: 9.61 us -> 12.5 us  [on_device(): lax.all_to_all(values.reshape(n_wide * n_narrow, 2 * inner, width // 2),...]
    unnamed x20 -> x10, local copies, waits for them, and re-layouts: 17.2 us -> 16.2 us
  transfers between devices with their start and end apart: 12 -> 11, of which waited for: 5 -> 4; matrix products, arithmetic and copies ran while one was open for 15% -> 17% of each run, Pallas kernels for 13% -> 13%
where the time goes in v10:
time: 184 us; the launch traced here: 183 us
  waiting for transfers between devices  61.5 us (33%)
  starting transfers between devices  40.5 us (22%)
  Pallas kernels  32.4 us (18%)
  local copies, waits for them, and re-layouts  25.7 us (14%)
  between operations  13.2 us (7%)
  matrix products  6.97 us (4%)
  other arithmetic  2.38 us (1%)
    ppermute x1, waiting for transfers between devices, on_device(): moved = lax.ppermute(moved, 'narrow', narrow_pairs)  26 us
    ppermute x1, waiting for transfers between devices, on_device(): theirs = lax.ppermute(mine, 'wide', across_y)  21.7 us
    unnamed x10, local copies, waits for them, and re-layouts  16.2 us
    all_to_all x1, starting transfers between devices, on_device(): lax.all_to_all(values.reshape(n_wide * n_narrow, 2 * inner, width // 2),...  12.5 us
    pallas_call x1, Pallas kernels, middle_pass(): pl.pallas_call(middle_step, grid=(2 * half,), in_specs=[pl.BlockSpec(valu...  11.5 us
    all_to_all x1, starting transfers between devices, on_device(): lax.all_to_all(jnp.swapaxes(local, 0, 1), 'wide', 0, 0, tiled=True)  9.03 us
    pallas_call x1, Pallas kernels, final_pass(): pl.pallas_call(final_step, grid_spec=pltpu.PrefetchScalarGridSpec(num_sca...  8.9 us
    ppermute x1, waiting for transfers between devices, on_device(): near = gather(both_sides(near, lax.ppermute(near, 'wide', across_y)))  7.02 us
  transfers between devices with their start and end apart: 11, of which 4 were waited for; matrix products, arithmetic and copies ran while one was open for 17% of the time, Pallas kernels for 13%

profile of v10, /device:TPU:1, one launch (start us, length us, event | category | flops | bytes accessed | tf_op | source)
XLA Modules:
  0.0 182.7 jit_solution(351053758981712875)
XLA Ops:
  6.5 0.0 copy-start
  6.5 1.0 convert_bitcast_fusion
  7.5 1.1 dynamic-slice_bitcast_fusion
  8.6 0.1 fusion.6
  8.6 2.2 %collective-permute-start.2 = (bf16[80,2048]{1,0:T(8,128)(2,1)S(1)}, bf16[80,2048]{1,0:T(8,128)(2,1)S(1)}, u32[]{:S(2)}, u32[]{:S(2)}) collective-permute-start(bf16[80,2048]{1,0:T(8,128)(2,1)S(1)} %get-tuple-element.26), channel_id=1, source_target_pairs={{0,64},{8,72},{16,80},{24,88},{32,96},{40,104},{48,112},{56,120},{... | collective-permute-start | bytes 983048 | tf_op jit(solution)/shard_map/ppermute | solution.py:291
  10.9 7.0 %collective-permute-done.2 = bf16[80,2048]{1,0:T(8,128)(2,1)S(1)} collective-permute-done((bf16[80,2048]{1,0:T(8,128)(2,1)S(1)}, bf16[80,2048]{1,0:T(8,128)(2,1)S(1)}, u32[]{:S(2)}, u32[]{:S(2)}) %collective-permute-start.2) | collective-permute-done | bytes 327712 | tf_op jit(solution)/shard_map/ppermute | solution.py:291
  17.9 1.0 maximum_select_fusion.1
  18.9 0.0 all-gather.6.cloned.1.call-update
  18.9 2.6 %copy.29 = bf16[8,16,16,256]{3,1,2,0:T(8,128)(2,1)} copy(bf16[8,16,16,256]{3,2,1,0:T(8,128)(2,1)} %bitcast.54) | data formatting | bytes 2097152 | tf_op jit(solution)/shard_map/reshape;squeeze | solution.py:296
  21.5 6.9 %all-to-all-start = ((bf16[8,256,256]{2,1,0:T(8,128)(2,1)}), bf16[8,256,256]{2,1,0:T(8,128)(2,1)S(1)}, u32[]{:S(2)}, u32[]{:S(2)}) async-start(bf16[8,256,256]{2,1,0:T(8,128)(2,1)} %bitcast.3), calls=%async_computation | async-start | bytes 2097152 | tf_op jit(solution)/shard_map/all_to_all | solution.py:297
  28.4 0.0 all-gather.10.cloned.1.call-start
  28.5 0.1 pad_maximum_fusion
  28.6 0.5 collective-permute-start
  29.0 21.7 %collective-permute-done = bf16[2,64,2048]{2,1,0:T(8,128)(2,1)S(1)} collective-permute-done((bf16[2,64,2048]{2,1,0:T(8,128)(2,1)S(1)}, bf16[2,64,2048]{2,1,0:T(8,128)(2,1)S(1)}, u32[]{:S(2)}, u32[]{:S(2)}) %collective-permute-start) | collective-permute-done | bytes 524320 | tf_op jit(solution)/shard_map/ppermute | solution.py:299
  50.8 0.0 all-to-all-done.own_ref
  50.8 0.2 maximum_select_fusion
  50.9 1.0 fusion.7
  52.0 0.0 all-gather.10.cloned.1.call-update
  52.0 0.0 all-gather.8.cloned.1.call-start
  52.1 0.7 all-gather.8.cloned.1.call-update
  52.8 1.3 collective-permute-start.1
  54.0 2.5 %copy.42 = bf16[1,128,16,256]{3,1,2,0:T(8,128)(2,1)} copy(bf16[1,128,16,256]{3,2,1,0:T(8,128)(2,1)} %param.7) | data formatting | bytes 2097152 | tf_op args[0]
  56.5 9.0 %all-to-all-start.1 = ((bf16[16,128,256]{2,1,0:T(8,128)(2,1)}), bf16[16,128,256]{2,1,0:T(8,128)(2,1)}, u32[]{:S(2)}, u32[]{:S(2)}) async-start(bf16[16,128,256]{2,1,0:T(8,128)(2,1)} %bitcast.55), calls=%async_computation.1 | async-start | bytes 2097152 | tf_op jit(solution)/shard_map/all_to_all | solution.py:306
  65.6 12.4 %copy.33 = bf16[2048,2048]{0,1:T(8,128)(2,1)} copy(bf16[2048,2048]{1,0:T(8,128)(2,1)} %grid_ref.1) | data formatting | bytes 16777216 | tf_op args[2]
  78.0 0.0 collective-permute-done.1.mate_ref
  78.0 0.0 all-gather.6.cloned.1.call-done.a0_ref.a1_ref.b0_ref.b1_ref.near_a0.near_a1.near_b0.near_b1
  78.0 6.2 %forward_pass.1 = bf16[16,8,2,16,128]{4,3,2,1,0:T(8,128)(2,1)} custom-call(bf16[8,256,256]{2,1,0:T(8,128)(2,1)S(1)} %all-to-all-done.own_ref, bf16[8,256,256]{2,1,0:T(8,128)(2,1)S(1)} %collective-permute-done.1.mate_ref, bf16[8,2,80,2048]{3,2,1,0:T(8,128)(2,1)} %all-gather.6.cloned.1.call-done.a0_ref.a1_ref.b0_ref.b1_ref.near_a0.near_a1.near_b0.near_b1, ...), custom_call_target="tpu_custom_call" | custom-call | flops 2147483648 | bytes 8388608 | tf_op jit(solution)/shard_map/forward_pass/pallas_call | solution.py:71
  84.2 0.0 all-to-all-done.1
  84.2 12.5 %all-to-all-start.2 = ((bf16[128,32,128]{2,1,0:T(8,128)(2,1)}), bf16[128,32,128]{2,1,0:T(8,128)(2,1)S(1)}, u32[]{:S(2)}, u32[]{:S(2)}) async-start(bf16[128,32,128]{2,1,0:T(8,128)(2,1)} %bitcast.14), calls=%async_computation.2 | async-start | bytes 2097152 | tf_op jit(solution)/shard_map/all_to_all | solution.py:312
  96.8 1.3 slice_bitcast_fusion
  98.1 1.0 copy.34
  99.1 2.3 %copy.35 = bf16[256,2048]{0,1:T(8,128)(2,1)} copy(bf16[256,2048]{1,0:T(8,128)(2,1)} %bitcast.56) | data formatting | bytes 2097152 | tf_op jit(solution)/shard_map/reshape | solution.py:317
  101.4 7.0 %fusion.across_ref = bf16[2048,256]{1,0:T(8,128)(2,1)} fusion(bf16[2048,2048]{1,0:T(8,128)(2,1)} %param.8, bf16[2048,256]{1,0:T(8,128)(2,1)} %bitcast.20), kind=kOutput, calls=%fused_computation.1 | convolution fusion | flops 2148007936 | bytes 10485760 | tf_op jit(solution)/shard_map/dot_general | solution.py:14
  108.4 6.0 %all-to-all-done.2 = bf16[128,32,128]{2,1,0:T(8,128)(2,1)S(1)} async-done(((bf16[128,32,128]{2,1,0:T(8,128)(2,1)}), bf16[128,32,128]{2,1,0:T(8,128)(2,1)S(1)}, u32[]{:S(2)}, u32[]{:S(2)}) %all-to-all-start.2) | async-done | bytes 1048608 | tf_op jit(solution)/shard_map/all_to_all | solution.py:312
  114.4 11.5 %middle_pass.1 = bf16[2048,512]{1,0:T(8,128)(2,1)} custom-call(bf16[64,2,2,16,128]{4,3,2,1,0:T(8,128)(2,1)S(1)} %bitcast.47, bf16[2048,2048]{1,0:T(8,128)(2,1)} %grid_ref.1, bf16[2048,2048]{1,0:T(8,128)(2,1)} %bitcast.52, bf16[2048,256]{1,0:T(8,128)(2,1)} %bitcast.57, bf16[2048,256]{1,0:T(8,128)(2,1)} %fusion.across_ref), custom_call_target="tpu_custom_call" | custom-call | flops 4294967296 | bytes 22020096 | tf_op jit(solution)/shard_map/middle_pass/pallas_call | solution.py:121
  125.9 6.6 %all-to-all-start.3 = ((bf16[128,16,512]{2,1,0:T(8,128)(2,1)}), bf16[128,16,512]{2,1,0:T(8,128)(2,1)}, u32[]{:S(2)}, u32[]{:S(2)}) async-start(bf16[128,16,512]{2,1,0:T(8,128)(2,1)} %bitcast.53), calls=%async_computation.3 | async-start | bytes 4194304 | tf_op jit(solution)/shard_map/all_to_all | solution.py:319
  132.5 0.0 all-gather.10.cloned.1.call-done
  132.5 0.0 copy-start.2
  132.5 1.2 copy-done.2
  133.8 5.8 %applied_pass.1 = (f32[256,1024]{1,0:T(8,128)S(1)}, bf16[256,1024]{1,0:T(8,128)(2,1)}) custom-call(bf16[8,256,256]{2,1,0:T(8,128)(2,1)S(1)} %all-to-all-done.own_ref, bf16[8,256,256]{2,1,0:T(8,128)(2,1)S(1)} %copy-done.2, bf16[8,2,64,2048]{3,2,1,0:T(8,128)(2,1)} %bitcast.62), custom_call_target="tpu_custom_call" | custom-call | flops 2147483648 | bytes 8388608 | tf_op jit(solution)/shard_map/applied_pass/pallas_call | solution.py:161
  139.5 1.4 collective-permute-start.3
  140.9 0.1 broadcast_in_dim.12
  141.0 0.1 broadcast_in_dim_reshape.4.energy_ref
  141.1 0.1 fusion.1.swap_ref
  141.2 0.0 all-gather.8.cloned.1.call-done
  141.3 26.0 %collective-permute-done.3.moved_ref = bf16[256,1024]{1,0:T(8,128)(2,1)S(1)} collective-permute-done((bf16[256,1024]{1,0:T(8,128)(2,1)}, bf16[256,1024]{1,0:T(8,128)(2,1)S(1)}, u32[]{:S(2)}, u32[]{:S(2)}) %collective-permute-start.3) | collective-permute-done | bytes 524320 | tf_op jit(solution)/shard_map/ppermute | solution.py:324
  167.2 0.0 all-to-all-done.3
  167.2 8.9 %final_pass.1 = bf16[16,16,2048]{2,1,0:T(8,128)(2,1)} custom-call(s32[1]{0:T(128)} %bitcast.half_ref, bf16[16,8,16,512]{3,2,1,0:T(8,128)(2,1)} %bitcast.23.near_ref.far_ref.across_ref, bf16[16,8,16,512]{3,2,1,0:T(8,128)(2,1)} %bitcast.23.near_ref.far_ref.across_ref, ...), custom_call_target="tpu_custom_call" | custom-call | flops 2415919104 | bytes 14680064 | tf_op jit(solution)/shard_map/final_pass/pallas_call | solution.py:231
  (8 shorter events, 0.0 us)
Async XLA Ops:
  6.5 21.9 %copy-start = (bf16[128,2048]{1,0:T(8,128)(2,1)S(1)}, bf16[128,2048]{1,0:T(8,128)(2,1)}, u32[]{:S(2)}) copy-start(bf16[128,2048]{1,0:T(8,128)(2,1)} %param.10) | copy-start | bytes 1572868
  6.5 71.5 %all-gather.6.cloned.1.call-start = ((), (), s32[]{:S(2)}) async-start(), calls=%async_computation.4 | async-start | bytes 5898240 | tf_op jit(solution)/shard_map/all_gather | solution.py:286
  8.6 9.2 %collective-permute-start.2 = (bf16[80,2048]{1,0:T(8,128)(2,1)S(1)}, bf16[80,2048]{1,0:T(8,128)(2,1)S(1)}, u32[]{:S(2)}, u32[]{:S(2)}) collective-permute-start(bf16[80,2048]{1,0:T(8,128)(2,1)S(1)} %get-tuple-element.26), channel_id=1, source_target_pairs={{0,64},{8,72},{16,80},{24,88},{32,96},{40,104},{48,112},{56,120},{... | collective-permute-start | bytes 983048 | tf_op jit(solution)/shard_map/ppermute | solution.py:291
  21.5 29.3 %all-to-all-start = ((bf16[8,256,256]{2,1,0:T(8,128)(2,1)}), bf16[8,256,256]{2,1,0:T(8,128)(2,1)S(1)}, u32[]{:S(2)}, u32[]{:S(2)}) async-start(bf16[8,256,256]{2,1,0:T(8,128)(2,1)} %bitcast.3), calls=%async_computation | async-start | bytes 2097152 | tf_op jit(solution)/shard_map/all_to_all | solution.py:297
  28.4 104.1 %all-gather.10.cloned.1.call-start = ((), (), s32[]{:S(2)}) async-start(), calls=%async_computation.6 | async-start | bytes 4718592 | tf_op jit(solution)/shard_map/all_gather | solution.py:286
  28.6 22.2 %collective-permute-start = (bf16[2,64,2048]{2,1,0:T(8,128)(2,1)S(1)}, bf16[2,64,2048]{2,1,0:T(8,128)(2,1)S(1)}, u32[]{:S(2)}, u32[]{:S(2)}) collective-permute-start(bf16[2,64,2048]{2,1,0:T(8,128)(2,1)S(1)} %pad_maximum_fusion), channel_id=1, source_target_pairs={{0,64},{8,72},{16,80},{24,88},{32,96},{40,104},{48,112},{56,120},{... | collective-permute-start | bytes 1572872 | tf_op jit(solution)/shard_map/ppermute | solution.py:299
  52.0 89.2 %all-gather.8.cloned.1.call-start = ((), (), s32[]{:S(2)}) async-start(), calls=%async_computation.5 | async-start | bytes 4718592 | tf_op jit(solution)/shard_map/all_gather | solution.py:286
  52.8 25.3 %collective-permute-start.1 = (bf16[8,256,256]{2,1,0:T(8,128)(2,1)S(1)}, bf16[8,256,256]{2,1,0:T(8,128)(2,1)S(1)}, u32[]{:S(2)}, u32[]{:S(2)}) collective-permute-start(bf16[8,256,256]{2,1,0:T(8,128)(2,1)S(1)} %all-to-all-done.own_ref), channel_id=1, source_target_pairs={{0,1},{1,0},{2,3},{3,2},{4,5},{5,4},{6,7},{7,6},{8,9},{9,8},{10,11... | collective-permute-start | bytes 3145736 | tf_op jit(solution)/shard_map/ppermute | solution.py:305
  56.5 27.7 %all-to-all-start.1 = ((bf16[16,128,256]{2,1,0:T(8,128)(2,1)}), bf16[16,128,256]{2,1,0:T(8,128)(2,1)}, u32[]{:S(2)}, u32[]{:S(2)}) async-start(bf16[16,128,256]{2,1,0:T(8,128)(2,1)} %bitcast.55), calls=%async_computation.1 | async-start | bytes 2097152 | tf_op jit(solution)/shard_map/all_to_all | solution.py:306
  78.0 6.2 %copy-start.1 = (bf16[8,256,256]{2,1,0:T(8,128)(2,1)}, bf16[8,256,256]{2,1,0:T(8,128)(2,1)S(1)}, u32[]{:S(2)}) copy-start(bf16[8,256,256]{2,1,0:T(8,128)(2,1)S(1)} %collective-permute-done.1.mate_ref) | copy-start | bytes 3145732
  84.2 30.1 %all-to-all-start.2 = ((bf16[128,32,128]{2,1,0:T(8,128)(2,1)}), bf16[128,32,128]{2,1,0:T(8,128)(2,1)S(1)}, u32[]{:S(2)}, u32[]{:S(2)}) async-start(bf16[128,32,128]{2,1,0:T(8,128)(2,1)} %bitcast.14), calls=%async_computation.2 | async-start | bytes 2097152 | tf_op jit(solution)/shard_map/all_to_all | solution.py:312
  125.9 15.1 %copy-start.3 = (f32[16]{0:T(128)S(1)}, f32[16]{0:T(128)}, u32[]{:S(2)}) copy-start(f32[16]{0:T(128)} %param.13) | copy-start | bytes 196
  125.9 41.4 %all-to-all-start.3 = ((bf16[128,16,512]{2,1,0:T(8,128)(2,1)}), bf16[128,16,512]{2,1,0:T(8,128)(2,1)}, u32[]{:S(2)}, u32[]{:S(2)}) async-start(bf16[128,16,512]{2,1,0:T(8,128)(2,1)} %bitcast.53), calls=%async_computation.3 | async-start | bytes 4194304 | tf_op jit(solution)/shard_map/all_to_all | solution.py:319
  132.5 1.2 copy-start.2
  139.5 27.7 %collective-permute-start.3 = (bf16[256,1024]{1,0:T(8,128)(2,1)}, bf16[256,1024]{1,0:T(8,128)(2,1)S(1)}, u32[]{:S(2)}, u32[]{:S(2)}) collective-permute-start(bf16[256,1024]{1,0:T(8,128)(2,1)} %get-tuple-element.20), channel_id=1, source_target_pairs={{0,1},{1,0},{2,3},{3,2},{4,5},{5,4},{6,7},{7,6},{8,9},{9,8},{10,11... | collective-permute-start | bytes 1572872 | tf_op jit(solution)/shard_map/ppermute | solution.py:324
Sparse Core Ops, SparseCore 0:
  19.0 40.6 all-gather.5
  61.4 38.0 all-gather.9
  101.2 32.1 all-gather.7

commit v11 on v10

--- a/solution.py
+++ b/solution.py
@@ -50,14 +50,14 @@
             out_ref[:, block, slot] = vals[slot, :, :, block * points : (block + 1) * points]
 
 
-def piece_specs(gathered, piece):
+def piece_specs(gathered, piece, first=0):
     shards, _, _, cols = gathered.shape
     block = (shards, 1, piece, cols)
     return [
-        pl.BlockSpec(block, lambda s, *_: (0, 0, 2 * s, 0)),
-        pl.BlockSpec(block, lambda s, *_: (0, 1, 2 * s, 0)),
-        pl.BlockSpec(block, lambda s, *_: (0, 0, 2 * s + 1, 0)),
-        pl.BlockSpec(block, lambda s, *_: (0, 1, 2 * s + 1, 0)),
+        pl.BlockSpec(block, lambda s, *_: (0, 0, first + 2 * s, 0)),
+        pl.BlockSpec(block, lambda s, *_: (0, 1, first + 2 * s, 0)),
+        pl.BlockSpec(block, lambda s, *_: (0, 0, first + 2 * s + 1, 0)),
+        pl.BlockSpec(block, lambda s, *_: (0, 1, first + 2 * s + 1, 0)),
     ]
 
 
@@ -154,6 +154,7 @@
 def applied_pass(own, mate, gathered, steps=4):
     n_narrow, height, width = own.shape
     shards, sides, depth, cols = gathered.shape
+    depth = depth // 2
     points = shards * sides * depth
     parts = steps // sides
     resident = pl.BlockSpec(own.shape, lambda s: (0, 0, 0))
@@ -237,7 +238,7 @@
                 pl.BlockSpec((states, 2, rows, points), lambda s, h: (0, s, 0, h[0])),
                 pl.BlockSpec((states, 2, rows, points), lambda s, h: (0, s, 0, 1 - h[0])),
                 *piece_specs(near, piece),
-                *piece_specs(far, piece),
+                *piece_specs(far, piece, blocks),
                 pl.BlockSpec((states, blocks, rows, width), lambda s, h: (0, 0, 0, 1)),
                 whole(kept),
                 whole(moved),
@@ -295,19 +296,16 @@
 
     own = local.reshape(n_narrow, inner, states, width).swapaxes(1, 2)
     own = lax.all_to_all(own.reshape(n_narrow, height, width), "narrow", 0, 0, tiled=True)
-    mine = jnp.stack([stay, far])
+    mine = jnp.concatenate([stay, far], 0)
     theirs = lax.ppermute(mine, "wide", across_y)
-    own, theirs, mine = lax.optimization_barrier((own, theirs, mine))
-    joined = both_sides(mine, theirs)
-    stay, far = joined[:, 0], joined[:, 1]
-    half_ham = gather(stay)
-    far = gather(far)
     mate = lax.ppermute(own, "narrow", narrow_pairs)
     by_state = lax.all_to_all(jnp.swapaxes(local, 0, 1), "wide", 0, 0, tiled=True)
 
     turned = lax.optimization_barrier(grid_one.T)
     values = forward_pass(own, mate, near, states, piece)
     values, by_state, turned = lax.optimization_barrier((values, by_state, turned))
+    by_state, theirs, mine = lax.optimization_barrier((by_state, theirs, mine))
+    far = gather(both_sides(mine, theirs))
     across = dot_f32(ham_one, by_state.reshape(n_one, width), NN).astype(jnp.bfloat16)
     values = lax.all_to_all(
         values.reshape(n_wide * n_narrow, 2 * inner, width // 2), both, 0, 0, tiled=True
@@ -320,7 +318,7 @@
         pair.reshape(n_wide * n_narrow, inner, 2 * width), both, 0, 0, tiled=True
     )
 
-    kept, moved = applied_pass(own, mate, half_ham)
+    kept, moved = applied_pass(own, mate, far)
     moved = lax.ppermute(moved, "narrow", narrow_pairs)
     energy = jnp.repeat(third_energy, inner)[:, None]
     target = jnp.arange(height)

time: 184 us -> 201 us (1.092)
  blocking collectives: 0 us -> 22.4 us
  starting transfers between devices: 40.5 us -> 27.2 us
  waiting for transfers between devices: 61.5 us -> 67.8 us
  other arithmetic: 2.38 us -> 4.64 us
    all_gather x3 -> x2, waiting for transfers between devices: 0.05 us -> 38.2 us  [gather(): lax.all_gather(value, 'wide', axis=0, tiled=False, axis_index_groups=memb...]
    all_to_all x0 -> x1, blocking collectives: none -> 22.4 us  [on_device(): lax.all_to_all(own.reshape(n_narrow, height, width), 'narrow', 0, 0, tile...]
    ppermute x1, waiting for transfers between devices: 21.7 us -> 4.97 us  [on_device(): theirs = lax.ppermute(mine, 'wide', across_y)]
    ppermute x1, waiting for transfers between devices: 26 us -> 12.1 us  [on_device(): moved = lax.ppermute(moved, 'narrow', narrow_pairs)]
    all_to_all x1 -> x0, starting transfers between devices: 6.91 us -> none  [on_device(): lax.all_to_all(own.reshape(n_narrow, height, width), 'narrow', 0, 0, tile...]
    all_to_all x1, starting transfers between devices: 12.5 us -> 7.23 us  [on_device(): lax.all_to_all(values.reshape(n_wide * n_narrow, 2 * inner, width // 2),...]
    select_n x2, other arithmetic: 1.19 us -> 3.46 us  [both_sides(): jnp.where(side == 0, jnp.stack([mine, theirs]), jnp.stack([theirs, mine]))]
    unnamed x10 -> x12, local copies, waits for them, and re-layouts: 16.2 us -> 18.1 us
  transfers between devices with their start and end apart: 11 -> 9, of which waited for: 4 -> 5; matrix products, arithmetic and copies ran while one was open for 17% -> 14% of each run, Pallas kernels for 13% -> 11%
where the time goes in v11:
time: 201 us; the launch traced here: 199 us
  waiting for transfers between devices  67.8 us (34%)
  Pallas kernels  31.1 us (15%)
  starting transfers between devices  27.2 us (14%)
  local copies, waits for them, and re-layouts  25.9 us (13%)
  blocking collectives  22.4 us (11%)
  between operations  13.5 us (7%)
  matrix products  6.94 us (3%)
  other arithmetic  4.64 us (2%)
    all_gather x2, waiting for transfers between devices, gather(): lax.all_gather(value, 'wide', axis=0, tiled=False, axis_index_groups=memb...  38.2 us
    all_to_all x1, blocking collectives, on_device(): lax.all_to_all(own.reshape(n_narrow, height, width), 'narrow', 0, 0, tile...  22.4 us
    unnamed x12, local copies, waits for them, and re-layouts  18.1 us
    ppermute x1, waiting for transfers between devices, on_device(): moved = lax.ppermute(moved, 'narrow', narrow_pairs)  12.1 us
    pallas_call x1, Pallas kernels, middle_pass(): pl.pallas_call(middle_step, grid=(2 * half,), in_specs=[pl.BlockSpec(valu...  12 us
    pallas_call x1, Pallas kernels, final_pass(): pl.pallas_call(final_step, grid_spec=pltpu.PrefetchScalarGridSpec(num_sca...  8.89 us
    all_to_all x1, starting transfers between devices, on_device(): lax.all_to_all(jnp.swapaxes(local, 0, 1), 'wide', 0, 0, tiled=True)  8.76 us
    all_to_all x1, starting transfers between devices, on_device(): lax.all_to_all(values.reshape(n_wide * n_narrow, 2 * inner, width // 2),...  7.23 us
  transfers between devices with their start and end apart: 9, of which 5 were waited for; matrix products, arithmetic and copies ran while one was open for 14% of the time, Pallas kernels for 11%

profile of v11, /device:TPU:1, one launch (start us, length us, event | category | flops | bytes accessed | tf_op | source)
XLA Modules:
  0.0 199.4 jit_solution(11113288488546072119)
XLA Ops:
  6.5 0.0 copy-start
  6.5 0.0 all-gather.3.cloned.1.call-start
  6.5 1.0 convert_bitcast_fusion
  7.5 1.1 dynamic-slice_bitcast_fusion
  8.6 0.1 fusion.6
  8.6 2.2 %collective-permute-start.1 = (bf16[80,2048]{1,0:T(8,128)(2,1)S(1)}, bf16[80,2048]{1,0:T(8,128)(2,1)S(1)}, u32[]{:S(2)}, u32[]{:S(2)}) collective-permute-start(bf16[80,2048]{1,0:T(8,128)(2,1)S(1)} %get-tuple-element.24), channel_id=1, source_target_pairs={{0,64},{8,72},{16,80},{24,88},{32,96},{40,104},{48,112},{56,120},{... | collective-permute-start | bytes 983048 | tf_op jit(solution)/shard_map/ppermute | solution.py:292
  10.9 7.0 %collective-permute-done.1 = bf16[80,2048]{1,0:T(8,128)(2,1)S(1)} collective-permute-done((bf16[80,2048]{1,0:T(8,128)(2,1)S(1)}, bf16[80,2048]{1,0:T(8,128)(2,1)S(1)}, u32[]{:S(2)}, u32[]{:S(2)}) %collective-permute-start.1) | collective-permute-done | bytes 327712 | tf_op jit(solution)/shard_map/ppermute | solution.py:292
  17.9 0.9 maximum_select_fusion.1
  18.8 0.0 all-gather.3.cloned.1.call-update
  18.8 1.6 copy.31
  20.4 22.4 %all_to_all.20.own_ref = bf16[8,256,256]{2,1,0:T(8,128)(2,1)S(1)} all-to-all(bf16[8,256,256]{2,1,0:T(8,128)(2,1)S(1)} %bitcast.49), channel_id=1, replica_groups=mesh['wide'=16,'narrow'=8] {'narrow'}, dimensions={0} | all-to-all | bytes 2097152 | tf_op jit(solution)/shard_map/all_to_all | solution.py:298
  42.9 0.0 collective-permute-start
  42.9 2.6 %copy.44 = bf16[1,128,16,256]{3,1,2,0:T(8,128)(2,1)} copy(bf16[1,128,16,256]{3,2,1,0:T(8,128)(2,1)} %param.7) | data formatting | bytes 2097152 | tf_op args[0]
  45.4 8.8 %all-to-all-start.1 = ((bf16[16,128,256]{2,1,0:T(8,128)(2,1)}), bf16[16,128,256]{2,1,0:T(8,128)(2,1)}, u32[]{:S(2)}, u32[]{:S(2)}) async-start(bf16[16,128,256]{2,1,0:T(8,128)(2,1)} %bitcast.47), calls=%async_computation.1 | async-start | bytes 2097152 | tf_op jit(solution)/shard_map/all_to_all | solution.py:302
  54.2 0.0 all-gather.5.cloned.1.call-start
  54.2 0.0 copy-done
  54.3 1.5 collective-permute-start.2
  55.8 12.4 %copy.34 = bf16[2048,2048]{0,1:T(8,128)(2,1)} copy(bf16[2048,2048]{1,0:T(8,128)(2,1)} %grid_ref.1) | data formatting | bytes 16777216 | tf_op args[2]
  68.2 0.0 collective-permute-done.mate_ref
  68.2 0.0 all-gather.3.cloned.1.call-done.a0_ref.a1_ref.b0_ref.b1_ref.near_a0.near_a1.near_b0.near_b1
  68.2 5.0 %forward_pass.1 = bf16[16,8,2,16,128]{4,3,2,1,0:T(8,128)(2,1)S(1)} custom-call(bf16[8,256,256]{2,1,0:T(8,128)(2,1)S(1)} %all_to_all.20.own_ref, bf16[8,256,256]{2,1,0:T(8,128)(2,1)S(1)} %collective-permute-done.mate_ref, bf16[8,2,80,2048]{3,2,1,0:T(8,128)(2,1)} %all-gather.3.cloned.1.call-done.a0_ref.a1_ref.b0_ref.b1_ref.near_a0.near_a1.near_b0.near_b1, ...), custom_call_target="tpu_custom_call" | custom-call | flops 2147483648 | bytes 8388608 | tf_op jit(solution)/shard_map/forward_pass/pallas_call | solution.py:71
  73.3 0.0 copy-start.1
  73.3 1.0 copy-done.1
  74.2 0.0 all-to-all-done.1
  74.2 5.0 %collective-permute-done.2 = bf16[128,2048]{1,0:T(8,128)(2,1)} collective-permute-done((bf16[128,2048]{1,0:T(8,128)(2,1)S(1)}, bf16[128,2048]{1,0:T(8,128)(2,1)}, u32[]{:S(2)}, u32[]{:S(2)}) %collective-permute-start.2) | collective-permute-done | bytes 524320 | tf_op jit(solution)/shard_map/ppermute | solution.py:300
  79.2 2.5 %maximum_select_fusion = bf16[1,2,128,2048]{3,2,1,0:T(8,128)(2,1)} fusion(bf16[1,1,128,2048]{3,2,1,0:T(8,128)(2,1)} %bitcast.24, bf16[1,1,128,2048]{3,2,1,0:T(8,128)(2,1)S(1)} %bitcast.51, pred[]{:T(512)S(6)} %eq.12), kind=kLoop, calls=%fused_computation.3 | loop fusion | flops 1572864 | bytes 2097153 | tf_op jit(solution)/shard_map/jit(_where)/select_n | solution.py:284
  81.7 0.0 all-gather.5.cloned.1.call-update
  81.8 7.2 %all-to-all-start.2 = ((bf16[128,32,128]{2,1,0:T(8,128)(2,1)}), bf16[128,32,128]{2,1,0:T(8,128)(2,1)}, u32[]{:S(2)}, u32[]{:S(2)}) async-start(bf16[128,32,128]{2,1,0:T(8,128)(2,1)} %bitcast.43), calls=%async_computation.2 | async-start | bytes 2097152 | tf_op jit(solution)/shard_map/all_to_all | solution.py:310
  89.0 1.4 slice_bitcast_fusion
  90.4 1.0 copy.35
  91.4 2.5 %copy.36 = bf16[256,2048]{0,1:T(8,128)(2,1)} copy(bf16[256,2048]{1,0:T(8,128)(2,1)} %bitcast.48) | data formatting | bytes 2097152 | tf_op jit(solution)/shard_map/reshape | solution.py:315
  93.9 6.9 %fusion.across_ref = bf16[2048,256]{1,0:T(8,128)(2,1)} fusion(bf16[2048,2048]{1,0:T(8,128)(2,1)} %param.8, bf16[2048,256]{1,0:T(8,128)(2,1)} %bitcast.19), kind=kOutput, calls=%fused_computation.1 | convolution fusion | flops 2148007936 | bytes 10485760 | tf_op jit(solution)/shard_map/dot_general | solution.py:14
  100.8 5.4 %all-to-all-done.2 = bf16[128,32,128]{2,1,0:T(8,128)(2,1)} async-done(((bf16[128,32,128]{2,1,0:T(8,128)(2,1)}), bf16[128,32,128]{2,1,0:T(8,128)(2,1)}, u32[]{:S(2)}, u32[]{:S(2)}) %all-to-all-start.2) | async-done | bytes 1048608 | tf_op jit(solution)/shard_map/all_to_all | solution.py:310
  106.2 12.0 %middle_pass.1 = bf16[2048,512]{1,0:T(8,128)(2,1)} custom-call(bf16[64,2,2,16,128]{4,3,2,1,0:T(8,128)(2,1)} %bitcast.13.values_ref, bf16[2048,2048]{1,0:T(8,128)(2,1)} %grid_ref.1, bf16[2048,2048]{1,0:T(8,128)(2,1)} %bitcast.44, bf16[2048,256]{1,0:T(8,128)(2,1)} %bitcast.50, bf16[2048,256]{1,0:T(8,128)(2,1)} %fusion.across_ref), custom_call_target="tpu_custom_call" | custom-call | flops 4294967296 | bytes 22020096 | tf_op jit(solution)/shard_map/middle_pass/pallas_call | solution.py:121
  118.2 6.7 %all-to-all-start.3 = ((bf16[128,16,512]{2,1,0:T(8,128)(2,1)}), bf16[128,16,512]{2,1,0:T(8,128)(2,1)}, u32[]{:S(2)}, u32[]{:S(2)}) async-start(bf16[128,16,512]{2,1,0:T(8,128)(2,1)} %bitcast.45), calls=%async_computation.3 | async-start | bytes 4194304 | tf_op jit(solution)/shard_map/all_to_all | solution.py:317
  124.9 38.2 %all-gather.5.cloned.1.call-done.ham_ref.far_a0.far_a1.far_b0.far_b1 = bf16[8,2,128,2048]{3,2,1,0:T(8,128)(2,1)} async-done(((bf16[1,2,128,2048]{3,2,1,0:T(8,128)(2,1)}), bf16[8,2,128,2048]{3,2,1,0:T(8,128)(2,1)}) %all-gather.5.cloned.1.call-update) | async-done | bytes 8388624 | tf_op jit(solution)/shard_map/all_gather | solution.py:287
  163.1 5.1 %applied_pass.1 = (f32[256,1024]{1,0:T(8,128)S(1)}, bf16[256,1024]{1,0:T(8,128)(2,1)S(1)}) custom-call(bf16[8,256,256]{2,1,0:T(8,128)(2,1)S(1)} %all_to_all.20.own_ref, bf16[8,256,256]{2,1,0:T(8,128)(2,1)S(1)} %collective-permute-done.mate_ref, bf16[8,2,128,2048]{3,2,1,0:T(8,128)(2,1)} %all-gather.5.cloned.1.call-done.ham_ref.far_a0.far_a1.far_b0.far_b1), custom_call_target="tpu_custom_call" | custom-call | flops 2147483648 | bytes 8388608 | tf_op jit(solution)/shard_map/applied_pass/pallas_call | solution.py:162
  168.2 0.0 copy-start.2
  168.3 1.0 copy-done.2
  169.2 0.8 collective-permute-start.3
  170.1 0.0 copy-done.4
  170.1 0.1 broadcast_in_dim.12
  170.1 0.1 broadcast_in_dim_reshape.4.energy_ref
  170.3 0.1 fusion.1.swap_ref
  170.4 0.0 all-to-all-done.3
  170.4 12.1 %collective-permute-done.3.moved_ref = bf16[256,1024]{1,0:T(8,128)(2,1)S(1)} collective-permute-done((bf16[256,1024]{1,0:T(8,128)(2,1)S(1)}, bf16[256,1024]{1,0:T(8,128)(2,1)S(1)}, u32[]{:S(2)}, u32[]{:S(2)}) %collective-permute-start.3) | collective-permute-done | bytes 524320 | tf_op jit(solution)/shard_map/ppermute | solution.py:322
  182.5 1.2 copy-done.3
  183.7 8.9 %final_pass.1 = bf16[16,16,2048]{2,1,0:T(8,128)(2,1)} custom-call(s32[1]{0:T(128)} %bitcast.half_ref, bf16[16,8,16,512]{3,2,1,0:T(8,128)(2,1)} %bitcast.22.near_ref.far_ref.across_ref, bf16[16,8,16,512]{3,2,1,0:T(8,128)(2,1)} %bitcast.22.near_ref.far_ref.across_ref, ...), custom_call_target="tpu_custom_call" | custom-call | flops 2415919104 | bytes 14680064 | tf_op jit(solution)/shard_map/final_pass/pallas_call | solution.py:232
  (5 shorter events, 0.1 us)
Async XLA Ops:
  6.5 47.7 %copy-start = (bf16[128,2048]{1,0:T(8,128)(2,1)S(1)}, bf16[128,2048]{1,0:T(8,128)(2,1)}, u32[]{:S(2)}) copy-start(bf16[128,2048]{1,0:T(8,128)(2,1)} %param.10) | copy-start | bytes 1572868
  6.5 61.7 %all-gather.3.cloned.1.call-start = ((), (), s32[]{:S(2)}) async-start(), calls=%async_computation.4 | async-start | bytes 5898240 | tf_op jit(solution)/shard_map/all_gather | solution.py:287
  8.6 9.2 %collective-permute-start.1 = (bf16[80,2048]{1,0:T(8,128)(2,1)S(1)}, bf16[80,2048]{1,0:T(8,128)(2,1)S(1)}, u32[]{:S(2)}, u32[]{:S(2)}) collective-permute-start(bf16[80,2048]{1,0:T(8,128)(2,1)S(1)} %get-tuple-element.24), channel_id=1, source_target_pairs={{0,64},{8,72},{16,80},{24,88},{32,96},{40,104},{48,112},{56,120},{... | collective-permute-start | bytes 983048 | tf_op jit(solution)/shard_map/ppermute | solution.py:292
  42.9 25.3 %collective-permute-start = (bf16[8,256,256]{2,1,0:T(8,128)(2,1)S(1)}, bf16[8,256,256]{2,1,0:T(8,128)(2,1)S(1)}, u32[]{:S(2)}, u32[]{:S(2)}) collective-permute-start(bf16[8,256,256]{2,1,0:T(8,128)(2,1)S(1)} %all_to_all.20.own_ref), channel_id=1, source_target_pairs={{0,1},{1,0},{2,3},{3,2},{4,5},{5,4},{6,7},{7,6},{8,9},{9,8},{10,11... | collective-permute-start | bytes 3145736 | tf_op jit(solution)/shard_map/ppermute | solution.py:301
  45.4 28.8 %all-to-all-start.1 = ((bf16[16,128,256]{2,1,0:T(8,128)(2,1)}), bf16[16,128,256]{2,1,0:T(8,128)(2,1)}, u32[]{:S(2)}, u32[]{:S(2)}) async-start(bf16[16,128,256]{2,1,0:T(8,128)(2,1)} %bitcast.47), calls=%async_computation.1 | async-start | bytes 2097152 | tf_op jit(solution)/shard_map/all_to_all | solution.py:302
  54.2 108.9 %all-gather.5.cloned.1.call-start = ((), (), s32[]{:S(2)}) async-start(), calls=%async_computation.5 | async-start | bytes 9437184 | tf_op jit(solution)/shard_map/all_gather | solution.py:287
  54.3 24.9 %collective-permute-start.2 = (bf16[128,2048]{1,0:T(8,128)(2,1)S(1)}, bf16[128,2048]{1,0:T(8,128)(2,1)}, u32[]{:S(2)}, u32[]{:S(2)}) collective-permute-start(bf16[128,2048]{1,0:T(8,128)(2,1)S(1)} %pad_maximum_fusion), channel_id=1, source_target_pairs={{0,64},{8,72},{16,80},{24,88},{32,96},{40,104},{48,112},{56,120},{... | collective-permute-start | bytes 1572872 | tf_op jit(solution)/shard_map/ppermute | solution.py:300
  73.3 1.0 copy-start.1
  81.8 24.5 %all-to-all-start.2 = ((bf16[128,32,128]{2,1,0:T(8,128)(2,1)}), bf16[128,32,128]{2,1,0:T(8,128)(2,1)}, u32[]{:S(2)}, u32[]{:S(2)}) async-start(bf16[128,32,128]{2,1,0:T(8,128)(2,1)} %bitcast.43), calls=%async_computation.2 | async-start | bytes 2097152 | tf_op jit(solution)/shard_map/all_to_all | solution.py:310
  118.2 51.8 %copy-start.4 = (f32[16]{0:T(128)S(1)}, f32[16]{0:T(128)}, u32[]{:S(2)}) copy-start(f32[16]{0:T(128)} %param.13) | copy-start | bytes 196
  118.2 52.1 %all-to-all-start.3 = ((bf16[128,16,512]{2,1,0:T(8,128)(2,1)}), bf16[128,16,512]{2,1,0:T(8,128)(2,1)}, u32[]{:S(2)}, u32[]{:S(2)}) async-start(bf16[128,16,512]{2,1,0:T(8,128)(2,1)} %bitcast.45), calls=%async_computation.3 | async-start | bytes 4194304 | tf_op jit(solution)/shard_map/all_to_all | solution.py:317
  168.2 1.0 copy-start.2
  169.2 13.3 %collective-permute-start.3 = (bf16[256,1024]{1,0:T(8,128)(2,1)S(1)}, bf16[256,1024]{1,0:T(8,128)(2,1)S(1)}, u32[]{:S(2)}, u32[]{:S(2)}) collective-permute-start(bf16[256,1024]{1,0:T(8,128)(2,1)S(1)} %get-tuple-element.20), channel_id=1, source_target_pairs={{0,1},{1,0},{2,3},{3,2},{4,5},{5,4},{6,7},{7,6},{8,9},{9,8},{10,11... | collective-permute-start | bytes 1572872 | tf_op jit(solution)/shard_map/ppermute | solution.py:322
  182.5 1.2 copy-start.3
Sparse Core Ops, SparseCore 0:
  19.0 40.6 all-gather.2
  81.9 81.1 all-gather.4

commit v12 on v10

--- a/solution.py
+++ b/solution.py
@@ -295,19 +295,18 @@
 
     own = local.reshape(n_narrow, inner, states, width).swapaxes(1, 2)
     own = lax.all_to_all(own.reshape(n_narrow, height, width), "narrow", 0, 0, tiled=True)
-    mine = jnp.stack([stay, far])
-    theirs = lax.ppermute(mine, "wide", across_y)
-    own, theirs, mine = lax.optimization_barrier((own, theirs, mine))
-    joined = both_sides(mine, theirs)
-    stay, far = joined[:, 0], joined[:, 1]
-    half_ham = gather(stay)
-    far = gather(far)
+    other_stay = lax.ppermute(stay, "wide", across_y)
+    own, other_stay = lax.optimization_barrier((own, other_stay))
+    half_ham = gather(both_sides(stay, other_stay))
+    other_far = lax.ppermute(far, "wide", across_y)
     mate = lax.ppermute(own, "narrow", narrow_pairs)
     by_state = lax.all_to_all(jnp.swapaxes(local, 0, 1), "wide", 0, 0, tiled=True)
 
     turned = lax.optimization_barrier(grid_one.T)
     values = forward_pass(own, mate, near, states, piece)
     values, by_state, turned = lax.optimization_barrier((values, by_state, turned))
+    by_state, other_far = lax.optimization_barrier((by_state, other_far))
+    far = gather(both_sides(far, other_far))
     across = dot_f32(ham_one, by_state.reshape(n_one, width), NN).astype(jnp.bfloat16)
     values = lax.all_to_all(
         values.reshape(n_wide * n_narrow, 2 * inner, width // 2), both, 0, 0, tiled=True

time: 184 us -> 177 us (0.962)
  waiting for transfers between devices: 61.5 us -> 55.8 us
  local copies, waits for them, and re-layouts: 25.7 us -> 23.5 us
    ppermute x1 -> x2, waiting for transfers between devices: 21.7 us -> 16.1 us  [the longest x1 16.1 us: on_device(): other_stay = lax.ppermute(stay, 'wide', across_y)]
    unnamed x10 -> x12, local copies, waits for them, and re-layouts: 16.2 us -> 16.2 us
  transfers between devices with their start and end apart: 11 -> 12, of which waited for: 4 -> 5; matrix products, arithmetic and copies ran while one was open for 17% -> 17% of each run, Pallas kernels for 13% -> 13%
where the time goes in v12:
time: 177 us; the launch traced here: 176 us
  waiting for transfers between devices  55.8 us (32%)
  starting transfers between devices  40.3 us (23%)
  Pallas kernels  32.3 us (18%)
  local copies, waits for them, and re-layouts  23.5 us (13%)
  between operations  13.2 us (7%)
  matrix products  6.96 us (4%)
  other arithmetic  3.9 us (2%)
    ppermute x1, waiting for transfers between devices, on_device(): moved = lax.ppermute(moved, 'narrow', narrow_pairs)  26 us
    unnamed x12, local copies, waits for them, and re-layouts  16.2 us
    ppermute x1, waiting for transfers between devices, on_device(): other_stay = lax.ppermute(stay, 'wide', across_y)  16.1 us
    pallas_call x1, Pallas kernels, middle_pass(): pl.pallas_call(middle_step, grid=(2 * half,), in_specs=[pl.BlockSpec(valu...  11.4 us
    all_to_all x1, starting transfers between devices, on_device(): lax.all_to_all(values.reshape(n_wide * n_narrow, 2 * inner, width // 2),...  11 us
    all_to_all x1, starting transfers between devices, on_device(): lax.all_to_all(jnp.swapaxes(local, 0, 1), 'wide', 0, 0, tiled=True)  9.03 us
    pallas_call x1, Pallas kernels, final_pass(): pl.pallas_call(final_step, grid_spec=pltpu.PrefetchScalarGridSpec(num_sca...  8.9 us
    all_to_all x1, starting transfers between devices, on_device(): lax.all_to_all(pair.reshape(n_wide * n_narrow, inner, 2 * width), both, 0...  7.04 us
  transfers between devices with their start and end apart: 12, of which 5 were waited for; matrix products, arithmetic and copies ran while one was open for 17% of the time, Pallas kernels for 13%

profile of v12, /device:TPU:1, one launch (start us, length us, event | category | flops | bytes accessed | tf_op | source)
XLA Modules:
  0.0 176.0 jit_solution(14391590289250828800)
XLA Ops:
  6.5 0.0 copy-start
  6.5 0.0 all-gather.4.cloned.1.call-start
  6.5 1.0 convert_bitcast_fusion
  7.6 1.1 dynamic-slice_bitcast_fusion.2
  8.7 0.1 fusion.6
  8.8 2.2 %collective-permute-start.2 = (bf16[80,2048]{1,0:T(8,128)(2,1)S(1)}, bf16[80,2048]{1,0:T(8,128)(2,1)S(1)}, u32[]{:S(2)}, u32[]{:S(2)}) collective-permute-start(bf16[80,2048]{1,0:T(8,128)(2,1)S(1)} %get-tuple-element.27), channel_id=1, source_target_pairs={{0,64},{8,72},{16,80},{24,88},{32,96},{40,104},{48,112},{56,120},{... | collective-permute-start | bytes 983048 | tf_op jit(solution)/shard_map/ppermute | solution.py:291
  11.0 7.0 %collective-permute-done.2 = bf16[80,2048]{1,0:T(8,128)(2,1)S(1)} collective-permute-done((bf16[80,2048]{1,0:T(8,128)(2,1)S(1)}, bf16[80,2048]{1,0:T(8,128)(2,1)S(1)}, u32[]{:S(2)}, u32[]{:S(2)}) %collective-permute-start.2) | collective-permute-done | bytes 327712 | tf_op jit(solution)/shard_map/ppermute | solution.py:291
  18.0 0.9 maximum_select_fusion
  18.9 0.0 all-gather.4.cloned.1.call-update
  19.0 1.3 copy.31
  20.3 6.9 %all-to-all-start = ((bf16[8,256,256]{2,1,0:T(8,128)(2,1)}), bf16[8,256,256]{2,1,0:T(8,128)(2,1)S(1)}, u32[]{:S(2)}, u32[]{:S(2)}) async-start(bf16[8,256,256]{2,1,0:T(8,128)(2,1)} %bitcast.3), calls=%async_computation | async-start | bytes 2097152 | tf_op jit(solution)/shard_map/all_to_all | solution.py:297
  27.2 0.0 all-gather.8.cloned.1.call-start
  27.3 0.5 collective-permute-start
  27.8 16.1 %collective-permute-done = bf16[64,2048]{1,0:T(8,128)(2,1)S(1)} collective-permute-done((bf16[64,2048]{1,0:T(8,128)(2,1)S(1)}, bf16[64,2048]{1,0:T(8,128)(2,1)S(1)}, u32[]{:S(2)}, u32[]{:S(2)}) %collective-permute-start) | collective-permute-done | bytes 262176 | tf_op jit(solution)/shard_map/ppermute | solution.py:298
  44.0 0.6 all-to-all-done.own_ref
  44.5 0.9 maximum_select_fusion.2
  45.4 0.0 all-gather.8.cloned.1.call-update
  45.4 0.7 collective-permute-start.1
  46.1 2.5 %copy.44 = bf16[1,128,16,256]{3,1,2,0:T(8,128)(2,1)} copy(bf16[1,128,16,256]{3,2,1,0:T(8,128)(2,1)} %param.7) | data formatting | bytes 2097152 | tf_op args[0]
  48.7 9.0 %all-to-all-start.1 = ((bf16[16,128,256]{2,1,0:T(8,128)(2,1)}), bf16[16,128,256]{2,1,0:T(8,128)(2,1)}, u32[]{:S(2)}, u32[]{:S(2)}) async-start(bf16[16,128,256]{2,1,0:T(8,128)(2,1)} %bitcast.52), calls=%async_computation.1 | async-start | bytes 2097152 | tf_op jit(solution)/shard_map/all_to_all | solution.py:303
  57.7 0.0 all-gather.6.cloned.1.call-start
  57.8 1.5 collective-permute-start.3
  59.2 12.4 %copy.34 = bf16[2048,2048]{0,1:T(8,128)(2,1)} copy(bf16[2048,2048]{1,0:T(8,128)(2,1)} %grid_ref.1) | data formatting | bytes 16777216 | tf_op args[2]
  71.6 0.0 collective-permute-done.1.mate_ref
  71.6 0.0 all-gather.4.cloned.1.call-done.a0_ref.a1_ref.b0_ref.b1_ref.near_a0.near_a1.near_b0.near_b1
  71.6 6.2 %forward_pass.1 = bf16[16,8,2,16,128]{4,3,2,1,0:T(8,128)(2,1)} custom-call(bf16[8,256,256]{2,1,0:T(8,128)(2,1)S(1)} %all-to-all-done.own_ref, bf16[8,256,256]{2,1,0:T(8,128)(2,1)S(1)} %collective-permute-done.1.mate_ref, bf16[8,2,80,2048]{3,2,1,0:T(8,128)(2,1)} %all-gather.4.cloned.1.call-done.a0_ref.a1_ref.b0_ref.b1_ref.near_a0.near_a1.near_b0.near_b1, ...), custom_call_target="tpu_custom_call" | custom-call | flops 2147483648 | bytes 8388608 | tf_op jit(solution)/shard_map/forward_pass/pallas_call | solution.py:71
  77.8 0.0 all-to-all-done.1
  77.8 0.0 collective-permute-done.3
  77.8 0.9 maximum_select_fusion.1
  78.7 0.0 all-gather.6.cloned.1.call-update
  78.7 11.0 %all-to-all-start.2 = ((bf16[128,32,128]{2,1,0:T(8,128)(2,1)}), bf16[128,32,128]{2,1,0:T(8,128)(2,1)S(1)}, u32[]{:S(2)}, u32[]{:S(2)}) async-start(bf16[128,32,128]{2,1,0:T(8,128)(2,1)} %bitcast.12), calls=%async_computation.2 | async-start | bytes 2097152 | tf_op jit(solution)/shard_map/all_to_all | solution.py:311
  89.8 1.3 slice_bitcast_fusion
  91.1 1.0 copy.35
  92.1 2.3 %copy.36 = bf16[256,2048]{0,1:T(8,128)(2,1)} copy(bf16[256,2048]{1,0:T(8,128)(2,1)} %bitcast.53) | data formatting | bytes 2097152 | tf_op jit(solution)/shard_map/reshape | solution.py:316
  94.4 7.0 %fusion.across_ref = bf16[2048,256]{1,0:T(8,128)(2,1)} fusion(bf16[2048,2048]{1,0:T(8,128)(2,1)} %param.8, bf16[2048,256]{1,0:T(8,128)(2,1)} %bitcast.19), kind=kOutput, calls=%fused_computation.1 | convolution fusion | flops 2148007936 | bytes 10485760 | tf_op jit(solution)/shard_map/dot_general | solution.py:14
  101.4 6.0 %all-to-all-done.2 = bf16[128,32,128]{2,1,0:T(8,128)(2,1)S(1)} async-done(((bf16[128,32,128]{2,1,0:T(8,128)(2,1)}), bf16[128,32,128]{2,1,0:T(8,128)(2,1)S(1)}, u32[]{:S(2)}, u32[]{:S(2)}) %all-to-all-start.2) | async-done | bytes 1048608 | tf_op jit(solution)/shard_map/all_to_all | solution.py:311
  107.4 11.4 %middle_pass.1 = bf16[2048,512]{1,0:T(8,128)(2,1)} custom-call(bf16[64,2,2,16,128]{4,3,2,1,0:T(8,128)(2,1)S(1)} %bitcast.48, bf16[2048,2048]{1,0:T(8,128)(2,1)} %grid_ref.1, bf16[2048,2048]{1,0:T(8,128)(2,1)} %bitcast.49, bf16[2048,256]{1,0:T(8,128)(2,1)} %bitcast.54, bf16[2048,256]{1,0:T(8,128)(2,1)} %fusion.across_ref), custom_call_target="tpu_custom_call" | custom-call | flops 4294967296 | bytes 22020096 | tf_op jit(solution)/shard_map/middle_pass/pallas_call | solution.py:121
  118.8 7.0 %all-to-all-start.3 = ((bf16[128,16,512]{2,1,0:T(8,128)(2,1)}), bf16[128,16,512]{2,1,0:T(8,128)(2,1)}, u32[]{:S(2)}, u32[]{:S(2)}) async-start(bf16[128,16,512]{2,1,0:T(8,128)(2,1)} %bitcast.50), calls=%async_computation.3 | async-start | bytes 4194304 | tf_op jit(solution)/shard_map/all_to_all | solution.py:318
  125.8 0.0 all-gather.8.cloned.1.call-done.ham_ref
  125.8 1.3 copy-done.2
  127.1 5.8 %applied_pass.1 = (f32[256,1024]{1,0:T(8,128)S(1)}, bf16[256,1024]{1,0:T(8,128)(2,1)}) custom-call(bf16[8,256,256]{2,1,0:T(8,128)(2,1)S(1)} %all-to-all-done.own_ref, bf16[8,256,256]{2,1,0:T(8,128)(2,1)S(1)} %copy-done.2, bf16[8,2,64,2048]{3,2,1,0:T(8,128)(2,1)} %all-gather.8.cloned.1.call-done.ham_ref), custom_call_target="tpu_custom_call" | custom-call | flops 2147483648 | bytes 8388608 | tf_op jit(solution)/shard_map/applied_pass/pallas_call | solution.py:161
  132.9 1.4 collective-permute-start.4
  134.3 0.1 broadcast_in_dim.12
  134.3 0.1 broadcast_in_dim_reshape.4.energy_ref
  134.4 0.1 fusion.1.swap_ref
  134.6 26.0 %collective-permute-done.4.moved_ref = bf16[256,1024]{1,0:T(8,128)(2,1)S(1)} collective-permute-done((bf16[256,1024]{1,0:T(8,128)(2,1)}, bf16[256,1024]{1,0:T(8,128)(2,1)S(1)}, u32[]{:S(2)}, u32[]{:S(2)}) %collective-permute-start.4) | collective-permute-done | bytes 524320 | tf_op jit(solution)/shard_map/ppermute | solution.py:323
  160.5 0.0 all-to-all-done.3
  160.6 8.9 %final_pass.1 = bf16[16,16,2048]{2,1,0:T(8,128)(2,1)} custom-call(s32[1]{0:T(128)} %bitcast.half_ref, bf16[16,8,16,512]{3,2,1,0:T(8,128)(2,1)} %bitcast.22.near_ref.far_ref.across_ref, bf16[16,8,16,512]{3,2,1,0:T(8,128)(2,1)} %bitcast.22.near_ref.far_ref.across_ref, ...), custom_call_target="tpu_custom_call" | custom-call | flops 2415919104 | bytes 14680064 | tf_op jit(solution)/shard_map/final_pass/pallas_call | solution.py:231
  (12 shorter events, 0.1 us)
Async XLA Ops:
  6.5 20.7 %copy-start = (bf16[128,2048]{1,0:T(8,128)(2,1)S(1)}, bf16[128,2048]{1,0:T(8,128)(2,1)}, u32[]{:S(2)}) copy-start(bf16[128,2048]{1,0:T(8,128)(2,1)} %param.10) | copy-start | bytes 1572868
  6.5 12.4 %copy-start.3 = (bf16[1,128,16,256]{3,2,1,0:T(8,128)(2,1)S(1)}, bf16[1,128,16,256]{3,2,1,0:T(8,128)(2,1)}, u32[]{:S(2)}) copy-start(bf16[1,128,16,256]{3,2,1,0:T(8,128)(2,1)} %param.7) | copy-start | bytes 3145732
  6.5 65.1 %all-gather.4.cloned.1.call-start = ((), (), s32[]{:S(2)}) async-start(), calls=%async_computation.4 | async-start | bytes 5898240 | tf_op jit(solution)/shard_map/all_gather | solution.py:286
  8.8 9.2 %collective-permute-start.2 = (bf16[80,2048]{1,0:T(8,128)(2,1)S(1)}, bf16[80,2048]{1,0:T(8,128)(2,1)S(1)}, u32[]{:S(2)}, u32[]{:S(2)}) collective-permute-start(bf16[80,2048]{1,0:T(8,128)(2,1)S(1)} %get-tuple-element.27), channel_id=1, source_target_pairs={{0,64},{8,72},{16,80},{24,88},{32,96},{40,104},{48,112},{56,120},{... | collective-permute-start | bytes 983048 | tf_op jit(solution)/shard_map/ppermute | solution.py:291
  20.3 24.2 %all-to-all-start = ((bf16[8,256,256]{2,1,0:T(8,128)(2,1)}), bf16[8,256,256]{2,1,0:T(8,128)(2,1)S(1)}, u32[]{:S(2)}, u32[]{:S(2)}) async-start(bf16[8,256,256]{2,1,0:T(8,128)(2,1)} %bitcast.3), calls=%async_computation | async-start | bytes 2097152 | tf_op jit(solution)/shard_map/all_to_all | solution.py:297
  27.2 98.6 %all-gather.8.cloned.1.call-start = ((), (), s32[]{:S(2)}) async-start(), calls=%async_computation.6 | async-start | bytes 4718592 | tf_op jit(solution)/shard_map/all_gather | solution.py:286
  27.3 16.6 %collective-permute-start = (bf16[64,2048]{1,0:T(8,128)(2,1)S(1)}, bf16[64,2048]{1,0:T(8,128)(2,1)S(1)}, u32[]{:S(2)}, u32[]{:S(2)}) collective-permute-start(bf16[64,2048]{1,0:T(8,128)(2,1)S(1)} %constant_dynamic-slice_fusion), channel_id=1, source_target_pairs={{0,64},{8,72},{16,80},{24,88},{32,96},{40,104},{48,112},{56,120},{... | collective-permute-start | bytes 786440 | tf_op jit(solution)/shard_map/ppermute | solution.py:298
  45.4 26.1 %collective-permute-start.1 = (bf16[8,256,256]{2,1,0:T(8,128)(2,1)S(1)}, bf16[8,256,256]{2,1,0:T(8,128)(2,1)S(1)}, u32[]{:S(2)}, u32[]{:S(2)}) collective-permute-start(bf16[8,256,256]{2,1,0:T(8,128)(2,1)S(1)} %all-to-all-done.own_ref), channel_id=1, source_target_pairs={{0,1},{1,0},{2,3},{3,2},{4,5},{5,4},{6,7},{7,6},{8,9},{9,8},{10,11... | collective-permute-start | bytes 3145736 | tf_op jit(solution)/shard_map/ppermute | solution.py:302
  48.7 29.1 %all-to-all-start.1 = ((bf16[16,128,256]{2,1,0:T(8,128)(2,1)}), bf16[16,128,256]{2,1,0:T(8,128)(2,1)}, u32[]{:S(2)}, u32[]{:S(2)}) async-start(bf16[16,128,256]{2,1,0:T(8,128)(2,1)} %bitcast.52), calls=%async_computation.1 | async-start | bytes 2097152 | tf_op jit(solution)/shard_map/all_to_all | solution.py:303
  57.7 102.8 %all-gather.6.cloned.1.call-start = ((), (), s32[]{:S(2)}) async-start(), calls=%async_computation.5 | async-start | bytes 4718592 | tf_op jit(solution)/shard_map/all_gather | solution.py:286
  57.8 20.1 %collective-permute-start.3 = (bf16[64,2048]{1,0:T(8,128)(2,1)S(1)}, bf16[64,2048]{1,0:T(8,128)(2,1)S(1)}, u32[]{:S(2)}, u32[]{:S(2)}) collective-permute-start(bf16[64,2048]{1,0:T(8,128)(2,1)S(1)} %get-tuple-element.24), channel_id=1, source_target_pairs={{0,64},{8,72},{16,80},{24,88},{32,96},{40,104},{48,112},{56,120},{... | collective-permute-start | bytes 786440 | tf_op jit(solution)/shard_map/ppermute | solution.py:301
  71.6 6.2 %copy-start.1 = (bf16[8,256,256]{2,1,0:T(8,128)(2,1)}, bf16[8,256,256]{2,1,0:T(8,128)(2,1)S(1)}, u32[]{:S(2)}) copy-start(bf16[8,256,256]{2,1,0:T(8,128)(2,1)S(1)} %collective-permute-done.1.mate_ref) | copy-start | bytes 3145732
  78.7 28.6 %all-to-all-start.2 = ((bf16[128,32,128]{2,1,0:T(8,128)(2,1)}), bf16[128,32,128]{2,1,0:T(8,128)(2,1)S(1)}, u32[]{:S(2)}, u32[]{:S(2)}) async-start(bf16[128,32,128]{2,1,0:T(8,128)(2,1)} %bitcast.12), calls=%async_computation.2 | async-start | bytes 2097152 | tf_op jit(solution)/shard_map/all_to_all | solution.py:311
  118.8 15.5 %copy-start.4 = (f32[16]{0:T(128)S(1)}, f32[16]{0:T(128)}, u32[]{:S(2)}) copy-start(f32[16]{0:T(128)} %param.13) | copy-start | bytes 196
  118.8 41.8 %all-to-all-start.3 = ((bf16[128,16,512]{2,1,0:T(8,128)(2,1)}), bf16[128,16,512]{2,1,0:T(8,128)(2,1)}, u32[]{:S(2)}, u32[]{:S(2)}) async-start(bf16[128,16,512]{2,1,0:T(8,128)(2,1)} %bitcast.50), calls=%async_computation.3 | async-start | bytes 4194304 | tf_op jit(solution)/shard_map/all_to_all | solution.py:318
  125.8 1.3 copy-start.2
  132.9 27.7 %collective-permute-start.4 = (bf16[256,1024]{1,0:T(8,128)(2,1)}, bf16[256,1024]{1,0:T(8,128)(2,1)S(1)}, u32[]{:S(2)}, u32[]{:S(2)}) collective-permute-start(bf16[256,1024]{1,0:T(8,128)(2,1)} %get-tuple-element.22), channel_id=1, source_target_pairs={{0,1},{1,0},{2,3},{3,2},{4,5},{5,4},{6,7},{7,6},{8,9},{9,8},{10,11... | collective-permute-start | bytes 1572872 | tf_op jit(solution)/shard_map/ppermute | solution.py:323
Sparse Core Ops, SparseCore 0:
  19.1 40.6 all-gather.3
  61.5 32.1 all-gather.7
  95.4 32.1 all-gather.5

commit v13 on v12

--- a/solution.py
+++ b/solution.py
@@ -36,32 +36,33 @@
             out_ref[rows, part * width : (part + 1) * width] = ref[part]
 
 
-def forward_step(own_ref, mate_ref, a0_ref, a1_ref, b0_ref, b1_ref, out_ref, rows_ref):
+def forward_step(own_ref, mate_ref, *refs):
+    *grid_refs, out_ref, rows_ref = refs
+
     @pl.when(pl.program_id(0) == 0)
     def _():
         side_by_side((own_ref, mate_ref), rows_ref)
 
-    right = jnp.concatenate([flatten(ref) for ref in (a0_ref, a1_ref, b0_ref, b1_ref)], 0)
+    right = jnp.concatenate([flatten(ref) for ref in grid_refs], 0)
     vals = dot_f32(rows_ref[...], right, NT).astype(out_ref.dtype)
-    states, _, _, inner, points = out_ref.shape
-    vals = vals.reshape(2, states, inner, 2 * points)
-    for block in range(2):
+    states, per, _, inner, points = out_ref.shape
+    vals = vals.reshape(2, states, inner, per * points)
+    for block in range(per):
         for slot in range(2):
             out_ref[:, block, slot] = vals[slot, :, :, block * points : (block + 1) * points]
 
 
-def piece_specs(gathered, piece):
-    shards, _, _, cols = gathered.shape
+def piece_specs(gathered, piece, per):
+    shards, sides, _, cols = gathered.shape
     block = (shards, 1, piece, cols)
-    return [
-        pl.BlockSpec(block, lambda s, *_: (0, 0, 2 * s, 0)),
-        pl.BlockSpec(block, lambda s, *_: (0, 1, 2 * s, 0)),
-        pl.BlockSpec(block, lambda s, *_: (0, 0, 2 * s + 1, 0)),
-        pl.BlockSpec(block, lambda s, *_: (0, 1, 2 * s + 1, 0)),
-    ]
-
-
-def forward_pass(own, mate, gathered, states, piece):
+
+    def spec(block_of_step, side):
+        return pl.BlockSpec(block, lambda s, *_: (0, side, per * s + block_of_step, 0))
+
+    return [spec(which, side) for which in range(per) for side in range(sides)]
+
+
+def forward_pass(own, mate, gathered, states, piece, per=4):
     n_narrow, height, width = own.shape
     shards, sides, _, cols = gathered.shape
     shards = shards * sides
@@ -70,19 +71,19 @@
     resident = pl.BlockSpec(own.shape, lambda s: (0, 0, 0))
     return pl.pallas_call(
         forward_step,
-        grid=(n_narrow // 2,),
+        grid=(n_narrow // per,),
         in_specs=[
             resident,
             resident,
-            *piece_specs(gathered, piece),
-        ],
-        out_specs=pl.BlockSpec((states, 2, 2, inner, points), lambda s: (0, s, 0, 0, 0)),
+            *piece_specs(gathered, piece, per),
+        ],
+        out_specs=pl.BlockSpec((states, per, 2, inner, points), lambda s: (0, s, 0, 0, 0)),
         out_shape=jax.ShapeDtypeStruct((states, n_narrow, 2, inner, points), jnp.bfloat16),
         scratch_shapes=[pltpu.VMEM((2 * height, cols), jnp.bfloat16)],
         compiler_params=params(50),
         cost_estimate=cost(4 * height * cols * points * n_narrow, 8 * MIB),
         name="forward_pass",
-    )(own, mate, gathered, gathered, gathered, gathered)
+    )(own, mate, *[gathered] * (sides * per))
 
 
 def middle_step(
@@ -178,16 +179,16 @@
     )(own, mate, gathered)
 
 
-def final_step(
-    half_ref, near_ref, far_ref, near_a0, near_a1, near_b0, near_b1, far_a0, far_a1, far_b0,
-    far_b1, across_ref, kept_ref, moved_ref, own_ref, energy_ref, swap_ref, out_ref, acc_ref,
-):
+def final_step(half_ref, near_ref, far_ref, *refs):
+    *grid_refs, across_ref, kept_ref, moved_ref, own_ref, energy_ref, swap_ref = refs[:-2]
+    out_ref, acc_ref = refs[-2:]
     step = pl.program_id(0)
-    states, _, rows, _ = near_ref.shape
+    states, per, rows, _ = near_ref.shape
     height = states * rows
-    lefts = [ref[:, block].reshape(height, -1) for ref in (near_ref, far_ref) for block in range(2)]
-    rights = (near_a0, near_a1, near_b0, near_b1, far_a0, far_a1, far_b0, far_b1)
-    rights = [flatten(ref) for ref in rights]
+    lefts = [
+        ref[:, block].reshape(height, -1) for ref in (near_ref, far_ref) for block in range(per)
+    ]
+    rights = [flatten(ref) for ref in grid_refs]
     total = dot_f32(jnp.concatenate(lefts, 1), jnp.concatenate(rights, 0), NN)
 
     @pl.when(step == 0)
@@ -221,7 +222,7 @@
             out_ref[:, :, cols] = swapped.astype(out_ref.dtype).reshape(rows, states, width)
 
 
-def final_pass(half, received, near, far, kept, moved, own, energy, swap, piece):
+def final_pass(half, received, near, far, kept, moved, own, energy, swap, piece, per=4):
     states, blocks, rows, double = received.shape
     width = double // 2
     height = states * rows
@@ -232,12 +233,12 @@
         final_step,
         grid_spec=pltpu.PrefetchScalarGridSpec(
             num_scalar_prefetch=1,
-            grid=(blocks // 2,),
+            grid=(blocks // per,),
             in_specs=[
-                pl.BlockSpec((states, 2, rows, points), lambda s, h: (0, s, 0, h[0])),
-                pl.BlockSpec((states, 2, rows, points), lambda s, h: (0, s, 0, 1 - h[0])),
-                *piece_specs(near, piece),
-                *piece_specs(far, piece),
+                pl.BlockSpec((states, per, rows, points), lambda s, h: (0, s, 0, h[0])),
+                pl.BlockSpec((states, per, rows, points), lambda s, h: (0, s, 0, 1 - h[0])),
+                *piece_specs(near, piece, per),
+                *piece_specs(far, piece, per),
                 pl.BlockSpec((states, blocks, rows, width), lambda s, h: (0, 0, 0, 1)),
                 whole(kept),
                 whole(moved),
@@ -253,7 +254,8 @@
         cost_estimate=cost(2 * height * cols * (cols + height), 14 * MIB),
         name="final_pass",
     )(
-        half, received, received, *[near] * 4, *[far] * 4, received, kept, moved, own, energy, swap
+        half, received, received, *[near] * (sides * per), *[far] * (sides * per), received, kept,
+        moved, own, energy, swap,
     )
 
 

time: 177 us -> 176 us (level)
  no operation moved by 1% of the time
where the time goes in v13:
time: 176 us; the launch traced here: 175 us
  waiting for transfers between devices  55.8 us (32%)
  starting transfers between devices  40.4 us (23%)
  Pallas kernels  30.8 us (18%)
  local copies, waits for them, and re-layouts  23.5 us (13%)
  between operations  13.3 us (8%)
  matrix products  6.96 us (4%)
  other arithmetic  3.9 us (2%)
    ppermute x1, waiting for transfers between devices, on_device(): moved = lax.ppermute(moved, 'narrow', narrow_pairs)  26 us
    ppermute x1, waiting for transfers between devices, on_device(): other_stay = lax.ppermute(stay, 'wide', across_y)  16.1 us
    unnamed x12, local copies, waits for them, and re-layouts  16.1 us
    pallas_call x1, Pallas kernels, middle_pass(): pl.pallas_call(middle_step, grid=(2 * half,), in_specs=[pl.BlockSpec(valu...  11.4 us
    all_to_all x1, starting transfers between devices, on_device(): lax.all_to_all(values.reshape(n_wide * n_narrow, 2 * inner, width // 2),...  11 us
    all_to_all x1, starting transfers between devices, on_device(): lax.all_to_all(jnp.swapaxes(local, 0, 1), 'wide', 0, 0, tiled=True)  9.03 us
    pallas_call x1, Pallas kernels, final_pass(): pl.pallas_call(final_step, grid_spec=pltpu.PrefetchScalarGridSpec(num_sca...  7.97 us
    all_to_all x1, starting transfers between devices, on_device(): lax.all_to_all(pair.reshape(n_wide * n_narrow, inner, 2 * width), both, 0...  7.13 us
  transfers between devices with their start and end apart: 12, of which 5 were waited for; matrix products, arithmetic and copies ran while one was open for 17% of the time, Pallas kernels for 13%

profile of v13, /device:TPU:1, one launch (start us, length us, event | category | flops | bytes accessed | tf_op | source)
XLA Modules:
  0.0 174.6 jit_solution(2819385145524203066)
XLA Ops:
  6.5 0.0 copy-start
  6.5 0.0 all-gather.4.cloned.1.call-start
  6.5 1.0 convert_bitcast_fusion
  7.6 1.1 dynamic-slice_bitcast_fusion.2
  8.7 0.1 fusion.6
  8.8 2.2 %collective-permute-start.2 = (bf16[80,2048]{1,0:T(8,128)(2,1)S(1)}, bf16[80,2048]{1,0:T(8,128)(2,1)S(1)}, u32[]{:S(2)}, u32[]{:S(2)}) collective-permute-start(bf16[80,2048]{1,0:T(8,128)(2,1)S(1)} %get-tuple-element.27), channel_id=1, source_target_pairs={{0,64},{8,72},{16,80},{24,88},{32,96},{40,104},{48,112},{56,120},{... | collective-permute-start | bytes 983048 | tf_op jit(solution)/shard_map/ppermute | solution.py:293
  11.0 7.0 %collective-permute-done.2 = bf16[80,2048]{1,0:T(8,128)(2,1)S(1)} collective-permute-done((bf16[80,2048]{1,0:T(8,128)(2,1)S(1)}, bf16[80,2048]{1,0:T(8,128)(2,1)S(1)}, u32[]{:S(2)}, u32[]{:S(2)}) %collective-permute-start.2) | collective-permute-done | bytes 327712 | tf_op jit(solution)/shard_map/ppermute | solution.py:293
  18.0 0.9 maximum_select_fusion
  18.9 0.0 all-gather.4.cloned.1.call-update
  19.0 1.3 copy.31
  20.3 6.9 %all-to-all-start = ((bf16[8,256,256]{2,1,0:T(8,128)(2,1)}), bf16[8,256,256]{2,1,0:T(8,128)(2,1)S(1)}, u32[]{:S(2)}, u32[]{:S(2)}) async-start(bf16[8,256,256]{2,1,0:T(8,128)(2,1)} %bitcast.3), calls=%async_computation | async-start | bytes 2097152 | tf_op jit(solution)/shard_map/all_to_all | solution.py:299
  27.2 0.0 all-gather.8.cloned.1.call-start
  27.3 0.5 collective-permute-start
  27.8 16.1 %collective-permute-done = bf16[64,2048]{1,0:T(8,128)(2,1)S(1)} collective-permute-done((bf16[64,2048]{1,0:T(8,128)(2,1)S(1)}, bf16[64,2048]{1,0:T(8,128)(2,1)S(1)}, u32[]{:S(2)}, u32[]{:S(2)}) %collective-permute-start) | collective-permute-done | bytes 262176 | tf_op jit(solution)/shard_map/ppermute | solution.py:300
  44.0 0.6 all-to-all-done.own_ref.refs_19_
  44.5 0.9 maximum_select_fusion.2
  45.4 0.0 all-gather.8.cloned.1.call-update
  45.4 0.7 collective-permute-start.1
  46.1 2.5 %copy.44 = bf16[1,128,16,256]{3,1,2,0:T(8,128)(2,1)} copy(bf16[1,128,16,256]{3,2,1,0:T(8,128)(2,1)} %param.7) | data formatting | bytes 2097152 | tf_op args[0]
  48.7 9.0 %all-to-all-start.1 = ((bf16[16,128,256]{2,1,0:T(8,128)(2,1)}), bf16[16,128,256]{2,1,0:T(8,128)(2,1)}, u32[]{:S(2)}, u32[]{:S(2)}) async-start(bf16[16,128,256]{2,1,0:T(8,128)(2,1)} %bitcast.52), calls=%async_computation.1 | async-start | bytes 2097152 | tf_op jit(solution)/shard_map/all_to_all | solution.py:305
  57.7 0.0 all-gather.6.cloned.1.call-start
  57.8 1.5 collective-permute-start.3
  59.2 12.4 %copy.34 = bf16[2048,2048]{0,1:T(8,128)(2,1)} copy(bf16[2048,2048]{1,0:T(8,128)(2,1)} %grid_ref.1) | data formatting | bytes 16777216 | tf_op args[2]
  71.6 0.0 collective-permute-done.1.mate_ref
  71.6 0.0 all-gather.4.cloned.1.call-done.refs_0_.refs_1_.refs_2_.refs_3_.refs_4_.refs_5_.refs_6_.refs_7_
  71.6 5.6 %forward_pass.1 = bf16[16,8,2,16,128]{4,3,2,1,0:T(8,128)(2,1)} custom-call(bf16[8,256,256]{2,1,0:T(8,128)(2,1)S(1)} %all-to-all-done.own_ref.refs_19_, bf16[8,256,256]{2,1,0:T(8,128)(2,1)S(1)} %collective-permute-done.1.mate_ref, bf16[8,2,80,2048]{3,2,1,0:T(8,128)(2,1)} %all-gather.4.cloned.1.call-done.refs_0_.refs_1_.refs_2_.refs_3_.refs_4_.refs_5_.refs_6_.refs_7_, ...), custom_call_target="tpu_custom_call" | custom-call | flops 2147483648 | bytes 8388608 | tf_op jit(solution)/shard_map/forward_pass/pallas_call | solution.py:72
  77.2 0.0 all-to-all-done.1
  77.3 0.0 collective-permute-done.3
  77.3 0.9 maximum_select_fusion.1
  78.1 0.0 all-gather.6.cloned.1.call-update
  78.1 11.0 %all-to-all-start.2 = ((bf16[128,32,128]{2,1,0:T(8,128)(2,1)}), bf16[128,32,128]{2,1,0:T(8,128)(2,1)S(1)}, u32[]{:S(2)}, u32[]{:S(2)}) async-start(bf16[128,32,128]{2,1,0:T(8,128)(2,1)} %bitcast.12), calls=%async_computation.2 | async-start | bytes 2097152 | tf_op jit(solution)/shard_map/all_to_all | solution.py:313
  89.2 1.3 slice_bitcast_fusion
  90.5 1.0 copy.35
  91.5 2.3 %copy.36 = bf16[256,2048]{0,1:T(8,128)(2,1)} copy(bf16[256,2048]{1,0:T(8,128)(2,1)} %bitcast.53) | data formatting | bytes 2097152 | tf_op jit(solution)/shard_map/reshape | solution.py:318
  93.8 7.0 %fusion.across_ref = bf16[2048,256]{1,0:T(8,128)(2,1)} fusion(bf16[2048,2048]{1,0:T(8,128)(2,1)} %param.8, bf16[2048,256]{1,0:T(8,128)(2,1)} %bitcast.19), kind=kOutput, calls=%fused_computation.1 | convolution fusion | flops 2148007936 | bytes 10485760 | tf_op jit(solution)/shard_map/dot_general | solution.py:14
  100.8 6.0 %all-to-all-done.2 = bf16[128,32,128]{2,1,0:T(8,128)(2,1)S(1)} async-done(((bf16[128,32,128]{2,1,0:T(8,128)(2,1)}), bf16[128,32,128]{2,1,0:T(8,128)(2,1)S(1)}, u32[]{:S(2)}, u32[]{:S(2)}) %all-to-all-start.2) | async-done | bytes 1048608 | tf_op jit(solution)/shard_map/all_to_all | solution.py:313
  106.8 11.4 %middle_pass.1 = bf16[2048,512]{1,0:T(8,128)(2,1)} custom-call(bf16[64,2,2,16,128]{4,3,2,1,0:T(8,128)(2,1)S(1)} %bitcast.48, bf16[2048,2048]{1,0:T(8,128)(2,1)} %grid_ref.1, bf16[2048,2048]{1,0:T(8,128)(2,1)} %bitcast.49, bf16[2048,256]{1,0:T(8,128)(2,1)} %bitcast.54, bf16[2048,256]{1,0:T(8,128)(2,1)} %fusion.across_ref), custom_call_target="tpu_custom_call" | custom-call | flops 4294967296 | bytes 22020096 | tf_op jit(solution)/shard_map/middle_pass/pallas_call | solution.py:122
  118.2 7.1 %all-to-all-start.3 = ((bf16[128,16,512]{2,1,0:T(8,128)(2,1)}), bf16[128,16,512]{2,1,0:T(8,128)(2,1)}, u32[]{:S(2)}, u32[]{:S(2)}) async-start(bf16[128,16,512]{2,1,0:T(8,128)(2,1)} %bitcast.50), calls=%async_computation.3 | async-start | bytes 4194304 | tf_op jit(solution)/shard_map/all_to_all | solution.py:320
  125.3 0.0 all-gather.8.cloned.1.call-done.ham_ref
  125.4 1.2 copy-done.2
  126.6 5.8 %applied_pass.1 = (f32[256,1024]{1,0:T(8,128)S(1)}, bf16[256,1024]{1,0:T(8,128)(2,1)}) custom-call(bf16[8,256,256]{2,1,0:T(8,128)(2,1)S(1)} %all-to-all-done.own_ref.refs_19_, bf16[8,256,256]{2,1,0:T(8,128)(2,1)S(1)} %copy-done.2, bf16[8,2,64,2048]{3,2,1,0:T(8,128)(2,1)} %all-gather.8.cloned.1.call-done.ham_ref), custom_call_target="tpu_custom_call" | custom-call | flops 2147483648 | bytes 8388608 | tf_op jit(solution)/shard_map/applied_pass/pallas_call | solution.py:162
  132.4 1.4 collective-permute-start.4
  133.8 0.1 broadcast_in_dim.12
  133.8 0.1 broadcast_in_dim_reshape.4.refs_20_
  133.9 0.1 fusion.1.refs_21_
  134.1 26.0 %collective-permute-done.4.refs_18_ = bf16[256,1024]{1,0:T(8,128)(2,1)S(1)} collective-permute-done((bf16[256,1024]{1,0:T(8,128)(2,1)}, bf16[256,1024]{1,0:T(8,128)(2,1)S(1)}, u32[]{:S(2)}, u32[]{:S(2)}) %collective-permute-start.4) | collective-permute-done | bytes 524320 | tf_op jit(solution)/shard_map/ppermute | solution.py:325
  160.1 0.0 all-to-all-done.3
  160.1 8.0 %final_pass.1 = bf16[16,16,2048]{2,1,0:T(8,128)(2,1)} custom-call(s32[1]{0:T(128)} %bitcast.half_ref, bf16[16,8,16,512]{3,2,1,0:T(8,128)(2,1)} %bitcast.22.near_ref.far_ref.refs_16_, bf16[16,8,16,512]{3,2,1,0:T(8,128)(2,1)} %bitcast.22.near_ref.far_ref.refs_16_, ...), custom_call_target="tpu_custom_call" | custom-call | flops 2415919104 | bytes 14680064 | tf_op jit(solution)/shard_map/final_pass/pallas_call | solution.py:232
  (12 shorter events, 0.1 us)
Async XLA Ops:
  6.5 20.7 %copy-start = (bf16[128,2048]{1,0:T(8,128)(2,1)S(1)}, bf16[128,2048]{1,0:T(8,128)(2,1)}, u32[]{:S(2)}) copy-start(bf16[128,2048]{1,0:T(8,128)(2,1)} %param.10) | copy-start | bytes 1572868
  6.5 12.4 %copy-start.3 = (bf16[1,128,16,256]{3,2,1,0:T(8,128)(2,1)S(1)}, bf16[1,128,16,256]{3,2,1,0:T(8,128)(2,1)}, u32[]{:S(2)}) copy-start(bf16[1,128,16,256]{3,2,1,0:T(8,128)(2,1)} %param.7) | copy-start | bytes 3145732
  6.5 65.1 %all-gather.4.cloned.1.call-start = ((), (), s32[]{:S(2)}) async-start(), calls=%async_computation.4 | async-start | bytes 5898240 | tf_op jit(solution)/shard_map/all_gather | solution.py:288
  8.8 9.2 %collective-permute-start.2 = (bf16[80,2048]{1,0:T(8,128)(2,1)S(1)}, bf16[80,2048]{1,0:T(8,128)(2,1)S(1)}, u32[]{:S(2)}, u32[]{:S(2)}) collective-permute-start(bf16[80,2048]{1,0:T(8,128)(2,1)S(1)} %get-tuple-element.27), channel_id=1, source_target_pairs={{0,64},{8,72},{16,80},{24,88},{32,96},{40,104},{48,112},{56,120},{... | collective-permute-start | bytes 983048 | tf_op jit(solution)/shard_map/ppermute | solution.py:293
  20.3 24.2 %all-to-all-start = ((bf16[8,256,256]{2,1,0:T(8,128)(2,1)}), bf16[8,256,256]{2,1,0:T(8,128)(2,1)S(1)}, u32[]{:S(2)}, u32[]{:S(2)}) async-start(bf16[8,256,256]{2,1,0:T(8,128)(2,1)} %bitcast.3), calls=%async_computation | async-start | bytes 2097152 | tf_op jit(solution)/shard_map/all_to_all | solution.py:299
  27.2 98.1 %all-gather.8.cloned.1.call-start = ((), (), s32[]{:S(2)}) async-start(), calls=%async_computation.6 | async-start | bytes 4718592 | tf_op jit(solution)/shard_map/all_gather | solution.py:288
  27.3 16.6 %collective-permute-start = (bf16[64,2048]{1,0:T(8,128)(2,1)S(1)}, bf16[64,2048]{1,0:T(8,128)(2,1)S(1)}, u32[]{:S(2)}, u32[]{:S(2)}) collective-permute-start(bf16[64,2048]{1,0:T(8,128)(2,1)S(1)} %constant_dynamic-slice_fusion), channel_id=1, source_target_pairs={{0,64},{8,72},{16,80},{24,88},{32,96},{40,104},{48,112},{56,120},{... | collective-permute-start | bytes 786440 | tf_op jit(solution)/shard_map/ppermute | solution.py:300
  45.4 26.1 %collective-permute-start.1 = (bf16[8,256,256]{2,1,0:T(8,128)(2,1)S(1)}, bf16[8,256,256]{2,1,0:T(8,128)(2,1)S(1)}, u32[]{:S(2)}, u32[]{:S(2)}) collective-permute-start(bf16[8,256,256]{2,1,0:T(8,128)(2,1)S(1)} %all-to-all-done.own_ref.refs_19_), channel_id=1, source_target_pairs={{0,1},{1,0},{2,3},{3,2},{4,5},{5,4},{6,7},{7,6},{8,9},{9,8},{10,11... | collective-permute-start | bytes 3145736 | tf_op jit(solution)/shard_map/ppermute | solution.py:304
  48.7 28.6 %all-to-all-start.1 = ((bf16[16,128,256]{2,1,0:T(8,128)(2,1)}), bf16[16,128,256]{2,1,0:T(8,128)(2,1)}, u32[]{:S(2)}, u32[]{:S(2)}) async-start(bf16[16,128,256]{2,1,0:T(8,128)(2,1)} %bitcast.52), calls=%async_computation.1 | async-start | bytes 2097152 | tf_op jit(solution)/shard_map/all_to_all | solution.py:305
  57.7 102.4 %all-gather.6.cloned.1.call-start = ((), (), s32[]{:S(2)}) async-start(), calls=%async_computation.5 | async-start | bytes 4718592 | tf_op jit(solution)/shard_map/all_gather | solution.py:288
  57.8 19.5 %collective-permute-start.3 = (bf16[64,2048]{1,0:T(8,128)(2,1)S(1)}, bf16[64,2048]{1,0:T(8,128)(2,1)S(1)}, u32[]{:S(2)}, u32[]{:S(2)}) collective-permute-start(bf16[64,2048]{1,0:T(8,128)(2,1)S(1)} %get-tuple-element.24), channel_id=1, source_target_pairs={{0,64},{8,72},{16,80},{24,88},{32,96},{40,104},{48,112},{56,120},{... | collective-permute-start | bytes 786440 | tf_op jit(solution)/shard_map/ppermute | solution.py:303
  71.6 5.6 %copy-start.1 = (bf16[8,256,256]{2,1,0:T(8,128)(2,1)}, bf16[8,256,256]{2,1,0:T(8,128)(2,1)S(1)}, u32[]{:S(2)}) copy-start(bf16[8,256,256]{2,1,0:T(8,128)(2,1)S(1)} %collective-permute-done.1.mate_ref) | copy-start | bytes 3145732
  78.1 28.6 %all-to-all-start.2 = ((bf16[128,32,128]{2,1,0:T(8,128)(2,1)}), bf16[128,32,128]{2,1,0:T(8,128)(2,1)S(1)}, u32[]{:S(2)}, u32[]{:S(2)}) async-start(bf16[128,32,128]{2,1,0:T(8,128)(2,1)} %bitcast.12), calls=%async_computation.2 | async-start | bytes 2097152 | tf_op jit(solution)/shard_map/all_to_all | solution.py:313
  118.2 15.6 %copy-start.4 = (f32[16]{0:T(128)S(1)}, f32[16]{0:T(128)}, u32[]{:S(2)}) copy-start(f32[16]{0:T(128)} %param.13) | copy-start | bytes 196
  118.2 41.9 %all-to-all-start.3 = ((bf16[128,16,512]{2,1,0:T(8,128)(2,1)}), bf16[128,16,512]{2,1,0:T(8,128)(2,1)}, u32[]{:S(2)}, u32[]{:S(2)}) async-start(bf16[128,16,512]{2,1,0:T(8,128)(2,1)} %bitcast.50), calls=%async_computation.3 | async-start | bytes 4194304 | tf_op jit(solution)/shard_map/all_to_all | solution.py:320
  125.4 1.2 copy-start.2
  132.4 27.7 %collective-permute-start.4 = (bf16[256,1024]{1,0:T(8,128)(2,1)}, bf16[256,1024]{1,0:T(8,128)(2,1)S(1)}, u32[]{:S(2)}, u32[]{:S(2)}) collective-permute-start(bf16[256,1024]{1,0:T(8,128)(2,1)} %get-tuple-element.22), channel_id=1, source_target_pairs={{0,1},{1,0},{2,3},{3,2},{4,5},{5,4},{6,7},{7,6},{8,9},{9,8},{10,11... | collective-permute-start | bytes 1572872 | tf_op jit(solution)/shard_map/ppermute | solution.py:325
Sparse Core Ops, SparseCore 0:
  19.1 40.6 all-gather.3
  61.5 32.1 all-gather.7
  95.4 32.1 all-gather.5

commit v14 on v13

--- a/solution.py
+++ b/solution.py
@@ -290,19 +290,23 @@
     pieces = grid_two.reshape(n_narrow, 2, piece, cols)
     near = lax.dynamic_index_in_dim(pieces, half, 1, False).reshape(share, cols)
     near = jnp.concatenate([near, pair_potential.T.astype(jnp.bfloat16)], 0)
-    near = gather(both_sides(near, lax.ppermute(near, "wide", across_y)))
+    other_near = lax.ppermute(near, "wide", across_y)
+    to_rows = local.reshape(n_narrow, inner, states, width).swapaxes(1, 2)
+    to_rows = to_rows.reshape(n_narrow, height, width)
+    to_states = jnp.swapaxes(local, 0, 1)
+    other_near, to_rows, to_states = lax.optimization_barrier((other_near, to_rows, to_states))
+    near = gather(both_sides(near, other_near))
 
     far = lax.dynamic_index_in_dim(pieces, 1 - half, 1, False).reshape(share, cols)
     stay = lax.dynamic_slice_in_dim(ham_two, half * share, share, 0)
 
-    own = local.reshape(n_narrow, inner, states, width).swapaxes(1, 2)
-    own = lax.all_to_all(own.reshape(n_narrow, height, width), "narrow", 0, 0, tiled=True)
+    own = lax.all_to_all(to_rows, "narrow", 0, 0, tiled=True)
     other_stay = lax.ppermute(stay, "wide", across_y)
     own, other_stay = lax.optimization_barrier((own, other_stay))
     half_ham = gather(both_sides(stay, other_stay))
     other_far = lax.ppermute(far, "wide", across_y)
     mate = lax.ppermute(own, "narrow", narrow_pairs)
-    by_state = lax.all_to_all(jnp.swapaxes(local, 0, 1), "wide", 0, 0, tiled=True)
+    by_state = lax.all_to_all(to_states, "wide", 0, 0, tiled=True)
 
     turned = lax.optimization_barrier(grid_one.T)
     values = forward_pass(own, mate, near, states, piece)

time: 176 us -> 182 us (1.034)
  waiting for transfers between devices: 55.8 us -> 60.2 us
  starting transfers between devices: 40.4 us -> 42.6 us
    all_gather x3, waiting for transfers between devices: 0.03 us -> 8.28 us  [gather(): lax.all_gather(value, 'wide', axis=0, tiled=False, axis_index_groups=memb...]
    ppermute x1, waiting for transfers between devices: 7.02 us -> 3.15 us  [on_device(): other_near = lax.ppermute(near, 'wide', across_y)]
    all_to_all x1, starting transfers between devices: 11 us -> 13.6 us  [on_device(): lax.all_to_all(values.reshape(n_wide * n_narrow, 2 * inner, width // 2),...]
  transfers between devices with their start and end apart: 12 -> 12, of which waited for: 5 -> 6; matrix products, arithmetic and copies ran while one was open for 17% -> 17% of each run, Pallas kernels for 13% -> 13%
where the time goes in v14:
time: 182 us; the launch traced here: 181 us
  waiting for transfers between devices  60.2 us (33%)
  starting transfers between devices  42.6 us (23%)
  Pallas kernels  30.6 us (17%)
  local copies, waits for them, and re-layouts  23.4 us (13%)
  between operations  13.3 us (7%)
  matrix products  6.98 us (4%)
  other arithmetic  3.9 us (2%)
    ppermute x1, waiting for transfers between devices, on_device(): moved = lax.ppermute(moved, 'narrow', narrow_pairs)  26.1 us
    ppermute x1, waiting for transfers between devices, on_device(): other_stay = lax.ppermute(stay, 'wide', across_y)  16.1 us
    unnamed x12, local copies, waits for them, and re-layouts  16.1 us
    all_to_all x1, starting transfers between devices, on_device(): lax.all_to_all(values.reshape(n_wide * n_narrow, 2 * inner, width // 2),...  13.6 us
    pallas_call x1, Pallas kernels, middle_pass(): pl.pallas_call(middle_step, grid=(2 * half,), in_specs=[pl.BlockSpec(valu...  11.3 us
    all_to_all x1, starting transfers between devices, on_device(): by_state = lax.all_to_all(to_states, 'wide', 0, 0, tiled=True)  9.03 us
    all_gather x3, waiting for transfers between devices, gather(): lax.all_gather(value, 'wide', axis=0, tiled=False, axis_index_groups=memb...  8.28 us
    pallas_call x1, Pallas kernels, final_pass(): pl.pallas_call(final_step, grid_spec=pltpu.PrefetchScalarGridSpec(num_sca...  7.97 us
  transfers between devices with their start and end apart: 12, of which 6 were waited for; matrix products, arithmetic and copies ran while one was open for 17% of the time, Pallas kernels for 13%

profile of v14, /device:TPU:1, one launch (start us, length us, event | category | flops | bytes accessed | tf_op | source)
XLA Modules:
  0.0 181.0 jit_solution(1525270394729231001)
XLA Ops:
  6.5 0.0 copy-start
  6.5 1.0 convert_bitcast_fusion
  7.6 1.1 dynamic-slice_bitcast_fusion.2
  8.7 0.1 fusion.6
  8.8 2.2 %collective-permute-start = (bf16[80,2048]{1,0:T(8,128)(2,1)S(1)}, bf16[80,2048]{1,0:T(8,128)(2,1)S(1)}, u32[]{:S(2)}, u32[]{:S(2)}) collective-permute-start(bf16[80,2048]{1,0:T(8,128)(2,1)S(1)} %get-tuple-element.33), channel_id=1, source_target_pairs={{0,64},{8,72},{16,80},{24,88},{32,96},{40,104},{48,112},{56,120},{... | collective-permute-start | bytes 983048 | tf_op jit(solution)/shard_map/ppermute | solution.py:293
  11.0 2.5 %copy.44 = bf16[1,128,16,256]{3,1,2,0:T(8,128)(2,1)} copy(bf16[1,128,16,256]{3,2,1,0:T(8,128)(2,1)} %param.7) | data formatting | bytes 2097152 | tf_op args[0]
  13.5 1.3 copy.32
  14.8 3.2 %collective-permute-done = bf16[80,2048]{1,0:T(8,128)(2,1)S(1)} collective-permute-done((bf16[80,2048]{1,0:T(8,128)(2,1)S(1)}, bf16[80,2048]{1,0:T(8,128)(2,1)S(1)}, u32[]{:S(2)}, u32[]{:S(2)}) %collective-permute-start) | collective-permute-done | bytes 327712 | tf_op jit(solution)/shard_map/ppermute | solution.py:293
  18.0 0.9 maximum_select_fusion
  18.9 0.0 all-gather.4.cloned.1.call-update
  19.0 6.9 %all-to-all-start = ((bf16[8,256,256]{2,1,0:T(8,128)(2,1)}), bf16[8,256,256]{2,1,0:T(8,128)(2,1)S(1)}, u32[]{:S(2)}, u32[]{:S(2)}) async-start(bf16[8,256,256]{2,1,0:T(8,128)(2,1)} %bitcast.6), calls=%async_computation | async-start | bytes 2097152 | tf_op jit(solution)/shard_map/all_to_all | solution.py:303
  25.9 0.0 all-gather.8.cloned.1.call-start
  26.0 0.5 collective-permute-start.1
  26.5 16.1 %collective-permute-done.1 = bf16[64,2048]{1,0:T(8,128)(2,1)S(1)} collective-permute-done((bf16[64,2048]{1,0:T(8,128)(2,1)S(1)}, bf16[64,2048]{1,0:T(8,128)(2,1)S(1)}, u32[]{:S(2)}, u32[]{:S(2)}) %collective-permute-start.1) | collective-permute-done | bytes 262176 | tf_op jit(solution)/shard_map/ppermute | solution.py:304
  42.6 0.6 all-to-all-done.own_ref.refs_19_
  43.2 0.9 maximum_select_fusion.2
  44.1 0.0 all-gather.8.cloned.1.call-update
  44.1 0.7 collective-permute-start.2
  44.8 9.0 %all-to-all-start.1 = ((bf16[16,128,256]{2,1,0:T(8,128)(2,1)}), bf16[16,128,256]{2,1,0:T(8,128)(2,1)}, u32[]{:S(2)}, u32[]{:S(2)}) async-start(bf16[16,128,256]{2,1,0:T(8,128)(2,1)} %bitcast.52), calls=%async_computation.1 | async-start | bytes 2097152 | tf_op jit(solution)/shard_map/all_to_all | solution.py:309
  53.8 0.0 all-gather.6.cloned.1.call-start
  53.9 1.5 collective-permute-start.3
  55.3 12.3 %copy.34 = bf16[2048,2048]{0,1:T(8,128)(2,1)} copy(bf16[2048,2048]{1,0:T(8,128)(2,1)} %grid_ref.1) | data formatting | bytes 16777216 | tf_op args[2]
  67.7 0.0 collective-permute-done.2.mate_ref
  67.7 0.0 all-gather.4.cloned.1.call-done.refs_0_.refs_1_.refs_2_.refs_3_.refs_4_.refs_5_.refs_6_.refs_7_
  67.7 5.6 %forward_pass.1 = bf16[16,8,2,16,128]{4,3,2,1,0:T(8,128)(2,1)} custom-call(bf16[8,256,256]{2,1,0:T(8,128)(2,1)S(1)} %all-to-all-done.own_ref.refs_19_, bf16[8,256,256]{2,1,0:T(8,128)(2,1)S(1)} %collective-permute-done.2.mate_ref, bf16[8,2,80,2048]{3,2,1,0:T(8,128)(2,1)} %all-gather.4.cloned.1.call-done.refs_0_.refs_1_.refs_2_.refs_3_.refs_4_.refs_5_.refs_6_.refs_7_, ...), custom_call_target="tpu_custom_call" | custom-call | flops 2147483648 | bytes 8388608 | tf_op jit(solution)/shard_map/forward_pass/pallas_call | solution.py:72
  73.3 0.0 all-to-all-done.1
  73.3 0.0 collective-permute-done.3
  73.3 0.9 maximum_select_fusion.1
  74.2 0.0 all-gather.6.cloned.1.call-update
  74.2 13.6 %all-to-all-start.2 = ((bf16[128,32,128]{2,1,0:T(8,128)(2,1)}), bf16[128,32,128]{2,1,0:T(8,128)(2,1)S(1)}, u32[]{:S(2)}, u32[]{:S(2)}) async-start(bf16[128,32,128]{2,1,0:T(8,128)(2,1)} %bitcast.12), calls=%async_computation.2 | async-start | bytes 2097152 | tf_op jit(solution)/shard_map/all_to_all | solution.py:317
  87.8 1.3 slice_bitcast_fusion
  89.2 1.0 copy.35
  90.2 2.3 %copy.36 = bf16[256,2048]{0,1:T(8,128)(2,1)} copy(bf16[256,2048]{1,0:T(8,128)(2,1)} %bitcast.53) | data formatting | bytes 2097152 | tf_op jit(solution)/shard_map/reshape | solution.py:322
  92.5 7.0 %fusion.across_ref = bf16[2048,256]{1,0:T(8,128)(2,1)} fusion(bf16[2048,2048]{1,0:T(8,128)(2,1)} %param.8, bf16[2048,256]{1,0:T(8,128)(2,1)} %bitcast.19), kind=kOutput, calls=%fused_computation.1 | convolution fusion | flops 2148007936 | bytes 10485760 | tf_op jit(solution)/shard_map/dot_general | solution.py:14
  99.5 5.9 %all-to-all-done.2 = bf16[128,32,128]{2,1,0:T(8,128)(2,1)S(1)} async-done(((bf16[128,32,128]{2,1,0:T(8,128)(2,1)}), bf16[128,32,128]{2,1,0:T(8,128)(2,1)S(1)}, u32[]{:S(2)}, u32[]{:S(2)}) %all-to-all-start.2) | async-done | bytes 1048608 | tf_op jit(solution)/shard_map/all_to_all | solution.py:317
  105.4 11.3 %middle_pass.1 = bf16[2048,512]{1,0:T(8,128)(2,1)} custom-call(bf16[64,2,2,16,128]{4,3,2,1,0:T(8,128)(2,1)S(1)} %bitcast.48, bf16[2048,2048]{1,0:T(8,128)(2,1)} %grid_ref.1, bf16[2048,2048]{1,0:T(8,128)(2,1)} %bitcast.49, bf16[2048,256]{1,0:T(8,128)(2,1)} %bitcast.54, bf16[2048,256]{1,0:T(8,128)(2,1)} %fusion.across_ref), custom_call_target="tpu_custom_call" | custom-call | flops 4294967296 | bytes 22020096 | tf_op jit(solution)/shard_map/middle_pass/pallas_call | solution.py:122
  116.7 6.7 %all-to-all-start.3 = ((bf16[128,16,512]{2,1,0:T(8,128)(2,1)}), bf16[128,16,512]{2,1,0:T(8,128)(2,1)}, u32[]{:S(2)}, u32[]{:S(2)}) async-start(bf16[128,16,512]{2,1,0:T(8,128)(2,1)} %bitcast.50), calls=%async_computation.3 | async-start | bytes 4194304 | tf_op jit(solution)/shard_map/all_to_all | solution.py:324
  123.4 0.0 all-gather.8.cloned.1.call-done.ham_ref
  123.5 1.2 copy-done.2
  124.7 5.8 %applied_pass.1 = (f32[256,1024]{1,0:T(8,128)S(1)}, bf16[256,1024]{1,0:T(8,128)(2,1)}) custom-call(bf16[8,256,256]{2,1,0:T(8,128)(2,1)S(1)} %all-to-all-done.own_ref.refs_19_, bf16[8,256,256]{2,1,0:T(8,128)(2,1)S(1)} %copy-done.2, bf16[8,2,64,2048]{3,2,1,0:T(8,128)(2,1)} %all-gather.8.cloned.1.call-done.ham_ref), custom_call_target="tpu_custom_call" | custom-call | flops 2147483648 | bytes 8388608 | tf_op jit(solution)/shard_map/applied_pass/pallas_call | solution.py:162
  130.5 1.4 collective-permute-start.4
  131.9 0.1 broadcast_in_dim.12
  131.9 0.1 broadcast_in_dim_reshape.4.refs_20_
  132.1 0.1 fusion.1.refs_21_
  132.2 26.1 %collective-permute-done.4.refs_18_ = bf16[256,1024]{1,0:T(8,128)(2,1)S(1)} collective-permute-done((bf16[256,1024]{1,0:T(8,128)(2,1)}, bf16[256,1024]{1,0:T(8,128)(2,1)S(1)}, u32[]{:S(2)}, u32[]{:S(2)}) %collective-permute-start.4) | collective-permute-done | bytes 524320 | tf_op jit(solution)/shard_map/ppermute | solution.py:329
  158.3 0.0 all-to-all-done.3
  158.3 8.2 %all-gather.6.cloned.1.call-done.refs_8_.refs_9_.refs_10_.refs_11_.refs_12_.refs_13_.refs_14_.refs_15_ = bf16[8,2,64,2048]{3,2,1,0:T(8,128)(2,1)} async-done(((bf16[1,2,64,2048]{3,2,1,0:T(8,128)(2,1)}), bf16[8,2,64,2048]{3,2,1,0:T(8,128)(2,1)}) %all-gather.6.cloned.1.call-update) | async-done | bytes 4194320 | tf_op jit(solution)/shard_map/all_gather | solution.py:288
  166.5 8.0 %final_pass.1 = bf16[16,16,2048]{2,1,0:T(8,128)(2,1)} custom-call(s32[1]{0:T(128)} %bitcast.half_ref, bf16[16,8,16,512]{3,2,1,0:T(8,128)(2,1)} %bitcast.22.near_ref.far_ref.refs_16_, bf16[16,8,16,512]{3,2,1,0:T(8,128)(2,1)} %bitcast.22.near_ref.far_ref.refs_16_, ...), custom_call_target="tpu_custom_call" | custom-call | flops 2415919104 | bytes 14680064 | tf_op jit(solution)/shard_map/final_pass/pallas_call | solution.py:232
  (12 shorter events, 0.1 us)
Async XLA Ops:
  6.5 19.4 %copy-start = (bf16[128,2048]{1,0:T(8,128)(2,1)S(1)}, bf16[128,2048]{1,0:T(8,128)(2,1)}, u32[]{:S(2)}) copy-start(bf16[128,2048]{1,0:T(8,128)(2,1)} %param.10) | copy-start | bytes 1572868
  6.5 6.9 %copy-start.3 = (bf16[1,128,16,256]{3,2,1,0:T(8,128)(2,1)S(1)}, bf16[1,128,16,256]{3,2,1,0:T(8,128)(2,1)}, u32[]{:S(2)}) copy-start(bf16[1,128,16,256]{3,2,1,0:T(8,128)(2,1)} %param.7) | copy-start | bytes 3145732
  6.5 61.2 %all-gather.4.cloned.1.call-start = ((), (), s32[]{:S(2)}) async-start(), calls=%async_computation.4 | async-start | bytes 5898240 | tf_op jit(solution)/shard_map/all_gather | solution.py:288
  8.8 9.2 %collective-permute-start = (bf16[80,2048]{1,0:T(8,128)(2,1)S(1)}, bf16[80,2048]{1,0:T(8,128)(2,1)S(1)}, u32[]{:S(2)}, u32[]{:S(2)}) collective-permute-start(bf16[80,2048]{1,0:T(8,128)(2,1)S(1)} %get-tuple-element.33), channel_id=1, source_target_pairs={{0,64},{8,72},{16,80},{24,88},{32,96},{40,104},{48,112},{56,120},{... | collective-permute-start | bytes 983048 | tf_op jit(solution)/shard_map/ppermute | solution.py:293
  19.0 24.2 %all-to-all-start = ((bf16[8,256,256]{2,1,0:T(8,128)(2,1)}), bf16[8,256,256]{2,1,0:T(8,128)(2,1)S(1)}, u32[]{:S(2)}, u32[]{:S(2)}) async-start(bf16[8,256,256]{2,1,0:T(8,128)(2,1)} %bitcast.6), calls=%async_computation | async-start | bytes 2097152 | tf_op jit(solution)/shard_map/all_to_all | solution.py:303
  25.9 97.6 %all-gather.8.cloned.1.call-start = ((), (), s32[]{:S(2)}) async-start(), calls=%async_computation.6 | async-start | bytes 4718592 | tf_op jit(solution)/shard_map/all_gather | solution.py:288
  26.0 16.6 %collective-permute-start.1 = (bf16[64,2048]{1,0:T(8,128)(2,1)S(1)}, bf16[64,2048]{1,0:T(8,128)(2,1)S(1)}, u32[]{:S(2)}, u32[]{:S(2)}) collective-permute-start(bf16[64,2048]{1,0:T(8,128)(2,1)S(1)} %constant_dynamic-slice_fusion), channel_id=1, source_target_pairs={{0,64},{8,72},{16,80},{24,88},{32,96},{40,104},{48,112},{56,120},{... | collective-permute-start | bytes 786440 | tf_op jit(solution)/shard_map/ppermute | solution.py:304
  44.1 23.6 %collective-permute-start.2 = (bf16[8,256,256]{2,1,0:T(8,128)(2,1)S(1)}, bf16[8,256,256]{2,1,0:T(8,128)(2,1)S(1)}, u32[]{:S(2)}, u32[]{:S(2)}) collective-permute-start(bf16[8,256,256]{2,1,0:T(8,128)(2,1)S(1)} %all-to-all-done.own_ref.refs_19_), channel_id=1, source_target_pairs={{0,1},{1,0},{2,3},{3,2},{4,5},{5,4},{6,7},{7,6},{8,9},{9,8},{10,11... | collective-permute-start | bytes 3145736 | tf_op jit(solution)/shard_map/ppermute | solution.py:308
  44.8 28.5 %all-to-all-start.1 = ((bf16[16,128,256]{2,1,0:T(8,128)(2,1)}), bf16[16,128,256]{2,1,0:T(8,128)(2,1)}, u32[]{:S(2)}, u32[]{:S(2)}) async-start(bf16[16,128,256]{2,1,0:T(8,128)(2,1)} %bitcast.52), calls=%async_computation.1 | async-start | bytes 2097152 | tf_op jit(solution)/shard_map/all_to_all | solution.py:309
  53.8 112.7 %all-gather.6.cloned.1.call-start = ((), (), s32[]{:S(2)}) async-start(), calls=%async_computation.5 | async-start | bytes 4718592 | tf_op jit(solution)/shard_map/all_gather | solution.py:288
  53.9 19.5 %collective-permute-start.3 = (bf16[64,2048]{1,0:T(8,128)(2,1)S(1)}, bf16[64,2048]{1,0:T(8,128)(2,1)S(1)}, u32[]{:S(2)}, u32[]{:S(2)}) collective-permute-start(bf16[64,2048]{1,0:T(8,128)(2,1)S(1)} %get-tuple-element.30), channel_id=1, source_target_pairs={{0,64},{8,72},{16,80},{24,88},{32,96},{40,104},{48,112},{56,120},{... | collective-permute-start | bytes 786440 | tf_op jit(solution)/shard_map/ppermute | solution.py:307
  67.7 5.6 %copy-start.1 = (bf16[8,256,256]{2,1,0:T(8,128)(2,1)}, bf16[8,256,256]{2,1,0:T(8,128)(2,1)S(1)}, u32[]{:S(2)}) copy-start(bf16[8,256,256]{2,1,0:T(8,128)(2,1)S(1)} %collective-permute-done.2.mate_ref) | copy-start | bytes 3145732
  74.2 31.2 %all-to-all-start.2 = ((bf16[128,32,128]{2,1,0:T(8,128)(2,1)}), bf16[128,32,128]{2,1,0:T(8,128)(2,1)S(1)}, u32[]{:S(2)}, u32[]{:S(2)}) async-start(bf16[128,32,128]{2,1,0:T(8,128)(2,1)} %bitcast.12), calls=%async_computation.2 | async-start | bytes 2097152 | tf_op jit(solution)/shard_map/all_to_all | solution.py:317
  116.7 15.2 %copy-start.4 = (f32[16]{0:T(128)S(1)}, f32[16]{0:T(128)}, u32[]{:S(2)}) copy-start(f32[16]{0:T(128)} %param.13) | copy-start | bytes 196
  116.7 41.6 %all-to-all-start.3 = ((bf16[128,16,512]{2,1,0:T(8,128)(2,1)}), bf16[128,16,512]{2,1,0:T(8,128)(2,1)}, u32[]{:S(2)}, u32[]{:S(2)}) async-start(bf16[128,16,512]{2,1,0:T(8,128)(2,1)} %bitcast.50), calls=%async_computation.3 | async-start | bytes 4194304 | tf_op jit(solution)/shard_map/all_to_all | solution.py:324
  123.5 1.2 copy-start.2
  130.5 27.8 %collective-permute-start.4 = (bf16[256,1024]{1,0:T(8,128)(2,1)}, bf16[256,1024]{1,0:T(8,128)(2,1)S(1)}, u32[]{:S(2)}, u32[]{:S(2)}) collective-permute-start(bf16[256,1024]{1,0:T(8,128)(2,1)} %get-tuple-element.28), channel_id=1, source_target_pairs={{0,1},{1,0},{2,3},{3,2},{4,5},{5,4},{6,7},{7,6},{8,9},{9,8},{10,11... | collective-permute-start | bytes 1572872 | tf_op jit(solution)/shard_map/ppermute | solution.py:329
Sparse Core Ops, SparseCore 0:
  19.1 40.7 all-gather.3
  61.5 48.6 all-gather.7
  111.9 54.5 all-gather.5

commit v15 on v13

--- a/solution.py
+++ b/solution.py
@@ -298,11 +298,12 @@
     own = local.reshape(n_narrow, inner, states, width).swapaxes(1, 2)
     own = lax.all_to_all(own.reshape(n_narrow, height, width), "narrow", 0, 0, tiled=True)
     other_stay = lax.ppermute(stay, "wide", across_y)
-    own, other_stay = lax.optimization_barrier((own, other_stay))
+    to_states = jnp.swapaxes(local, 0, 1)
+    own, other_stay, to_states = lax.optimization_barrier((own, other_stay, to_states))
     half_ham = gather(both_sides(stay, other_stay))
     other_far = lax.ppermute(far, "wide", across_y)
     mate = lax.ppermute(own, "narrow", narrow_pairs)
-    by_state = lax.all_to_all(jnp.swapaxes(local, 0, 1), "wide", 0, 0, tiled=True)
+    by_state = lax.all_to_all(to_states, "wide", 0, 0, tiled=True)
 
     turned = lax.optimization_barrier(grid_one.T)
     values = forward_pass(own, mate, near, states, piece)

time: 176 us -> 176 us (level)
  starting transfers between devices: 40.4 us -> 42.9 us
    all_to_all x1, starting transfers between devices: 11 us -> 13.5 us  [on_device(): lax.all_to_all(values.reshape(n_wide * n_narrow, 2 * inner, width // 2),...]
  transfers between devices with their start and end apart: 12 -> 12, of which waited for: 5 -> 5; matrix products, arithmetic and copies ran while one was open for 17% -> 16% of each run, Pallas kernels for 13% -> 13%
where the time goes in v15:
time: 176 us; the launch traced here: 175 us
  waiting for transfers between devices  54.5 us (31%)
  starting transfers between devices  42.9 us (24%)
  Pallas kernels  30.9 us (18%)
  local copies, waits for them, and re-layouts  22.2 us (13%)
  between operations  13.3 us (8%)
  matrix products  6.96 us (4%)
  other arithmetic  3.9 us (2%)
    ppermute x1, waiting for transfers between devices, on_device(): moved = lax.ppermute(moved, 'narrow', narrow_pairs)  26 us
    unnamed x12, local copies, waits for them, and re-layouts  14.9 us
    ppermute x1, waiting for transfers between devices, on_device(): other_stay = lax.ppermute(stay, 'wide', across_y)  14.8 us
    all_to_all x1, starting transfers between devices, on_device(): lax.all_to_all(values.reshape(n_wide * n_narrow, 2 * inner, width // 2),...  13.5 us
    pallas_call x1, Pallas kernels, middle_pass(): pl.pallas_call(middle_step, grid=(2 * half,), in_specs=[pl.BlockSpec(valu...  11.5 us
    all_to_all x1, starting transfers between devices, on_device(): by_state = lax.all_to_all(to_states, 'wide', 0, 0, tiled=True)  9.03 us
    pallas_call x1, Pallas kernels, final_pass(): pl.pallas_call(final_step, grid_spec=pltpu.PrefetchScalarGridSpec(num_sca...  7.97 us
    all_to_all x1, starting transfers between devices, on_device(): lax.all_to_all(pair.reshape(n_wide * n_narrow, inner, 2 * width), both, 0...  7.17 us
  transfers between devices with their start and end apart: 12, of which 5 were waited for; matrix products, arithmetic and copies ran while one was open for 16% of the time, Pallas kernels for 13%

profile of v15, /device:TPU:1, one launch (start us, length us, event | category | flops | bytes accessed | tf_op | source)
XLA Modules:
  0.0 174.7 jit_solution(13065519357864172209)
XLA Ops:
  6.5 0.0 copy-start
  6.5 1.0 convert_bitcast_fusion
  7.6 1.1 dynamic-slice_bitcast_fusion.2
  8.7 0.1 fusion.6
  8.8 2.2 %collective-permute-start.2 = (bf16[80,2048]{1,0:T(8,128)(2,1)S(1)}, bf16[80,2048]{1,0:T(8,128)(2,1)S(1)}, u32[]{:S(2)}, u32[]{:S(2)}) collective-permute-start(bf16[80,2048]{1,0:T(8,128)(2,1)S(1)} %get-tuple-element.29), channel_id=1, source_target_pairs={{0,64},{8,72},{16,80},{24,88},{32,96},{40,104},{48,112},{56,120},{... | collective-permute-start | bytes 983048 | tf_op jit(solution)/shard_map/ppermute | solution.py:293
  11.0 7.0 %collective-permute-done.2 = bf16[80,2048]{1,0:T(8,128)(2,1)S(1)} collective-permute-done((bf16[80,2048]{1,0:T(8,128)(2,1)S(1)}, bf16[80,2048]{1,0:T(8,128)(2,1)S(1)}, u32[]{:S(2)}, u32[]{:S(2)}) %collective-permute-start.2) | collective-permute-done | bytes 327712 | tf_op jit(solution)/shard_map/ppermute | solution.py:293
  18.0 0.9 maximum_select_fusion
  18.9 0.0 all-gather.4.cloned.1.call-update
  19.0 1.3 copy.31
  20.3 6.9 %all-to-all-start = ((bf16[8,256,256]{2,1,0:T(8,128)(2,1)}), bf16[8,256,256]{2,1,0:T(8,128)(2,1)S(1)}, u32[]{:S(2)}, u32[]{:S(2)}) async-start(bf16[8,256,256]{2,1,0:T(8,128)(2,1)} %bitcast.53), calls=%async_computation | async-start | bytes 2097152 | tf_op jit(solution)/shard_map/all_to_all | solution.py:299
  27.2 0.0 all-gather.8.cloned.1.call-start
  27.3 0.5 collective-permute-start
  27.8 1.3 copy.44
  29.1 14.8 %collective-permute-done = bf16[64,2048]{1,0:T(8,128)(2,1)S(1)} collective-permute-done((bf16[64,2048]{1,0:T(8,128)(2,1)S(1)}, bf16[64,2048]{1,0:T(8,128)(2,1)S(1)}, u32[]{:S(2)}, u32[]{:S(2)}) %collective-permute-start) | collective-permute-done | bytes 262176 | tf_op jit(solution)/shard_map/ppermute | solution.py:300
  44.0 0.6 all-to-all-done.own_ref.refs_19_
  44.5 0.9 maximum_select_fusion.2
  45.4 0.0 all-gather.8.cloned.1.call-update
  45.4 0.7 collective-permute-start.1
  46.1 9.0 %all-to-all-start.1 = ((bf16[16,128,256]{2,1,0:T(8,128)(2,1)}), bf16[16,128,256]{2,1,0:T(8,128)(2,1)}, u32[]{:S(2)}, u32[]{:S(2)}) async-start(bf16[16,128,256]{2,1,0:T(8,128)(2,1)} %bitcast.52), calls=%async_computation.1 | async-start | bytes 2097152 | tf_op jit(solution)/shard_map/all_to_all | solution.py:306
  55.2 0.0 all-gather.6.cloned.1.call-start
  55.2 1.5 collective-permute-start.3
  56.7 12.4 %copy.34 = bf16[2048,2048]{0,1:T(8,128)(2,1)} copy(bf16[2048,2048]{1,0:T(8,128)(2,1)} %grid_ref.1) | data formatting | bytes 16777216 | tf_op args[2]
  69.0 0.0 collective-permute-done.1.mate_ref
  69.0 0.0 all-gather.4.cloned.1.call-done.refs_0_.refs_1_.refs_2_.refs_3_.refs_4_.refs_5_.refs_6_.refs_7_
  69.1 5.7 %forward_pass.1 = bf16[16,8,2,16,128]{4,3,2,1,0:T(8,128)(2,1)} custom-call(bf16[8,256,256]{2,1,0:T(8,128)(2,1)S(1)} %all-to-all-done.own_ref.refs_19_, bf16[8,256,256]{2,1,0:T(8,128)(2,1)S(1)} %collective-permute-done.1.mate_ref, bf16[8,2,80,2048]{3,2,1,0:T(8,128)(2,1)} %all-gather.4.cloned.1.call-done.refs_0_.refs_1_.refs_2_.refs_3_.refs_4_.refs_5_.refs_6_.refs_7_, ...), custom_call_target="tpu_custom_call" | custom-call | flops 2147483648 | bytes 8388608 | tf_op jit(solution)/shard_map/forward_pass/pallas_call | solution.py:72
  74.8 0.0 copy-done.1
  74.8 0.0 all-to-all-done.1
  74.8 0.0 collective-permute-done.3
  74.8 0.9 maximum_select_fusion.1
  75.7 0.0 all-gather.6.cloned.1.call-update
  75.7 13.5 %all-to-all-start.2 = ((bf16[128,32,128]{2,1,0:T(8,128)(2,1)}), bf16[128,32,128]{2,1,0:T(8,128)(2,1)S(1)}, u32[]{:S(2)}, u32[]{:S(2)}) async-start(bf16[128,32,128]{2,1,0:T(8,128)(2,1)} %bitcast.12), calls=%async_computation.2 | async-start | bytes 2097152 | tf_op jit(solution)/shard_map/all_to_all | solution.py:314
  89.2 1.3 slice_bitcast_fusion
  90.5 1.0 copy.35
  91.5 2.3 %copy.36 = bf16[256,2048]{0,1:T(8,128)(2,1)} copy(bf16[256,2048]{1,0:T(8,128)(2,1)} %bitcast.54) | data formatting | bytes 2097152 | tf_op jit(solution)/shard_map/reshape | solution.py:319
  93.8 7.0 %fusion.across_ref = bf16[2048,256]{1,0:T(8,128)(2,1)} fusion(bf16[2048,2048]{1,0:T(8,128)(2,1)} %param.8, bf16[2048,256]{1,0:T(8,128)(2,1)} %bitcast.19), kind=kOutput, calls=%fused_computation.1 | convolution fusion | flops 2148007936 | bytes 10485760 | tf_op jit(solution)/shard_map/dot_general | solution.py:14
  100.8 6.0 %all-to-all-done.2 = bf16[128,32,128]{2,1,0:T(8,128)(2,1)S(1)} async-done(((bf16[128,32,128]{2,1,0:T(8,128)(2,1)}), bf16[128,32,128]{2,1,0:T(8,128)(2,1)S(1)}, u32[]{:S(2)}, u32[]{:S(2)}) %all-to-all-start.2) | async-done | bytes 1048608 | tf_op jit(solution)/shard_map/all_to_all | solution.py:314
  106.8 11.5 %middle_pass.1 = bf16[2048,512]{1,0:T(8,128)(2,1)} custom-call(bf16[64,2,2,16,128]{4,3,2,1,0:T(8,128)(2,1)S(1)} %bitcast.48, bf16[2048,2048]{1,0:T(8,128)(2,1)} %grid_ref.1, bf16[2048,2048]{1,0:T(8,128)(2,1)} %bitcast.49, bf16[2048,256]{1,0:T(8,128)(2,1)} %bitcast.55, bf16[2048,256]{1,0:T(8,128)(2,1)} %fusion.across_ref), custom_call_target="tpu_custom_call" | custom-call | flops 4294967296 | bytes 22020096 | tf_op jit(solution)/shard_map/middle_pass/pallas_call | solution.py:122
  118.2 7.2 %all-to-all-start.3 = ((bf16[128,16,512]{2,1,0:T(8,128)(2,1)}), bf16[128,16,512]{2,1,0:T(8,128)(2,1)}, u32[]{:S(2)}, u32[]{:S(2)}) async-start(bf16[128,16,512]{2,1,0:T(8,128)(2,1)} %bitcast.50), calls=%async_computation.3 | async-start | bytes 4194304 | tf_op jit(solution)/shard_map/all_to_all | solution.py:321
  125.4 0.0 all-gather.8.cloned.1.call-done.ham_ref
  125.4 1.2 copy-done.2
  126.7 5.8 %applied_pass.1 = (f32[256,1024]{1,0:T(8,128)S(1)}, bf16[256,1024]{1,0:T(8,128)(2,1)}) custom-call(bf16[8,256,256]{2,1,0:T(8,128)(2,1)S(1)} %all-to-all-done.own_ref.refs_19_, bf16[8,256,256]{2,1,0:T(8,128)(2,1)S(1)} %copy-done.2, bf16[8,2,64,2048]{3,2,1,0:T(8,128)(2,1)} %all-gather.8.cloned.1.call-done.ham_ref), custom_call_target="tpu_custom_call" | custom-call | flops 2147483648 | bytes 8388608 | tf_op jit(solution)/shard_map/applied_pass/pallas_call | solution.py:162
  132.4 1.4 collective-permute-start.4
  133.8 0.1 broadcast_in_dim.12
  133.9 0.1 broadcast_in_dim_reshape.4.refs_20_
  134.0 0.1 fusion.1.refs_21_
  134.1 26.0 %collective-permute-done.4.refs_18_ = bf16[256,1024]{1,0:T(8,128)(2,1)S(1)} collective-permute-done((bf16[256,1024]{1,0:T(8,128)(2,1)}, bf16[256,1024]{1,0:T(8,128)(2,1)S(1)}, u32[]{:S(2)}, u32[]{:S(2)}) %collective-permute-start.4) | collective-permute-done | bytes 524320 | tf_op jit(solution)/shard_map/ppermute | solution.py:326
  160.1 0.0 all-to-all-done.3
  160.1 8.0 %final_pass.1 = bf16[16,16,2048]{2,1,0:T(8,128)(2,1)} custom-call(s32[1]{0:T(128)} %bitcast.half_ref, bf16[16,8,16,512]{3,2,1,0:T(8,128)(2,1)} %bitcast.22.near_ref.far_ref.refs_16_, bf16[16,8,16,512]{3,2,1,0:T(8,128)(2,1)} %bitcast.22.near_ref.far_ref.refs_16_, ...), custom_call_target="tpu_custom_call" | custom-call | flops 2415919104 | bytes 14680064 | tf_op jit(solution)/shard_map/final_pass/pallas_call | solution.py:232
  (12 shorter events, 0.1 us)
Async XLA Ops:
  6.5 20.7 %copy-start = (bf16[128,2048]{1,0:T(8,128)(2,1)S(1)}, bf16[128,2048]{1,0:T(8,128)(2,1)}, u32[]{:S(2)}) copy-start(bf16[128,2048]{1,0:T(8,128)(2,1)} %param.10) | copy-start | bytes 1572868
  6.5 12.4 %copy-start.3 = (bf16[1,128,16,256]{3,2,1,0:T(8,128)(2,1)S(1)}, bf16[1,128,16,256]{3,2,1,0:T(8,128)(2,1)}, u32[]{:S(2)}) copy-start(bf16[1,128,16,256]{3,2,1,0:T(8,128)(2,1)} %param.7) | copy-start | bytes 3145732
  6.5 62.5 %all-gather.4.cloned.1.call-start = ((), (), s32[]{:S(2)}) async-start(), calls=%async_computation.4 | async-start | bytes 5898240 | tf_op jit(solution)/shard_map/all_gather | solution.py:288
  8.8 9.2 %collective-permute-start.2 = (bf16[80,2048]{1,0:T(8,128)(2,1)S(1)}, bf16[80,2048]{1,0:T(8,128)(2,1)S(1)}, u32[]{:S(2)}, u32[]{:S(2)}) collective-permute-start(bf16[80,2048]{1,0:T(8,128)(2,1)S(1)} %get-tuple-element.29), channel_id=1, source_target_pairs={{0,64},{8,72},{16,80},{24,88},{32,96},{40,104},{48,112},{56,120},{... | collective-permute-start | bytes 983048 | tf_op jit(solution)/shard_map/ppermute | solution.py:293
  20.3 24.2 %all-to-all-start = ((bf16[8,256,256]{2,1,0:T(8,128)(2,1)}), bf16[8,256,256]{2,1,0:T(8,128)(2,1)S(1)}, u32[]{:S(2)}, u32[]{:S(2)}) async-start(bf16[8,256,256]{2,1,0:T(8,128)(2,1)} %bitcast.53), calls=%async_computation | async-start | bytes 2097152 | tf_op jit(solution)/shard_map/all_to_all | solution.py:299
  27.2 98.2 %all-gather.8.cloned.1.call-start = ((), (), s32[]{:S(2)}) async-start(), calls=%async_computation.6 | async-start | bytes 4718592 | tf_op jit(solution)/shard_map/all_gather | solution.py:288
  27.3 16.6 %collective-permute-start = (bf16[64,2048]{1,0:T(8,128)(2,1)S(1)}, bf16[64,2048]{1,0:T(8,128)(2,1)S(1)}, u32[]{:S(2)}, u32[]{:S(2)}) collective-permute-start(bf16[64,2048]{1,0:T(8,128)(2,1)S(1)} %constant_dynamic-slice_fusion), channel_id=1, source_target_pairs={{0,64},{8,72},{16,80},{24,88},{32,96},{40,104},{48,112},{56,120},{... | collective-permute-start | bytes 786440 | tf_op jit(solution)/shard_map/ppermute | solution.py:300
  45.4 23.6 %collective-permute-start.1 = (bf16[8,256,256]{2,1,0:T(8,128)(2,1)S(1)}, bf16[8,256,256]{2,1,0:T(8,128)(2,1)S(1)}, u32[]{:S(2)}, u32[]{:S(2)}) collective-permute-start(bf16[8,256,256]{2,1,0:T(8,128)(2,1)S(1)} %all-to-all-done.own_ref.refs_19_), channel_id=1, source_target_pairs={{0,1},{1,0},{2,3},{3,2},{4,5},{5,4},{6,7},{7,6},{8,9},{9,8},{10,11... | collective-permute-start | bytes 3145736 | tf_op jit(solution)/shard_map/ppermute | solution.py:305
  46.1 28.6 %all-to-all-start.1 = ((bf16[16,128,256]{2,1,0:T(8,128)(2,1)}), bf16[16,128,256]{2,1,0:T(8,128)(2,1)}, u32[]{:S(2)}, u32[]{:S(2)}) async-start(bf16[16,128,256]{2,1,0:T(8,128)(2,1)} %bitcast.52), calls=%async_computation.1 | async-start | bytes 2097152 | tf_op jit(solution)/shard_map/all_to_all | solution.py:306
  55.2 105.0 %all-gather.6.cloned.1.call-start = ((), (), s32[]{:S(2)}) async-start(), calls=%async_computation.5 | async-start | bytes 4718592 | tf_op jit(solution)/shard_map/all_gather | solution.py:288
  55.2 19.6 %collective-permute-start.3 = (bf16[64,2048]{1,0:T(8,128)(2,1)S(1)}, bf16[64,2048]{1,0:T(8,128)(2,1)S(1)}, u32[]{:S(2)}, u32[]{:S(2)}) collective-permute-start(bf16[64,2048]{1,0:T(8,128)(2,1)S(1)} %get-tuple-element.26), channel_id=1, source_target_pairs={{0,64},{8,72},{16,80},{24,88},{32,96},{40,104},{48,112},{56,120},{... | collective-permute-start | bytes 786440 | tf_op jit(solution)/shard_map/ppermute | solution.py:304
  69.0 5.7 %copy-start.1 = (bf16[8,256,256]{2,1,0:T(8,128)(2,1)}, bf16[8,256,256]{2,1,0:T(8,128)(2,1)S(1)}, u32[]{:S(2)}) copy-start(bf16[8,256,256]{2,1,0:T(8,128)(2,1)S(1)} %collective-permute-done.1.mate_ref) | copy-start | bytes 3145732
  75.7 31.1 %all-to-all-start.2 = ((bf16[128,32,128]{2,1,0:T(8,128)(2,1)}), bf16[128,32,128]{2,1,0:T(8,128)(2,1)S(1)}, u32[]{:S(2)}, u32[]{:S(2)}) async-start(bf16[128,32,128]{2,1,0:T(8,128)(2,1)} %bitcast.12), calls=%async_computation.2 | async-start | bytes 2097152 | tf_op jit(solution)/shard_map/all_to_all | solution.py:314
  118.2 15.6 %copy-start.4 = (f32[16]{0:T(128)S(1)}, f32[16]{0:T(128)}, u32[]{:S(2)}) copy-start(f32[16]{0:T(128)} %param.13) | copy-start | bytes 196
  118.2 41.9 %all-to-all-start.3 = ((bf16[128,16,512]{2,1,0:T(8,128)(2,1)}), bf16[128,16,512]{2,1,0:T(8,128)(2,1)}, u32[]{:S(2)}, u32[]{:S(2)}) async-start(bf16[128,16,512]{2,1,0:T(8,128)(2,1)} %bitcast.50), calls=%async_computation.3 | async-start | bytes 4194304 | tf_op jit(solution)/shard_map/all_to_all | solution.py:321
  125.4 1.2 copy-start.2
  132.4 27.7 %collective-permute-start.4 = (bf16[256,1024]{1,0:T(8,128)(2,1)}, bf16[256,1024]{1,0:T(8,128)(2,1)S(1)}, u32[]{:S(2)}, u32[]{:S(2)}) collective-permute-start(bf16[256,1024]{1,0:T(8,128)(2,1)} %get-tuple-element.24), channel_id=1, source_target_pairs={{0,1},{1,0},{2,3},{3,2},{4,5},{5,4},{6,7},{7,6},{8,9},{9,8},{10,11... | collective-permute-start | bytes 1572872 | tf_op jit(solution)/shard_map/ppermute | solution.py:326
Sparse Core Ops, SparseCore 0:
  19.1 40.6 all-gather.3
  61.5 32.4 all-gather.7
  95.7 32.1 all-gather.5
